TPU v7x, 128 devices: a whole 4x4x4 slice. The times are simulated.
128 devices in a mesh: px: 16 (over y, x), py: 8 (over z, core).
Axes of the slice: x: 4, y: 4, z: 4, core: 2. Of those that a mesh axis runs over, the one named last changes fastest.
Arguments:
- node_latents: bfloat16 [256, 160, 512], P('px', 'py'), may hold values from -6 to 6
- fine_edges: bfloat16 [256, 160, 6, 512], P('px', 'py'), may hold values from -6 to 6
- long_edges: bfloat16 [20480, 512], P(('px', 'py')), may hold values from -6 to 6
- neighbours: int32 [256, 160, 6], P('px', 'py'), may hold values from 0 to 7, as said below
- coarse_slots: int32 [2560], P(('px', 'py')), may hold values from 0 to 319, as said below
- long_senders: int32 [20480], P(('px', 'py')), may hold values from 0 to 2559
- long_receivers: int32 [20480], P(('px', 'py')), may hold values from 0 to 2559, as said below
- edge_inner: bfloat16 [2, 1536, 512], replicated, may hold values from -0.15625 to 0.15625
- edge_outer: bfloat16 [2, 512, 512], replicated, may hold values from -0.25 to 0.25
- edge_gain: float32 [2, 512], replicated, may hold values from 0.5 to 1.5
- node_inner: bfloat16 [2, 1024, 512], replicated, may hold values from -0.1875 to 0.1875
- node_outer: bfloat16 [2, 512, 512], replicated, may hold values from -0.25 to 0.25
- node_gain: float32 [2, 512], replicated, may hold values from 0.5 to 1.5
Outputs:
- new_nodes: bfloat16 [256, 160, 512], P('px', 'py')
- new_fine: bfloat16 [256, 160, 6, 512], P('px', 'py')
- new_long: bfloat16 [20480, 512], P(('px', 'py'))
Inputs may be any that keep to these rules, and one draw needn't show every extreme that they name: `neighbours`: the 6 codes of one node are different. `coarse_slots`: the 20 entries of one device's block are different. `long_receivers`: among the 160 long edges of one device, at most 3 have receivers c with the same c // 20, and on every device some such group has exactly 3.
All inputs are finite; a program needn't handle non-finite values.
Results may differ from a plain program's by a relative error of at most 0.0095.
Values may be sent and summed in bfloat16 or wider, within the bound.
No kernel may reach another device: no remote copies, remote signals or barrier semaphores. Data moves between devices by JAX's collectives and lax.ppermute only.
A program may use at most 128 MiB of HBM per device.

v0:
```python
import jax
import jax.numpy as jnp
from jax import lax
from jax.sharding import PartitionSpec as P

EPSILON = 1e-05


def with_halo(cells, sides, width):
    for axis, dim in sides:
        count = lax.axis_size(axis)
        head = lax.slice_in_dim(cells, 0, width, axis=dim)
        tail = lax.slice_in_dim(cells, cells.shape[dim] - width, cells.shape[dim], axis=dim)
        cells = jnp.concatenate(
            [
                lax.ppermute(tail, axis, [(i, (i + 1) % count) for i in range(count)]),
                cells,
                lax.ppermute(head, axis, [((i + 1) % count, i) for i in range(count)]),
            ],
            axis=dim,
        )
    return cells


def layer_norm(values, gains):
    center = values - jnp.mean(values, axis=-1, keepdims=True)
    spread = jnp.mean(center * center, axis=-1, keepdims=True)
    return center * lax.rsqrt(spread + EPSILON) * gains


def finish(before, inner_sum, outer, gains):
    hidden = jax.nn.silu(inner_sum).astype(jnp.bfloat16)
    output = jnp.dot(hidden, outer, preferred_element_type=jnp.float32)
    return (before.astype(jnp.float32) + layer_norm(output, gains)).astype(jnp.bfloat16)


def extended_index(neighbours, patch_columns):
    shifted_code = neighbours + (neighbours >= 4).astype(jnp.int32)
    rows_here = lax.broadcasted_iota(jnp.int32, neighbours.shape, 0)
    cols_here = lax.broadcasted_iota(jnp.int32, neighbours.shape, 1)
    row_step = shifted_code // 3 - 1
    column_step = shifted_code % 3 - 1
    return ((rows_here + 1 + row_step) * (patch_columns + 2) + cols_here + 1 + column_step).reshape(
        -1
    )


def owner_sums(receivers, messages, coarse_count, devices):
    long_count, features = messages.shape
    capacity = (2 * long_count + devices - 1) // devices
    owners = receivers // coarse_count
    matches = (owners[:, None] == lax.iota(jnp.int32, devices)[None, :]).astype(jnp.int32)
    before = jnp.cumsum(matches, axis=0) - matches
    ranking = jnp.sum(before * matches, axis=1)
    placed = owners * capacity + ranking
    bucket = jnp.zeros((devices * capacity, features), jnp.bfloat16).at[placed].set(messages)
    labels = (
        jnp.full((devices * capacity,), coarse_count, jnp.int32)
        .at[placed]
        .set(receivers % coarse_count)
    )
    arrived, arrived_tags = (
        lax.all_to_all(
            bucket.reshape(devices, capacity, features),
            ("px", "py"),
            split_axis=0,
            concat_axis=0,
            tiled=True,
        ),
        lax.all_to_all(
            labels.astype(jnp.bfloat16).reshape(devices, capacity),
            ("px", "py"),
            split_axis=0,
            concat_axis=0,
            tiled=True,
        ),
    )
    tag_values = arrived_tags.reshape(-1).astype(jnp.int32)
    chooser = (tag_values[:, None] == lax.iota(jnp.int32, coarse_count)[None, :]).astype(
        jnp.bfloat16
    )
    return lax.dot_general(
        chooser,
        arrived.reshape(-1, features),
        (((0,), (0,)), ((), ())),
        preferred_element_type=jnp.float32,
    )


def shards(
    node_latents,
    fine_edges,
    long_edges,
    neighbours,
    coarse_slots,
    long_senders,
    long_receivers,
    edge_inner,
    edge_outer,
    edge_gain,
    node_inner,
    node_outer,
    node_gain,
):
    patch_rows, patch_columns, features = node_latents.shape
    degree = fine_edges.shape[2]
    coarse_count = coarse_slots.shape[0]
    layers = edge_inner.shape[0]
    devices = lax.axis_size("px") * lax.axis_size("py")
    patch_cells = patch_rows * patch_columns
    sender_index = extended_index(neighbours, patch_columns)
    latents = node_latents.reshape(patch_cells, features)
    fine_rows = fine_edges.reshape(patch_cells * degree, features)
    long_rows = long_edges
    for layer_index in range(layers):
        edge_part = edge_inner[layer_index, :features]
        send_part = edge_inner[layer_index, features : 2 * features]
        receive_part = edge_inner[layer_index, 2 * features :]
        own_coarse = jnp.take(latents, coarse_slots, axis=0)
        coarse = lax.all_gather(own_coarse, ("px", "py"), axis=0, tiled=True)
        padded = with_halo(
            latents.reshape(patch_rows, patch_columns, features), (("px", 0), ("py", 1)), 1
        )
        sender_terms = jnp.dot(
            padded.reshape(-1, features), send_part, preferred_element_type=jnp.float32
        )
        receiver_terms = jnp.dot(latents, receive_part, preferred_element_type=jnp.float32)
        inner_sum = jnp.dot(fine_rows, edge_part, preferred_element_type=jnp.float32) + jnp.take(
            sender_terms, sender_index, axis=0
        )
        inner_sum = (
            inner_sum.reshape(patch_cells, degree, -1) + receiver_terms[:, None, :]
        ).reshape(patch_cells * degree, -1)
        fine_rows = finish(fine_rows, inner_sum, edge_outer[layer_index], edge_gain[layer_index])
        long_sum = jnp.dot(long_rows, edge_part, preferred_element_type=jnp.float32)
        long_sum = long_sum + jnp.dot(
            jnp.take(coarse, long_senders, axis=0), send_part, preferred_element_type=jnp.float32
        )
        long_sum = long_sum + jnp.dot(
            jnp.take(coarse, long_receivers, axis=0),
            receive_part,
            preferred_element_type=jnp.float32,
        )
        long_rows = finish(long_rows, long_sum, edge_outer[layer_index], edge_gain[layer_index])
        coarse_sum = owner_sums(long_receivers, long_rows, coarse_count, devices)
        incoming = jnp.sum(
            fine_rows.reshape(patch_cells, degree, features), axis=1, dtype=jnp.float32
        )
        incoming = incoming.at[coarse_slots].add(coarse_sum).astype(jnp.bfloat16)
        node_sum = jnp.dot(
            latents, node_inner[layer_index, :features], preferred_element_type=jnp.float32
        )
        node_sum = node_sum + jnp.dot(
            incoming, node_inner[layer_index, features:], preferred_element_type=jnp.float32
        )
        latents = finish(latents, node_sum, node_outer[layer_index], node_gain[layer_index])
    return (
        latents.reshape(patch_rows, patch_columns, features),
        fine_rows.reshape(fine_edges.shape),
        long_rows,
    )


def solution(mesh):
    in_specs = (
        P("px", "py", None),
        P("px", "py", None, None),
        P(("px", "py"), None),
        P("px", "py", None),
        P(("px", "py")),
        P(("px", "py")),
        P(("px", "py")),
        P(),
        P(),
        P(),
        P(),
        P(),
        P(),
    )
    out_specs = (P("px", "py", None), P("px", "py", None, None), P(("px", "py"), None))
    return jax.shard_map(shards, mesh=mesh, in_specs=in_specs, out_specs=out_specs, check_vma=False)
```

profile of v0, /device:TPU:1, one launch (start us, length us, event | category | flops | bytes accessed | tf_op | source)
XLA Modules:
  0.0 250.8 jit_solution(7708276694184682371)
XLA Ops:
  7.3 1.8 fusion.141
  9.1 5.8 %collective-permute-start.1 = (bf16[1,20,512]{2,0,1:T(2,128)(2,1)}, bf16[1,20,512]{2,0,1:T(2,128)(2,1)S(1)}, u32[]{:S(2)}, u32[]{:S(2)}) collective-permute-start(bf16[1,20,512]{2,0,1:T(2,128)(2,1)} %get-tuple-element.22), channel_id=1, source_target_pairs={{8,0},{16,8},{24,16},{32,24},{40,32},{48,40},{56,48},{64,56},{72,6... | collective-permute-start | bytes 61448 | tf_op jit(solution)/shard_map/ppermute | solution.py:18
  22.0 10.6 %all-to-all-start = ((bf16[128,1,3]{2,1,0:T(2,128)(2,1)}), bf16[128,1,3]{2,1,0:T(2,128)(2,1)S(1)}, u32[]{:S(2)}, u32[]{:S(2)}) async-start(bf16[128,1,3]{2,1,0:T(2,128)(2,1)} %all_to_all.17), calls=%async_computation | async-start | bytes 131072 | tf_op jit(solution)/shard_map/all_to_all | solution.py:70
  37.4 2.3 fusion.33
  39.6 2.2 fusion.42
  41.9 2.7 %copy.29 = bf16[16,20,6,512]{3,2,1,0:T(8,128)(2,1)S(1)} copy(bf16[16,20,6,512]{3,0,2,1:T(8,128)(2,1)} %param.20) | data formatting | bytes 3932160 | tf_op args[1]
  44.6 2.1 reshape.173
  46.6 4.1 %add.211 = f32[320,6,512]{2,1,0:T(8,128)} broadcast(f32[320,512]{1,0:T(8,128)} %fusion.33), dimensions={0,2} | broadcast | bytes 4587520 | tf_op jit(solution)/shard_map/add | solution.py:132
  50.7 5.6 %add.212 = f32[1920,512]{1,0:T(8,128)} reshape(f32[320,6,512]{2,1,0:T(8,128)} %add.211) | data formatting | bytes 7864320 | tf_op jit(solution)/shard_map/add | solution.py:132
  58.6 1.5 collective-permute-done.3
  62.7 6.2 %gather_fusion = f32[1920,512]{1,0:T(8,128)} fusion(f32[396,512]{1,0:T(8,128)S(1)} %fusion.36, s32[2048]{0:T(1024)S(1)} %pad_clamp_fusion), kind=kCustom, calls=%fused_computation.clone | custom fusion | bytes 7872000 | tf_op jit(solution)/shard_map/jit(_take)/gather | solution.py:128
  68.9 8.3 %fusion.144 = (f32[1920]{0:T(1024)S(1)}, f32[1920,512]{1,0:T(8,128)}) fusion(bf16[2,512,512]{2,1,0:T(8,128)(2,1)} %param.27, f32[1920,512]{1,0:T(8,128)} %add.212, f32[1920,512]{1,0:T(8,128)} %gather_fusion, bf16[1920,512]{1,0:T(8,128)(2,1)S(1)} %copy-done.2, pred[1920]{0:T(1024)(128)(4,1)S(1)} %copy-done.27, bf16[2,1536,512]{2,1,0:T(8,128)(2,1)} %param.26), kind=kOutput, calls=%fused_computation.210 | convolution fusion | flops 2022111360 | bytes 14820736 | tf_op jit(solution)/shard_map/dot_general | solution.py:33
  77.2 2.8 %multiply_reduce_fusion.1 = f32[1920]{0:T(1024)S(1)} fusion(f32[1920,512]{1,0:T(8,128)} %get-tuple-element.31, f32[1920]{0:T(1024)S(1)} %broadcast_multiply_fusion.1), kind=kLoop, calls=%fused_computation.21 | loop fusion | flops 2947200 | bytes 3947520 | tf_op jit(solution)/shard_map/reduce_sum | solution.py:27
  80.0 7.5 %all-gather.5.cloned.1.call-done = bf16[128,20,512]{2,1,0:T(8,128)(2,1)} async-done(((bf16[1,20,512]{2,1,0:T(8,128)(2,1)}), bf16[128,20,512]{2,1,0:T(8,128)(2,1)}) %all-gather.5.cloned.1.call-update) | async-done | bytes 2621456 | tf_op jit(solution)/shard_map/all_gather | solution.py:120
  87.5 3.6 %reshape.308 = bf16[2560,512]{1,0:T(8,128)(2,1)S(1)} reshape(bf16[128,20,512]{2,1,0:T(8,128)(2,1)} %all-gather.5.cloned.1.call-done) | data formatting | bytes 5242880
  91.2 1.6 gather_fusion.2
  92.8 1.6 gather_fusion.3
  95.8 1.9 fusion.147
  98.1 1.4 scatter_custom_fusion.1
  100.6 5.3 %all-to-all-start.1 = ((bf16[128,3,512]{2,1,0:T(4,128)(2,1)}), bf16[128,3,512]{2,1,0:T(4,128)(2,1)S(1)}, u32[]{:S(2)}, u32[]{:S(2)}) async-start(bf16[128,3,512]{2,1,0:T(4,128)(2,1)} %reshape.178), calls=%async_computation.1 | async-start | bytes 1048576 | tf_op jit(solution)/shard_map/all_to_all | solution.py:63
  106.1 3.4 %add_convert_fusion.1 = bf16[1920,512]{1,0:T(8,128)(2,1)S(1)} fusion(bf16[1920,512]{1,0:T(8,128)(2,1)} %reshape.173, f32[1920,512]{1,0:T(8,128)} %get-tuple-element.31, f32[512]{0:T(512)S(1)} %bitcast.134, f32[1920]{0:T(1024)S(1)} %add_rsqrt_fusion.1, f32[1920]{0:T(1024)S(1)} %broadcast_multiply_fusion.1), kind=kLoop, calls=%fused_computation.20 | loop fusion | flops 5898240 | bytes 7881728 | tf_op jit(solution)/shard_map/convert_element_type | solution.py:34
  109.5 2.8 %reshape.186 = f32[320,6,512]{2,1,0:T(8,128)} reshape(bf16[1920,512]{1,0:T(8,128)(2,1)S(1)} %add_convert_fusion.1) | data formatting | bytes 5898240 | tf_op jit(solution)/shard_map/convert_element_type | solution.py:146
  112.4 5.0 %reduce_sum.141 = f32[320,512]{1,0:T(8,128)} reduce(f32[320,6,512]{2,1,0:T(8,128)} %reshape.186, f32[]{:T(128)} %constant.121.clone.1), dimensions={1}, to_apply=%region_2.4 | reduce | flops 819200 | bytes 4587524 | tf_op jit(solution)/shard_map/reduce_sum | solution.py:146
  117.3 2.1 all-to-all-done.1
  121.8 2.6 %scatter_fusion = f32[320,512]{1,0:T(8,128)} fusion(f32[320,512]{1,0:T(8,128)} %reduce_sum.141, s32[20]{0:T(128)S(1)} %copy-done.19, f32[20,512]{1,0:T(8,128)S(1)} %fusion.89), kind=kCustom, calls=%fused_computation.10 | custom fusion | flops 10240 | bytes 122960 | tf_op jit(solution)/shard_map/scatter-add | solution.py:149
  124.4 2.3 fusion.152
  128.5 2.0 fusion.20
  131.0 2.2 fusion.24
  133.3 4.5 %collective-permute-start.5 = (bf16[1,20,512]{2,1,0:T(8,128)(2,1)S(1)}, bf16[1,20,512]{2,1,0:T(8,128)(2,1)S(1)}, u32[]{:S(2)}, u32[]{:S(2)}) collective-permute-start(bf16[1,20,512]{2,1,0:T(8,128)(2,1)S(1)} %get-tuple-element.19), channel_id=1, source_target_pairs={{8,0},{16,8},{24,16},{32,24},{40,32},{48,40},{56,48},{64,56},{72,6... | collective-permute-start | bytes 61448 | tf_op jit(solution)/shard_map/ppermute | solution.py:18
  138.8 2.4 collective-permute-start.7
  142.5 3.0 %add.231 = f32[320,6,512]{2,1,0:T(8,128)} broadcast(f32[320,512]{1,0:T(8,128)S(1)} %fusion.15), dimensions={0,2} | broadcast | bytes 4587520 | tf_op jit(solution)/shard_map/add | solution.py:132
  145.5 5.5 %add.232 = f32[1920,512]{1,0:T(8,128)} reshape(f32[320,6,512]{2,1,0:T(8,128)} %add.231) | data formatting | bytes 7864320 | tf_op jit(solution)/shard_map/add | solution.py:132
  152.9 6.4 %gather_fusion.4 = f32[1920,512]{1,0:T(8,128)} fusion(f32[396,512]{1,0:T(8,128)S(1)} %fusion.18, s32[2048]{0:T(1024)} %copy-done.10), kind=kCustom, calls=%fused_computation.3.clone | custom fusion | bytes 7872000 | tf_op jit(solution)/shard_map/jit(_take)/gather | solution.py:128
  159.3 8.1 %fusion.157 = (f32[1920]{0:T(1024)S(1)}, f32[1920,512]{1,0:T(8,128)}) fusion(bf16[2,512,512]{2,1,0:T(8,128)(2,1)} %param.27, f32[1920,512]{1,0:T(8,128)} %add.232, f32[1920,512]{1,0:T(8,128)} %gather_fusion.4, pred[1920]{0:T(1024)(128)(4,1)S(1)} %copy-done.28, bf16[1920,512]{1,0:T(8,128)(2,1)S(1)} %add_convert_fusion.1, bf16[2,1536,512]{2,1,0:T(8,128)(2,1)} %param.26), kind=kOutput, calls=%fused_computation.213 | convolution fusion | flops 2022111360 | bytes 14820736 | tf_op jit(solution)/shard_map/dot_general | solution.py:33
  167.4 2.8 %multiply_reduce_fusion = f32[1920]{0:T(1024)S(1)} fusion(f32[1920,512]{1,0:T(8,128)} %get-tuple-element.37, f32[1920]{0:T(1024)S(1)} %broadcast_multiply_fusion), kind=kLoop, calls=%fused_computation.18 | loop fusion | flops 2947200 | bytes 3947520 | tf_op jit(solution)/shard_map/reduce_sum | solution.py:27
  170.3 24.0 %all-gather.7.cloned.1.call-done = bf16[128,20,512]{2,1,0:T(8,128)(2,1)} async-done(((bf16[1,20,512]{2,1,0:T(8,128)(2,1)}), bf16[128,20,512]{2,1,0:T(8,128)(2,1)}) %all-gather.7.cloned.1.call-update) | async-done | bytes 2621456 | tf_op jit(solution)/shard_map/all_gather | solution.py:120
  194.3 5.2 %reshape.310 = bf16[2560,512]{1,0:T(8,128)(2,1)} reshape(bf16[128,20,512]{2,1,0:T(8,128)(2,1)} %all-gather.7.cloned.1.call-done) | data formatting | bytes 5242880
  199.5 3.2 %gather_fusion.6 = bf16[160,512]{1,0:T(8,128)(2,1)S(1)} fusion(bf16[2560,512]{1,0:T(8,128)(2,1)} %reshape.310, s32[1024]{0:T(1024)} %copy-done.16), kind=kCustom, calls=%fused_computation.6.clone | custom fusion | bytes 328320 | tf_op jit(solution)/shard_map/jit(_take)/gather | solution.py:137
  202.7 3.2 %gather_fusion.7 = bf16[160,512]{1,0:T(8,128)(2,1)S(1)} fusion(bf16[2560,512]{1,0:T(8,128)(2,1)} %reshape.310, s32[1024]{0:T(1024)} %copy-done.15), kind=kCustom, calls=%fused_computation.7.clone | custom fusion | bytes 328320 | tf_op jit(solution)/shard_map/jit(_take)/gather | solution.py:140
  207.3 1.8 fusion.160
  212.0 5.7 %all-to-all-start.2 = ((bf16[128,3,512]{2,1,0:T(4,128)(2,1)}), bf16[128,3,512]{2,1,0:T(4,128)(2,1)}, u32[]{:S(2)}, u32[]{:S(2)}) async-start(bf16[128,3,512]{2,1,0:T(4,128)(2,1)} %reshape.182), calls=%async_computation.2 | async-start | bytes 1048576 | tf_op jit(solution)/shard_map/all_to_all | solution.py:63
  217.8 3.7 %add_convert_fusion = bf16[1920,512]{1,0:T(8,128)(2,1)} fusion(f32[1920,512]{1,0:T(8,128)} %get-tuple-element.37, f32[512]{0:T(512)S(1)} %bitcast.132, f32[1920]{0:T(1024)S(1)} %add_rsqrt_fusion, f32[1920]{0:T(1024)S(1)} %broadcast_multiply_fusion, bf16[1920,512]{1,0:T(8,128)(2,1)S(1)} %add_convert_fusion.1), kind=kLoop, calls=%fused_computation.17 | loop fusion | flops 5898240 | bytes 7881728 | tf_op jit(solution)/shard_map/convert_element_type | solution.py:34
  221.5 4.6 %reshape.189 = f32[320,6,512]{2,1,0:T(8,128)} reshape(bf16[1920,512]{1,0:T(8,128)(2,1)} %add_convert_fusion) | data formatting | bytes 5898240 | tf_op jit(solution)/shard_map/convert_element_type | solution.py:146
  226.1 2.3 reshape.185
  228.4 5.2 %reduce_sum.149 = f32[320,512]{1,0:T(8,128)} reduce(f32[320,6,512]{2,1,0:T(8,128)} %reshape.189, f32[]{:T(128)} %constant.121.clone.1), dimensions={1}, to_apply=%region_15.19 | reduce | flops 819200 | bytes 4587524 | tf_op jit(solution)/shard_map/reduce_sum | solution.py:146
  233.6 2.4 copy.36
  237.6 2.7 %scatter_fusion.1 = f32[320,512]{1,0:T(8,128)} fusion(f32[320,512]{1,0:T(8,128)} %reduce_sum.149, s32[20]{0:T(128)S(1)} %copy-done.20, f32[20,512]{1,0:T(8,128)S(1)} %fusion.88), kind=kCustom, calls=%fused_computation.12 | custom fusion | flops 10240 | bytes 122960 | tf_op jit(solution)/shard_map/scatter-add | solution.py:149
  240.3 2.4 fusion.165
  (172 shorter events, 35.8 us)
Async XLA Ops:
  7.2 26.0 %copy-start.31 = (s32[160]{0:T(256)S(1)}, s32[160]{0:T(256)}, u32[]{:S(2)}) copy-start(s32[160]{0:T(256)} %param.25) | copy-start | bytes 1924
  7.2 25.5 %copy-start.11 = (s32[16,20,6]{1,0,2:T(8,128)S(1)}, s32[16,20,6]{1,0,2:T(8,128)}, u32[]{:S(2)}) copy-start(s32[16,20,6]{1,0,2:T(8,128)} %param.22) | copy-start | bytes 23044
  7.2 26.6 %copy-start.30 = (s32[160]{0:T(256)S(1)}, s32[160]{0:T(256)}, u32[]{:S(2)}) copy-start(s32[160]{0:T(256)} %param.24) | copy-start | bytes 1924
  7.2 27.1 %copy-start.21 = (f32[2,512]{1,0:T(2,128)S(1)}, f32[2,512]{1,0:T(2,128)}, u32[]{:S(2)}) copy-start(f32[2,512]{1,0:T(2,128)} %param.28) | copy-start | bytes 12292
  7.2 27.7 %copy-start.22 = (f32[2,512]{1,0:T(2,128)S(1)}, f32[2,512]{1,0:T(2,128)}, u32[]{:S(2)}) copy-start(f32[2,512]{1,0:T(2,128)} %param.31) | copy-start | bytes 12292
  7.2 28.9 %copy-start.7 = (bf16[160,512]{1,0:T(8,128)(2,1)S(1)}, bf16[160,512]{1,0:T(8,128)(2,1)}, u32[]{:S(2)}) copy-start(bf16[160,512]{1,0:T(8,128)(2,1)} %param.21) | copy-start | bytes 491524
  7.2 80.3 %all-gather.5.cloned.1.call-start = ((), (), s32[]{:S(2)}) async-start(), calls=%async_computation.3 | async-start | bytes 3170304 | tf_op jit(solution)/shard_map/all_gather | solution.py:120
  9.1 47.2 %collective-permute-start.1 = (bf16[1,20,512]{2,0,1:T(2,128)(2,1)}, bf16[1,20,512]{2,0,1:T(2,128)(2,1)S(1)}, u32[]{:S(2)}, u32[]{:S(2)}) collective-permute-start(bf16[1,20,512]{2,0,1:T(2,128)(2,1)} %get-tuple-element.22), channel_id=1, source_target_pairs={{8,0},{16,8},{24,16},{32,24},{40,32},{48,40},{56,48},{64,56},{72,6... | collective-permute-start | bytes 61448 | tf_op jit(solution)/shard_map/ppermute | solution.py:18
  14.9 41.5 %collective-permute-start = (bf16[1,20,512]{2,0,1:T(2,128)(2,1)S(1)}, bf16[1,20,512]{2,0,1:T(2,128)(2,1)S(1)}, u32[]{:S(2)}, u32[]{:S(2)}) collective-permute-start(bf16[1,20,512]{2,0,1:T(2,128)(2,1)S(1)} %get-tuple-element.21), channel_id=1, source_target_pairs={{0,8},{8,16},{16,24},{24,32},{32,40},{40,48},{48,56},{56,64},{64,7... | collective-permute-start | bytes 61448 | tf_op jit(solution)/shard_map/ppermute | solution.py:16
  16.7 3.0 %copy-start.18 = (s32[20]{0:T(128)}, s32[20]{0:T(128)S(1)}, u32[]{:S(2)}) copy-start(s32[20]{0:T(128)S(1)} %compare_select_fusion.4) | copy-start | bytes 244
  17.4 16.9 %copy-start.25 = (pred[20]{0:T(512)(128)(4,1)}, pred[20]{0:T(512)(128)(4,1)S(1)}, u32[]{:S(2)}) copy-start(pred[20]{0:T(512)(128)(4,1)S(1)} %compare_and_fusion.3) | copy-start | bytes 64
  20.0 13.1 %copy-start.29 = (s32[160]{0:T(256)}, s32[160]{0:T(256)S(1)}, u32[]{:S(2)}) copy-start(s32[160]{0:T(256)S(1)} %compare_select_fusion.3) | copy-start | bytes 1924
  22.0 36.2 %all-to-all-start = ((bf16[128,1,3]{2,1,0:T(2,128)(2,1)}), bf16[128,1,3]{2,1,0:T(2,128)(2,1)S(1)}, u32[]{:S(2)}, u32[]{:S(2)}) async-start(bf16[128,1,3]{2,1,0:T(2,128)(2,1)} %all_to_all.17), calls=%async_computation | async-start | bytes 131072 | tf_op jit(solution)/shard_map/all_to_all | solution.py:70
  33.2 29.5 %copy-start.10 = (s32[2048]{0:T(1024)}, s32[2048]{0:T(1024)S(1)}, u32[]{:S(2)}) copy-start(s32[2048]{0:T(1024)S(1)} %pad_clamp_fusion) | copy-start | bytes 24580
  41.9 49.3 %copy-start.16 = (s32[1024]{0:T(1024)}, s32[1024]{0:T(1024)S(1)}, u32[]{:S(2)}) copy-start(s32[1024]{0:T(1024)S(1)} %get-tuple-element.43) | copy-start | bytes 12292
  41.9 50.9 %copy-start.15 = (s32[1024]{0:T(1024)}, s32[1024]{0:T(1024)S(1)}, u32[]{:S(2)}) copy-start(s32[1024]{0:T(1024)S(1)} %get-tuple-element.42) | copy-start | bytes 12292
  50.7 5.6 %copy-start.3 = (bf16[16,20,512]{2,0,1:T(8,128)(2,1)S(1)}, bf16[16,20,512]{2,0,1:T(8,128)(2,1)}, u32[]{:S(2)}) copy-start(bf16[16,20,512]{2,0,1:T(8,128)(2,1)} %param.19) | copy-start | bytes 983044
  56.4 3.7 %collective-permute-start.3 = (bf16[18,1,512]{2,0,1:T(8,128)(2,1)S(1)}, bf16[18,1,512]{2,0,1:T(8,128)(2,1)S(1)}, u32[]{:S(2)}, u32[]{:S(2)}) collective-permute-start(bf16[18,1,512]{2,0,1:T(8,128)(2,1)S(1)} %get-tuple-element.18), channel_id=1, source_target_pairs={{1,0},{2,1},{3,2},{4,3},{5,4},{6,5},{7,6},{0,7},{9,8},{10,9},{11,1... | collective-permute-start | bytes 55304 | tf_op jit(solution)/shard_map/ppermute | solution.py:18
  57.6 3.1 %collective-permute-start.2 = (bf16[18,1,512]{2,0,1:T(8,128)(2,1)S(1)}, bf16[18,1,512]{2,0,1:T(8,128)(2,1)S(1)}, u32[]{:S(2)}, u32[]{:S(2)}) collective-permute-start(bf16[18,1,512]{2,0,1:T(8,128)(2,1)S(1)} %get-tuple-element.17), channel_id=1, source_target_pairs={{0,1},{1,2},{2,3},{3,4},{4,5},{5,6},{6,7},{7,0},{8,9},{9,10},{10,1... | collective-permute-start | bytes 55304 | tf_op jit(solution)/shard_map/ppermute | solution.py:16
  58.6 61.9 %copy-start.12 = (s32[384]{0:T(512)}, s32[384]{0:T(512)S(1)}, u32[]{:S(2)}) copy-start(s32[384]{0:T(512)S(1)} %reshape.188) | copy-start | bytes 4612
  62.7 6.2 %copy-start.2 = (bf16[1920,512]{1,0:T(8,128)(2,1)S(1)}, bf16[1920,512]{1,0:T(8,128)(2,1)}, u32[]{:S(2)}) copy-start(bf16[1920,512]{1,0:T(8,128)(2,1)} %reshape.173) | copy-start | bytes 5898244
  62.7 6.2 %copy-start.27 = (pred[1920]{0:T(1024)(128)(4,1)S(1)}, pred[1920]{0:T(1024)(128)(4,1)}, u32[]{:S(2)}) copy-start(pred[1920]{0:T(1024)(128)(4,1)} %compare_and_fusion) | copy-start | bytes 5764
  80.0 14.4 %copy-start.23 = (pred[160]{0:T(512)(128)(4,1)S(1)}, pred[160]{0:T(512)(128)(4,1)}, u32[]{:S(2)}) copy-start(pred[160]{0:T(512)(128)(4,1)} %compare_and_fusion.2) | copy-start | bytes 484
  91.2 4.7 %copy-start.32 = (pred[160]{0:T(512)(128)(4,1)S(1)}, pred[160]{0:T(512)(128)(4,1)}, u32[]{:S(2)}) copy-start(pred[160]{0:T(512)(128)(4,1)} %compare_and_fusion.1) | copy-start | bytes 484
  92.8 5.2 %copy-start.8 = (bf16[160,512]{1,0:T(8,128)(2,1)S(1)}, bf16[160,512]{1,0:T(8,128)(2,1)}, u32[]{:S(2)}) copy-start(bf16[160,512]{1,0:T(8,128)(2,1)} %param.21) | copy-start | bytes 491524
  98.1 30.4 %copy-start.4 = (bf16[160,512]{1,0:T(8,128)(2,1)}, bf16[160,512]{1,0:T(8,128)(2,1)S(1)}, u32[]{:S(2)}) copy-start(bf16[160,512]{1,0:T(8,128)(2,1)S(1)} %add_convert_fusion.5) | copy-start | bytes 491524
  100.6 18.8 %all-to-all-start.1 = ((bf16[128,3,512]{2,1,0:T(4,128)(2,1)}), bf16[128,3,512]{2,1,0:T(4,128)(2,1)S(1)}, u32[]{:S(2)}, u32[]{:S(2)}) async-start(bf16[128,3,512]{2,1,0:T(4,128)(2,1)} %reshape.178), calls=%async_computation.1 | async-start | bytes 1048576 | tf_op jit(solution)/shard_map/all_to_all | solution.py:63
  105.9 88.4 %all-gather.7.cloned.1.call-start = ((), (), s32[]{:S(2)}) async-start(), calls=%async_computation.4 | async-start | bytes 3170304 | tf_op jit(solution)/shard_map/all_gather | solution.py:120
  112.4 9.4 %copy-start.19 = (s32[20]{0:T(128)S(1)}, s32[20]{0:T(128)}, u32[]{:S(2)}) copy-start(s32[20]{0:T(128)} %copy-done.18) | copy-start | bytes 244
  124.4 3.4 %copy-start.26 = (pred[20]{0:T(512)(128)(4,1)S(1)}, pred[20]{0:T(512)(128)(4,1)}, u32[]{:S(2)}) copy-start(pred[20]{0:T(512)(128)(4,1)} %copy-done.25) | copy-start | bytes 64
  130.6 7.2 %collective-permute-start.4 = (bf16[1,20,512]{2,1,0:T(8,128)(2,1)S(1)}, bf16[1,20,512]{2,1,0:T(8,128)(2,1)S(1)}, u32[]{:S(2)}, u32[]{:S(2)}) collective-permute-start(bf16[1,20,512]{2,1,0:T(8,128)(2,1)S(1)} %get-tuple-element.20), channel_id=1, source_target_pairs={{0,8},{8,16},{16,24},{24,32},{32,40},{40,48},{48,56},{56,64},{64,7... | collective-permute-start | bytes 61448 | tf_op jit(solution)/shard_map/ppermute | solution.py:16
  133.3 5.4 %collective-permute-start.5 = (bf16[1,20,512]{2,1,0:T(8,128)(2,1)S(1)}, bf16[1,20,512]{2,1,0:T(8,128)(2,1)S(1)}, u32[]{:S(2)}, u32[]{:S(2)}) collective-permute-start(bf16[1,20,512]{2,1,0:T(8,128)(2,1)S(1)} %get-tuple-element.19), channel_id=1, source_target_pairs={{8,0},{16,8},{24,16},{32,24},{40,32},{48,40},{56,48},{64,56},{72,6... | collective-permute-start | bytes 61448 | tf_op jit(solution)/shard_map/ppermute | solution.py:18
  138.8 12.3 %collective-permute-start.7 = (bf16[18,1,512]{2,1,0:T(2,128)(2,1)S(1)}, bf16[18,1,512]{2,1,0:T(2,128)(2,1)S(1)}, u32[]{:S(2)}, u32[]{:S(2)}) collective-permute-start(bf16[18,1,512]{2,1,0:T(2,128)(2,1)S(1)} %get-tuple-element.16), channel_id=1, source_target_pairs={{1,0},{2,1},{3,2},{4,3},{5,4},{6,5},{7,6},{0,7},{9,8},{10,9},{11,1... | collective-permute-start | bytes 55304 | tf_op jit(solution)/shard_map/ppermute | solution.py:18
  141.2 9.9 %collective-permute-start.6 = (bf16[18,1,512]{2,1,0:T(2,128)(2,1)S(1)}, bf16[18,1,512]{2,1,0:T(2,128)(2,1)S(1)}, u32[]{:S(2)}, u32[]{:S(2)}) collective-permute-start(bf16[18,1,512]{2,1,0:T(2,128)(2,1)S(1)} %get-tuple-element.15), channel_id=1, source_target_pairs={{0,1},{1,2},{2,3},{3,4},{4,5},{5,6},{6,7},{7,0},{8,9},{9,10},{10,1... | collective-permute-start | bytes 55304 | tf_op jit(solution)/shard_map/ppermute | solution.py:16
  152.9 6.4 %copy-start.28 = (pred[1920]{0:T(1024)(128)(4,1)S(1)}, pred[1920]{0:T(1024)(128)(4,1)}, u32[]{:S(2)}) copy-start(pred[1920]{0:T(1024)(128)(4,1)} %compare_and_fusion) | copy-start | bytes 5764
  170.2 35.7 %copy-start.6 = (f32[160,512]{1,0:T(8,128)S(1)}, f32[160,512]{1,0:T(8,128)}, u32[]{:S(2)}) copy-start(f32[160,512]{1,0:T(8,128)} %fusion.20) | copy-start | bytes 983044
  170.2 35.7 %copy-start.24 = (pred[160]{0:T(512)(128)(4,1)S(1)}, pred[160]{0:T(512)(128)(4,1)}, u32[]{:S(2)}) copy-start(pred[160]{0:T(512)(128)(4,1)} %compare_and_fusion.2) | copy-start | bytes 484
  199.5 7.8 %copy-start.33 = (pred[160]{0:T(512)(128)(4,1)S(1)}, pred[160]{0:T(512)(128)(4,1)}, u32[]{:S(2)}) copy-start(pred[160]{0:T(512)(128)(4,1)} %compare_and_fusion.1) | copy-start | bytes 484
  202.7 6.7 %copy-start.5 = (bf16[160,512]{1,0:T(8,128)(2,1)S(1)}, bf16[160,512]{1,0:T(8,128)(2,1)}, u32[]{:S(2)}) copy-start(bf16[160,512]{1,0:T(8,128)(2,1)} %copy-done.4) | copy-start | bytes 491524
  202.7 6.7 %copy-start.14 = (f32[1,512]{1,0:T(1,128)S(1)}, f32[1,512]{1,0:T(1,128)}, u32[]{:S(2)}) copy-start(f32[1,512]{1,0:T(1,128)} %get-tuple-element.25) | copy-start | bytes 6148
  209.5 12.0 %copy-start.9 = (bf16[160,512]{1,0:T(8,128)(2,1)}, bf16[160,512]{1,0:T(8,128)(2,1)S(1)}, u32[]{:S(2)}) copy-start(bf16[160,512]{1,0:T(8,128)(2,1)S(1)} %add_convert_fusion.4) | copy-start | bytes 491524
  212.0 23.9 %all-to-all-start.2 = ((bf16[128,3,512]{2,1,0:T(4,128)(2,1)}), bf16[128,3,512]{2,1,0:T(4,128)(2,1)}, u32[]{:S(2)}, u32[]{:S(2)}) async-start(bf16[128,3,512]{2,1,0:T(4,128)(2,1)} %reshape.182), calls=%async_computation.2 | async-start | bytes 1048576 | tf_op jit(solution)/shard_map/all_to_all | solution.py:63
  221.5 4.7 %copy-start = (bf16[1920,512]{1,0:T(8,128)(2,1)S(1)}, bf16[1920,512]{1,0:T(8,128)(2,1)}, u32[]{:S(2)}) copy-start(bf16[1920,512]{1,0:T(8,128)(2,1)} %add_convert_fusion) | copy-start | bytes 5898244
  228.4 5.2 %copy-start.1 = (bf16[16,20,6,512]{3,2,1,0:T(8,128)(2,1)S(1)}, bf16[16,20,6,512]{3,2,1,0:T(8,128)(2,1)}, u32[]{:S(2)}) copy-start(bf16[16,20,6,512]{3,2,1,0:T(8,128)(2,1)} %reshape.185) | copy-start | bytes 5898244
  233.6 3.8 %copy-start.13 = (s32[384]{0:T(512)S(1)}, s32[384]{0:T(512)}, u32[]{:S(2)}) copy-start(s32[384]{0:T(512)} %copy-done.12) | copy-start | bytes 4612
  233.6 4.1 %copy-start.20 = (s32[20]{0:T(128)S(1)}, s32[20]{0:T(128)}, u32[]{:S(2)}) copy-start(s32[20]{0:T(128)} %copy-done.18) | copy-start | bytes 244
  237.6 5.3 %copy-start.17 = (f32[1,512]{1,0:T(1,128)S(1)}, f32[1,512]{1,0:T(1,128)}, u32[]{:S(2)}) copy-start(f32[1,512]{1,0:T(1,128)} %get-tuple-element.23) | copy-start | bytes 6148
Sparse Core Ops, SparseCore 0:
  18.9 68.5 all-gather.4
  128.7 65.5 all-gather.6
where the time goes:
time: 253 us; the launch traced here: 251 us
  local copies, waits for them, and re-layouts  83.1 us (33%)
  matrix products  43.4 us (17%)
  starting transfers between devices  36.8 us (15%)
  waiting for transfers between devices  36.7 us (15%)
  other arithmetic  36.1 us (14%)
  between operations  14.7 us (6%)
    all_gather x2, waiting for transfers between devices, shards(): coarse = lax.all_gather(own_coarse, ('px', 'py'), axis=0, tiled=True)  31.5 us
    dot_general x6, matrix products, finish(): output = jnp.dot(hidden, outer, preferred_element_type=jnp.float32)  24.9 us
    add x4, local copies, waits for them, and re-layouts, shards(): inner_sum.reshape(patch_cells, degree, -1) + receiver_terms[:, None, :]  18.3 us
    unnamed x77, local copies, waits for them, and re-layouts  16 us
    ppermute x4, starting transfers between devices, with_halo(): lax.ppermute(head, axis, [((i + 1) % count, i) for i in range(count)])  13.8 us
    gather x2, local copies, waits for them, and re-layouts, shards(): jnp.take(sender_terms, sender_index, axis=0)  12.6 us
    all_to_all x2, starting transfers between devices, owner_sums(): lax.all_to_all(bucket.reshape(devices, capacity, features), ('px', 'py'),...  11 us
    all_to_all x1, starting transfers between devices, owner_sums(): lax.all_to_all(labels.astype(jnp.bfloat16).reshape(devices, capacity), ('...  10.6 us
  transfers between devices with their start and end apart: 13, of which 6 were waited for; matrix products, arithmetic and copies ran while one was open for 45% of the time, Pallas kernels for 0%

commit v1 on v0

v1 whole, which is shorter than its diff:
```python
import jax
import jax.numpy as jnp
from jax import lax
from jax.experimental import pallas as pl
from jax.experimental.pallas import tpu as pltpu
from jax.sharding import PartitionSpec as P

EPSILON = 1e-05
AXES = ("px", "py")
DIGITS = ((32, 4), (8, 4), (2, 4), (1, 2))
CORE = DIGITS[3]
SLOT = 32
BAND = 2
BUCKET = 4
VMEM = 48 * 1024 * 1024


def shift(values, digit, step):
    stride, size = digit
    pairs = []
    for i in range(128):
        here = i // stride % size
        pairs.append((i, i + ((here + step) % size - here) * stride))
    return lax.ppermute(values, AXES, pairs)


def spread(rows):
    pieces = [rows]
    for digit in DIGITS[:3]:
        joined = jnp.concatenate(pieces, axis=0) if len(pieces) > 1 else pieces[0]
        pieces = [joined] + [shift(joined, digit, s) for s in range(1, digit[1])]
    return pieces + [shift(piece, CORE, 1) for piece in pieces]


def table_index(device, row, coarse_count):
    me = lax.axis_index(AXES)

    def back(digit):
        stride, size = digit
        return (me // stride - device // stride) % size

    ky, kx, kz, kc = (back(digit) for digit in DIGITS)
    return (((kc * 4 + kz) * 4 + kx) * 4 + ky) * coarse_count + row


def along(values, axis, step):
    count = lax.axis_size(axis)
    return lax.ppermute(values, axis, [(i, (i + step) % count) for i in range(count)])


def extended(latents):
    rows, columns, features = latents.shape
    above = along(latents[-1:], "px", 1)
    below = along(latents[:1], "px", -1)
    tall = jnp.concatenate([above, latents, below], axis=0)
    left = along(tall[:, -1:], "py", 1)
    right = along(tall[:, :1], "py", -1)
    rest = jnp.zeros((rows + 2, SLOT - columns - 2, features), latents.dtype)
    return jnp.concatenate([tall, left, right, rest], axis=1).reshape(-1, features)


def selection(neighbours):
    rows, columns, degree = neighbours.shape
    q = neighbours + (neighbours >= 4).astype(jnp.int32)
    band_row = lax.broadcasted_iota(jnp.int32, neighbours.shape, 0) % BAND
    column = lax.broadcasted_iota(jnp.int32, neighbours.shape, 1)
    sent = column + q % 3 - 1
    sent = jnp.where(sent < 0, columns, jnp.where(sent >= columns, columns + 1, sent))
    sender = ((band_row + q // 3) * SLOT + sent).reshape(-1, 1)
    receiver = (128 + band_row * SLOT + column).reshape(-1, 1)
    lanes = lax.broadcasted_iota(jnp.int32, (rows * columns * degree, 256), 1)
    return ((lanes == sender) | (lanes == receiver)).astype(jnp.bfloat16)


def dot(a, b):
    return jnp.dot(a, b, preferred_element_type=jnp.float32)


def finish(before, inner_sum, outer, gains):
    hidden = jax.nn.silu(inner_sum).astype(jnp.bfloat16)
    output = dot(hidden, outer)
    center = output - jnp.mean(output, axis=-1, keepdims=True)
    spread_of = jnp.mean(center * center, axis=-1, keepdims=True)
    scaled = center * lax.rsqrt(spread_of + EPSILON) * gains
    return (before.astype(jnp.float32) + scaled).astype(jnp.bfloat16)


def fine_layer(layer, fine, picks, ext, inner, outer, gain, nodes):
    edges, features = fine.shape
    hidden = inner.shape[2]
    bands = 8
    block = edges // bands
    per_band = nodes // bands
    degree = block // per_band
    near = (BAND + 2) * SLOT

    def body(fine_ref, picks_ref, ext_ref, inner_ref, outer_ref, gain_ref, next_ref, sum_ref, send_ref, recv_ref):
        step = pl.program_id(0)

        @pl.when(step == 0)
        def _():
            send_ref[...] = dot(ext_ref[...], inner_ref[0, features : 2 * features]).astype(jnp.bfloat16)
            recv_ref[...] = dot(ext_ref[...], inner_ref[0, 2 * features :]).astype(jnp.bfloat16)

        start = pl.multiple_of(step * BAND * SLOT, BAND * SLOT)
        mine = pl.multiple_of(step * BAND * SLOT + SLOT, SLOT)
        before = fine_ref[...]
        total = dot(before, inner_ref[0, :features])
        total += dot(picks_ref[:, :near], send_ref[pl.ds(start, near), :])
        total += dot(picks_ref[:, near : near + BAND * SLOT], recv_ref[pl.ds(mine, BAND * SLOT), :])
        after = finish(before, total, outer_ref[0], gain_ref[layer : layer + 1, :])
        next_ref[...] = after
        node = lax.broadcasted_iota(jnp.int32, (per_band, block), 0) * degree
        edge = lax.broadcasted_iota(jnp.int32, (per_band, block), 1)
        pool = ((edge >= node) & (edge < node + degree)).astype(jnp.bfloat16)
        sum_ref[...] = dot(pool, after)

    whole = lambda shape: pl.BlockSpec(shape, lambda i: (layer,) + (0,) * (len(shape) - 1))
    fixed = lambda shape: pl.BlockSpec(shape, lambda i: (0,) * len(shape))
    return pl.pallas_call(
        body,
        name=f"fine{layer}",
        out_shape=(
            jax.ShapeDtypeStruct(fine.shape, jnp.bfloat16),
            jax.ShapeDtypeStruct((nodes, features), jnp.float32),
        ),
        grid=(bands,),
        in_specs=[
            pl.BlockSpec((block, features), lambda i: (i, 0)),
            pl.BlockSpec((block, 256), lambda i: (i, 0)),
            fixed(ext.shape),
            whole((1,) + inner.shape[1:]),
            whole((1,) + outer.shape[1:]),
            fixed(gain.shape),
        ],
        out_specs=(
            pl.BlockSpec((block, features), lambda i: (i, 0)),
            pl.BlockSpec((per_band, features), lambda i: (i, 0)),
        ),
        scratch_shapes=[
            pltpu.VMEM((ext.shape[0], hidden), jnp.bfloat16),
            pltpu.VMEM((ext.shape[0], hidden), jnp.bfloat16),
        ],
        compiler_params=pltpu.CompilerParams(
            dimension_semantics=("arbitrary",), vmem_limit_bytes=VMEM
        ),
    )(fine, picks, ext, inner, outer, gain)


def long_layer(layer, held, sender, receiver, pieces, inner, outer, gain):
    slots, features = held.shape
    count = len(pieces)
    each = pieces[0].shape[0]
    tile = 128

    def body(held_ref, sender_ref, receiver_ref, inner_ref, outer_ref, gain_ref, *rest):
        piece_refs, next_ref, table, arrived = rest[:count], rest[count], rest[count + 1], rest[count + 2]
        copies = [
            pltpu.make_async_copy(piece_refs[p], table.at[pl.ds(p * each, each), :], arrived.at[p])
            for p in range(count)
        ]
        for copy in copies:
            copy.start()
        for copy in copies:
            copy.wait()
        for m in range(slots // tile):
            rows = slice(m * tile, (m + 1) * tile)
            lanes = lax.broadcasted_iota(jnp.int32, (tile, count * each), 1)
            sent = dot((lanes == sender_ref[rows, :]).astype(jnp.bfloat16), table[...]).astype(jnp.bfloat16)
            lanes = lax.broadcasted_iota(jnp.int32, (tile, 32), 1)
            got = dot((lanes == receiver_ref[rows, :]).astype(jnp.bfloat16), table[:32, :]).astype(jnp.bfloat16)
            before = held_ref[rows, :]
            total = dot(before, inner_ref[0, :features])
            total += dot(sent, inner_ref[0, features : 2 * features])
            total += dot(got, inner_ref[0, 2 * features :])
            next_ref[rows, :] = finish(before, total, outer_ref[0], gain_ref[layer : layer + 1, :])

    whole = lambda shape: pl.BlockSpec(shape, lambda i: (layer,) + (0,) * (len(shape) - 1))
    fixed = lambda shape: pl.BlockSpec(shape, lambda i: (0,) * len(shape))
    return pl.pallas_call(
        body,
        name=f"long{layer}",
        out_shape=jax.ShapeDtypeStruct(held.shape, jnp.bfloat16),
        grid=(1,),
        in_specs=[
            fixed(held.shape),
            fixed(sender.shape),
            fixed(receiver.shape),
            whole((1,) + inner.shape[1:]),
            whole((1,) + outer.shape[1:]),
            fixed(gain.shape),
        ]
        + [pl.BlockSpec(memory_space=pl.ANY)] * count,
        out_specs=fixed(held.shape),
        scratch_shapes=[
            pltpu.VMEM((count * each, features), jnp.bfloat16),
            pltpu.SemaphoreType.DMA((count,)),
        ],
        compiler_params=pltpu.CompilerParams(vmem_limit_bytes=VMEM),
    )(held, sender, receiver, inner, outer, gain, *pieces)


def node_layer(layer, latents, fine_sum, held, target, coarse_column, inner, outer, gain, coarse_count):
    nodes, features = latents.shape
    slots = held.shape[0]

    def body(latents_ref, sum_ref, held_ref, target_ref, coarse_ref, inner_ref, outer_ref, gain_ref, next_ref, own_ref):
        node = lax.broadcasted_iota(jnp.int32, (nodes, slots), 0)
        adds = (node == target_ref[...]).astype(jnp.bfloat16)
        incoming = (sum_ref[...] + dot(adds, held_ref[...])).astype(jnp.bfloat16)
        before = latents_ref[...]
        total = dot(before, inner_ref[0, :features]) + dot(incoming, inner_ref[0, features:])
        after = finish(before, total, outer_ref[0], gain_ref[layer : layer + 1, :])
        next_ref[...] = after
        lanes = lax.broadcasted_iota(jnp.int32, (coarse_ref.shape[0], nodes), 1)
        own = dot((lanes == coarse_ref[...]).astype(jnp.bfloat16), after)
        own_ref[...] = own[:coarse_count].astype(jnp.bfloat16)

    whole = lambda shape: pl.BlockSpec(shape, lambda i: (layer,) + (0,) * (len(shape) - 1))
    fixed = lambda shape: pl.BlockSpec(shape, lambda i: (0,) * len(shape))
    return pl.pallas_call(
        body,
        name=f"node{layer}",
        out_shape=(
            jax.ShapeDtypeStruct(latents.shape, jnp.bfloat16),
            jax.ShapeDtypeStruct((coarse_count, features), jnp.bfloat16),
        ),
        grid=(1,),
        in_specs=[
            fixed(latents.shape),
            fixed(fine_sum.shape),
            fixed(held.shape),
            fixed(target.shape),
            fixed(coarse_column.shape),
            whole((1,) + inner.shape[1:]),
            whole((1,) + outer.shape[1:]),
            fixed(gain.shape),
        ],
        out_specs=(fixed(latents.shape), fixed((coarse_count, features))),
        compiler_params=pltpu.CompilerParams(vmem_limit_bytes=VMEM),
    )(latents, fine_sum, held, target, coarse_column, inner, outer, gain)


def bucketed(long_edges, senders, receivers, coarse_count, devices):
    count, features = long_edges.shape
    owner = receivers // coarse_count
    same = owner[:, None] == owner[None, :]
    index = lax.iota(jnp.int32, count)
    rank = jnp.sum((same & (index[None, :] < index[:, None])).astype(jnp.int32), axis=1)
    place = owner * BUCKET + rank
    spots = lax.broadcasted_iota(jnp.int32, (devices * BUCKET, count), 0)
    to_edge = (spots == place[None, :]).astype(jnp.bfloat16)
    to_tags = (spots == owner[None, :] * BUCKET + BUCKET - 1).astype(jnp.bfloat16)
    lane = lax.broadcasted_iota(jnp.int32, (count, features), 1)
    field = lane % 4
    tag = jnp.where(
        field == 0,
        (senders // coarse_count)[:, None],
        jnp.where(
            field == 1,
            (senders % coarse_count)[:, None],
            jnp.where(field == 2, (receivers % coarse_count)[:, None], 1),
        ),
    )
    tag = jnp.where(lane // 4 == rank[:, None], tag, 0).astype(jnp.bfloat16)
    filled = dot(to_edge, long_edges) + dot(to_tags, tag)
    return filled.astype(jnp.bfloat16).reshape(devices, BUCKET, features), owner * 3 + rank


def exchange(rows):
    return lax.all_to_all(rows, AXES, split_axis=0, concat_axis=0, tiled=True)


def shards(
    node_latents,
    fine_edges,
    long_edges,
    neighbours,
    coarse_slots,
    long_senders,
    long_receivers,
    edge_inner,
    edge_outer,
    edge_gain,
    node_inner,
    node_outer,
    node_gain,
):
    patch_rows, patch_columns, features = node_latents.shape
    nodes = patch_rows * patch_columns
    coarse_count = coarse_slots.shape[0]
    layers = edge_inner.shape[0]
    devices = lax.axis_size("px") * lax.axis_size("py")

    latents = node_latents.reshape(nodes, features)
    own = jnp.take(latents, coarse_slots, axis=0, mode="clip")
    payload, back = bucketed(long_edges, long_senders, long_receivers, coarse_count, devices)
    arrived = exchange(payload)
    held = arrived.reshape(devices * BUCKET, features)
    tags = arrived[:, BUCKET - 1, : 4 * (BUCKET - 1)].astype(jnp.int32)
    tags = jnp.pad(tags, ((0, 0), (0, 4))).reshape(devices * BUCKET, 4)
    valid = tags[:, 3:] > 0
    sender = jnp.where(valid, table_index(tags[:, :1], tags[:, 1:2], coarse_count), -1)
    receiver = jnp.where(valid, tags[:, 2:3], -1)
    match = receiver == lax.iota(jnp.int32, coarse_count)[None, :]
    target = jnp.sum(jnp.where(match, coarse_slots[None, :] + 1, 0), axis=1)[None, :] - 1
    coarse_column = jnp.pad(coarse_slots, (0, 32 - coarse_count), constant_values=-1)[:, None]
    picks = selection(neighbours)
    fine = fine_edges.reshape(-1, features)
    for layer in range(layers):
        pieces = spread(own)
        ext = extended(latents.reshape(node_latents.shape))
        fine, fine_sum = fine_layer(layer, fine, picks, ext, edge_inner, edge_outer, edge_gain, nodes)
        held = long_layer(layer, held, sender, receiver, pieces, edge_inner, edge_outer, edge_gain)
        latents, own = node_layer(
            layer, latents, fine_sum, held, target, coarse_column, node_inner, node_outer, node_gain, coarse_count
        )
    home = exchange(held.reshape(devices, BUCKET, features)[:, : BUCKET - 1])
    picked = back[:, None] == lax.iota(jnp.int32, devices * (BUCKET - 1))[None, :]
    new_long = dot(picked.astype(jnp.bfloat16), home.reshape(-1, features)).astype(jnp.bfloat16)
    return latents.reshape(node_latents.shape), fine.reshape(fine_edges.shape), new_long


def solution(mesh):
    in_specs = (
        P("px", "py", None),
        P("px", "py", None, None),
        P(AXES, None),
        P("px", "py", None),
        P(AXES),
        P(AXES),
        P(AXES),
        P(),
        P(),
        P(),
        P(),
        P(),
        P(),
    )
    out_specs = (P("px", "py", None), P("px", "py", None, None), P(AXES, None))
    return jax.shard_map(shards, mesh=mesh, in_specs=in_specs, out_specs=out_specs, check_vma=False)
```

time: 253 us -> 178 us (0.70)
  the two profiles are of different devices: /device:TPU:1 before, /device:TPU:20 now
where the time goes in v1:
time: 178 us; the launch traced here: 176 us
  starting transfers between devices  59.8 us (34%)
  local copies, waits for them, and re-layouts  46 us (26%)
  Pallas kernels  37 us (21%)
  waiting for transfers between devices  20.8 us (12%)
  other arithmetic  9.53 us (5%)
    ppermute x26, starting transfers between devices, shift(): return lax.ppermute(values, AXES, pairs)  28.1 us
    unnamed x79, local copies, waits for them, and re-layouts  21.4 us
    all_to_all x2, starting transfers between devices, exchange(): return lax.all_to_all(rows, AXES, split_axis=0, concat_axis=0, tiled=True)  21.3 us
    pallas_call x2, Pallas kernels, fine_layer(): pl.pallas_call(body, name=f'fine{layer}', out_shape=(jax.ShapeDtypeStruct...  19.9 us
    ppermute x26, waiting for transfers between devices, shift(): return lax.ppermute(values, AXES, pairs)  14.5 us
    pallas_call x2, Pallas kernels, long_layer(): pl.pallas_call(body, name=f'long{layer}', out_shape=jax.ShapeDtypeStruct(...  13.7 us
    ppermute x8, starting transfers between devices, along(): lax.ppermute(values, axis, [(i, (i + step) % count) for i in range(count)])  10.4 us
    ppermute x8, waiting for transfers between devices, along(): lax.ppermute(values, axis, [(i, (i + step) % count) for i in range(count)])  6.28 us
  transfers between devices with their start and end apart: 36, of which 7 were waited for; matrix products, arithmetic and copies ran while one was open for 22% of the time, Pallas kernels for 12%

profile of v1, /device:TPU:20, one launch (start us, length us, event | category | flops | bytes accessed | tf_op | source)
XLA Modules:
  0.0 176.1 jit_solution(2523752318286544365)
XLA Ops:
  0.7 1.2 copy.60
  3.2 1.4 collective-permute-start.4
  5.2 1.1 collective-permute-start.6
  8.8 11.1 %all-to-all-start = ((bf16[128,4,512]{2,1,0:T(4,128)(2,1)}), bf16[128,4,512]{2,1,0:T(4,128)(2,1)}, u32[]{:S(2)}, u32[]{:S(2)}) async-start(bf16[128,4,512]{2,1,0:T(4,128)(2,1)} %reshape.120), calls=%async_computation | async-start | bytes 1048576 | tf_op jit(solution)/shard_map/all_to_all | solution.py:271
  20.0 1.3 collective-permute-start
  22.9 1.1 fusion.1.picks_ref
  25.4 1.3 collective-permute-start.7
  26.7 1.6 collective-permute-start.8
  28.2 2.5 %collective-permute-start.9 = (bf16[80,512]{1,0:T(8,128)(2,1)S(1)}, bf16[80,512]{1,0:T(8,128)(2,1)S(1)}, u32[]{:S(2)}, u32[]{:S(2)}) collective-permute-start(bf16[80,512]{1,0:T(8,128)(2,1)S(1)} %pad_maximum_fusion), channel_id=1, source_target_pairs={{0,24},{1,25},{2,26},{3,27},{4,28},{5,29},{6,30},{7,31},{8,0},{9,1... | collective-permute-start | bytes 245768 | tf_op jit(solution)/shard_map/ppermute | solution.py:24
  31.4 3.0 %collective-permute-start.3 = (bf16[18,1,512]{2,0,1:T(8,128)(2,1)}, bf16[18,1,512]{2,0,1:T(8,128)(2,1)}, u32[]{:S(2)}, u32[]{:S(2)}) collective-permute-start(bf16[18,1,512]{2,0,1:T(8,128)(2,1)} %get-tuple-element.40), channel_id=1, source_target_pairs={{0,7},{1,0},{2,1},{3,2},{4,3},{5,4},{6,5},{7,6},{8,15},{9,8},{10,9... | collective-permute-start | bytes 55304 | tf_op jit(solution)/shard_map/ppermute | solution.py:48
  34.4 1.0 concatenate.29.rest_0_
  36.0 3.2 %collective-permute-start.11 = (bf16[320,512]{1,0:T(8,128)(2,1)S(1)}, bf16[320,512]{1,0:T(8,128)(2,1)}, u32[]{:S(2)}, u32[]{:S(2)}) collective-permute-start(bf16[320,512]{1,0:T(8,128)(2,1)S(1)} %concatenate.29.rest_0_), channel_id=1, source_target_pairs={{0,4},{1,5},{2,6},{3,7},{4,0},{5,1},{6,2},{7,3},{8,12},{9,13},{10,... | collective-permute-start | bytes 983048 | tf_op jit(solution)/shard_map/ppermute | solution.py:24
  39.2 1.2 collective-permute-start.12
  40.4 4.2 %copy.61 = bf16[16,20,6,512]{3,2,1,0:T(8,128)(2,1)} copy(bf16[16,20,6,512]{3,0,2,1:T(8,128)(2,1)} %param.14) | data formatting | bytes 3932160 | tf_op args[1]
  44.6 4.6 %reshape.118.fine_ref = bf16[1920,512]{1,0:T(8,128)(2,1)} reshape(bf16[16,20,6,512]{3,2,1,0:T(8,128)(2,1)} %copy.61) | data formatting | bytes 3932160 | tf_op jit(solution)/shard_map/reshape | solution.py:309
  49.4 1.2 maximum_maximum_fusion
  50.8 10.0 %fine0.1 = (bf16[1920,512]{1,0:T(8,128)(2,1)S(1)}, f32[320,512]{1,0:T(8,128)S(1)}) custom-call(bf16[1920,512]{1,0:T(8,128)(2,1)} %reshape.118.fine_ref, bf16[1920,256]{1,0:T(8,128)(2,1)S(1)} %fusion.1.picks_ref, bf16[576,512]{1,0:T(8,128)(2,1)S(1)} %bitcast.14, bf16[2,1536,512]{2,1,0:T(8,128)(2,1)} %inner_ref.10, bf16[2,512,512]{2,1,0:T(8,128)(2,1)S(1)} %copy-done.1, ...), custom_call_target="tpu_custom_call" | custom-call | tf_op jit(solution)/shard_map/fine0/pallas_call | solution.py:120
  60.7 1.3 copy-done.9
  63.9 1.0 slice.66
  65.9 1.3 fusion.61
  67.4 2.0 %reshape.121.held_ref = bf16[512,512]{1,0:T(8,128)(2,1)} reshape(bf16[128,4,512]{2,1,0:T(4,128)(2,1)} %all-to-all-done) | data formatting | bytes 1048576 | tf_op jit(solution)/shard_map/reshape | solution.py:299
  69.3 1.9 %fusion.13.sender_ref = s32[512,1]{1,0:T(8,128)S(1)} fusion(pred[512,1]{1,0:T(8,128)(4,1)S(1)} %get-tuple-element.34, s32[512,4]{1,0:T(8,128)} %reshape.132, s32[]{:T(128)S(6)} %select_n.152, s32[]{:T(128)S(6)} %select_n.149, s32[]{:T(128)S(6)} %select_n.146, s32[]{:T(128)S(6)} %add.161), kind=kLoop, calls=%fused_computation.49 | loop fusion | flops 47104 | bytes 6672 | tf_op jit(solution)/shard_map/jit(_where)/select_n | solution.py:303
  71.3 1.1 copy-done.8
  74.4 7.2 %long0.1.held_ref = bf16[512,512]{1,0:T(8,128)(2,1)S(1)} custom-call(bf16[512,512]{1,0:T(8,128)(2,1)S(1)} %copy-done.8, s32[512,1]{1,0:T(8,128)S(1)} %fusion.13.sender_ref, s32[512,1]{1,0:T(8,128)S(1)} %get-tuple-element.33.receiver_ref, bf16[2,1536,512]{2,1,0:T(8,128)(2,1)} %inner_ref.10, bf16[2,512,512]{2,1,0:T(8,128)(2,1)S(1)} %copy-done.1, ...), custom_call_target="tpu_custom_call" | custom-call | tf_op jit(solution)/shard_map/long0/pallas_call | solution.py:180
  81.6 1.4 node0.1
  83.7 1.2 collective-permute-start.21
  85.7 2.3 %collective-permute-start.23 = (bf16[20,512]{1,0:T(8,128)(2,1)S(1)}, bf16[20,512]{1,0:T(8,128)(2,1)S(1)}, u32[]{:S(2)}, u32[]{:S(2)}) collective-permute-start(bf16[20,512]{1,0:T(8,128)(2,1)S(1)} %get-tuple-element.14), channel_id=1, source_target_pairs={{0,96},{1,97},{2,98},{3,99},{4,100},{5,101},{6,102},{7,103},{8,104... | collective-permute-start | bytes 61448 | tf_op jit(solution)/shard_map/ppermute | solution.py:24
  88.0 2.3 %collective-permute-done.22 = bf16[20,512]{1,0:T(8,128)(2,1)S(1)} collective-permute-done((bf16[20,512]{1,0:T(8,128)(2,1)S(1)}, bf16[20,512]{1,0:T(8,128)(2,1)S(1)}, u32[]{:S(2)}, u32[]{:S(2)}) %collective-permute-start.22) | collective-permute-done | bytes 20512 | tf_op jit(solution)/shard_map/ppermute | solution.py:24
  90.3 2.9 %collective-permute-start.24 = (bf16[80,512]{1,0:T(8,128)(2,1)S(1)}, bf16[80,512]{1,0:T(8,128)(2,1)S(1)}, u32[]{:S(2)}, u32[]{:S(2)}) collective-permute-start(bf16[80,512]{1,0:T(8,128)(2,1)S(1)} %pad_maximum_fusion.1), channel_id=1, source_target_pairs={{0,8},{1,9},{2,10},{3,11},{4,12},{5,13},{6,14},{7,15},{8,16},{9,17... | collective-permute-start | bytes 245768 | tf_op jit(solution)/shard_map/ppermute | solution.py:24
  93.8 1.6 collective-permute-start.26
  95.3 3.8 %collective-permute-done.25 = bf16[80,512]{1,0:T(8,128)(2,1)S(1)} collective-permute-done((bf16[80,512]{1,0:T(8,128)(2,1)S(1)}, bf16[80,512]{1,0:T(8,128)(2,1)S(1)}, u32[]{:S(2)}, u32[]{:S(2)}) %collective-permute-start.25) | collective-permute-done | bytes 81952 | tf_op jit(solution)/shard_map/ppermute | solution.py:24
  99.8 3.0 %concatenate.33.rest_0_ = bf16[320,512]{1,0:T(8,128)(2,1)S(1)} concatenate(bf16[20,512]{1,0:T(8,128)(2,1)S(1)} %get-tuple-element.14, bf16[20,512]{1,0:T(8,128)(2,1)S(1)} %collective-permute-done.21, bf16[20,512]{1,0:T(8,128)(2,1)S(1)} %collective-permute-done.22, bf16[20,512]{1,0:T(8,128)(2,1)S(1)} %collective-permute-done.23, bf16[80,512]{1,0:T(8,128)(2,1)} %copy-done.28, ...), dimensions={0} | concatenate | bytes 655360 | tf_op jit(solution)/shard_map/concatenate | solution.py:30
  104.3 2.1 %collective-permute-start.29 = (bf16[320,512]{1,0:T(8,128)(2,1)S(1)}, bf16[320,512]{1,0:T(8,128)(2,1)}, u32[]{:S(2)}, u32[]{:S(2)}) collective-permute-start(bf16[320,512]{1,0:T(8,128)(2,1)S(1)} %concatenate.33.rest_0_), channel_id=1, source_target_pairs={{0,6},{1,7},{2,0},{3,1},{4,2},{5,3},{6,4},{7,5},{8,14},{9,15},{10,... | collective-permute-start | bytes 983048 | tf_op jit(solution)/shard_map/ppermute | solution.py:24
  107.2 1.2 collective-permute-start.17
  108.3 1.8 %reshape.124 = bf16[16,20,512]{2,1,0:T(8,128)(2,1)} reshape(bf16[320,512]{1,0:T(8,128)(2,1)} %copy-done.11) | data formatting | bytes 655360 | tf_op jit(solution)/shard_map/reshape | solution.py:312
  111.1 7.4 %collective-permute-done.27.rest_1_ = bf16[320,512]{1,0:T(8,128)(2,1)} collective-permute-done((bf16[320,512]{1,0:T(8,128)(2,1)S(1)}, bf16[320,512]{1,0:T(8,128)(2,1)}, u32[]{:S(2)}, u32[]{:S(2)}) %collective-permute-start.27) | collective-permute-done | bytes 327712 | tf_op jit(solution)/shard_map/ppermute | solution.py:24
  119.3 1.0 constant_dynamic-update-slice_fusion.1
  122.2 1.0 copy-done.16
  123.2 6.6 %long1.1.held_ref = bf16[512,512]{1,0:T(8,128)(2,1)S(1)} custom-call(bf16[512,512]{1,0:T(8,128)(2,1)S(1)} %long0.1.held_ref, s32[512,1]{1,0:T(8,128)S(1)} %copy-done.7, s32[512,1]{1,0:T(8,128)S(1)} %get-tuple-element.33.receiver_ref, bf16[2,1536,512]{2,1,0:T(8,128)(2,1)} %inner_ref.10, bf16[2,512,512]{2,1,0:T(8,128)(2,1)S(1)} %copy-done.1, ...), custom_call_target="tpu_custom_call" | custom-call | tf_op jit(solution)/shard_map/long1/pallas_call | solution.py:180
  130.7 10.2 %all-to-all-start.1 = ((bf16[128,3,512]{2,1,0:T(4,128)(2,1)}), bf16[128,3,512]{2,1,0:T(4,128)(2,1)}, u32[]{:S(2)}, u32[]{:S(2)}) async-start(bf16[128,3,512]{2,1,0:T(4,128)(2,1)} %bitcast.12), calls=%async_computation.1 | async-start | bytes 1048576 | tf_op jit(solution)/shard_map/all_to_all | solution.py:271
  141.2 3.1 %collective-permute-start.20 = (bf16[18,1,512]{2,1,0:T(2,128)(2,1)S(1)}, bf16[18,1,512]{2,1,0:T(2,128)(2,1)S(1)}, u32[]{:S(2)}, u32[]{:S(2)}) collective-permute-start(bf16[18,1,512]{2,1,0:T(2,128)(2,1)S(1)} %get-tuple-element.38), channel_id=1, source_target_pairs={{0,7},{1,0},{2,1},{3,2},{4,3},{5,4},{6,5},{7,6},{8,15},{9,8},{10,9... | collective-permute-start | bytes 55304 | tf_op jit(solution)/shard_map/ppermute | solution.py:48
  144.3 6.3 %collective-permute-done.19 = bf16[18,1,512]{2,1,0:T(2,128)(2,1)S(1)} collective-permute-done((bf16[18,1,512]{2,1,0:T(2,128)(2,1)S(1)}, bf16[18,1,512]{2,1,0:T(2,128)(2,1)S(1)}, u32[]{:S(2)}, u32[]{:S(2)}) %collective-permute-start.19) | collective-permute-done | bytes 18464 | tf_op jit(solution)/shard_map/ppermute | solution.py:48
  150.8 10.0 %fine1.1 = (bf16[1920,512]{1,0:T(8,128)(2,1)S(1)}, f32[320,512]{1,0:T(8,128)S(1)}) custom-call(bf16[1920,512]{1,0:T(8,128)(2,1)} %copy-done.9, bf16[1920,256]{1,0:T(8,128)(2,1)S(1)} %fusion.1.picks_ref, bf16[576,512]{1,0:T(8,128)(2,1)S(1)} %bitcast.13, bf16[2,1536,512]{2,1,0:T(8,128)(2,1)} %inner_ref.10, bf16[2,512,512]{2,1,0:T(8,128)(2,1)S(1)} %copy-done.1, ...), custom_call_target="tpu_custom_call" | custom-call | tf_op jit(solution)/shard_map/fine1/pallas_call | solution.py:120
  160.8 1.3 copy-done.10
  162.1 4.5 %reshape.127 = bf16[16,20,6,512]{3,2,1,0:T(8,128)(2,1)} reshape(bf16[1920,512]{1,0:T(8,128)(2,1)} %copy-done.10) | data formatting | bytes 3932160 | tf_op jit(solution)/shard_map/reshape | solution.py:321
  166.5 4.2 %copy.71 = bf16[16,20,6,512]{3,0,2,1:T(8,128)(2,1)} copy(bf16[16,20,6,512]{3,2,1,0:T(8,128)(2,1)} %reshape.127) | data formatting | bytes 3932160
  170.8 2.0 %node1.1 = (bf16[320,512]{1,0:T(8,128)(2,1)S(1)}, bf16[20,512]{1,0:T(8,128)(2,1)}) custom-call(bf16[320,512]{1,0:T(8,128)(2,1)S(1)} %copy-done.12, f32[320,512]{1,0:T(8,128)S(1)} %get-tuple-element.13.sum_ref, bf16[512,512]{1,0:T(8,128)(2,1)S(1)} %long1.1.held_ref, s32[1,512]{1,0:T(1,128)S(1)} %bitcast.16, s32[32,1]{1,0:T(8,128)S(1)} %copy.68.coarse_ref, ...), custom_call_target="tpu_custom_call" | custom-call | tf_op jit(solution)/shard_map/node1/pallas_call | solution.py:221
  173.7 1.4 reshape.129
  (162 shorter events, 26.0 us)
Async XLA Ops:
  3.2 21.4 %collective-permute-start.4 = (bf16[20,512]{1,0:T(8,128)(2,1)S(1)}, bf16[20,512]{1,0:T(8,128)(2,1)S(1)}, u32[]{:S(2)}, u32[]{:S(2)}) collective-permute-start(bf16[20,512]{1,0:T(8,128)(2,1)S(1)} %gather_fusion), channel_id=1, source_target_pairs={{0,32},{1,33},{2,34},{3,35},{4,36},{5,37},{6,38},{7,39},{8,40},{9,... | collective-permute-start | bytes 61448 | tf_op jit(solution)/shard_map/ppermute | solution.py:24
  4.6 20.1 %collective-permute-start.5 = (bf16[20,512]{1,0:T(8,128)(2,1)S(1)}, bf16[20,512]{1,0:T(8,128)(2,1)S(1)}, u32[]{:S(2)}, u32[]{:S(2)}) collective-permute-start(bf16[20,512]{1,0:T(8,128)(2,1)S(1)} %gather_fusion), channel_id=1, source_target_pairs={{0,64},{1,65},{2,66},{3,67},{4,68},{5,69},{6,70},{7,71},{8,72},{9,... | collective-permute-start | bytes 61448 | tf_op jit(solution)/shard_map/ppermute | solution.py:24
  5.2 19.4 %collective-permute-start.6 = (bf16[20,512]{1,0:T(8,128)(2,1)S(1)}, bf16[20,512]{1,0:T(8,128)(2,1)}, u32[]{:S(2)}, u32[]{:S(2)}) collective-permute-start(bf16[20,512]{1,0:T(8,128)(2,1)S(1)} %gather_fusion), channel_id=1, source_target_pairs={{0,96},{1,97},{2,98},{3,99},{4,100},{5,101},{6,102},{7,103},{8,104... | collective-permute-start | bytes 61448 | tf_op jit(solution)/shard_map/ppermute | solution.py:24
  7.4 12.5 %copy-start.23 = (bf16[16,20,512]{2,0,1:T(8,128)(2,1)S(1)}, bf16[16,20,512]{2,0,1:T(8,128)(2,1)}, u32[]{:S(2)}) copy-start(bf16[16,20,512]{2,0,1:T(8,128)(2,1)} %param.13) | copy-start | bytes 983044
  7.8 14.2 %copy-start.30 = (s32[16,20,6]{1,0,2:T(8,128)S(1)}, s32[16,20,6]{1,0,2:T(8,128)}, u32[]{:S(2)}) copy-start(s32[16,20,6]{1,0,2:T(8,128)} %param.16) | copy-start | bytes 23044
  8.8 15.2 %copy-start.34 = (s32[20]{0:T(128)S(1)}, s32[20]{0:T(128)}, u32[]{:S(2)}) copy-start(s32[20]{0:T(128)} %param.17) | copy-start | bytes 244
  8.8 55.1 %all-to-all-start = ((bf16[128,4,512]{2,1,0:T(4,128)(2,1)}), bf16[128,4,512]{2,1,0:T(4,128)(2,1)}, u32[]{:S(2)}, u32[]{:S(2)}) async-start(bf16[128,4,512]{2,1,0:T(4,128)(2,1)} %reshape.120), calls=%async_computation | async-start | bytes 1048576 | tf_op jit(solution)/shard_map/all_to_all | solution.py:271
  20.0 10.8 %collective-permute-start = (bf16[1,20,512]{2,0,1:T(2,128)(2,1)S(1)}, bf16[1,20,512]{2,0,1:T(2,128)(2,1)S(1)}, u32[]{:S(2)}, u32[]{:S(2)}) collective-permute-start(bf16[1,20,512]{2,0,1:T(2,128)(2,1)S(1)} %get-tuple-element.43), channel_id=1, source_target_pairs={{0,8},{8,16},{16,24},{24,32},{32,40},{40,48},{48,56},{56,64},{64,7... | collective-permute-start | bytes 61448 | tf_op jit(solution)/shard_map/ppermute | solution.py:48
  21.2 9.5 %collective-permute-start.1 = (bf16[1,20,512]{2,0,1:T(2,128)(2,1)S(1)}, bf16[1,20,512]{2,0,1:T(2,128)(2,1)S(1)}, u32[]{:S(2)}, u32[]{:S(2)}) collective-permute-start(bf16[1,20,512]{2,0,1:T(2,128)(2,1)S(1)} %get-tuple-element.44), channel_id=1, source_target_pairs={{0,120},{8,0},{16,8},{24,16},{32,24},{40,32},{48,40},{56,48},{64,5... | collective-permute-start | bytes 61448 | tf_op jit(solution)/shard_map/ppermute | solution.py:48
  25.4 9.0 %collective-permute-start.7 = (bf16[80,512]{1,0:T(8,128)(2,1)S(1)}, bf16[80,512]{1,0:T(8,128)(2,1)S(1)}, u32[]{:S(2)}, u32[]{:S(2)}) collective-permute-start(bf16[80,512]{1,0:T(8,128)(2,1)S(1)} %pad_maximum_fusion), channel_id=1, source_target_pairs={{0,8},{1,9},{2,10},{3,11},{4,12},{5,13},{6,14},{7,15},{8,16},{9,17... | collective-permute-start | bytes 245768 | tf_op jit(solution)/shard_map/ppermute | solution.py:24
  26.7 7.7 %collective-permute-start.8 = (bf16[80,512]{1,0:T(8,128)(2,1)S(1)}, bf16[80,512]{1,0:T(8,128)(2,1)S(1)}, u32[]{:S(2)}, u32[]{:S(2)}) collective-permute-start(bf16[80,512]{1,0:T(8,128)(2,1)S(1)} %pad_maximum_fusion), channel_id=1, source_target_pairs={{0,16},{1,17},{2,18},{3,19},{4,20},{5,21},{6,22},{7,23},{8,24},{9,... | collective-permute-start | bytes 245768 | tf_op jit(solution)/shard_map/ppermute | solution.py:24
  28.2 6.2 %collective-permute-start.9 = (bf16[80,512]{1,0:T(8,128)(2,1)S(1)}, bf16[80,512]{1,0:T(8,128)(2,1)S(1)}, u32[]{:S(2)}, u32[]{:S(2)}) collective-permute-start(bf16[80,512]{1,0:T(8,128)(2,1)S(1)} %pad_maximum_fusion), channel_id=1, source_target_pairs={{0,24},{1,25},{2,26},{3,27},{4,28},{5,29},{6,30},{7,31},{8,0},{9,1... | collective-permute-start | bytes 245768 | tf_op jit(solution)/shard_map/ppermute | solution.py:24
  31.4 18.0 %collective-permute-start.2 = (bf16[18,1,512]{2,0,1:T(8,128)(2,1)}, bf16[18,1,512]{2,0,1:T(8,128)(2,1)}, u32[]{:S(2)}, u32[]{:S(2)}) collective-permute-start(bf16[18,1,512]{2,0,1:T(8,128)(2,1)} %get-tuple-element.39), channel_id=1, source_target_pairs={{0,1},{1,2},{2,3},{3,4},{4,5},{5,6},{6,7},{7,0},{8,9},{9,10},{10,1... | collective-permute-start | bytes 55304 | tf_op jit(solution)/shard_map/ppermute | solution.py:48
  31.4 18.0 %collective-permute-start.3 = (bf16[18,1,512]{2,0,1:T(8,128)(2,1)}, bf16[18,1,512]{2,0,1:T(8,128)(2,1)}, u32[]{:S(2)}, u32[]{:S(2)}) collective-permute-start(bf16[18,1,512]{2,0,1:T(8,128)(2,1)} %get-tuple-element.40), channel_id=1, source_target_pairs={{0,7},{1,0},{2,1},{3,2},{4,3},{5,4},{6,5},{7,6},{8,15},{9,8},{10,9... | collective-permute-start | bytes 55304 | tf_op jit(solution)/shard_map/ppermute | solution.py:48
  35.4 25.3 %copy-start.13 = (bf16[320,512]{1,0:T(8,128)(2,1)}, bf16[320,512]{1,0:T(8,128)(2,1)S(1)}, u32[]{:S(2)}) copy-start(bf16[320,512]{1,0:T(8,128)(2,1)S(1)} %concatenate.29.rest_0_) | copy-start | bytes 983044
  35.4 27.4 %collective-permute-start.10 = (bf16[320,512]{1,0:T(8,128)(2,1)S(1)}, bf16[320,512]{1,0:T(8,128)(2,1)S(1)}, u32[]{:S(2)}, u32[]{:S(2)}) collective-permute-start(bf16[320,512]{1,0:T(8,128)(2,1)S(1)} %concatenate.29.rest_0_), channel_id=1, source_target_pairs={{0,2},{1,3},{2,4},{3,5},{4,6},{5,7},{6,0},{7,1},{8,10},{9,11},{10,... | collective-permute-start | bytes 983048 | tf_op jit(solution)/shard_map/ppermute | solution.py:24
  36.0 27.4 %collective-permute-start.11 = (bf16[320,512]{1,0:T(8,128)(2,1)S(1)}, bf16[320,512]{1,0:T(8,128)(2,1)}, u32[]{:S(2)}, u32[]{:S(2)}) collective-permute-start(bf16[320,512]{1,0:T(8,128)(2,1)S(1)} %concatenate.29.rest_0_), channel_id=1, source_target_pairs={{0,4},{1,5},{2,6},{3,7},{4,0},{5,1},{6,2},{7,3},{8,12},{9,13},{10,... | collective-permute-start | bytes 983048 | tf_op jit(solution)/shard_map/ppermute | solution.py:24
  39.2 24.2 %collective-permute-start.12 = (bf16[320,512]{1,0:T(8,128)(2,1)S(1)}, bf16[320,512]{1,0:T(8,128)(2,1)}, u32[]{:S(2)}, u32[]{:S(2)}) collective-permute-start(bf16[320,512]{1,0:T(8,128)(2,1)S(1)} %concatenate.29.rest_0_), channel_id=1, source_target_pairs={{0,6},{1,7},{2,0},{3,1},{4,2},{5,3},{6,4},{7,5},{8,14},{9,15},{10,... | collective-permute-start | bytes 983048 | tf_op jit(solution)/shard_map/ppermute | solution.py:24
  50.8 16.5 %copy-start.35 = (s32[20]{0:T(128)S(1)}, s32[20]{0:T(128)}, u32[]{:S(2)}) copy-start(s32[20]{0:T(128)} %broadcast_add_fusion.2) | copy-start | bytes 244
  62.9 8.4 %collective-permute-start.13 = (bf16[320,512]{1,0:T(8,128)(2,1)S(1)}, bf16[320,512]{1,0:T(8,128)(2,1)}, u32[]{:S(2)}, u32[]{:S(2)}) collective-permute-start(bf16[320,512]{1,0:T(8,128)(2,1)S(1)} %concatenate.29.rest_0_), channel_id=1, source_target_pairs={{0,1},{1,0},{2,3},{3,2},{4,5},{5,4},{6,7},{7,6},{8,9},{9,8},{10,11... | collective-permute-start | bytes 983048 | tf_op jit(solution)/shard_map/ppermute | solution.py:24
  62.9 8.4 %copy-start.19 = (bf16[320,512]{1,0:T(8,128)(2,1)}, bf16[320,512]{1,0:T(8,128)(2,1)S(1)}, u32[]{:S(2)}) copy-start(bf16[320,512]{1,0:T(8,128)(2,1)S(1)} %collective-permute-done.10.rest_1_) | copy-start | bytes 983044
  62.9 8.4 %collective-permute-start.14 = (bf16[320,512]{1,0:T(8,128)(2,1)S(1)}, bf16[320,512]{1,0:T(8,128)(2,1)}, u32[]{:S(2)}, u32[]{:S(2)}) collective-permute-start(bf16[320,512]{1,0:T(8,128)(2,1)S(1)} %collective-permute-done.10.rest_1_), channel_id=1, source_target_pairs={{0,1},{1,0},{2,3},{3,2},{4,5},{5,4},{6,7},{7,6},{8,9},{9,8},{10,11... | collective-permute-start | bytes 983048 | tf_op jit(solution)/shard_map/ppermute | solution.py:24
  63.4 7.9 %collective-permute-start.15 = (bf16[320,512]{1,0:T(8,128)(2,1)}, bf16[320,512]{1,0:T(8,128)(2,1)}, u32[]{:S(2)}, u32[]{:S(2)}) collective-permute-start(bf16[320,512]{1,0:T(8,128)(2,1)} %collective-permute-done.11.rest_2_), channel_id=1, source_target_pairs={{0,1},{1,0},{2,3},{3,2},{4,5},{5,4},{6,7},{7,6},{8,9},{9,8},{10,11... | collective-permute-start | bytes 983048 | tf_op jit(solution)/shard_map/ppermute | solution.py:24
  63.5 7.8 %collective-permute-start.16 = (bf16[320,512]{1,0:T(8,128)(2,1)}, bf16[320,512]{1,0:T(8,128)(2,1)}, u32[]{:S(2)}, u32[]{:S(2)}) collective-permute-start(bf16[320,512]{1,0:T(8,128)(2,1)} %collective-permute-done.12.rest_3_), channel_id=1, source_target_pairs={{0,1},{1,0},{2,3},{3,2},{4,5},{5,4},{6,7},{7,6},{8,9},{9,8},{10,11... | collective-permute-start | bytes 983048 | tf_op jit(solution)/shard_map/ppermute | solution.py:24
  71.3 10.3 %copy-start.6 = (s32[512,1]{1,0:T(8,128)}, s32[512,1]{1,0:T(8,128)S(1)}, u32[]{:S(2)}) copy-start(s32[512,1]{1,0:T(8,128)S(1)} %fusion.13.sender_ref) | copy-start | bytes 6148
  74.4 7.2 %copy-start.4 = (bf16[2,512,512]{2,1,0:T(8,128)(2,1)S(1)}, bf16[2,512,512]{2,1,0:T(8,128)(2,1)}, u32[]{:S(2)}) copy-start(bf16[2,512,512]{2,1,0:T(8,128)(2,1)} %outer_ref.11) | copy-start | bytes 3145732
  74.4 7.2 %copy-start.18 = (f32[320,512]{1,0:T(8,128)S(1)}, f32[320,512]{1,0:T(8,128)}, u32[]{:S(2)}) copy-start(f32[320,512]{1,0:T(8,128)} %copy-done.17) | copy-start | bytes 1966084
  74.4 7.2 %copy-start.22 = (f32[2,512]{1,0:T(2,128)S(1)}, f32[2,512]{1,0:T(2,128)}, u32[]{:S(2)}) copy-start(f32[2,512]{1,0:T(2,128)} %gain_ref.11) | copy-start | bytes 12292
  83.7 4.3 %collective-permute-start.21 = (bf16[20,512]{1,0:T(8,128)(2,1)S(1)}, bf16[20,512]{1,0:T(8,128)(2,1)S(1)}, u32[]{:S(2)}, u32[]{:S(2)}) collective-permute-start(bf16[20,512]{1,0:T(8,128)(2,1)S(1)} %get-tuple-element.14), channel_id=1, source_target_pairs={{0,32},{1,33},{2,34},{3,35},{4,36},{5,37},{6,38},{7,39},{8,40},{9,... | collective-permute-start | bytes 61448 | tf_op jit(solution)/shard_map/ppermute | solution.py:24
  84.9 5.3 %collective-permute-start.22 = (bf16[20,512]{1,0:T(8,128)(2,1)S(1)}, bf16[20,512]{1,0:T(8,128)(2,1)S(1)}, u32[]{:S(2)}, u32[]{:S(2)}) collective-permute-start(bf16[20,512]{1,0:T(8,128)(2,1)S(1)} %get-tuple-element.14), channel_id=1, source_target_pairs={{0,64},{1,65},{2,66},{3,67},{4,68},{5,69},{6,70},{7,71},{8,72},{9,... | collective-permute-start | bytes 61448 | tf_op jit(solution)/shard_map/ppermute | solution.py:24
  85.7 4.6 %collective-permute-start.23 = (bf16[20,512]{1,0:T(8,128)(2,1)S(1)}, bf16[20,512]{1,0:T(8,128)(2,1)S(1)}, u32[]{:S(2)}, u32[]{:S(2)}) collective-permute-start(bf16[20,512]{1,0:T(8,128)(2,1)S(1)} %get-tuple-element.14), channel_id=1, source_target_pairs={{0,96},{1,97},{2,98},{3,99},{4,100},{5,101},{6,102},{7,103},{8,104... | collective-permute-start | bytes 61448 | tf_op jit(solution)/shard_map/ppermute | solution.py:24
  90.3 5.0 %collective-permute-start.24 = (bf16[80,512]{1,0:T(8,128)(2,1)S(1)}, bf16[80,512]{1,0:T(8,128)(2,1)S(1)}, u32[]{:S(2)}, u32[]{:S(2)}) collective-permute-start(bf16[80,512]{1,0:T(8,128)(2,1)S(1)} %pad_maximum_fusion.1), channel_id=1, source_target_pairs={{0,8},{1,9},{2,10},{3,11},{4,12},{5,13},{6,14},{7,15},{8,16},{9,17... | collective-permute-start | bytes 245768 | tf_op jit(solution)/shard_map/ppermute | solution.py:24
  93.2 5.9 %collective-permute-start.25 = (bf16[80,512]{1,0:T(8,128)(2,1)S(1)}, bf16[80,512]{1,0:T(8,128)(2,1)S(1)}, u32[]{:S(2)}, u32[]{:S(2)}) collective-permute-start(bf16[80,512]{1,0:T(8,128)(2,1)S(1)} %pad_maximum_fusion.1), channel_id=1, source_target_pairs={{0,16},{1,17},{2,18},{3,19},{4,20},{5,21},{6,22},{7,23},{8,24},{9,... | collective-permute-start | bytes 245768 | tf_op jit(solution)/shard_map/ppermute | solution.py:24
  93.8 6.0 %collective-permute-start.26 = (bf16[80,512]{1,0:T(8,128)(2,1)S(1)}, bf16[80,512]{1,0:T(8,128)(2,1)}, u32[]{:S(2)}, u32[]{:S(2)}) collective-permute-start(bf16[80,512]{1,0:T(8,128)(2,1)S(1)} %pad_maximum_fusion.1), channel_id=1, source_target_pairs={{0,24},{1,25},{2,26},{3,27},{4,28},{5,29},{6,30},{7,31},{8,0},{9,1... | collective-permute-start | bytes 245768 | tf_op jit(solution)/shard_map/ppermute | solution.py:24
  102.7 18.1 %copy-start.15 = (bf16[320,512]{1,0:T(8,128)(2,1)}, bf16[320,512]{1,0:T(8,128)(2,1)S(1)}, u32[]{:S(2)}) copy-start(bf16[320,512]{1,0:T(8,128)(2,1)S(1)} %concatenate.33.rest_0_) | copy-start | bytes 983044
  102.7 15.7 %collective-permute-start.27 = (bf16[320,512]{1,0:T(8,128)(2,1)S(1)}, bf16[320,512]{1,0:T(8,128)(2,1)}, u32[]{:S(2)}, u32[]{:S(2)}) collective-permute-start(bf16[320,512]{1,0:T(8,128)(2,1)S(1)} %concatenate.33.rest_0_), channel_id=1, source_target_pairs={{0,2},{1,3},{2,4},{3,5},{4,6},{5,7},{6,0},{7,1},{8,10},{9,11},{10,... | collective-permute-start | bytes 983048 | tf_op jit(solution)/shard_map/ppermute | solution.py:24
  103.6 14.8 %collective-permute-start.28 = (bf16[320,512]{1,0:T(8,128)(2,1)S(1)}, bf16[320,512]{1,0:T(8,128)(2,1)}, u32[]{:S(2)}, u32[]{:S(2)}) collective-permute-start(bf16[320,512]{1,0:T(8,128)(2,1)S(1)} %concatenate.33.rest_0_), channel_id=1, source_target_pairs={{0,4},{1,5},{2,6},{3,7},{4,0},{5,1},{6,2},{7,3},{8,12},{9,13},{10,... | collective-permute-start | bytes 983048 | tf_op jit(solution)/shard_map/ppermute | solution.py:24
  104.3 14.8 %collective-permute-start.29 = (bf16[320,512]{1,0:T(8,128)(2,1)S(1)}, bf16[320,512]{1,0:T(8,128)(2,1)}, u32[]{:S(2)}, u32[]{:S(2)}) collective-permute-start(bf16[320,512]{1,0:T(8,128)(2,1)S(1)} %concatenate.33.rest_0_), channel_id=1, source_target_pairs={{0,6},{1,7},{2,0},{3,1},{4,2},{5,3},{6,4},{7,5},{8,14},{9,15},{10,... | collective-permute-start | bytes 983048 | tf_op jit(solution)/shard_map/ppermute | solution.py:24
  107.2 3.9 %collective-permute-start.17 = (bf16[1,20,512]{2,1,0:T(8,128)(2,1)S(1)}, bf16[1,20,512]{2,1,0:T(8,128)(2,1)S(1)}, u32[]{:S(2)}, u32[]{:S(2)}) collective-permute-start(bf16[1,20,512]{2,1,0:T(8,128)(2,1)S(1)} %get-tuple-element.42), channel_id=1, source_target_pairs={{0,8},{8,16},{16,24},{24,32},{32,40},{40,48},{48,56},{56,64},{64,7... | collective-permute-start | bytes 61448 | tf_op jit(solution)/shard_map/ppermute | solution.py:48
  110.2 10.2 %collective-permute-start.18 = (bf16[1,20,512]{2,1,0:T(8,128)(2,1)S(1)}, bf16[1,20,512]{2,1,0:T(8,128)(2,1)S(1)}, u32[]{:S(2)}, u32[]{:S(2)}) collective-permute-start(bf16[1,20,512]{2,1,0:T(8,128)(2,1)S(1)} %get-tuple-element.41), channel_id=1, source_target_pairs={{0,120},{8,0},{16,8},{24,16},{32,24},{40,32},{48,40},{56,48},{64,5... | collective-permute-start | bytes 61448 | tf_op jit(solution)/shard_map/ppermute | solution.py:48
  111.1 9.3 %collective-permute-start.30 = (bf16[320,512]{1,0:T(8,128)(2,1)S(1)}, bf16[320,512]{1,0:T(8,128)(2,1)S(1)}, u32[]{:S(2)}, u32[]{:S(2)}) collective-permute-start(bf16[320,512]{1,0:T(8,128)(2,1)S(1)} %concatenate.33.rest_0_), channel_id=1, source_target_pairs={{0,1},{1,0},{2,3},{3,2},{4,5},{5,4},{6,7},{7,6},{8,9},{9,8},{10,11... | collective-permute-start | bytes 983048 | tf_op jit(solution)/shard_map/ppermute | solution.py:24
  118.5 1.9 %collective-permute-start.31 = (bf16[320,512]{1,0:T(8,128)(2,1)}, bf16[320,512]{1,0:T(8,128)(2,1)S(1)}, u32[]{:S(2)}, u32[]{:S(2)}) collective-permute-start(bf16[320,512]{1,0:T(8,128)(2,1)} %collective-permute-done.27.rest_1_), channel_id=1, source_target_pairs={{0,1},{1,0},{2,3},{3,2},{4,5},{5,4},{6,7},{7,6},{8,9},{9,8},{10,11... | collective-permute-start | bytes 983048 | tf_op jit(solution)/shard_map/ppermute | solution.py:24
  118.5 2.3 %collective-permute-start.32 = (bf16[320,512]{1,0:T(8,128)(2,1)}, bf16[320,512]{1,0:T(8,128)(2,1)S(1)}, u32[]{:S(2)}, u32[]{:S(2)}) collective-permute-start(bf16[320,512]{1,0:T(8,128)(2,1)} %collective-permute-done.28.rest_2_), channel_id=1, source_target_pairs={{0,1},{1,0},{2,3},{3,2},{4,5},{5,4},{6,7},{7,6},{8,9},{9,8},{10,11... | collective-permute-start | bytes 983048 | tf_op jit(solution)/shard_map/ppermute | solution.py:24
  119.1 2.2 %collective-permute-start.33 = (bf16[320,512]{1,0:T(8,128)(2,1)}, bf16[320,512]{1,0:T(8,128)(2,1)S(1)}, u32[]{:S(2)}, u32[]{:S(2)}) collective-permute-start(bf16[320,512]{1,0:T(8,128)(2,1)} %collective-permute-done.29.rest_3_), channel_id=1, source_target_pairs={{0,1},{1,0},{2,3},{3,2},{4,5},{5,4},{6,7},{7,6},{8,9},{9,8},{10,11... | collective-permute-start | bytes 983048 | tf_op jit(solution)/shard_map/ppermute | solution.py:24
  129.7 11.2 %copy-start.25 = (bf16[18,20,512]{2,1,0:T(8,128)(2,1)S(1)}, bf16[18,20,512]{2,1,0:T(8,128)(2,1)}, u32[]{:S(2)}) copy-start(bf16[18,20,512]{2,1,0:T(8,128)(2,1)} %copy-done.24) | copy-start | bytes 1105924
  130.7 43.0 %all-to-all-start.1 = ((bf16[128,3,512]{2,1,0:T(4,128)(2,1)}), bf16[128,3,512]{2,1,0:T(4,128)(2,1)}, u32[]{:S(2)}, u32[]{:S(2)}) async-start(bf16[128,3,512]{2,1,0:T(4,128)(2,1)} %bitcast.12), calls=%async_computation.1 | async-start | bytes 1048576 | tf_op jit(solution)/shard_map/all_to_all | solution.py:271
  141.0 9.5 %collective-permute-start.19 = (bf16[18,1,512]{2,1,0:T(2,128)(2,1)S(1)}, bf16[18,1,512]{2,1,0:T(2,128)(2,1)S(1)}, u32[]{:S(2)}, u32[]{:S(2)}) collective-permute-start(bf16[18,1,512]{2,1,0:T(2,128)(2,1)S(1)} %get-tuple-element.37), channel_id=1, source_target_pairs={{0,1},{1,2},{2,3},{3,4},{4,5},{5,6},{6,7},{7,0},{8,9},{9,10},{10,1... | collective-permute-start | bytes 55304 | tf_op jit(solution)/shard_map/ppermute | solution.py:48
  141.2 9.4 %collective-permute-start.20 = (bf16[18,1,512]{2,1,0:T(2,128)(2,1)S(1)}, bf16[18,1,512]{2,1,0:T(2,128)(2,1)S(1)}, u32[]{:S(2)}, u32[]{:S(2)}) collective-permute-start(bf16[18,1,512]{2,1,0:T(2,128)(2,1)S(1)} %get-tuple-element.38), channel_id=1, source_target_pairs={{0,7},{1,0},{2,1},{3,2},{4,3},{5,4},{6,5},{7,6},{8,15},{9,8},{10,9... | collective-permute-start | bytes 55304 | tf_op jit(solution)/shard_map/ppermute | solution.py:48
  (24 other events, 64.7 us)

commit v2 on v0

v2 whole, which is shorter than its diff:
```python
import jax
import jax.numpy as jnp
from jax import lax
from jax.experimental import pallas as pl
from jax.experimental.pallas import tpu as pltpu
from jax.sharding import PartitionSpec as P

EPSILON = 1e-05
AXES = ("px", "py")
DIGITS = ((32, 4), (8, 4), (2, 4), (1, 2))
CORE = DIGITS[3]
BAND = 4
TAGS = 128
LOW = 64
CAP = 3
VMEM = 24 * 1024 * 1024


def shift(values, digit, step):
    stride, size = digit
    pairs = []
    for i in range(128):
        here = i // stride % size
        pairs.append((i, i + ((here + step) % size - here) * stride))
    return lax.ppermute(values, AXES, pairs)


def tie(*values):
    return lax.optimization_barrier(values)


def stage(rows, digit):
    return [rows] + [shift(rows, digit, s) for s in range(1, digit[1])]


def table_row(device, coarse, coarse_count):
    home, row = coarse // coarse_count, coarse % coarse_count
    ky, kx, kz, kc = ((device // stride - home // stride) % size for stride, size in DIGITS)
    return (((kc * 4 + kz) * 4 + kx) * 4 + ky) * coarse_count + row


def along(values, axis, step):
    count = lax.axis_size(axis)
    return lax.ppermute(values, axis, [(i, (i + step) % count) for i in range(count)])


def selection(neighbours):
    rows, columns, degree = neighbours.shape
    codes = neighbours.transpose(1, 2, 0)
    q = codes + (codes >= 4).astype(jnp.int32)
    column = lax.broadcasted_iota(jnp.int32, codes.shape, 0)
    row = lax.broadcasted_iota(jnp.int32, codes.shape, 2)
    from_row = row + q // 3 - 1
    step = q % 3
    near = (column % BAND + step) * rows + from_row
    sender = jnp.where(from_row < 0, 160 + column + step, jnp.where(from_row >= rows, 192 + column + step, near))
    receiver = 96 + column % BAND * rows + row
    lanes = lax.broadcasted_iota(jnp.int32, codes.shape + (256,), 3)
    picks = (lanes == sender[..., None]) | (lanes == receiver[..., None])
    return picks.astype(jnp.bfloat16).reshape(-1, 256)


def dot(a, b):
    return jnp.dot(a, b, preferred_element_type=jnp.float32)


def finish(before, inner_sum, outer, gains):
    hidden = jax.nn.silu(inner_sum).astype(jnp.bfloat16)
    output = dot(hidden, outer)
    center = output - jnp.mean(output, axis=-1, keepdims=True)
    spread_of = jnp.mean(center * center, axis=-1, keepdims=True)
    scaled = center * lax.rsqrt(spread_of + EPSILON) * gains
    return (before.astype(jnp.float32) + scaled).astype(jnp.bfloat16)


def fine_layer(layer, fine, picks, latents, left, right, above, below, inner, outer, gain, rows):
    edges, features = fine.shape
    nodes = latents.shape[0]
    hidden = inner.shape[2]
    near = (BAND + 2) * rows
    own = BAND * rows
    steps = nodes // own
    block = edges // steps
    degree = edges // nodes
    columns = above.shape[0]

    def body(fine_ref, picks_ref, latents_ref, left_ref, right_ref, above_ref, below_ref, inner_ref, outer_ref, gain_ref,
             next_ref, sum_ref, send_ref, recv_ref, table_ref):
        step = pl.program_id(0)

        @pl.when(step == 0)
        def _():
            send = inner_ref[layer, features : 2 * features, :]
            project = lambda ref: dot(ref[...], send).astype(jnp.bfloat16)
            send_ref[:rows, :] = project(left_ref)
            send_ref[rows : rows + nodes, :] = project(latents_ref)
            send_ref[rows + nodes :, :] = project(right_ref)
            recv_ref[...] = dot(latents_ref[...], inner_ref[layer, 2 * features :, :]).astype(jnp.bfloat16)
            table_ref[...] = jnp.zeros(table_ref.shape, jnp.bfloat16)
            table_ref[160 : 160 + columns, :] = project(above_ref)
            table_ref[192 : 192 + columns, :] = project(below_ref)

        start = pl.multiple_of(step * own, own)
        table_ref[:near, :] = send_ref[pl.ds(start, near), :]
        table_ref[near : near + own, :] = recv_ref[pl.ds(start, own), :]
        before = fine_ref[...]
        total = dot(before, inner_ref[layer, :features, :]) + dot(picks_ref[...], table_ref[...])
        after = finish(before, total, outer_ref[layer], gain_ref[layer : layer + 1, :])
        next_ref[...] = after
        split = after.astype(jnp.float32).reshape(BAND, degree, rows, features)
        sum_ref[...] = jnp.sum(split, axis=1).reshape(own, features)

    held = pl.BlockSpec(memory_space=pltpu.VMEM)
    return pl.pallas_call(
        body,
        name=f"fine{layer}",
        out_shape=(
            jax.ShapeDtypeStruct(fine.shape, jnp.bfloat16),
            jax.ShapeDtypeStruct((nodes, features), jnp.float32),
        ),
        grid=(steps,),
        in_specs=[
            pl.BlockSpec((block, features), lambda i: (i, 0)),
            pl.BlockSpec((block, 256), lambda i: (i, 0)),
        ]
        + [held] * 8,
        out_specs=(
            pl.BlockSpec((block, features), lambda i: (i, 0)),
            pl.BlockSpec((own, features), lambda i: (i, 0)),
        ),
        scratch_shapes=[
            pltpu.VMEM((nodes + 2 * rows, hidden), jnp.bfloat16),
            pltpu.VMEM((nodes, hidden), jnp.bfloat16),
            pltpu.VMEM((256, hidden), jnp.bfloat16),
        ],
        compiler_params=pltpu.CompilerParams(dimension_semantics=("arbitrary",), vmem_limit_bytes=VMEM),
    )(fine, picks, latents, left, right, above, below, inner, outer, gain)


def coarse_layer(layer, long_rows, tagged, pieces, latents, fine_sum, coarse_row, coarse_column,
                 edge_inner, edge_outer, edge_gain, node_inner, node_outer, node_gain, slots, coarse_count):
    edges = tagged.shape[0]
    nodes, features = latents.shape
    count = len(pieces)
    each = pieces[0].shape[0]
    table_rows = count * each
    pad = coarse_row.shape[1]

    def body(long_ref, tag_ref, latents_ref, sum_ref, row_ref, column_ref, ei_ref, eo_ref, eg_ref, ni_ref, no_ref, ng_ref, *rest):
        piece_refs = rest[:count]
        long_next_ref, next_ref, own_ref, table = rest[count:]
        for p in range(count):
            table[p * each : (p + 1) * each, :] = piece_refs[p][...]
        tags = tag_ref[:, features : features + TAGS].astype(jnp.float32).astype(jnp.int32)
        valid = tags[:, 4:5] > 0
        sender = jnp.where(valid, tags[:, 0:1] * LOW + tags[:, 1:2], -1)
        receiver = jnp.where(valid, tags[:, 2:3] * LOW + tags[:, 3:4], -1)

        def pick(index, width):
            lanes = lax.broadcasted_iota(jnp.int32, (index.shape[0], width), 1)
            return (lanes == index).astype(jnp.bfloat16)

        sent = dot(pick(sender, table_rows), table[...]).astype(jnp.bfloat16)
        here = pick(receiver[:slots], pad)
        got_here = dot(here, table[:pad, :]).astype(jnp.bfloat16)
        got_away = dot(pick(receiver[slots:], table_rows), table[...]).astype(jnp.bfloat16)
        got = jnp.concatenate([got_here, got_away], axis=0)
        before = long_ref[:, :features]
        total = dot(before, ei_ref[layer, :features, :])
        total += dot(sent, ei_ref[layer, features : 2 * features, :])
        total += dot(got, ei_ref[layer, 2 * features :, :])
        after = finish(before, total, eo_ref[layer], eg_ref[layer : layer + 1, :])
        long_next_ref[...] = after

        node = lax.broadcasted_iota(jnp.int32, (nodes, pad), 0)
        place = (node == row_ref[...]).astype(jnp.bfloat16)
        adds = lax.dot_general(place, here, (((1,), (1,)), ((), ())), preferred_element_type=jnp.float32)
        incoming = (sum_ref[...] + dot(adds.astype(jnp.bfloat16), after[:slots])).astype(jnp.bfloat16)
        old = latents_ref[...]
        total = dot(old, ni_ref[layer, :features, :]) + dot(incoming, ni_ref[layer, features:, :])
        new = finish(old, total, no_ref[layer], ng_ref[layer : layer + 1, :])
        next_ref[...] = new
        own_ref[...] = dot(pick(column_ref[...], nodes), new)[:coarse_count].astype(jnp.bfloat16)

    held = pl.BlockSpec(memory_space=pltpu.VMEM)
    return pl.pallas_call(
        body,
        name=f"coarse{layer}",
        out_shape=(
            jax.ShapeDtypeStruct((edges, features), jnp.bfloat16),
            jax.ShapeDtypeStruct(latents.shape, jnp.bfloat16),
            jax.ShapeDtypeStruct((coarse_count, features), jnp.bfloat16),
        ),
        in_specs=[held] * (12 + count),
        out_specs=(held, held, held),
        scratch_shapes=[pltpu.VMEM((table_rows, features), jnp.bfloat16)],
        compiler_params=pltpu.CompilerParams(vmem_limit_bytes=VMEM),
    )(long_rows, tagged, latents, fine_sum, coarse_row, coarse_column,
      edge_inner, edge_outer, edge_gain, node_inner, node_outer, node_gain, *pieces)


def tag_lanes(device, senders, receivers, coarse_count):
    sender = table_row(device, senders, coarse_count)
    receiver = table_row(device, receivers, coarse_count)
    fields = (sender // LOW, sender % LOW, receiver // LOW, receiver % LOW)
    lane = lax.broadcasted_iota(jnp.int32, (senders.shape[0], TAGS), 1)
    tags = jnp.where(lane == len(fields), 1, 0)
    for at, field in enumerate(fields):
        tags = jnp.where(lane == at, field[:, None], tags)
    return tags.astype(jnp.bfloat16)


def bucketed(long_edges, senders, receivers, coarse_count, devices):
    count = receivers.shape[0]
    owner = receivers // coarse_count
    same = owner[:, None] == owner[None, :]
    index = lax.iota(jnp.int32, count)
    rank = jnp.sum((same & (index[None, :] < index[:, None])).astype(jnp.int32), axis=1)
    place = owner * CAP + rank
    spots = lax.broadcasted_iota(jnp.int32, (devices * CAP, count), 0)
    to_edge = (spots == place[None, :]).astype(jnp.bfloat16)
    tagged = jnp.concatenate([long_edges, tag_lanes(owner, senders, receivers, coarse_count)], axis=1)
    return dot(to_edge, tagged).astype(jnp.bfloat16)


def shards(
    node_latents,
    fine_edges,
    long_edges,
    neighbours,
    coarse_slots,
    long_senders,
    long_receivers,
    edge_inner,
    edge_outer,
    edge_gain,
    node_inner,
    node_outer,
    node_gain,
):
    rows, columns, features = node_latents.shape
    degree = fine_edges.shape[2]
    nodes = rows * columns
    coarse_count = coarse_slots.shape[0]
    layers = edge_inner.shape[0]
    devices = lax.axis_size("px") * lax.axis_size("py")
    slots = devices * CAP

    latents = node_latents.transpose(1, 0, 2).reshape(nodes, features)
    fine = fine_edges.transpose(1, 2, 0, 3).reshape(nodes * degree, features)
    coarse_at = coarse_slots % columns * rows + coarse_slots // columns
    own = jnp.take(latents, coarse_at, axis=0, mode="clip")
    padded = jnp.pad(coarse_at, (0, 32 - coarse_count), constant_values=-1)
    coarse_row, coarse_column = padded[None, :], padded[:, None]
    me = lax.axis_index(AXES)
    mine = jnp.concatenate([long_edges, tag_lanes(me, long_senders, long_receivers, coarse_count)], axis=1)
    payload = bucketed(long_edges, long_senders, long_receivers, coarse_count, devices)
    picks = selection(neighbours)
    tagged = None
    for layer in range(layers):
        joined = jnp.concatenate(stage(own, DIGITS[0]), axis=0)
        joined, grid = tie(joined, latents.reshape(columns, rows, features))
        left = along(grid[-1], "py", 1)
        right = along(grid[0], "py", -1)
        joined = jnp.concatenate(stage(joined, DIGITS[1]), axis=0)
        joined, left, right, payload = tie(joined, left, right, payload)
        pieces = stage(joined, DIGITS[2])
        high = jnp.concatenate([left[-1:], grid[:, -1], right[-1:]], axis=0)
        low = jnp.concatenate([left[:1], grid[:, 0], right[:1]], axis=0)
        above = along(high, "px", 1)
        below = along(low, "px", -1)
        if tagged is None:
            sent = payload.reshape(devices, CAP, features + TAGS)
            arrived = lax.all_to_all(sent, AXES, split_axis=0, concat_axis=0, tiled=True)
            tagged = jnp.concatenate([arrived.reshape(slots, features + TAGS), mine], axis=0)
            long_rows = tagged
        fine, fine_sum = fine_layer(
            layer, fine, picks, latents, left, right, above, below, edge_inner, edge_outer, edge_gain, rows
        )
        pieces = pieces + [shift(piece, CORE, 1) for piece in pieces]
        long_rows, latents, own = coarse_layer(
            layer, long_rows, tagged, pieces, latents, fine_sum, coarse_row, coarse_column,
            edge_inner, edge_outer, edge_gain, node_inner, node_outer, node_gain, slots, coarse_count,
        )
    return (
        latents.reshape(columns, rows, features).transpose(1, 0, 2),
        fine.reshape(columns, degree, rows, features).transpose(2, 0, 1, 3),
        long_rows[slots:],
    )


def solution(mesh):
    in_specs = (
        P("px", "py", None),
        P("px", "py", None, None),
        P(AXES, None),
        P("px", "py", None),
        P(AXES),
        P(AXES),
        P(AXES),
        P(),
        P(),
        P(),
        P(),
        P(),
        P(),
    )
    out_specs = (P("px", "py", None), P("px", "py", None, None), P(AXES, None))
    return jax.shard_map(shards, mesh=mesh, in_specs=in_specs, out_specs=out_specs, check_vma=False)
```

time: 253 us -> 150 us (0.59)
  local copies, waits for them, and re-layouts: 83.1 us -> 19.8 us
  matrix products: 43.4 us -> 1.09 us
  Pallas kernels: 0 us -> 26.2 us
  other arithmetic: 36.1 us -> 10.8 us
  starting transfers between devices: 36.8 us -> 57.4 us
  between operations: 14.7 us -> 1.02 us
  waiting for transfers between devices: 36.7 us -> 32.4 us
    dot_general x18 -> x1, matrix products: 43.4 us -> 1.09 us  [dot(): return jnp.dot(a, b, preferred_element_type=jnp.float32)]
    ppermute x8 -> x34, starting transfers between devices: 14.8 us -> 50.5 us  [the longest x26 34.4 us: shift(): return lax.ppermute(values, AXES, pairs)]
    all_gather x2 -> x0, waiting for transfers between devices: 31.5 us -> none  [shards(): coarse = lax.all_gather(own_coarse, ('px', 'py'), axis=0, tiled=True)]
    ppermute x8 -> x34, waiting for transfers between devices: 3.03 us -> 32.4 us  [the longest x26 21.7 us: shift(): return lax.ppermute(values, AXES, pairs)]
    pallas_call x0 -> x4, Pallas kernels: none -> 26.2 us  [the longest x2 13.5 us: fine_layer(): pl.pallas_call(body, name=f'fine{layer}', out_shape=(jax.ShapeDtypeStruct...]
    gather x8 -> x1, local copies, waits for them, and re-layouts: 23.4 us -> 1.62 us  [shards(): own = jnp.take(latents, coarse_at, axis=0, mode='clip')]
    add x5 -> x2, local copies, waits for them, and re-layouts: 18.5 us -> 0.21 us  [selection(): receiver = 96 + column % BAND * rows + row]
    reduce_sum x9 -> x1, other arithmetic: 16.8 us -> 0.19 us  [bucketed(): jnp.sum((same & (index[None, :] < index[:, None])).astype(jnp.int32), axi...]
  transfers between devices with their start and end apart: 13 -> 35, of which waited for: 6 -> 13; matrix products, arithmetic and copies ran while one was open for 45% -> 12% of each run, Pallas kernels for 0% -> 9%
where the time goes in v2:
time: 150 us; the launch traced here: 149 us
  starting transfers between devices  57.4 us (38%)
  waiting for transfers between devices  32.4 us (22%)
  Pallas kernels  26.2 us (17%)
  local copies, waits for them, and re-layouts  19.8 us (13%)
  other arithmetic  10.8 us (7%)
    ppermute x26, starting transfers between devices, shift(): return lax.ppermute(values, AXES, pairs)  34.4 us
    ppermute x26, waiting for transfers between devices, shift(): return lax.ppermute(values, AXES, pairs)  21.7 us
    ppermute x8, starting transfers between devices, along(): lax.ppermute(values, axis, [(i, (i + step) % count) for i in range(count)])  16.2 us
    pallas_call x2, Pallas kernels, fine_layer(): pl.pallas_call(body, name=f'fine{layer}', out_shape=(jax.ShapeDtypeStruct...  13.5 us
    pallas_call x2, Pallas kernels, coarse_layer(): pl.pallas_call(body, name=f'coarse{layer}', out_shape=(jax.ShapeDtypeStru...  12.7 us
    unnamed x42, local copies, waits for them, and re-layouts  10.8 us
    ppermute x8, waiting for transfers between devices, along(): lax.ppermute(values, axis, [(i, (i + step) % count) for i in range(count)])  10.7 us
    all_to_all x1, starting transfers between devices, shards(): lax.all_to_all(sent, AXES, split_axis=0, concat_axis=0, tiled=True)  6.83 us
  transfers between devices with their start and end apart: 35, of which 13 were waited for; matrix products, arithmetic and copies ran while one was open for 12% of the time, Pallas kernels for 9%

profile of v2, /device:TPU:1, one launch (start us, length us, event | category | flops | bytes accessed | tf_op | source)
XLA Modules:
  0.0 148.6 jit_solution(9998962926342603709)
XLA Ops:
  1.4 1.6 %gather_fusion = bf16[20,512]{1,0:T(8,128)(2,1)S(1)} fusion(bf16[320,512]{1,0:T(8,128)(2,1)} %bitcast.44, s32[1024]{0:T(1024)S(1)} %pad_clamp_fusion), kind=kCustom, calls=%fused_computation | custom fusion | bytes 41040 | tf_op jit(solution)/shard_map/jit(_take)/gather | solution.py:252
  3.0 3.6 %collective-permute-start.2 = (bf16[20,512]{1,0:T(8,128)(2,1)S(1)}, bf16[20,512]{1,0:T(8,128)(2,1)S(1)}, u32[]{:S(2)}, u32[]{:S(2)}) collective-permute-start(bf16[20,512]{1,0:T(8,128)(2,1)S(1)} %gather_fusion), channel_id=1, source_target_pairs={{0,96},{1,97},{2,98},{3,99},{4,100},{5,101},{6,102},{7,103},{8,104... | collective-permute-start | bytes 61448 | tf_op jit(solution)/shard_map/ppermute | solution.py:25
  10.8 2.2 %fusion.1.picks_ref = bf16[1920,256]{1,0:T(8,128)(2,1)} fusion(s32[1920]{0:T(1024)S(1)} %add.288, s32[1920]{0:T(1024)S(1)} %eq.117), kind=kLoop, calls=%fused_computation.4 | loop fusion | flops 1966080 | bytes 998400 | tf_op jit(solution)/shard_map/convert_element_type | solution.py:60
  13.9 1.1 convolution_convert_fusion
  15.0 0.9 pad_maximum_fusion.2
  15.9 2.5 %collective-permute-start.5 = (bf16[80,512]{1,0:T(8,128)(2,1)S(1)}, bf16[80,512]{1,0:T(8,128)(2,1)S(1)}, u32[]{:S(2)}, u32[]{:S(2)}) collective-permute-start(bf16[80,512]{1,0:T(8,128)(2,1)S(1)} %pad_maximum_fusion.2), channel_id=1, source_target_pairs={{0,24},{1,25},{2,26},{3,27},{4,28},{5,29},{6,30},{7,31},{8,0},{9,1... | collective-permute-start | bytes 245768 | tf_op jit(solution)/shard_map/ppermute | solution.py:25
  19.7 2.4 %collective-permute-start.7 = (bf16[16,512]{1,0:T(8,128)(2,1)S(1)}, bf16[16,512]{1,0:T(8,128)(2,1)S(1)}, u32[]{:S(2)}, u32[]{:S(2)}) collective-permute-start(bf16[16,512]{1,0:T(8,128)(2,1)S(1)} %get-tuple-element.56), channel_id=1, source_target_pairs={{0,7},{1,0},{2,1},{3,2},{4,3},{5,4},{6,5},{7,6},{8,15},{9,8},{10,9... | collective-permute-start | bytes 49160 | tf_op jit(solution)/shard_map/ppermute | solution.py:44
  22.0 1.5 %collective-permute-start.6 = (bf16[16,512]{1,0:T(8,128)(2,1)S(1)}, bf16[16,512]{1,0:T(8,128)(2,1)S(1)}, u32[]{:S(2)}, u32[]{:S(2)}) collective-permute-start(bf16[16,512]{1,0:T(8,128)(2,1)S(1)} %get-tuple-element.57), channel_id=1, source_target_pairs={{0,1},{1,2},{2,3},{3,4},{4,5},{5,6},{6,7},{7,0},{8,9},{9,10},{10,1... | collective-permute-start | bytes 49160 | tf_op jit(solution)/shard_map/ppermute | solution.py:44
  25.3 2.9 %collective-permute-start.13 = (bf16[320,512]{1,0:T(8,128)(2,1)}, bf16[320,512]{1,0:T(8,128)(2,1)}, u32[]{:S(2)}, u32[]{:S(2)}) collective-permute-start(bf16[320,512]{1,0:T(8,128)(2,1)} %pad_maximum_fusion.rest_0_), channel_id=1, source_target_pairs={{0,1},{1,0},{2,3},{3,2},{4,5},{5,4},{6,7},{7,6},{8,9},{9,8},{10,11... | collective-permute-start | bytes 983048 | tf_op jit(solution)/shard_map/ppermute | solution.py:25
  28.2 3.4 %collective-permute-start.12 = (bf16[320,512]{1,0:T(8,128)(2,1)}, bf16[320,512]{1,0:T(8,128)(2,1)}, u32[]{:S(2)}, u32[]{:S(2)}) collective-permute-start(bf16[320,512]{1,0:T(8,128)(2,1)} %pad_maximum_fusion.rest_0_), channel_id=1, source_target_pairs={{0,6},{1,7},{2,0},{3,1},{4,2},{5,3},{6,4},{7,5},{8,14},{9,15},{10,... | collective-permute-start | bytes 983048 | tf_op jit(solution)/shard_map/ppermute | solution.py:25
  32.3 2.2 %reshape.62 = bf16[128,3,640]{2,1,0:T(4,128)(2,1)} reshape(bf16[384,640]{1,0:T(8,128)(2,1)} %convolution_convert_fusion) | data formatting | bytes 983040 | tf_op jit(solution)/shard_map/reshape | solution.py:273
  34.5 6.8 %all-to-all-start = ((bf16[128,3,640]{2,1,0:T(4,128)(2,1)}), bf16[128,3,640]{2,1,0:T(4,128)(2,1)}, u32[]{:S(2)}, u32[]{:S(2)}) async-start(bf16[128,3,640]{2,1,0:T(4,128)(2,1)} %reshape.62), calls=%async_computation | async-start | bytes 1310720 | tf_op jit(solution)/shard_map/all_to_all | solution.py:274
  41.4 4.9 %collective-permute-start.9 = (bf16[22,512]{1,0:T(8,128)(2,1)S(1)}, bf16[22,512]{1,0:T(8,128)(2,1)S(1)}, u32[]{:S(2)}, u32[]{:S(2)}) collective-permute-start(bf16[22,512]{1,0:T(8,128)(2,1)S(1)} %pad_maximum_fusion.5), channel_id=1, source_target_pairs={{0,120},{8,0},{16,8},{24,16},{32,24},{40,32},{48,40},{56,48},{64,5... | collective-permute-start | bytes 67592 | tf_op jit(solution)/shard_map/ppermute | solution.py:44
  46.3 6.1 %collective-permute-done.12.rest_3_ = bf16[320,512]{1,0:T(8,128)(2,1)} collective-permute-done((bf16[320,512]{1,0:T(8,128)(2,1)}, bf16[320,512]{1,0:T(8,128)(2,1)}, u32[]{:S(2)}, u32[]{:S(2)}) %collective-permute-start.12) | collective-permute-done | bytes 327712 | tf_op jit(solution)/shard_map/ppermute | solution.py:25
  52.4 1.3 collective-permute-start.16
  53.7 2.2 %collective-permute-done.10.rest_1_ = bf16[320,512]{1,0:T(8,128)(2,1)} collective-permute-done((bf16[320,512]{1,0:T(8,128)(2,1)}, bf16[320,512]{1,0:T(8,128)(2,1)}, u32[]{:S(2)}, u32[]{:S(2)}) %collective-permute-start.10) | collective-permute-done | bytes 327712 | tf_op jit(solution)/shard_map/ppermute | solution.py:25
  55.9 1.1 collective-permute-start.14
  57.0 1.4 pad_maximum_fusion.4
  58.4 1.1 pad_bitcast_fusion
  60.1 4.6 %collective-permute-done.8.above_ref = bf16[22,512]{1,0:T(8,128)(2,1)} collective-permute-done((bf16[22,512]{1,0:T(8,128)(2,1)}, bf16[22,512]{1,0:T(8,128)(2,1)}, u32[]{:S(2)}, u32[]{:S(2)}) %collective-permute-start.8) | collective-permute-done | bytes 22560 | tf_op jit(solution)/shard_map/ppermute | solution.py:44
  64.7 1.2 copy-done.1
  65.9 1.2 copy-done.3
  67.1 1.5 %copy-done.10 = bf16[16,20,6,512]{3,0,2,1:T(8,128)(2,1)S(1)} copy-done((bf16[16,20,6,512]{3,0,2,1:T(8,128)(2,1)S(1)}, bf16[16,20,6,512]{3,0,2,1:T(8,128)(2,1)}, u32[]{:S(2)}) %copy-start.10) | copy-done | bytes 1966104
  68.7 6.7 %fine0.1 = (bf16[1920,512]{1,0:T(8,128)(2,1)S(1)}, f32[320,512]{1,0:T(8,128)S(1)}) custom-call(bf16[1920,512]{1,0:T(8,128)(2,1)S(1)} %bitcast.49, bf16[1920,256]{1,0:T(8,128)(2,1)S(1)} %copy-done.3, bf16[320,512]{1,0:T(8,128)(2,1)S(1)} %bitcast.47, bf16[16,512]{1,0:T(8,128)(2,1)S(1)} %collective-permute-done.6.left_ref, ...), custom_call_target="tpu_custom_call" | custom-call | tf_op jit(solution)/shard_map/fine0/pallas_call | solution.py:114
  75.4 1.3 copy-done.11
  77.5 2.2 %reshape.63 = bf16[384,640]{1,0:T(8,128)(2,1)} reshape(bf16[128,3,640]{2,1,0:T(4,128)(2,1)} %all-to-all-done) | data formatting | bytes 983040 | tf_op jit(solution)/shard_map/reshape | solution.py:275
  79.7 1.3 maximum_maximum_fusion.long_ref.tag_ref
  81.1 1.6 %copy-done.5 = bf16[2,1024,512]{2,1,0:T(8,128)(2,1)S(1)} copy-done((bf16[2,1024,512]{2,1,0:T(8,128)(2,1)S(1)}, bf16[2,1024,512]{2,1,0:T(8,128)(2,1)}, u32[]{:S(2)}) %copy-start.5) | copy-done | bytes 2097176
  82.7 1.2 copy-done.7
  84.0 1.1 copy-done.14
  85.0 6.9 %coarse0.1 = (bf16[544,512]{1,0:T(8,128)(2,1)S(1)}, bf16[320,512]{1,0:T(8,128)(2,1)S(1)}, bf16[20,512]{1,0:T(8,128)(2,1)S(1)}) custom-call(bf16[544,640]{1,0:T(8,128)(2,1)S(1)} %maximum_maximum_fusion.long_ref.tag_ref, bf16[544,640]{1,0:T(8,128)(2,1)S(1)} %maximum_maximum_fusion.long_ref.tag_ref, bf16[320,512]{1,0:T(8,128)(2,1)S(1)} %bitcast.48, ...), custom_call_target="tpu_custom_call" | custom-call | tf_op jit(solution)/shard_map/coarse0/pallas_call | solution.py:186
  92.0 0.9 collective-permute-start.19
  92.9 1.4 collective-permute-start.18
  94.7 2.3 %collective-permute-done.18 = bf16[20,512]{1,0:T(8,128)(2,1)S(1)} collective-permute-done((bf16[20,512]{1,0:T(8,128)(2,1)S(1)}, bf16[20,512]{1,0:T(8,128)(2,1)S(1)}, u32[]{:S(2)}, u32[]{:S(2)}) %collective-permute-start.18) | collective-permute-done | bytes 20512 | tf_op jit(solution)/shard_map/ppermute | solution.py:25
  97.1 1.1 collective-permute-done.17
  98.7 1.1 collective-permute-start.20
  99.8 3.4 %collective-permute-start.24 = (bf16[16,512]{1,0:T(8,128)(2,1)S(1)}, bf16[16,512]{1,0:T(8,128)(2,1)S(1)}, u32[]{:S(2)}, u32[]{:S(2)}) collective-permute-start(bf16[16,512]{1,0:T(8,128)(2,1)S(1)} %get-tuple-element.52), channel_id=1, source_target_pairs={{0,7},{1,0},{2,1},{3,2},{4,3},{5,4},{6,5},{7,6},{8,15},{9,8},{10,9... | collective-permute-start | bytes 49160 | tf_op jit(solution)/shard_map/ppermute | solution.py:44
  104.4 3.1 %collective-permute-start.29 = (bf16[320,512]{1,0:T(8,128)(2,1)S(1)}, bf16[320,512]{1,0:T(8,128)(2,1)S(1)}, u32[]{:S(2)}, u32[]{:S(2)}) collective-permute-start(bf16[320,512]{1,0:T(8,128)(2,1)S(1)} %pad_maximum_fusion.1.rest_0_), channel_id=1, source_target_pairs={{0,6},{1,7},{2,0},{3,1},{4,2},{5,3},{6,4},{7,5},{8,14},{9,15},{10,... | collective-permute-start | bytes 983048 | tf_op jit(solution)/shard_map/ppermute | solution.py:25
  108.1 2.4 %collective-permute-start.30 = (bf16[320,512]{1,0:T(8,128)(2,1)S(1)}, bf16[320,512]{1,0:T(8,128)(2,1)S(1)}, u32[]{:S(2)}, u32[]{:S(2)}) collective-permute-start(bf16[320,512]{1,0:T(8,128)(2,1)S(1)} %pad_maximum_fusion.1.rest_0_), channel_id=1, source_target_pairs={{0,1},{1,0},{2,3},{3,2},{4,5},{5,4},{6,7},{7,6},{8,9},{9,8},{10,11... | collective-permute-start | bytes 983048 | tf_op jit(solution)/shard_map/ppermute | solution.py:25
  110.6 6.0 %collective-permute-done.29.rest_3_ = bf16[320,512]{1,0:T(8,128)(2,1)S(1)} collective-permute-done((bf16[320,512]{1,0:T(8,128)(2,1)S(1)}, bf16[320,512]{1,0:T(8,128)(2,1)S(1)}, u32[]{:S(2)}, u32[]{:S(2)}) %collective-permute-start.29) | collective-permute-done | bytes 327712 | tf_op jit(solution)/shard_map/ppermute | solution.py:25
  116.6 5.8 %collective-permute-start.33 = (bf16[320,512]{1,0:T(8,128)(2,1)S(1)}, bf16[320,512]{1,0:T(8,128)(2,1)S(1)}, u32[]{:S(2)}, u32[]{:S(2)}) collective-permute-start(bf16[320,512]{1,0:T(8,128)(2,1)S(1)} %collective-permute-done.29.rest_3_), channel_id=1, source_target_pairs={{0,1},{1,0},{2,3},{3,2},{4,5},{5,4},{6,7},{7,6},{8,9},{9,8},{10,11... | collective-permute-start | bytes 983048 | tf_op jit(solution)/shard_map/ppermute | solution.py:25
  122.4 2.6 %collective-permute-done.27.rest_1_ = bf16[320,512]{1,0:T(8,128)(2,1)S(1)} collective-permute-done((bf16[320,512]{1,0:T(8,128)(2,1)S(1)}, bf16[320,512]{1,0:T(8,128)(2,1)S(1)}, u32[]{:S(2)}, u32[]{:S(2)}) %collective-permute-start.27) | collective-permute-done | bytes 327712 | tf_op jit(solution)/shard_map/ppermute | solution.py:25
  125.8 2.3 %collective-permute-start.26 = (bf16[22,512]{1,0:T(8,128)(2,1)S(1)}, bf16[22,512]{1,0:T(8,128)(2,1)S(1)}, u32[]{:S(2)}, u32[]{:S(2)}) collective-permute-start(bf16[22,512]{1,0:T(8,128)(2,1)S(1)} %pad_maximum_fusion.7), channel_id=1, source_target_pairs={{0,120},{8,0},{16,8},{24,16},{32,24},{40,32},{48,40},{56,48},{64,5... | collective-permute-start | bytes 67592 | tf_op jit(solution)/shard_map/ppermute | solution.py:44
  128.2 0.9 collective-permute-done.26.below_ref
  129.1 1.6 %collective-permute-start.25 = (bf16[22,512]{1,0:T(8,128)(2,1)S(1)}, bf16[22,512]{1,0:T(8,128)(2,1)S(1)}, u32[]{:S(2)}, u32[]{:S(2)}) collective-permute-start(bf16[22,512]{1,0:T(8,128)(2,1)S(1)} %pad_maximum_fusion.6), channel_id=1, source_target_pairs={{0,8},{8,16},{16,24},{24,32},{32,40},{40,48},{48,56},{56,64},{64,7... | collective-permute-start | bytes 67592 | tf_op jit(solution)/shard_map/ppermute | solution.py:44
  130.7 4.6 %collective-permute-done.25.above_ref = bf16[22,512]{1,0:T(8,128)(2,1)S(1)} collective-permute-done((bf16[22,512]{1,0:T(8,128)(2,1)S(1)}, bf16[22,512]{1,0:T(8,128)(2,1)S(1)}, u32[]{:S(2)}, u32[]{:S(2)}) %collective-permute-start.25) | collective-permute-done | bytes 22560 | tf_op jit(solution)/shard_map/ppermute | solution.py:44
  135.4 6.8 %fine1.1 = (bf16[1920,512]{1,0:T(8,128)(2,1)}, f32[320,512]{1,0:T(8,128)S(1)}) custom-call(bf16[1920,512]{1,0:T(8,128)(2,1)S(1)} %copy-done.12, bf16[1920,256]{1,0:T(8,128)(2,1)S(1)} %copy-done.4, bf16[320,512]{1,0:T(8,128)(2,1)S(1)} %get-tuple-element.31.latents_ref, bf16[16,512]{1,0:T(8,128)(2,1)S(1)} %collective-permute-done.23.left_ref, ...), custom_call_target="tpu_custom_call" | custom-call | tf_op jit(solution)/shard_map/fine1/pallas_call | solution.py:114
  142.2 5.7 %coarse1.1 = (bf16[544,512]{1,0:T(8,128)(2,1)S(1)}, bf16[320,512]{1,0:T(8,128)(2,1)}, bf16[20,512]{1,0:T(8,128)(2,1)}) custom-call(bf16[544,512]{1,0:T(8,128)(2,1)S(1)} %get-tuple-element.30.long_ref, bf16[544,640]{1,0:T(8,128)(2,1)S(1)} %maximum_maximum_fusion.long_ref.tag_ref, bf16[320,512]{1,0:T(8,128)(2,1)S(1)} %get-tuple-element.31.latents_ref, ...), custom_call_target="tpu_custom_call" | custom-call | tf_op jit(solution)/shard_map/coarse1/pallas_call | solution.py:186
  (112 shorter events, 15.3 us)
Async XLA Ops:
  0.6 18.9 %copy-start.9 = (bf16[16,20,512]{2,0,1:T(8,128)(2,1)S(1)}, bf16[16,20,512]{2,0,1:T(8,128)(2,1)}, u32[]{:S(2)}) copy-start(bf16[16,20,512]{2,0,1:T(8,128)(2,1)} %param.13) | copy-start | bytes 983044
  0.6 13.2 %copy-start.17 = (bf16[160,512]{1,0:T(8,128)(2,1)S(1)}, bf16[160,512]{1,0:T(8,128)(2,1)}, u32[]{:S(2)}) copy-start(bf16[160,512]{1,0:T(8,128)(2,1)} %param.15) | copy-start | bytes 491524
  1.4 7.4 %copy-start.18 = (s32[20]{0:T(128)}, s32[20]{0:T(128)S(1)}, u32[]{:S(2)}) copy-start(s32[20]{0:T(128)S(1)} %fusion.41) | copy-start | bytes 244
  3.0 11.9 %collective-permute-start.2 = (bf16[20,512]{1,0:T(8,128)(2,1)S(1)}, bf16[20,512]{1,0:T(8,128)(2,1)S(1)}, u32[]{:S(2)}, u32[]{:S(2)}) collective-permute-start(bf16[20,512]{1,0:T(8,128)(2,1)S(1)} %gather_fusion), channel_id=1, source_target_pairs={{0,96},{1,97},{2,98},{3,99},{4,100},{5,101},{6,102},{7,103},{8,104... | collective-permute-start | bytes 61448 | tf_op jit(solution)/shard_map/ppermute | solution.py:25
  6.7 8.3 %collective-permute-start.1 = (bf16[20,512]{1,0:T(8,128)(2,1)S(1)}, bf16[20,512]{1,0:T(8,128)(2,1)S(1)}, u32[]{:S(2)}, u32[]{:S(2)}) collective-permute-start(bf16[20,512]{1,0:T(8,128)(2,1)S(1)} %gather_fusion), channel_id=1, source_target_pairs={{0,64},{1,65},{2,66},{3,67},{4,68},{5,69},{6,70},{7,71},{8,72},{9,... | collective-permute-start | bytes 61448 | tf_op jit(solution)/shard_map/ppermute | solution.py:25
  7.0 8.0 %collective-permute-start = (bf16[20,512]{1,0:T(8,128)(2,1)S(1)}, bf16[20,512]{1,0:T(8,128)(2,1)}, u32[]{:S(2)}, u32[]{:S(2)}) collective-permute-start(bf16[20,512]{1,0:T(8,128)(2,1)S(1)} %gather_fusion), channel_id=1, source_target_pairs={{0,32},{1,33},{2,34},{3,35},{4,36},{5,37},{6,38},{7,39},{8,40},{9,... | collective-permute-start | bytes 61448 | tf_op jit(solution)/shard_map/ppermute | solution.py:25
  15.0 49.7 %copy-start = (bf16[2,1536,512]{2,1,0:T(8,128)(2,1)S(1)}, bf16[2,1536,512]{2,1,0:T(8,128)(2,1)}, u32[]{:S(2)}) copy-start(bf16[2,1536,512]{2,1,0:T(8,128)(2,1)} %ei_ref.3) | copy-start | bytes 9437188
  15.0 49.7 %copy-start.15 = (f32[2,512]{1,0:T(2,128)S(1)}, f32[2,512]{1,0:T(2,128)}, u32[]{:S(2)}) copy-start(f32[2,512]{1,0:T(2,128)} %eg_ref.3) | copy-start | bytes 12292
  15.9 8.3 %collective-permute-start.5 = (bf16[80,512]{1,0:T(8,128)(2,1)S(1)}, bf16[80,512]{1,0:T(8,128)(2,1)S(1)}, u32[]{:S(2)}, u32[]{:S(2)}) collective-permute-start(bf16[80,512]{1,0:T(8,128)(2,1)S(1)} %pad_maximum_fusion.2), channel_id=1, source_target_pairs={{0,24},{1,25},{2,26},{3,27},{4,28},{5,29},{6,30},{7,31},{8,0},{9,1... | collective-permute-start | bytes 245768 | tf_op jit(solution)/shard_map/ppermute | solution.py:25
  18.4 5.8 %collective-permute-start.4 = (bf16[80,512]{1,0:T(8,128)(2,1)S(1)}, bf16[80,512]{1,0:T(8,128)(2,1)S(1)}, u32[]{:S(2)}, u32[]{:S(2)}) collective-permute-start(bf16[80,512]{1,0:T(8,128)(2,1)S(1)} %pad_maximum_fusion.2), channel_id=1, source_target_pairs={{0,16},{1,17},{2,18},{3,19},{4,20},{5,21},{6,22},{7,23},{8,24},{9,... | collective-permute-start | bytes 245768 | tf_op jit(solution)/shard_map/ppermute | solution.py:25
  19.0 5.2 %collective-permute-start.3 = (bf16[80,512]{1,0:T(8,128)(2,1)S(1)}, bf16[80,512]{1,0:T(8,128)(2,1)S(1)}, u32[]{:S(2)}, u32[]{:S(2)}) collective-permute-start(bf16[80,512]{1,0:T(8,128)(2,1)S(1)} %pad_maximum_fusion.2), channel_id=1, source_target_pairs={{0,8},{1,9},{2,10},{3,11},{4,12},{5,13},{6,14},{7,15},{8,16},{9,17... | collective-permute-start | bytes 245768 | tf_op jit(solution)/shard_map/ppermute | solution.py:25
  19.7 5.6 %collective-permute-start.7 = (bf16[16,512]{1,0:T(8,128)(2,1)S(1)}, bf16[16,512]{1,0:T(8,128)(2,1)S(1)}, u32[]{:S(2)}, u32[]{:S(2)}) collective-permute-start(bf16[16,512]{1,0:T(8,128)(2,1)S(1)} %get-tuple-element.56), channel_id=1, source_target_pairs={{0,7},{1,0},{2,1},{3,2},{4,3},{5,4},{6,5},{7,6},{8,15},{9,8},{10,9... | collective-permute-start | bytes 49160 | tf_op jit(solution)/shard_map/ppermute | solution.py:44
  22.0 3.2 %collective-permute-start.6 = (bf16[16,512]{1,0:T(8,128)(2,1)S(1)}, bf16[16,512]{1,0:T(8,128)(2,1)S(1)}, u32[]{:S(2)}, u32[]{:S(2)}) collective-permute-start(bf16[16,512]{1,0:T(8,128)(2,1)S(1)} %get-tuple-element.57), channel_id=1, source_target_pairs={{0,1},{1,2},{2,3},{3,4},{4,5},{5,6},{6,7},{7,0},{8,9},{9,10},{10,1... | collective-permute-start | bytes 49160 | tf_op jit(solution)/shard_map/ppermute | solution.py:44
  25.3 55.7 %collective-permute-start.13 = (bf16[320,512]{1,0:T(8,128)(2,1)}, bf16[320,512]{1,0:T(8,128)(2,1)}, u32[]{:S(2)}, u32[]{:S(2)}) collective-permute-start(bf16[320,512]{1,0:T(8,128)(2,1)} %pad_maximum_fusion.rest_0_), channel_id=1, source_target_pairs={{0,1},{1,0},{2,3},{3,2},{4,5},{5,4},{6,7},{7,6},{8,9},{9,8},{10,11... | collective-permute-start | bytes 983048 | tf_op jit(solution)/shard_map/ppermute | solution.py:25
  28.2 24.2 %collective-permute-start.12 = (bf16[320,512]{1,0:T(8,128)(2,1)}, bf16[320,512]{1,0:T(8,128)(2,1)}, u32[]{:S(2)}, u32[]{:S(2)}) collective-permute-start(bf16[320,512]{1,0:T(8,128)(2,1)} %pad_maximum_fusion.rest_0_), channel_id=1, source_target_pairs={{0,6},{1,7},{2,0},{3,1},{4,2},{5,3},{6,4},{7,5},{8,14},{9,15},{10,... | collective-permute-start | bytes 983048 | tf_op jit(solution)/shard_map/ppermute | solution.py:25
  31.6 22.2 %collective-permute-start.11 = (bf16[320,512]{1,0:T(8,128)(2,1)}, bf16[320,512]{1,0:T(8,128)(2,1)}, u32[]{:S(2)}, u32[]{:S(2)}) collective-permute-start(bf16[320,512]{1,0:T(8,128)(2,1)} %pad_maximum_fusion.rest_0_), channel_id=1, source_target_pairs={{0,4},{1,5},{2,6},{3,7},{4,0},{5,1},{6,2},{7,3},{8,12},{9,13},{10,... | collective-permute-start | bytes 983048 | tf_op jit(solution)/shard_map/ppermute | solution.py:25
  31.6 24.4 %collective-permute-start.10 = (bf16[320,512]{1,0:T(8,128)(2,1)}, bf16[320,512]{1,0:T(8,128)(2,1)}, u32[]{:S(2)}, u32[]{:S(2)}) collective-permute-start(bf16[320,512]{1,0:T(8,128)(2,1)} %pad_maximum_fusion.rest_0_), channel_id=1, source_target_pairs={{0,2},{1,3},{2,4},{3,5},{4,6},{5,7},{6,0},{7,1},{8,10},{9,11},{10,... | collective-permute-start | bytes 983048 | tf_op jit(solution)/shard_map/ppermute | solution.py:25
  34.5 43.0 %all-to-all-start = ((bf16[128,3,640]{2,1,0:T(4,128)(2,1)}), bf16[128,3,640]{2,1,0:T(4,128)(2,1)}, u32[]{:S(2)}, u32[]{:S(2)}) async-start(bf16[128,3,640]{2,1,0:T(4,128)(2,1)} %reshape.62), calls=%async_computation | async-start | bytes 1310720 | tf_op jit(solution)/shard_map/all_to_all | solution.py:274
  41.4 17.0 %collective-permute-start.9 = (bf16[22,512]{1,0:T(8,128)(2,1)S(1)}, bf16[22,512]{1,0:T(8,128)(2,1)S(1)}, u32[]{:S(2)}, u32[]{:S(2)}) collective-permute-start(bf16[22,512]{1,0:T(8,128)(2,1)S(1)} %pad_maximum_fusion.5), channel_id=1, source_target_pairs={{0,120},{8,0},{16,8},{24,16},{32,24},{40,32},{48,40},{56,48},{64,5... | collective-permute-start | bytes 67592 | tf_op jit(solution)/shard_map/ppermute | solution.py:44
  52.4 28.6 %collective-permute-start.16 = (bf16[320,512]{1,0:T(8,128)(2,1)}, bf16[320,512]{1,0:T(8,128)(2,1)}, u32[]{:S(2)}, u32[]{:S(2)}) collective-permute-start(bf16[320,512]{1,0:T(8,128)(2,1)} %collective-permute-done.12.rest_3_), channel_id=1, source_target_pairs={{0,1},{1,0},{2,3},{3,2},{4,5},{5,4},{6,7},{7,6},{8,9},{9,8},{10,11... | collective-permute-start | bytes 983048 | tf_op jit(solution)/shard_map/ppermute | solution.py:25
  53.7 27.2 %collective-permute-start.15 = (bf16[320,512]{1,0:T(8,128)(2,1)}, bf16[320,512]{1,0:T(8,128)(2,1)}, u32[]{:S(2)}, u32[]{:S(2)}) collective-permute-start(bf16[320,512]{1,0:T(8,128)(2,1)} %collective-permute-done.11.rest_2_), channel_id=1, source_target_pairs={{0,1},{1,0},{2,3},{3,2},{4,5},{5,4},{6,7},{7,6},{8,9},{9,8},{10,11... | collective-permute-start | bytes 983048 | tf_op jit(solution)/shard_map/ppermute | solution.py:25
  55.9 25.0 %collective-permute-start.14 = (bf16[320,512]{1,0:T(8,128)(2,1)}, bf16[320,512]{1,0:T(8,128)(2,1)}, u32[]{:S(2)}, u32[]{:S(2)}) collective-permute-start(bf16[320,512]{1,0:T(8,128)(2,1)} %collective-permute-done.10.rest_1_), channel_id=1, source_target_pairs={{0,1},{1,0},{2,3},{3,2},{4,5},{5,4},{6,7},{7,6},{8,9},{9,8},{10,11... | collective-permute-start | bytes 983048 | tf_op jit(solution)/shard_map/ppermute | solution.py:25
  58.4 6.3 %collective-permute-start.8 = (bf16[22,512]{1,0:T(8,128)(2,1)}, bf16[22,512]{1,0:T(8,128)(2,1)}, u32[]{:S(2)}, u32[]{:S(2)}) collective-permute-start(bf16[22,512]{1,0:T(8,128)(2,1)} %pad_maximum_fusion.4), channel_id=1, source_target_pairs={{0,8},{8,16},{16,24},{24,32},{32,40},{40,48},{48,56},{56,64},{64,7... | collective-permute-start | bytes 67592 | tf_op jit(solution)/shard_map/ppermute | solution.py:44
  67.1 1.5 %copy-start.10 = (bf16[16,20,6,512]{3,0,2,1:T(8,128)(2,1)S(1)}, bf16[16,20,6,512]{3,0,2,1:T(8,128)(2,1)}, u32[]{:S(2)}) copy-start(bf16[16,20,6,512]{3,0,2,1:T(8,128)(2,1)} %param.14) | copy-start | bytes 5898244
  77.5 3.5 %copy-start.16 = (f32[2,512]{1,0:T(2,128)S(1)}, f32[2,512]{1,0:T(2,128)}, u32[]{:S(2)}) copy-start(f32[2,512]{1,0:T(2,128)} %ng_ref.3) | copy-start | bytes 12292
  79.7 1.5 copy-start.2
  81.1 1.6 %copy-start.5 = (bf16[2,1024,512]{2,1,0:T(8,128)(2,1)S(1)}, bf16[2,1024,512]{2,1,0:T(8,128)(2,1)}, u32[]{:S(2)}) copy-start(bf16[2,1024,512]{2,1,0:T(8,128)(2,1)} %ni_ref.3) | copy-start | bytes 6291460
  85.0 50.3 %copy-start.12 = (bf16[1920,512]{1,0:T(8,128)(2,1)S(1)}, bf16[1920,512]{1,0:T(8,128)(2,1)}, u32[]{:S(2)}) copy-start(bf16[1920,512]{1,0:T(8,128)(2,1)} %copy-done.11) | copy-start | bytes 5898244
  92.0 43.4 %copy-start.4 = (bf16[1920,256]{1,0:T(8,128)(2,1)S(1)}, bf16[1920,256]{1,0:T(8,128)(2,1)}, u32[]{:S(2)}) copy-start(bf16[1920,256]{1,0:T(8,128)(2,1)} %fusion.1.picks_ref) | copy-start | bytes 2949124
  92.0 2.7 %collective-permute-start.19 = (bf16[20,512]{1,0:T(8,128)(2,1)S(1)}, bf16[20,512]{1,0:T(8,128)(2,1)S(1)}, u32[]{:S(2)}, u32[]{:S(2)}) collective-permute-start(bf16[20,512]{1,0:T(8,128)(2,1)S(1)} %get-tuple-element.33), channel_id=1, source_target_pairs={{0,96},{1,97},{2,98},{3,99},{4,100},{5,101},{6,102},{7,103},{8,104... | collective-permute-start | bytes 61448 | tf_op jit(solution)/shard_map/ppermute | solution.py:25
  92.9 4.2 %collective-permute-start.18 = (bf16[20,512]{1,0:T(8,128)(2,1)S(1)}, bf16[20,512]{1,0:T(8,128)(2,1)S(1)}, u32[]{:S(2)}, u32[]{:S(2)}) collective-permute-start(bf16[20,512]{1,0:T(8,128)(2,1)S(1)} %get-tuple-element.33), channel_id=1, source_target_pairs={{0,64},{1,65},{2,66},{3,67},{4,68},{5,69},{6,70},{7,71},{8,72},{9,... | collective-permute-start | bytes 61448 | tf_op jit(solution)/shard_map/ppermute | solution.py:25
  94.3 3.9 %collective-permute-start.17 = (bf16[20,512]{1,0:T(8,128)(2,1)S(1)}, bf16[20,512]{1,0:T(8,128)(2,1)S(1)}, u32[]{:S(2)}, u32[]{:S(2)}) collective-permute-start(bf16[20,512]{1,0:T(8,128)(2,1)S(1)} %get-tuple-element.33), channel_id=1, source_target_pairs={{0,32},{1,33},{2,34},{3,35},{4,36},{5,37},{6,38},{7,39},{8,40},{9,... | collective-permute-start | bytes 61448 | tf_op jit(solution)/shard_map/ppermute | solution.py:25
  98.2 5.0 %collective-permute-start.22 = (bf16[80,512]{1,0:T(8,128)(2,1)S(1)}, bf16[80,512]{1,0:T(8,128)(2,1)S(1)}, u32[]{:S(2)}, u32[]{:S(2)}) collective-permute-start(bf16[80,512]{1,0:T(8,128)(2,1)S(1)} %pad_maximum_fusion.3), channel_id=1, source_target_pairs={{0,24},{1,25},{2,26},{3,27},{4,28},{5,29},{6,30},{7,31},{8,0},{9,1... | collective-permute-start | bytes 245768 | tf_op jit(solution)/shard_map/ppermute | solution.py:25
  98.3 4.9 %collective-permute-start.21 = (bf16[80,512]{1,0:T(8,128)(2,1)S(1)}, bf16[80,512]{1,0:T(8,128)(2,1)S(1)}, u32[]{:S(2)}, u32[]{:S(2)}) collective-permute-start(bf16[80,512]{1,0:T(8,128)(2,1)S(1)} %pad_maximum_fusion.3), channel_id=1, source_target_pairs={{0,16},{1,17},{2,18},{3,19},{4,20},{5,21},{6,22},{7,23},{8,24},{9,... | collective-permute-start | bytes 245768 | tf_op jit(solution)/shard_map/ppermute | solution.py:25
  98.7 5.4 %collective-permute-start.20 = (bf16[80,512]{1,0:T(8,128)(2,1)S(1)}, bf16[80,512]{1,0:T(8,128)(2,1)S(1)}, u32[]{:S(2)}, u32[]{:S(2)}) collective-permute-start(bf16[80,512]{1,0:T(8,128)(2,1)S(1)} %pad_maximum_fusion.3), channel_id=1, source_target_pairs={{0,8},{1,9},{2,10},{3,11},{4,12},{5,13},{6,14},{7,15},{8,16},{9,17... | collective-permute-start | bytes 245768 | tf_op jit(solution)/shard_map/ppermute | solution.py:25
  99.8 4.3 %collective-permute-start.24 = (bf16[16,512]{1,0:T(8,128)(2,1)S(1)}, bf16[16,512]{1,0:T(8,128)(2,1)S(1)}, u32[]{:S(2)}, u32[]{:S(2)}) collective-permute-start(bf16[16,512]{1,0:T(8,128)(2,1)S(1)} %get-tuple-element.52), channel_id=1, source_target_pairs={{0,7},{1,0},{2,1},{3,2},{4,3},{5,4},{6,5},{7,6},{8,15},{9,8},{10,9... | collective-permute-start | bytes 49160 | tf_op jit(solution)/shard_map/ppermute | solution.py:44
  103.2 1.2 collective-permute-start.23
  104.4 12.2 %collective-permute-start.29 = (bf16[320,512]{1,0:T(8,128)(2,1)S(1)}, bf16[320,512]{1,0:T(8,128)(2,1)S(1)}, u32[]{:S(2)}, u32[]{:S(2)}) collective-permute-start(bf16[320,512]{1,0:T(8,128)(2,1)S(1)} %pad_maximum_fusion.1.rest_0_), channel_id=1, source_target_pairs={{0,6},{1,7},{2,0},{3,1},{4,2},{5,3},{6,4},{7,5},{8,14},{9,15},{10,... | collective-permute-start | bytes 983048 | tf_op jit(solution)/shard_map/ppermute | solution.py:25
  107.5 14.9 %collective-permute-start.28 = (bf16[320,512]{1,0:T(8,128)(2,1)S(1)}, bf16[320,512]{1,0:T(8,128)(2,1)S(1)}, u32[]{:S(2)}, u32[]{:S(2)}) collective-permute-start(bf16[320,512]{1,0:T(8,128)(2,1)S(1)} %pad_maximum_fusion.1.rest_0_), channel_id=1, source_target_pairs={{0,4},{1,5},{2,6},{3,7},{4,0},{5,1},{6,2},{7,3},{8,12},{9,13},{10,... | collective-permute-start | bytes 983048 | tf_op jit(solution)/shard_map/ppermute | solution.py:25
  107.5 17.5 %collective-permute-start.27 = (bf16[320,512]{1,0:T(8,128)(2,1)S(1)}, bf16[320,512]{1,0:T(8,128)(2,1)S(1)}, u32[]{:S(2)}, u32[]{:S(2)}) collective-permute-start(bf16[320,512]{1,0:T(8,128)(2,1)S(1)} %pad_maximum_fusion.1.rest_0_), channel_id=1, source_target_pairs={{0,2},{1,3},{2,4},{3,5},{4,6},{5,7},{6,0},{7,1},{8,10},{9,11},{10,... | collective-permute-start | bytes 983048 | tf_op jit(solution)/shard_map/ppermute | solution.py:25
  108.1 34.0 %collective-permute-start.30 = (bf16[320,512]{1,0:T(8,128)(2,1)S(1)}, bf16[320,512]{1,0:T(8,128)(2,1)S(1)}, u32[]{:S(2)}, u32[]{:S(2)}) collective-permute-start(bf16[320,512]{1,0:T(8,128)(2,1)S(1)} %pad_maximum_fusion.1.rest_0_), channel_id=1, source_target_pairs={{0,1},{1,0},{2,3},{3,2},{4,5},{5,4},{6,7},{7,6},{8,9},{9,8},{10,11... | collective-permute-start | bytes 983048 | tf_op jit(solution)/shard_map/ppermute | solution.py:25
  116.6 25.6 %collective-permute-start.33 = (bf16[320,512]{1,0:T(8,128)(2,1)S(1)}, bf16[320,512]{1,0:T(8,128)(2,1)S(1)}, u32[]{:S(2)}, u32[]{:S(2)}) collective-permute-start(bf16[320,512]{1,0:T(8,128)(2,1)S(1)} %collective-permute-done.29.rest_3_), channel_id=1, source_target_pairs={{0,1},{1,0},{2,3},{3,2},{4,5},{5,4},{6,7},{7,6},{8,9},{9,8},{10,11... | collective-permute-start | bytes 983048 | tf_op jit(solution)/shard_map/ppermute | solution.py:25
  122.4 19.8 %collective-permute-start.32 = (bf16[320,512]{1,0:T(8,128)(2,1)S(1)}, bf16[320,512]{1,0:T(8,128)(2,1)S(1)}, u32[]{:S(2)}, u32[]{:S(2)}) collective-permute-start(bf16[320,512]{1,0:T(8,128)(2,1)S(1)} %collective-permute-done.28.rest_2_), channel_id=1, source_target_pairs={{0,1},{1,0},{2,3},{3,2},{4,5},{5,4},{6,7},{7,6},{8,9},{9,8},{10,11... | collective-permute-start | bytes 983048 | tf_op jit(solution)/shard_map/ppermute | solution.py:25
  125.0 17.2 %collective-permute-start.31 = (bf16[320,512]{1,0:T(8,128)(2,1)S(1)}, bf16[320,512]{1,0:T(8,128)(2,1)S(1)}, u32[]{:S(2)}, u32[]{:S(2)}) collective-permute-start(bf16[320,512]{1,0:T(8,128)(2,1)S(1)} %collective-permute-done.27.rest_1_), channel_id=1, source_target_pairs={{0,1},{1,0},{2,3},{3,2},{4,5},{5,4},{6,7},{7,6},{8,9},{9,8},{10,11... | collective-permute-start | bytes 983048 | tf_op jit(solution)/shard_map/ppermute | solution.py:25
  125.8 3.2 %collective-permute-start.26 = (bf16[22,512]{1,0:T(8,128)(2,1)S(1)}, bf16[22,512]{1,0:T(8,128)(2,1)S(1)}, u32[]{:S(2)}, u32[]{:S(2)}) collective-permute-start(bf16[22,512]{1,0:T(8,128)(2,1)S(1)} %pad_maximum_fusion.7), channel_id=1, source_target_pairs={{0,120},{8,0},{16,8},{24,16},{32,24},{40,32},{48,40},{56,48},{64,5... | collective-permute-start | bytes 67592 | tf_op jit(solution)/shard_map/ppermute | solution.py:44
  129.1 6.3 %collective-permute-start.25 = (bf16[22,512]{1,0:T(8,128)(2,1)S(1)}, bf16[22,512]{1,0:T(8,128)(2,1)S(1)}, u32[]{:S(2)}, u32[]{:S(2)}) collective-permute-start(bf16[22,512]{1,0:T(8,128)(2,1)S(1)} %pad_maximum_fusion.6), channel_id=1, source_target_pairs={{0,8},{8,16},{16,24},{24,32},{32,40},{40,48},{48,56},{56,64},{64,7... | collective-permute-start | bytes 67592 | tf_op jit(solution)/shard_map/ppermute | solution.py:44
  135.4 6.8 %copy-start.6 = (bf16[2,1024,512]{2,1,0:T(8,128)(2,1)S(1)}, bf16[2,1024,512]{2,1,0:T(8,128)(2,1)}, u32[]{:S(2)}) copy-start(bf16[2,1024,512]{2,1,0:T(8,128)(2,1)} %ni_ref.3) | copy-start | bytes 6291460
  135.4 6.8 %copy-start.8 = (bf16[2,512,512]{2,1,0:T(8,128)(2,1)S(1)}, bf16[2,512,512]{2,1,0:T(8,128)(2,1)}, u32[]{:S(2)}) copy-start(bf16[2,512,512]{2,1,0:T(8,128)(2,1)} %no_ref.3) | copy-start | bytes 3145732
  (6 other events, 6.9 us)

commit v3 on v2

v3 whole, which is shorter than its diff:
```python
import jax
import jax.numpy as jnp
from jax import lax
from jax.experimental import pallas as pl
from jax.experimental.pallas import tpu as pltpu
from jax.sharding import PartitionSpec as P

EPSILON = 1e-05
AXES = ("px", "py")
DIGITS = ((32, 4), (8, 4), (2, 4), (1, 2))
CORE = DIGITS[3]
BAND = 4
TAGS = 128
LOW = 64
CAP = 3
MIB = 1024 * 1024


def shift(values, digit, step):
    stride, size = digit
    pairs = []
    for i in range(128):
        here = i // stride % size
        pairs.append((i, i + ((here + step) % size - here) * stride))
    return lax.ppermute(values, AXES, pairs)


def tie(*values):
    return lax.optimization_barrier(values)


def stage(rows, digit):
    return [rows] + [shift(rows, digit, s) for s in range(1, digit[1])]


def table_row(digits, coarse, coarse_count):
    home = jnp.floor((coarse.astype(jnp.float32) + 0.5) * (1.0 / coarse_count)).astype(jnp.int32)
    row = coarse - home * coarse_count
    ky, kx, kz, kc = (
        (mine - lax.shift_right_logical(home, stride.bit_length() - 1)) & (size - 1)
        for mine, (stride, size) in zip(digits, DIGITS, strict=True)
    )
    return (((kc * 4 + kz) * 4 + kx) * 4 + ky) * coarse_count + row, home, row


def along(values, axis, step):
    count = lax.axis_size(axis)
    return lax.ppermute(values, axis, [(i, (i + step) % count) for i in range(count)])


def selection(neighbours):
    rows, columns, degree = neighbours.shape
    codes = neighbours.transpose(1, 2, 0)
    q = codes + (codes >= 4).astype(jnp.int32)
    column = lax.broadcasted_iota(jnp.int32, codes.shape, 0)
    row = lax.broadcasted_iota(jnp.int32, codes.shape, 2)
    from_row = row + q // 3 - 1
    step = q % 3
    near = (column % BAND + step) * rows + from_row
    sender = jnp.where(from_row < 0, 160 + column + step, jnp.where(from_row >= rows, 192 + column + step, near))
    receiver = 96 + column % BAND * rows + row
    lanes = lax.broadcasted_iota(jnp.int32, codes.shape + (256,), 3)
    picks = (lanes == sender[..., None]) | (lanes == receiver[..., None])
    return picks.astype(jnp.bfloat16).reshape(-1, 256)


def dot(a, b):
    return jnp.dot(a, b, preferred_element_type=jnp.float32)


def finish(before, inner_sum, outer, gains):
    hidden = jax.nn.silu(inner_sum).astype(jnp.bfloat16)
    output = dot(hidden, outer)
    center = output - jnp.mean(output, axis=-1, keepdims=True)
    spread_of = jnp.mean(center * center, axis=-1, keepdims=True)
    scaled = center * lax.rsqrt(spread_of + EPSILON) * gains
    return (before.astype(jnp.float32) + scaled).astype(jnp.bfloat16)


def fine_layer(layer, fine, picks, latents, left, right, above, below, inner, outer, gain, rows):
    edges, features = fine.shape
    nodes = latents.shape[0]
    hidden = inner.shape[2]
    near = (BAND + 2) * rows
    own = BAND * rows
    steps = nodes // own
    block = edges // steps
    degree = edges // nodes
    columns = above.shape[0]

    def body(fine_ref, picks_ref, latents_ref, left_ref, right_ref, above_ref, below_ref, inner_ref, outer_ref, gain_ref,
             next_ref, sum_ref, send_ref, recv_ref, table_ref):
        step = pl.program_id(0)

        @pl.when(step == 0)
        def _():
            send = inner_ref[layer, features : 2 * features, :]
            project = lambda ref: dot(ref[...], send).astype(jnp.bfloat16)
            send_ref[:rows, :] = project(left_ref)
            send_ref[rows : rows + nodes, :] = project(latents_ref)
            send_ref[rows + nodes :, :] = project(right_ref)
            recv_ref[...] = dot(latents_ref[...], inner_ref[layer, 2 * features :, :]).astype(jnp.bfloat16)
            table_ref[...] = jnp.zeros(table_ref.shape, jnp.bfloat16)
            table_ref[160 : 160 + columns, :] = project(above_ref)
            table_ref[192 : 192 + columns, :] = project(below_ref)

        start = pl.multiple_of(step * own, own)
        table_ref[:near, :] = send_ref[pl.ds(start, near), :]
        table_ref[near : near + own, :] = recv_ref[pl.ds(start, own), :]
        before = fine_ref[...]
        total = dot(before, inner_ref[layer, :features, :]) + dot(picks_ref[...], table_ref[...])
        after = finish(before, total, outer_ref[layer], gain_ref[layer : layer + 1, :])
        next_ref[...] = after
        split = after.astype(jnp.float32).reshape(BAND, degree, rows, features)
        sum_ref[...] = jnp.sum(split, axis=1).reshape(own, features)

    held = pl.BlockSpec(memory_space=pltpu.VMEM)
    return pl.pallas_call(
        body,
        name=f"fine{layer}",
        out_shape=(
            jax.ShapeDtypeStruct(fine.shape, jnp.bfloat16),
            jax.ShapeDtypeStruct((nodes, features), jnp.float32),
        ),
        grid=(steps,),
        in_specs=[
            pl.BlockSpec((block, features), lambda i: (i, 0)),
            pl.BlockSpec((block, 256), lambda i: (i, 0)),
        ]
        + [held] * 8,
        out_specs=(
            pl.BlockSpec((block, features), lambda i: (i, 0)),
            pl.BlockSpec((own, features), lambda i: (i, 0)),
        ),
        scratch_shapes=[
            pltpu.VMEM((nodes + 2 * rows, hidden), jnp.bfloat16),
            pltpu.VMEM((nodes, hidden), jnp.bfloat16),
            pltpu.VMEM((256, hidden), jnp.bfloat16),
        ],
        compiler_params=pltpu.CompilerParams(dimension_semantics=("arbitrary",), vmem_limit_bytes=14 * MIB),
    )(fine, picks, latents, left, right, above, below, inner, outer, gain)


def pick(index, width):
    lanes = lax.broadcasted_iota(jnp.int32, (index.shape[0], width), 1)
    return (lanes == index).astype(jnp.bfloat16)


def rows_to_columns(left, right):
    return lax.dot_general(left, right, (((1,), (1,)), ((), ())), preferred_element_type=jnp.float32)


def decode(tags, at):
    numbers = tags.astype(jnp.int32)
    return jnp.where(numbers[:, 4:5] > 0, numbers[:, at : at + 1] * LOW + numbers[:, at + 1 : at + 2], -1)


def coarse_start(coarse_slots, latents, rows, columns):
    count = coarse_slots.shape[1]
    nodes, features = latents.shape

    def body(slots_ref, latents_ref, own_ref, choose_ref):
        slot = slots_ref[...]
        row = jnp.floor((slot.astype(jnp.float32) + 0.5) * (1.0 / columns)).astype(jnp.int32)
        at = (slot - row * columns) * rows + row
        place = (lax.broadcasted_iota(jnp.int32, (nodes, count), 0) == at).astype(jnp.bfloat16)
        same = lax.broadcasted_iota(jnp.int32, (32, count), 0) == lax.broadcasted_iota(jnp.int32, (32, count), 1)
        choose = rows_to_columns(same.astype(jnp.bfloat16), place).astype(jnp.bfloat16)
        choose_ref[...] = choose
        own_ref[...] = dot(choose, latents_ref[...])[:count].astype(jnp.bfloat16)

    held = pl.BlockSpec(memory_space=pltpu.VMEM)
    return pl.pallas_call(
        body,
        name="coarse_start",
        out_shape=(
            jax.ShapeDtypeStruct((count, features), jnp.bfloat16),
            jax.ShapeDtypeStruct((32, nodes), jnp.bfloat16),
        ),
        in_specs=[held] * 2,
        out_specs=(held, held),
        compiler_params=pltpu.CompilerParams(vmem_limit_bytes=4 * MIB),
    )(coarse_slots, latents)


def pack_edges(long_edges, senders, receivers, me, coarse_count, devices):
    count, features = long_edges.shape
    blocks = features // TAGS
    slots = devices * CAP

    def body(me_ref, long_ref, send_ref, recv_ref, sent_ref, mine_ref, wide):
        send, recv = send_ref[...], recv_ref[...]
        here = [
            lax.shift_right_logical(me_ref[0], stride.bit_length() - 1) & (size - 1) for stride, size in DIGITS
        ]
        _, owner, row = table_row(here, recv, coarse_count)
        there = [
            lax.shift_right_logical(owner, stride.bit_length() - 1) & (size - 1) for stride, size in DIGITS
        ]
        field = lax.broadcasted_iota(jnp.int32, (TAGS, count), 0)

        def fields(digits):
            sender = table_row(digits, send, coarse_count)[0]
            receiver = table_row(digits, recv, coarse_count)[0]
            both = jnp.where(field < 2, sender, receiver)
            high = lax.shift_right_logical(both, LOW.bit_length() - 1)
            value = jnp.where(field % 2 == 0, high, both & (LOW - 1))
            value = jnp.where(field == 4, 1, jnp.where(field == 5, owner, value))
            return jnp.where(field < 6, value, 0).astype(jnp.float32).astype(jnp.bfloat16)

        down = lax.broadcasted_iota(jnp.int32, (count, count), 0)
        across = lax.broadcasted_iota(jnp.int32, (count, count), 1)
        mine = rows_to_columns((down == across).astype(jnp.bfloat16), fields(here))
        mine_ref[...] = mine.astype(jnp.bfloat16)
        same = (mine[:, 5:6].astype(jnp.int32) == owner) & (down < across)
        rank = jnp.sum(same.astype(jnp.float32), axis=0, keepdims=True).astype(jnp.int32)
        spot = rank * devices + owner
        place = (lax.broadcasted_iota(jnp.int32, (slots, count), 0) == spot).astype(jnp.bfloat16)
        edges = dot(place, long_ref[...])
        tags = rows_to_columns(place, fields(there))
        for j in range(CAP):
            part = slice(j * devices, (j + 1) * devices)
            for b in range(blocks):
                wide[pl.ds(j * blocks + b, devices, stride=16), :] = edges[part, b * TAGS : (b + 1) * TAGS]
            wide[pl.ds(CAP * blocks + j, devices, stride=16), :] = tags[part]
        wide[pl.ds(15, devices, stride=16), :] = jnp.zeros((devices, TAGS), jnp.float32)
        sent_ref[...] = wide[...].astype(jnp.bfloat16)

    held = pl.BlockSpec(memory_space=pltpu.VMEM)
    return pl.pallas_call(
        body,
        name="pack_edges",
        out_shape=(
            jax.ShapeDtypeStruct((devices * 16, TAGS), jnp.bfloat16),
            jax.ShapeDtypeStruct((count, TAGS), jnp.bfloat16),
        ),
        in_specs=[pl.BlockSpec(memory_space=pltpu.SMEM)] + [held] * 3,
        out_specs=(held, held),
        scratch_shapes=[pltpu.VMEM((devices * 16, TAGS), jnp.float32)],
        compiler_params=pltpu.CompilerParams(vmem_limit_bytes=8 * MIB),
    )(me, long_edges, senders, receivers)


def unpack_edges(arrived, choose, features, table_rows):
    devices = arrived.shape[0] // 16
    blocks = features // TAGS
    slots = devices * CAP
    pad, nodes = choose.shape

    def body(arrived_ref, choose_ref, rows_ref, send_ref, recv_ref, adds_ref, wide):
        wide[...] = arrived_ref[...].astype(jnp.float32)
        for j in range(CAP):
            part = slice(j * devices, (j + 1) * devices)
            for b in range(blocks):
                lanes = slice(b * TAGS, (b + 1) * TAGS)
                rows_ref[part, lanes] = wide[pl.ds(j * blocks + b, devices, stride=16), :].astype(jnp.bfloat16)
            tags = wide[pl.ds(CAP * blocks + j, devices, stride=16), :]
            send_ref[part, :] = pick(decode(tags, 0), table_rows)
            recv_ref[part, :] = pick(decode(tags, 2), TAGS)
        here = recv_ref[:, :pad]
        place = lax.dot_general(choose_ref[...], here, (((0,), (1,)), ((), ())), preferred_element_type=jnp.float32)
        adds_ref[...] = place.astype(jnp.bfloat16)

    held = pl.BlockSpec(memory_space=pltpu.VMEM)
    return pl.pallas_call(
        body,
        name="unpack_edges",
        out_shape=(
            jax.ShapeDtypeStruct((slots, features), jnp.bfloat16),
            jax.ShapeDtypeStruct((slots, table_rows), jnp.bfloat16),
            jax.ShapeDtypeStruct((slots, TAGS), jnp.bfloat16),
            jax.ShapeDtypeStruct((nodes, slots), jnp.bfloat16),
        ),
        in_specs=[held] * 2,
        out_specs=(held,) * 4,
        scratch_shapes=[pltpu.VMEM(arrived.shape, jnp.float32)],
        compiler_params=pltpu.CompilerParams(vmem_limit_bytes=8 * MIB),
    )(arrived, choose)


def long_step(before, sent, got, inner_ref, outer_ref, gain_ref, layer):
    features = before.shape[1]
    total = dot(before, inner_ref[layer, :features, :])
    total += dot(sent, inner_ref[layer, features : 2 * features, :])
    total += dot(got, inner_ref[layer, 2 * features :, :])
    return finish(before, total, outer_ref[layer], gain_ref[layer : layer + 1, :])


def coarse_layer(layer, long_rows, sends, recvs, adds, choose, pieces, latents, fine_sum,
                 edge_inner, edge_outer, edge_gain, node_inner, node_outer, node_gain, coarse_count):
    slots = long_rows.shape[0]
    nodes, features = latents.shape
    count = len(pieces)
    each = pieces[0].shape[0]
    table_rows = count * each

    def body(long_ref, sends_ref, recvs_ref, adds_ref, choose_ref, latents_ref, sum_ref,
             ei_ref, eo_ref, eg_ref, ni_ref, no_ref, ng_ref, *rest):
        piece_refs = rest[:count]
        long_next_ref, next_ref, own_ref, table, ni, no, sems = rest[count:]
        weights = [
            pltpu.make_async_copy(ni_ref.at[layer], ni, sems.at[0]),
            pltpu.make_async_copy(no_ref.at[layer], no, sems.at[1]),
        ]
        for copy in weights:
            copy.start()
        for p in range(count):
            table[p * each : (p + 1) * each, :] = piece_refs[p][...]
        sent = dot(sends_ref[...], table[...]).astype(jnp.bfloat16)
        got = dot(recvs_ref[...], table[:TAGS, :]).astype(jnp.bfloat16)
        after = long_step(long_ref[...], sent, got, ei_ref, eo_ref, eg_ref, layer)
        long_next_ref[...] = after
        incoming = (sum_ref[...] + dot(adds_ref[...], after)).astype(jnp.bfloat16)
        old = latents_ref[...]
        for copy in weights:
            copy.wait()
        total = dot(old, ni[:features, :]) + dot(incoming, ni[features:, :])
        new = finish(old, total, no[...], ng_ref[layer : layer + 1, :])
        next_ref[...] = new
        own_ref[...] = dot(choose_ref[...], new)[:coarse_count].astype(jnp.bfloat16)

    held = pl.BlockSpec(memory_space=pltpu.VMEM)
    away = pl.BlockSpec(memory_space=pl.ANY)
    return pl.pallas_call(
        body,
        name=f"coarse{layer}",
        out_shape=(
            jax.ShapeDtypeStruct((slots, features), jnp.bfloat16),
            jax.ShapeDtypeStruct(latents.shape, jnp.bfloat16),
            jax.ShapeDtypeStruct((coarse_count, features), jnp.bfloat16),
            jax.ShapeDtypeStruct((table_rows, features), jnp.bfloat16),
        ),
        in_specs=[held] * 10 + [away] * 2 + [held] * (1 + count),
        out_specs=(held,) * 4,
        scratch_shapes=[
            pltpu.VMEM(node_inner.shape[1:], jnp.bfloat16),
            pltpu.VMEM(node_outer.shape[1:], jnp.bfloat16),
            pltpu.SemaphoreType.DMA((2,)),
        ],
        compiler_params=pltpu.CompilerParams(vmem_limit_bytes=14 * MIB),
    )(long_rows, sends, recvs, adds, choose, latents, fine_sum,
      edge_inner, edge_outer, edge_gain, node_inner, node_outer, node_gain, *pieces)


def own_layer(layer, long_rows, tags, table, edge_inner, edge_outer, edge_gain):
    def body(long_ref, tag_ref, table_ref, ei_ref, eo_ref, eg_ref, next_ref):
        rows = table_ref.shape[0]
        numbers = tag_ref[...].astype(jnp.float32)
        sent = dot(pick(decode(numbers, 0), rows), table_ref[...]).astype(jnp.bfloat16)
        got = dot(pick(decode(numbers, 2), rows), table_ref[...]).astype(jnp.bfloat16)
        next_ref[...] = long_step(long_ref[...], sent, got, ei_ref, eo_ref, eg_ref, layer)

    held = pl.BlockSpec(memory_space=pltpu.VMEM)
    return pl.pallas_call(
        body,
        name=f"own{layer}",
        out_shape=jax.ShapeDtypeStruct(long_rows.shape, jnp.bfloat16),
        in_specs=[held] * 6,
        out_specs=held,
        compiler_params=pltpu.CompilerParams(vmem_limit_bytes=10 * MIB),
    )(long_rows, tags, table, edge_inner, edge_outer, edge_gain)


def shards(
    node_latents,
    fine_edges,
    long_edges,
    neighbours,
    coarse_slots,
    long_senders,
    long_receivers,
    edge_inner,
    edge_outer,
    edge_gain,
    node_inner,
    node_outer,
    node_gain,
):
    rows, columns, features = node_latents.shape
    degree = fine_edges.shape[2]
    nodes = rows * columns
    coarse_count = coarse_slots.shape[0]
    layers = edge_inner.shape[0]
    devices = lax.axis_size("px") * lax.axis_size("py")

    latents = node_latents.transpose(1, 0, 2).reshape(nodes, features)
    fine = fine_edges.transpose(1, 2, 0, 3).reshape(nodes * degree, features)
    own, choose = coarse_start(coarse_slots[None, :], latents, rows, columns)
    own_rows = long_edges
    me = lax.axis_index(AXES).reshape(1)
    payload, own_tags = pack_edges(long_edges, long_senders[None, :], long_receivers[None, :], me, coarse_count, devices)
    for layer in range(layers):
        grid = latents.reshape(columns, rows, features)
        joined = jnp.concatenate(stage(own, DIGITS[0]), axis=0)
        left = along(grid[-1], "py", 1)
        right = along(grid[0], "py", -1)
        if layer == 0:
            packed = payload.reshape(devices, 16, TAGS)
            arrived = lax.all_to_all(packed, AXES, split_axis=0, concat_axis=0, tiled=True).reshape(payload.shape)
        joined, left, right, payload = tie(joined, left, right, payload)
        high = jnp.concatenate([left[-1:], grid[:, -1], right[-1:]], axis=0)
        low = jnp.concatenate([left[:1], grid[:, 0], right[:1]], axis=0)
        joined = jnp.concatenate(stage(joined, DIGITS[1]), axis=0)
        above = along(high, "px", 1)
        below = along(low, "px", -1)
        joined, above, below, arrived, own_rows, neighbours = tie(joined, above, below, arrived, own_rows, neighbours)
        pieces = stage(joined, DIGITS[2])
        if layer == 0:
            long_rows, sends, recvs, adds = unpack_edges(arrived, choose, features, 2 * len(pieces) * joined.shape[0])
            picks = selection(neighbours)
        else:
            own_rows = own_layer(layer - 1, own_rows, own_tags, table, edge_inner, edge_outer, edge_gain)
        fine, fine_sum = fine_layer(
            layer, fine, picks, latents, left, right, above, below, edge_inner, edge_outer, edge_gain, rows
        )
        first, *others, fine_sum, own_rows, long_rows = tie(*pieces, fine_sum, own_rows, long_rows)
        pieces = [first] + others
        pieces = pieces + [shift(piece, CORE, 1) for piece in pieces]
        long_rows, latents, own, table = coarse_layer(
            layer, long_rows, sends, recvs, adds, choose, pieces, latents, fine_sum,
            edge_inner, edge_outer, edge_gain, node_inner, node_outer, node_gain, coarse_count,
        )
    own_rows = own_layer(layers - 1, own_rows, own_tags, table, edge_inner, edge_outer, edge_gain)
    return (
        latents.reshape(columns, rows, features).transpose(1, 0, 2),
        fine.reshape(columns, degree, rows, features).transpose(2, 0, 1, 3),
        own_rows,
    )


def solution(mesh):
    in_specs = (
        P("px", "py", None),
        P("px", "py", None, None),
        P(AXES, None),
        P("px", "py", None),
        P(AXES),
        P(AXES),
        P(AXES),
        P(),
        P(),
        P(),
        P(),
        P(),
        P(),
    )
    out_specs = (P("px", "py", None), P("px", "py", None, None), P(AXES, None))
    return jax.shard_map(shards, mesh=mesh, in_specs=in_specs, out_specs=out_specs, check_vma=False)
```

time: 150 us -> 129 us (0.86)
  waiting for transfers between devices: 32.4 us -> 18 us
  Pallas kernels: 26.2 us -> 32.6 us
  starting transfers between devices: 57.4 us -> 51.7 us
  other arithmetic: 10.8 us -> 6.63 us
  local copies, waits for them, and re-layouts: 19.8 us -> 17.8 us
    pallas_call x0 -> x5, Pallas kernels: none -> 9.14 us  [the longest x2 4.39 us: own_layer(): pl.pallas_call(body, name=f'own{layer}', out_shape=jax.ShapeDtypeStruct(l...]
    ppermute x26, waiting for transfers between devices: 21.7 us -> 13.4 us  [shift(): return lax.ppermute(values, AXES, pairs)]
    ppermute x26, starting transfers between devices: 34.4 us -> 26.4 us  [shift(): return lax.ppermute(values, AXES, pairs)]
    ppermute x8, waiting for transfers between devices: 10.7 us -> 4.61 us  [along(): lax.ppermute(values, axis, [(i, (i + step) % count) for i in range(count)])]
    reshape x2 -> x0, local copies, waits for them, and re-layouts: 4.37 us -> none  [the longest x1 2.21 us: shards(): sent = payload.reshape(devices, CAP, features + TAGS)]
    pallas_call x2, Pallas kernels: 12.7 us -> 9.73 us  [coarse_layer(): pl.pallas_call(body, name=f'coarse{layer}', out_shape=(jax.ShapeDtypeStru...]
    add x2, local copies, waits for them, and re-layouts: 0.21 us -> 3.12 us  [selection(): receiver = 96 + column % BAND * rows + row]
    all_to_all x1, starting transfers between devices: 6.83 us -> 9.55 us  [shards(): lax.all_to_all(packed, AXES, split_axis=0, concat_axis=0, tiled=True)]
  transfers between devices with their start and end apart: 35 -> 35, of which waited for: 13 -> 16; matrix products, arithmetic and copies ran while one was open for 12% -> 12% of each run, Pallas kernels for 9% -> 15%
where the time goes in v3:
time: 129 us; the launch traced here: 128 us
  starting transfers between devices  51.7 us (40%)
  Pallas kernels  32.6 us (25%)
  waiting for transfers between devices  18 us (14%)
  local copies, waits for them, and re-layouts  17.8 us (14%)
  other arithmetic  6.63 us (5%)
    ppermute x26, starting transfers between devices, shift(): return lax.ppermute(values, AXES, pairs)  26.4 us
    ppermute x8, starting transfers between devices, along(): lax.ppermute(values, axis, [(i, (i + step) % count) for i in range(count)])  15.8 us
    pallas_call x2, Pallas kernels, fine_layer(): pl.pallas_call(body, name=f'fine{layer}', out_shape=(jax.ShapeDtypeStruct...  13.7 us
    ppermute x26, waiting for transfers between devices, shift(): return lax.ppermute(values, AXES, pairs)  13.4 us
    pallas_call x2, Pallas kernels, coarse_layer(): pl.pallas_call(body, name=f'coarse{layer}', out_shape=(jax.ShapeDtypeStru...  9.73 us
    all_to_all x1, starting transfers between devices, shards(): lax.all_to_all(packed, AXES, split_axis=0, concat_axis=0, tiled=True)  9.55 us
    unnamed x42, local copies, waits for them, and re-layouts  9.41 us
    ppermute x8, waiting for transfers between devices, along(): lax.ppermute(values, axis, [(i, (i + step) % count) for i in range(count)])  4.61 us
  transfers between devices with their start and end apart: 35, of which 16 were waited for; matrix products, arithmetic and copies ran while one was open for 12% of the time, Pallas kernels for 15%

profile of v3, /device:TPU:1, one launch (start us, length us, event | category | flops | bytes accessed | tf_op | source)
XLA Modules:
  0.0 127.8 jit_solution(1513237879033707624)
XLA Ops:
  0.6 1.0 copy-done.4
  2.3 0.9 coarse_start.1
  3.2 3.6 %collective-permute-start.2 = (bf16[20,512]{1,0:T(8,128)(2,1)}, bf16[20,512]{1,0:T(8,128)(2,1)}, u32[]{:S(2)}, u32[]{:S(2)}) collective-permute-start(bf16[20,512]{1,0:T(8,128)(2,1)} %get-tuple-element.51), channel_id=1, source_target_pairs={{0,96},{1,97},{2,98},{3,99},{4,100},{5,101},{6,102},{7,103},{8,104... | collective-permute-start | bytes 61448 | tf_op jit(solution)/shard_map/ppermute | solution.py:25
  8.4 1.5 %collective-permute-start.4 = (bf16[16,512]{1,0:T(8,128)(2,1)}, bf16[16,512]{1,0:T(8,128)(2,1)}, u32[]{:S(2)}, u32[]{:S(2)}) collective-permute-start(bf16[16,512]{1,0:T(8,128)(2,1)} %get-tuple-element.105), channel_id=1, source_target_pairs={{0,7},{1,0},{2,1},{3,2},{4,3},{5,4},{6,5},{7,6},{8,15},{9,8},{10,9... | collective-permute-start | bytes 49160 | tf_op jit(solution)/shard_map/ppermute | solution.py:48
  9.9 1.5 %collective-permute-start.3 = (bf16[16,512]{1,0:T(8,128)(2,1)}, bf16[16,512]{1,0:T(8,128)(2,1)}, u32[]{:S(2)}, u32[]{:S(2)}) collective-permute-start(bf16[16,512]{1,0:T(8,128)(2,1)} %get-tuple-element.106), channel_id=1, source_target_pairs={{0,1},{1,2},{2,3},{3,4},{4,5},{5,6},{6,7},{7,0},{8,9},{9,10},{10,1... | collective-permute-start | bytes 49160 | tf_op jit(solution)/shard_map/ppermute | solution.py:48
  11.4 0.9 copy-done.8
  13.7 1.6 %pack_edges.1 = (bf16[2048,128]{1,0:T(8,128)(2,1)}, bf16[160,128]{1,0:T(8,128)(2,1)S(1)}) custom-call(s32[1]{0:T(128)} %bitcast.5.me_ref, bf16[160,512]{1,0:T(8,128)(2,1)S(1)} %copy-done.8, s32[1,160]{1,0:T(1,128)S(1)} %bitcast.49, s32[1,160]{1,0:T(1,128)S(1)} %bitcast.50), custom_call_target="tpu_custom_call" | custom-call | tf_op jit(solution)/shard_map/pack_edges/pallas_call | solution.py:230
  15.3 9.6 %all-to-all-start = ((bf16[128,16,128]{2,1,0:T(8,128)(2,1)}), bf16[128,16,128]{2,1,0:T(8,128)(2,1)}, u32[]{:S(2)}, u32[]{:S(2)}) async-start(bf16[128,16,128]{2,1,0:T(8,128)(2,1)} %bitcast.8), calls=%async_computation | async-start | bytes 1048576 | tf_op jit(solution)/shard_map/all_to_all | solution.py:399
  25.4 1.3 %fusion.13 = (bf16[20,1,512]{2,1,0:T(2,128)(2,1)S(1)}, bf16[20,1,512]{2,1,0:T(2,128)(2,1)S(1)}) fusion(bf16[20,16,512]{2,1,0:T(8,128)(2,1)} %bitcast.42), kind=kLoop, calls=%fused_computation.41 | loop fusion | bytes 81920 | tf_op jit(solution)/shard_map/slice | solution.py:402
  27.3 0.8 pad_maximum_fusion.2
  28.1 2.7 %collective-permute-start.7 = (bf16[80,512]{1,0:T(8,128)(2,1)S(1)}, bf16[80,512]{1,0:T(8,128)(2,1)S(1)}, u32[]{:S(2)}, u32[]{:S(2)}) collective-permute-start(bf16[80,512]{1,0:T(8,128)(2,1)S(1)} %pad_maximum_fusion.2), channel_id=1, source_target_pairs={{0,24},{1,25},{2,26},{3,27},{4,28},{5,29},{6,30},{7,31},{8,0},{9,1... | collective-permute-start | bytes 245768 | tf_op jit(solution)/shard_map/ppermute | solution.py:25
  31.9 0.8 fusion.16
  32.7 1.6 %collective-permute-start.8 = (bf16[22,512]{1,0:T(8,128)(2,1)S(1)}, bf16[22,512]{1,0:T(8,128)(2,1)S(1)}, u32[]{:S(2)}, u32[]{:S(2)}) collective-permute-start(bf16[22,512]{1,0:T(8,128)(2,1)S(1)} %pad_maximum_fusion.4), channel_id=1, source_target_pairs={{0,8},{8,16},{16,24},{24,32},{32,40},{40,48},{48,56},{56,64},{64,7... | collective-permute-start | bytes 67592 | tf_op jit(solution)/shard_map/ppermute | solution.py:48
  34.3 3.4 %collective-permute-start.9 = (bf16[22,512]{1,0:T(8,128)(2,1)S(1)}, bf16[22,512]{1,0:T(8,128)(2,1)S(1)}, u32[]{:S(2)}, u32[]{:S(2)}) collective-permute-start(bf16[22,512]{1,0:T(8,128)(2,1)S(1)} %pad_maximum_fusion.5), channel_id=1, source_target_pairs={{0,120},{8,0},{16,8},{24,16},{32,24},{40,32},{48,40},{56,48},{64,5... | collective-permute-start | bytes 67592 | tf_op jit(solution)/shard_map/ppermute | solution.py:48
  38.1 0.7 pad_maximum_fusion.rest_0_
  38.8 1.6 %collective-permute-done.8.above_ref = bf16[22,512]{1,0:T(8,128)(2,1)S(1)} collective-permute-done((bf16[22,512]{1,0:T(8,128)(2,1)S(1)}, bf16[22,512]{1,0:T(8,128)(2,1)S(1)}, u32[]{:S(2)}, u32[]{:S(2)}) %collective-permute-start.8) | collective-permute-done | bytes 22560 | tf_op jit(solution)/shard_map/ppermute | solution.py:48
  41.6 3.2 %collective-permute-start.12 = (bf16[320,512]{1,0:T(8,128)(2,1)}, bf16[320,512]{1,0:T(8,128)(2,1)}, u32[]{:S(2)}, u32[]{:S(2)}) collective-permute-start(bf16[320,512]{1,0:T(8,128)(2,1)} %pad_maximum_fusion.rest_0_), channel_id=1, source_target_pairs={{0,6},{1,7},{2,0},{3,1},{4,2},{5,3},{6,4},{7,5},{8,14},{9,15},{10,... | collective-permute-start | bytes 983048 | tf_op jit(solution)/shard_map/ppermute | solution.py:25
  44.9 0.8 collective-permute-start.10
  45.7 1.5 %fusion.5 = (s32[20,6,16]{0,2,1:T(8,128)}, s32[20,6,16]{0,2,1:T(8,128)}) fusion(s32[16,20,6]{1,0,2:T(8,128)} %param.16, s32[20]{0:T(128)S(1)} %get-tuple-element.119, s32[20]{0:T(128)S(1)} %get-tuple-element.122, s32[20]{0:T(128)} %get-tuple-element.120, s32[20]{0:T(128)S(1)} %get-tuple-element.121, pred[20]{0:T(512)(128)(4,1)} %compare_and_fusion), kind=kLoop, calls=%fused_computation.15 | loop fusion | flops 57600 | bytes 23380 | tf_op jit(solution)/shard_map/jit(_where)/select_n | solution.py:60
  47.2 1.6 %copy.16 = s32[20,6,16]{2,1,0:T(8,128)} copy(s32[20,6,16]{0,2,1:T(8,128)} %get-tuple-element.115) | data formatting | bytes 15360 | tf_op jit(solution)/shard_map/jit(_where)/select_n | solution.py:60
  48.8 1.0 eq.24
  49.8 1.6 %copy.17 = s32[20,6,16]{2,1,0:T(8,128)} copy(s32[20,6,16]{0,2,1:T(8,128)} %get-tuple-element.116) | data formatting | bytes 15360 | tf_op jit(solution)/shard_map/add | solution.py:61
  51.3 1.6 %add.89 = s32[1920]{0:T(1024)} reshape(s32[20,6,16]{2,1,0:T(8,128)} %copy.17) | data formatting | bytes 15360 | tf_op jit(solution)/shard_map/add | solution.py:61
  52.9 2.2 %unpack_edges.1 = (bf16[384,512]{1,0:T(8,128)(2,1)S(1)}, bf16[384,2560]{1,0:T(8,128)(2,1)S(1)}, bf16[384,128]{1,0:T(8,128)(2,1)S(1)}, bf16[320,384]{1,0:T(8,128)(2,1)S(1)}) custom-call(bf16[2048,128]{1,0:T(8,128)(2,1)} %bitcast.9.arrived_ref, bf16[32,320]{1,0:T(8,128)(2,1)S(1)} %get-tuple-element.63.choose_ref), custom_call_target="tpu_custom_call" | custom-call | tf_op jit(solution)/shard_map/unpack_edges/pallas_call | solution.py:265
  55.1 2.5 %fusion.1.picks_ref = bf16[1920,256]{1,0:T(8,128)(2,1)S(1)} fusion(s32[1920]{0:T(1024)} %add.89, s32[1920]{0:T(1024)S(1)} %eq.24), kind=kLoop, calls=%fused_computation.3 | loop fusion | flops 1966080 | bytes 998400 | tf_op jit(solution)/shard_map/convert_element_type | solution.py:64
  57.6 1.2 copy-done.1
  58.9 1.5 %copy-done.6 = bf16[16,20,6,512]{3,0,2,1:T(8,128)(2,1)S(1)} copy-done((bf16[16,20,6,512]{3,0,2,1:T(8,128)(2,1)S(1)}, bf16[16,20,6,512]{3,0,2,1:T(8,128)(2,1)}, u32[]{:S(2)}) %copy-start.6) | copy-done | bytes 1966104
  60.4 0.7 copy-done.12
  61.9 6.9 %fine0.1 = (bf16[1920,512]{1,0:T(8,128)(2,1)S(1)}, f32[320,512]{1,0:T(8,128)S(1)}) custom-call(bf16[1920,512]{1,0:T(8,128)(2,1)S(1)} %bitcast.47, bf16[1920,256]{1,0:T(8,128)(2,1)S(1)} %fusion.1.picks_ref, bf16[320,512]{1,0:T(8,128)(2,1)S(1)} %bitcast.45, bf16[16,512]{1,0:T(8,128)(2,1)} %collective-permute-done.3.left_ref, ...), custom_call_target="tpu_custom_call" | custom-call | tf_op jit(solution)/shard_map/fine0/pallas_call | solution.py:118
  68.8 2.2 %collective-permute-start.13 = (bf16[320,512]{1,0:T(8,128)(2,1)S(1)}, bf16[320,512]{1,0:T(8,128)(2,1)S(1)}, u32[]{:S(2)}, u32[]{:S(2)}) collective-permute-start(bf16[320,512]{1,0:T(8,128)(2,1)S(1)} %copy-done.7), channel_id=1, source_target_pairs={{0,1},{1,0},{2,3},{3,2},{4,5},{5,4},{6,7},{7,6},{8,9},{9,8},{10,11... | collective-permute-start | bytes 983048 | tf_op jit(solution)/shard_map/ppermute | solution.py:25
  73.9 5.2 %coarse0.1 = (bf16[384,512]{1,0:T(8,128)(2,1)S(1)}, bf16[320,512]{1,0:T(8,128)(2,1)S(1)}, bf16[20,512]{1,0:T(8,128)(2,1)S(1)}, bf16[2560,512]{1,0:T(8,128)(2,1)S(1)}) custom-call(bf16[384,512]{1,0:T(8,128)(2,1)S(1)} %get-tuple-element.65.long_ref, bf16[384,2560]{1,0:T(8,128)(2,1)S(1)} %get-tuple-element.66.sends_ref, ...), custom_call_target="tpu_custom_call" | custom-call | tf_op jit(solution)/shard_map/coarse0/pallas_call | solution.py:324
  79.1 0.8 collective-permute-start.19
  81.0 1.2 collective-permute-start.21
  82.2 1.6 %collective-permute-start.20 = (bf16[16,512]{1,0:T(8,128)(2,1)S(1)}, bf16[16,512]{1,0:T(8,128)(2,1)S(1)}, u32[]{:S(2)}, u32[]{:S(2)}) collective-permute-start(bf16[16,512]{1,0:T(8,128)(2,1)S(1)} %get-tuple-element.102), channel_id=1, source_target_pairs={{0,1},{1,2},{2,3},{3,4},{4,5},{5,6},{6,7},{7,0},{8,9},{9,10},{10,1... | collective-permute-start | bytes 49160 | tf_op jit(solution)/shard_map/ppermute | solution.py:48
  84.4 1.2 collective-permute-done.21.right_ref
  85.6 3.1 %collective-permute-start.24 = (bf16[80,512]{1,0:T(8,128)(2,1)S(1)}, bf16[80,512]{1,0:T(8,128)(2,1)S(1)}, u32[]{:S(2)}, u32[]{:S(2)}) collective-permute-start(bf16[80,512]{1,0:T(8,128)(2,1)S(1)} %pad_maximum_fusion.3), channel_id=1, source_target_pairs={{0,24},{1,25},{2,26},{3,27},{4,28},{5,29},{6,30},{7,31},{8,0},{9,1... | collective-permute-start | bytes 245768 | tf_op jit(solution)/shard_map/ppermute | solution.py:25
  89.3 2.2 %collective-permute-start.25 = (bf16[22,512]{1,0:T(8,128)(2,1)S(1)}, bf16[22,512]{1,0:T(8,128)(2,1)S(1)}, u32[]{:S(2)}, u32[]{:S(2)}) collective-permute-start(bf16[22,512]{1,0:T(8,128)(2,1)S(1)} %pad_maximum_fusion.6), channel_id=1, source_target_pairs={{0,8},{8,16},{16,24},{24,32},{32,40},{40,48},{48,56},{56,64},{64,7... | collective-permute-start | bytes 67592 | tf_op jit(solution)/shard_map/ppermute | solution.py:48
  91.5 2.8 %collective-permute-start.26 = (bf16[22,512]{1,0:T(8,128)(2,1)S(1)}, bf16[22,512]{1,0:T(8,128)(2,1)S(1)}, u32[]{:S(2)}, u32[]{:S(2)}) collective-permute-start(bf16[22,512]{1,0:T(8,128)(2,1)S(1)} %pad_maximum_fusion.7), channel_id=1, source_target_pairs={{0,120},{8,0},{16,8},{24,16},{32,24},{40,32},{48,40},{56,48},{64,5... | collective-permute-start | bytes 67592 | tf_op jit(solution)/shard_map/ppermute | solution.py:48
  94.3 1.8 %collective-permute-done.25.above_ref = bf16[22,512]{1,0:T(8,128)(2,1)S(1)} collective-permute-done((bf16[22,512]{1,0:T(8,128)(2,1)S(1)}, bf16[22,512]{1,0:T(8,128)(2,1)S(1)}, u32[]{:S(2)}, u32[]{:S(2)}) %collective-permute-start.25) | collective-permute-done | bytes 22560 | tf_op jit(solution)/shard_map/ppermute | solution.py:48
  96.1 3.6 %collective-permute-start.29 = (bf16[320,512]{1,0:T(8,128)(2,1)S(1)}, bf16[320,512]{1,0:T(8,128)(2,1)S(1)}, u32[]{:S(2)}, u32[]{:S(2)}) collective-permute-start(bf16[320,512]{1,0:T(8,128)(2,1)S(1)} %pad_maximum_fusion.1.rest_0_), channel_id=1, source_target_pairs={{0,6},{1,7},{2,0},{3,1},{4,2},{5,3},{6,4},{7,5},{8,14},{9,15},{10,... | collective-permute-start | bytes 983048 | tf_op jit(solution)/shard_map/ppermute | solution.py:25
  100.2 1.9 %own0.1.long_ref = bf16[160,512]{1,0:T(8,128)(2,1)S(1)} custom-call(bf16[160,512]{1,0:T(8,128)(2,1)S(1)} %copy-done.9, bf16[160,128]{1,0:T(8,128)(2,1)S(1)} %get-tuple-element.86.tag_ref, bf16[2560,512]{1,0:T(8,128)(2,1)S(1)} %get-tuple-element.87.table_ref, bf16[2,1536,512]{2,1,0:T(8,128)(2,1)S(1)} %copy-done, bf16[2,512,512]{2,1,0:T(8,128)(2,1)S(1)} %copy-done.1, ...), custom_call_target="tpu_custom_call" | custom-call | tf_op jit(solution)/shard_map/own0/pallas_call | solution.py:354
  102.1 6.8 %fine1.1 = (bf16[1920,512]{1,0:T(8,128)(2,1)}, f32[320,512]{1,0:T(8,128)S(1)}) custom-call(bf16[1920,512]{1,0:T(8,128)(2,1)S(1)} %get-tuple-element.81.fine_ref, bf16[1920,256]{1,0:T(8,128)(2,1)S(1)} %fusion.1.picks_ref, bf16[320,512]{1,0:T(8,128)(2,1)S(1)} %get-tuple-element.75.latents_ref, bf16[16,512]{1,0:T(8,128)(2,1)S(1)} %collective-permute-done.20.left_ref, ...), custom_call_target="tpu_custom_call" | custom-call | tf_op jit(solution)/shard_map/fine1/pallas_call | solution.py:118
  108.9 3.9 %collective-permute-done.29.rest_3_ = bf16[320,512]{1,0:T(8,128)(2,1)S(1)} collective-permute-done((bf16[320,512]{1,0:T(8,128)(2,1)S(1)}, bf16[320,512]{1,0:T(8,128)(2,1)S(1)}, u32[]{:S(2)}, u32[]{:S(2)}) %collective-permute-start.29) | collective-permute-done | bytes 327712 | tf_op jit(solution)/shard_map/ppermute | solution.py:25
  112.8 4.4 %collective-permute-done.27.rest_1_ = bf16[320,512]{1,0:T(8,128)(2,1)S(1)} collective-permute-done((bf16[320,512]{1,0:T(8,128)(2,1)S(1)}, bf16[320,512]{1,0:T(8,128)(2,1)S(1)}, u32[]{:S(2)}, u32[]{:S(2)}) %collective-permute-start.27) | collective-permute-done | bytes 327712 | tf_op jit(solution)/shard_map/ppermute | solution.py:25
  117.2 0.9 collective-permute-start.30
  118.5 0.7 collective-permute-done.30.rest_4_
  120.7 4.6 %coarse1.1 = (bf16[384,512]{1,0:T(8,128)(2,1)}, bf16[320,512]{1,0:T(8,128)(2,1)}, bf16[20,512]{1,0:T(8,128)(2,1)}, bf16[2560,512]{1,0:T(8,128)(2,1)S(1)}) custom-call(bf16[384,512]{1,0:T(8,128)(2,1)S(1)} %get-tuple-element.89.long_ref, bf16[384,2560]{1,0:T(8,128)(2,1)S(1)} %get-tuple-element.66.sends_ref, bf16[384,128]{1,0:T(8,128)(2,1)S(1)} %get-tuple-element.67.recvs_ref, ...), custom_call_target="tpu_custom_call" | custom-call | tf_op jit(solution)/shard_map/coarse1/pallas_call | solution.py:324
  125.3 2.5 %own1.1 = bf16[160,512]{1,0:T(8,128)(2,1)} custom-call(bf16[160,512]{1,0:T(8,128)(2,1)S(1)} %own0.1.long_ref, bf16[160,128]{1,0:T(8,128)(2,1)S(1)} %get-tuple-element.86.tag_ref, bf16[2560,512]{1,0:T(8,128)(2,1)S(1)} %get-tuple-element.98.table_ref, bf16[2,1536,512]{2,1,0:T(8,128)(2,1)S(1)} %copy-done, bf16[2,512,512]{2,1,0:T(8,128)(2,1)S(1)} %copy-done.1, ...), custom_call_target="tpu_custom_call" | custom-call | tf_op jit(solution)/shard_map/own1/pallas_call | solution.py:354
  (97 shorter events, 15.9 us)
Async XLA Ops:
  0.6 1.0 copy-start.4
  3.2 24.1 %collective-permute-start.2 = (bf16[20,512]{1,0:T(8,128)(2,1)}, bf16[20,512]{1,0:T(8,128)(2,1)}, u32[]{:S(2)}, u32[]{:S(2)}) collective-permute-start(bf16[20,512]{1,0:T(8,128)(2,1)} %get-tuple-element.51), channel_id=1, source_target_pairs={{0,96},{1,97},{2,98},{3,99},{4,100},{5,101},{6,102},{7,103},{8,104... | collective-permute-start | bytes 61448 | tf_op jit(solution)/shard_map/ppermute | solution.py:25
  6.7 20.5 %collective-permute-start.1 = (bf16[20,512]{1,0:T(8,128)(2,1)}, bf16[20,512]{1,0:T(8,128)(2,1)}, u32[]{:S(2)}, u32[]{:S(2)}) collective-permute-start(bf16[20,512]{1,0:T(8,128)(2,1)} %get-tuple-element.51), channel_id=1, source_target_pairs={{0,64},{1,65},{2,66},{3,67},{4,68},{5,69},{6,70},{7,71},{8,72},{9,... | collective-permute-start | bytes 61448 | tf_op jit(solution)/shard_map/ppermute | solution.py:25
  7.1 20.2 %collective-permute-start = (bf16[20,512]{1,0:T(8,128)(2,1)}, bf16[20,512]{1,0:T(8,128)(2,1)}, u32[]{:S(2)}, u32[]{:S(2)}) collective-permute-start(bf16[20,512]{1,0:T(8,128)(2,1)} %get-tuple-element.51), channel_id=1, source_target_pairs={{0,32},{1,33},{2,34},{3,35},{4,36},{5,37},{6,38},{7,39},{8,40},{9,... | collective-permute-start | bytes 61448 | tf_op jit(solution)/shard_map/ppermute | solution.py:25
  8.4 19.7 %collective-permute-start.4 = (bf16[16,512]{1,0:T(8,128)(2,1)}, bf16[16,512]{1,0:T(8,128)(2,1)}, u32[]{:S(2)}, u32[]{:S(2)}) collective-permute-start(bf16[16,512]{1,0:T(8,128)(2,1)} %get-tuple-element.105), channel_id=1, source_target_pairs={{0,7},{1,0},{2,1},{3,2},{4,3},{5,4},{6,5},{7,6},{8,15},{9,8},{10,9... | collective-permute-start | bytes 49160 | tf_op jit(solution)/shard_map/ppermute | solution.py:48
  9.9 18.2 %collective-permute-start.3 = (bf16[16,512]{1,0:T(8,128)(2,1)}, bf16[16,512]{1,0:T(8,128)(2,1)}, u32[]{:S(2)}, u32[]{:S(2)}) collective-permute-start(bf16[16,512]{1,0:T(8,128)(2,1)} %get-tuple-element.106), channel_id=1, source_target_pairs={{0,1},{1,2},{2,3},{3,4},{4,5},{5,6},{6,7},{7,0},{8,9},{9,10},{10,1... | collective-permute-start | bytes 49160 | tf_op jit(solution)/shard_map/ppermute | solution.py:48
  11.4 0.9 copy-start.8
  15.3 42.3 %copy-start.5 = (bf16[16,20,512]{2,0,1:T(8,128)(2,1)S(1)}, bf16[16,20,512]{2,0,1:T(8,128)(2,1)}, u32[]{:S(2)}) copy-start(bf16[16,20,512]{2,0,1:T(8,128)(2,1)} %param.13) | copy-start | bytes 983044
  15.3 26.3 %all-to-all-start = ((bf16[128,16,128]{2,1,0:T(8,128)(2,1)}), bf16[128,16,128]{2,1,0:T(8,128)(2,1)}, u32[]{:S(2)}, u32[]{:S(2)}) async-start(bf16[128,16,128]{2,1,0:T(8,128)(2,1)} %bitcast.8), calls=%async_computation | async-start | bytes 1048576 | tf_op jit(solution)/shard_map/all_to_all | solution.py:399
  24.9 32.7 %copy-start = (bf16[2,1536,512]{2,1,0:T(8,128)(2,1)S(1)}, bf16[2,1536,512]{2,1,0:T(8,128)(2,1)}, u32[]{:S(2)}) copy-start(bf16[2,1536,512]{2,1,0:T(8,128)(2,1)} %ei_ref.7) | copy-start | bytes 9437188
  24.9 32.7 %copy-start.10 = (f32[2,512]{1,0:T(2,128)S(1)}, f32[2,512]{1,0:T(2,128)}, u32[]{:S(2)}) copy-start(f32[2,512]{1,0:T(2,128)} %eg_ref.7) | copy-start | bytes 12292
  28.1 9.6 %collective-permute-start.7 = (bf16[80,512]{1,0:T(8,128)(2,1)S(1)}, bf16[80,512]{1,0:T(8,128)(2,1)S(1)}, u32[]{:S(2)}, u32[]{:S(2)}) collective-permute-start(bf16[80,512]{1,0:T(8,128)(2,1)S(1)} %pad_maximum_fusion.2), channel_id=1, source_target_pairs={{0,24},{1,25},{2,26},{3,27},{4,28},{5,29},{6,30},{7,31},{8,0},{9,1... | collective-permute-start | bytes 245768 | tf_op jit(solution)/shard_map/ppermute | solution.py:25
  30.8 6.9 %collective-permute-start.6 = (bf16[80,512]{1,0:T(8,128)(2,1)S(1)}, bf16[80,512]{1,0:T(8,128)(2,1)S(1)}, u32[]{:S(2)}, u32[]{:S(2)}) collective-permute-start(bf16[80,512]{1,0:T(8,128)(2,1)S(1)} %pad_maximum_fusion.2), channel_id=1, source_target_pairs={{0,16},{1,17},{2,18},{3,19},{4,20},{5,21},{6,22},{7,23},{8,24},{9,... | collective-permute-start | bytes 245768 | tf_op jit(solution)/shard_map/ppermute | solution.py:25
  31.4 6.7 %collective-permute-start.5 = (bf16[80,512]{1,0:T(8,128)(2,1)S(1)}, bf16[80,512]{1,0:T(8,128)(2,1)S(1)}, u32[]{:S(2)}, u32[]{:S(2)}) collective-permute-start(bf16[80,512]{1,0:T(8,128)(2,1)S(1)} %pad_maximum_fusion.2), channel_id=1, source_target_pairs={{0,8},{1,9},{2,10},{3,11},{4,12},{5,13},{6,14},{7,15},{8,16},{9,17... | collective-permute-start | bytes 245768 | tf_op jit(solution)/shard_map/ppermute | solution.py:25
  32.7 7.7 %collective-permute-start.8 = (bf16[22,512]{1,0:T(8,128)(2,1)S(1)}, bf16[22,512]{1,0:T(8,128)(2,1)S(1)}, u32[]{:S(2)}, u32[]{:S(2)}) collective-permute-start(bf16[22,512]{1,0:T(8,128)(2,1)S(1)} %pad_maximum_fusion.4), channel_id=1, source_target_pairs={{0,8},{8,16},{16,24},{24,32},{32,40},{40,48},{48,56},{56,64},{64,7... | collective-permute-start | bytes 67592 | tf_op jit(solution)/shard_map/ppermute | solution.py:48
  34.3 6.7 %collective-permute-start.9 = (bf16[22,512]{1,0:T(8,128)(2,1)S(1)}, bf16[22,512]{1,0:T(8,128)(2,1)S(1)}, u32[]{:S(2)}, u32[]{:S(2)}) collective-permute-start(bf16[22,512]{1,0:T(8,128)(2,1)S(1)} %pad_maximum_fusion.5), channel_id=1, source_target_pairs={{0,120},{8,0},{16,8},{24,16},{32,24},{40,32},{48,40},{56,48},{64,5... | collective-permute-start | bytes 67592 | tf_op jit(solution)/shard_map/ppermute | solution.py:48
  41.6 27.2 %collective-permute-start.12 = (bf16[320,512]{1,0:T(8,128)(2,1)}, bf16[320,512]{1,0:T(8,128)(2,1)}, u32[]{:S(2)}, u32[]{:S(2)}) collective-permute-start(bf16[320,512]{1,0:T(8,128)(2,1)} %pad_maximum_fusion.rest_0_), channel_id=1, source_target_pairs={{0,6},{1,7},{2,0},{3,1},{4,2},{5,3},{6,4},{7,5},{8,14},{9,15},{10,... | collective-permute-start | bytes 983048 | tf_op jit(solution)/shard_map/ppermute | solution.py:25
  44.8 24.0 %collective-permute-start.11 = (bf16[320,512]{1,0:T(8,128)(2,1)}, bf16[320,512]{1,0:T(8,128)(2,1)}, u32[]{:S(2)}, u32[]{:S(2)}) collective-permute-start(bf16[320,512]{1,0:T(8,128)(2,1)} %pad_maximum_fusion.rest_0_), channel_id=1, source_target_pairs={{0,4},{1,5},{2,6},{3,7},{4,0},{5,1},{6,2},{7,3},{8,12},{9,13},{10,... | collective-permute-start | bytes 983048 | tf_op jit(solution)/shard_map/ppermute | solution.py:25
  44.9 24.0 %collective-permute-start.10 = (bf16[320,512]{1,0:T(8,128)(2,1)}, bf16[320,512]{1,0:T(8,128)(2,1)}, u32[]{:S(2)}, u32[]{:S(2)}) collective-permute-start(bf16[320,512]{1,0:T(8,128)(2,1)} %pad_maximum_fusion.rest_0_), channel_id=1, source_target_pairs={{0,2},{1,3},{2,4},{3,5},{4,6},{5,7},{6,0},{7,1},{8,10},{9,11},{10,... | collective-permute-start | bytes 983048 | tf_op jit(solution)/shard_map/ppermute | solution.py:25
  57.6 1.2 copy-start.1
  58.9 1.5 %copy-start.6 = (bf16[16,20,6,512]{3,0,2,1:T(8,128)(2,1)S(1)}, bf16[16,20,6,512]{3,0,2,1:T(8,128)(2,1)}, u32[]{:S(2)}) copy-start(bf16[16,20,6,512]{3,0,2,1:T(8,128)(2,1)} %param.14) | copy-start | bytes 5898244
  60.4 0.7 copy-start.12
  61.9 7.0 %copy-start.7 = (bf16[320,512]{1,0:T(8,128)(2,1)S(1)}, bf16[320,512]{1,0:T(8,128)(2,1)}, u32[]{:S(2)}) copy-start(bf16[320,512]{1,0:T(8,128)(2,1)} %pad_maximum_fusion.rest_0_) | copy-start | bytes 983044
  61.9 12.0 %copy-start.2 = (bf16[2,1024,512]{2,1,0:T(8,128)(2,1)S(1)}, bf16[2,1024,512]{2,1,0:T(8,128)(2,1)}, u32[]{:S(2)}) copy-start(bf16[2,1024,512]{2,1,0:T(8,128)(2,1)} %ni_ref.3) | copy-start | bytes 6291460
  61.9 12.0 %copy-start.3 = (bf16[2,512,512]{2,1,0:T(8,128)(2,1)S(1)}, bf16[2,512,512]{2,1,0:T(8,128)(2,1)}, u32[]{:S(2)}) copy-start(bf16[2,512,512]{2,1,0:T(8,128)(2,1)} %no_ref.3) | copy-start | bytes 3145732
  61.9 12.0 %copy-start.15 = (f32[2,512]{1,0:T(2,128)S(1)}, f32[2,512]{1,0:T(2,128)}, u32[]{:S(2)}) copy-start(f32[2,512]{1,0:T(2,128)} %ng_ref.3) | copy-start | bytes 12292
  68.8 3.4 %collective-permute-start.13 = (bf16[320,512]{1,0:T(8,128)(2,1)S(1)}, bf16[320,512]{1,0:T(8,128)(2,1)S(1)}, u32[]{:S(2)}, u32[]{:S(2)}) collective-permute-start(bf16[320,512]{1,0:T(8,128)(2,1)S(1)} %copy-done.7), channel_id=1, source_target_pairs={{0,1},{1,0},{2,3},{3,2},{4,5},{5,4},{6,7},{7,6},{8,9},{9,8},{10,11... | collective-permute-start | bytes 983048 | tf_op jit(solution)/shard_map/ppermute | solution.py:25
  71.0 1.9 %collective-permute-start.14 = (bf16[320,512]{1,0:T(8,128)(2,1)}, bf16[320,512]{1,0:T(8,128)(2,1)S(1)}, u32[]{:S(2)}, u32[]{:S(2)}) collective-permute-start(bf16[320,512]{1,0:T(8,128)(2,1)} %collective-permute-done.10.rest_1_), channel_id=1, source_target_pairs={{0,1},{1,0},{2,3},{3,2},{4,5},{5,4},{6,7},{7,6},{8,9},{9,8},{10,11... | collective-permute-start | bytes 983048 | tf_op jit(solution)/shard_map/ppermute | solution.py:25
  71.1 2.3 %collective-permute-start.15 = (bf16[320,512]{1,0:T(8,128)(2,1)}, bf16[320,512]{1,0:T(8,128)(2,1)S(1)}, u32[]{:S(2)}, u32[]{:S(2)}) collective-permute-start(bf16[320,512]{1,0:T(8,128)(2,1)} %collective-permute-done.11.rest_2_), channel_id=1, source_target_pairs={{0,1},{1,0},{2,3},{3,2},{4,5},{5,4},{6,7},{7,6},{8,9},{9,8},{10,11... | collective-permute-start | bytes 983048 | tf_op jit(solution)/shard_map/ppermute | solution.py:25
  71.5 2.4 %collective-permute-start.16 = (bf16[320,512]{1,0:T(8,128)(2,1)}, bf16[320,512]{1,0:T(8,128)(2,1)S(1)}, u32[]{:S(2)}, u32[]{:S(2)}) collective-permute-start(bf16[320,512]{1,0:T(8,128)(2,1)} %collective-permute-done.12.rest_3_), channel_id=1, source_target_pairs={{0,1},{1,0},{2,3},{3,2},{4,5},{5,4},{6,7},{7,6},{8,9},{9,8},{10,11... | collective-permute-start | bytes 983048 | tf_op jit(solution)/shard_map/ppermute | solution.py:25
  73.9 26.4 %copy-start.9 = (bf16[160,512]{1,0:T(8,128)(2,1)S(1)}, bf16[160,512]{1,0:T(8,128)(2,1)}, u32[]{:S(2)}) copy-start(bf16[160,512]{1,0:T(8,128)(2,1)} %long_ref.2) | copy-start | bytes 491524
  79.1 4.9 %collective-permute-start.19 = (bf16[20,512]{1,0:T(8,128)(2,1)S(1)}, bf16[20,512]{1,0:T(8,128)(2,1)S(1)}, u32[]{:S(2)}, u32[]{:S(2)}) collective-permute-start(bf16[20,512]{1,0:T(8,128)(2,1)S(1)} %get-tuple-element.74), channel_id=1, source_target_pairs={{0,96},{1,97},{2,98},{3,99},{4,100},{5,101},{6,102},{7,103},{8,104... | collective-permute-start | bytes 61448 | tf_op jit(solution)/shard_map/ppermute | solution.py:25
  79.9 4.2 %collective-permute-start.18 = (bf16[20,512]{1,0:T(8,128)(2,1)S(1)}, bf16[20,512]{1,0:T(8,128)(2,1)S(1)}, u32[]{:S(2)}, u32[]{:S(2)}) collective-permute-start(bf16[20,512]{1,0:T(8,128)(2,1)S(1)} %get-tuple-element.74), channel_id=1, source_target_pairs={{0,64},{1,65},{2,66},{3,67},{4,68},{5,69},{6,70},{7,71},{8,72},{9,... | collective-permute-start | bytes 61448 | tf_op jit(solution)/shard_map/ppermute | solution.py:25
  80.3 4.0 %collective-permute-start.17 = (bf16[20,512]{1,0:T(8,128)(2,1)S(1)}, bf16[20,512]{1,0:T(8,128)(2,1)S(1)}, u32[]{:S(2)}, u32[]{:S(2)}) collective-permute-start(bf16[20,512]{1,0:T(8,128)(2,1)S(1)} %get-tuple-element.74), channel_id=1, source_target_pairs={{0,32},{1,33},{2,34},{3,35},{4,36},{5,37},{6,38},{7,39},{8,40},{9,... | collective-permute-start | bytes 61448 | tf_op jit(solution)/shard_map/ppermute | solution.py:25
  81.0 4.6 %collective-permute-start.21 = (bf16[16,512]{1,0:T(8,128)(2,1)S(1)}, bf16[16,512]{1,0:T(8,128)(2,1)S(1)}, u32[]{:S(2)}, u32[]{:S(2)}) collective-permute-start(bf16[16,512]{1,0:T(8,128)(2,1)S(1)} %get-tuple-element.101), channel_id=1, source_target_pairs={{0,7},{1,0},{2,1},{3,2},{4,3},{5,4},{6,5},{7,6},{8,15},{9,8},{10,9... | collective-permute-start | bytes 49160 | tf_op jit(solution)/shard_map/ppermute | solution.py:48
  82.2 3.4 %collective-permute-start.20 = (bf16[16,512]{1,0:T(8,128)(2,1)S(1)}, bf16[16,512]{1,0:T(8,128)(2,1)S(1)}, u32[]{:S(2)}, u32[]{:S(2)}) collective-permute-start(bf16[16,512]{1,0:T(8,128)(2,1)S(1)} %get-tuple-element.102), channel_id=1, source_target_pairs={{0,1},{1,2},{2,3},{3,4},{4,5},{5,6},{6,7},{7,0},{8,9},{9,10},{10,1... | collective-permute-start | bytes 49160 | tf_op jit(solution)/shard_map/ppermute | solution.py:48
  85.6 8.7 %collective-permute-start.24 = (bf16[80,512]{1,0:T(8,128)(2,1)S(1)}, bf16[80,512]{1,0:T(8,128)(2,1)S(1)}, u32[]{:S(2)}, u32[]{:S(2)}) collective-permute-start(bf16[80,512]{1,0:T(8,128)(2,1)S(1)} %pad_maximum_fusion.3), channel_id=1, source_target_pairs={{0,24},{1,25},{2,26},{3,27},{4,28},{5,29},{6,30},{7,31},{8,0},{9,1... | collective-permute-start | bytes 245768 | tf_op jit(solution)/shard_map/ppermute | solution.py:25
  88.7 5.6 %collective-permute-start.23 = (bf16[80,512]{1,0:T(8,128)(2,1)S(1)}, bf16[80,512]{1,0:T(8,128)(2,1)S(1)}, u32[]{:S(2)}, u32[]{:S(2)}) collective-permute-start(bf16[80,512]{1,0:T(8,128)(2,1)S(1)} %pad_maximum_fusion.3), channel_id=1, source_target_pairs={{0,16},{1,17},{2,18},{3,19},{4,20},{5,21},{6,22},{7,23},{8,24},{9,... | collective-permute-start | bytes 245768 | tf_op jit(solution)/shard_map/ppermute | solution.py:25
  88.7 5.6 %collective-permute-start.22 = (bf16[80,512]{1,0:T(8,128)(2,1)S(1)}, bf16[80,512]{1,0:T(8,128)(2,1)S(1)}, u32[]{:S(2)}, u32[]{:S(2)}) collective-permute-start(bf16[80,512]{1,0:T(8,128)(2,1)S(1)} %pad_maximum_fusion.3), channel_id=1, source_target_pairs={{0,8},{1,9},{2,10},{3,11},{4,12},{5,13},{6,14},{7,15},{8,16},{9,17... | collective-permute-start | bytes 245768 | tf_op jit(solution)/shard_map/ppermute | solution.py:25
  89.3 6.8 %collective-permute-start.25 = (bf16[22,512]{1,0:T(8,128)(2,1)S(1)}, bf16[22,512]{1,0:T(8,128)(2,1)S(1)}, u32[]{:S(2)}, u32[]{:S(2)}) collective-permute-start(bf16[22,512]{1,0:T(8,128)(2,1)S(1)} %pad_maximum_fusion.6), channel_id=1, source_target_pairs={{0,8},{8,16},{16,24},{24,32},{32,40},{40,48},{48,56},{56,64},{64,7... | collective-permute-start | bytes 67592 | tf_op jit(solution)/shard_map/ppermute | solution.py:48
  91.5 4.6 %collective-permute-start.26 = (bf16[22,512]{1,0:T(8,128)(2,1)S(1)}, bf16[22,512]{1,0:T(8,128)(2,1)S(1)}, u32[]{:S(2)}, u32[]{:S(2)}) collective-permute-start(bf16[22,512]{1,0:T(8,128)(2,1)S(1)} %pad_maximum_fusion.7), channel_id=1, source_target_pairs={{0,120},{8,0},{16,8},{24,16},{32,24},{40,32},{48,40},{56,48},{64,5... | collective-permute-start | bytes 67592 | tf_op jit(solution)/shard_map/ppermute | solution.py:48
  96.1 16.7 %collective-permute-start.29 = (bf16[320,512]{1,0:T(8,128)(2,1)S(1)}, bf16[320,512]{1,0:T(8,128)(2,1)S(1)}, u32[]{:S(2)}, u32[]{:S(2)}) collective-permute-start(bf16[320,512]{1,0:T(8,128)(2,1)S(1)} %pad_maximum_fusion.1.rest_0_), channel_id=1, source_target_pairs={{0,6},{1,7},{2,0},{3,1},{4,2},{5,3},{6,4},{7,5},{8,14},{9,15},{10,... | collective-permute-start | bytes 983048 | tf_op jit(solution)/shard_map/ppermute | solution.py:25
  99.7 13.1 %collective-permute-start.28 = (bf16[320,512]{1,0:T(8,128)(2,1)S(1)}, bf16[320,512]{1,0:T(8,128)(2,1)S(1)}, u32[]{:S(2)}, u32[]{:S(2)}) collective-permute-start(bf16[320,512]{1,0:T(8,128)(2,1)S(1)} %pad_maximum_fusion.1.rest_0_), channel_id=1, source_target_pairs={{0,4},{1,5},{2,6},{3,7},{4,0},{5,1},{6,2},{7,3},{8,12},{9,13},{10,... | collective-permute-start | bytes 983048 | tf_op jit(solution)/shard_map/ppermute | solution.py:25
  99.7 17.5 %collective-permute-start.27 = (bf16[320,512]{1,0:T(8,128)(2,1)S(1)}, bf16[320,512]{1,0:T(8,128)(2,1)S(1)}, u32[]{:S(2)}, u32[]{:S(2)}) collective-permute-start(bf16[320,512]{1,0:T(8,128)(2,1)S(1)} %pad_maximum_fusion.1.rest_0_), channel_id=1, source_target_pairs={{0,2},{1,3},{2,4},{3,5},{4,6},{5,7},{6,0},{7,1},{8,10},{9,11},{10,... | collective-permute-start | bytes 983048 | tf_op jit(solution)/shard_map/ppermute | solution.py:25
  117.2 2.1 %collective-permute-start.30 = (bf16[320,512]{1,0:T(8,128)(2,1)S(1)}, bf16[320,512]{1,0:T(8,128)(2,1)S(1)}, u32[]{:S(2)}, u32[]{:S(2)}) collective-permute-start(bf16[320,512]{1,0:T(8,128)(2,1)S(1)} %pad_maximum_fusion.1.rest_0_), channel_id=1, source_target_pairs={{0,1},{1,0},{2,3},{3,2},{4,5},{5,4},{6,7},{7,6},{8,9},{9,8},{10,11... | collective-permute-start | bytes 983048 | tf_op jit(solution)/shard_map/ppermute | solution.py:25
  118.0 1.7 %collective-permute-start.31 = (bf16[320,512]{1,0:T(8,128)(2,1)S(1)}, bf16[320,512]{1,0:T(8,128)(2,1)S(1)}, u32[]{:S(2)}, u32[]{:S(2)}) collective-permute-start(bf16[320,512]{1,0:T(8,128)(2,1)S(1)} %collective-permute-done.27.rest_1_), channel_id=1, source_target_pairs={{0,1},{1,0},{2,3},{3,2},{4,5},{5,4},{6,7},{7,6},{8,9},{9,8},{10,11... | collective-permute-start | bytes 983048 | tf_op jit(solution)/shard_map/ppermute | solution.py:25
  118.0 2.2 %collective-permute-start.32 = (bf16[320,512]{1,0:T(8,128)(2,1)S(1)}, bf16[320,512]{1,0:T(8,128)(2,1)S(1)}, u32[]{:S(2)}, u32[]{:S(2)}) collective-permute-start(bf16[320,512]{1,0:T(8,128)(2,1)S(1)} %collective-permute-done.28.rest_2_), channel_id=1, source_target_pairs={{0,1},{1,0},{2,3},{3,2},{4,5},{5,4},{6,7},{7,6},{8,9},{9,8},{10,11... | collective-permute-start | bytes 983048 | tf_op jit(solution)/shard_map/ppermute | solution.py:25
  118.5 2.2 %collective-permute-start.33 = (bf16[320,512]{1,0:T(8,128)(2,1)S(1)}, bf16[320,512]{1,0:T(8,128)(2,1)S(1)}, u32[]{:S(2)}, u32[]{:S(2)}) collective-permute-start(bf16[320,512]{1,0:T(8,128)(2,1)S(1)} %collective-permute-done.29.rest_3_), channel_id=1, source_target_pairs={{0,1},{1,0},{2,3},{3,2},{4,5},{5,4},{6,7},{7,6},{8,9},{9,8},{10,11... | collective-permute-start | bytes 983048 | tf_op jit(solution)/shard_map/ppermute | solution.py:25
  (6 other events, 4.0 us)

commit v4 on v3

v4 whole, which is shorter than its diff:
```python
import jax
import jax.numpy as jnp
from jax import lax
from jax.experimental import pallas as pl
from jax.experimental.pallas import tpu as pltpu
from jax.sharding import PartitionSpec as P

EPSILON = 1e-05
AXES = ("px", "py")
RING = 16
Z, CORE = (2, 4), (1, 2)
BAND = 4
TAGS = 128
LOW = 64
CAP = 3
ABOVE, BELOW = 160, 192
MIB = 1024 * 1024


def shift(values, digit, step):
    stride, size = digit
    pairs = []
    for i in range(8):
        here = i // stride % size
        pairs.append((i, i + ((here + step) % size - here) * stride))
    return lax.ppermute(values, "py", pairs)


def tie(*values):
    return lax.optimization_barrier(values)


def table_row(px, py, coarse, coarse_count):
    home = jnp.floor((coarse.astype(jnp.float32) + 0.5) * (1.0 / coarse_count)).astype(jnp.int32)
    row = coarse - home * coarse_count
    away = (px - lax.shift_right_logical(home, 3)) & (RING - 1)
    near, far = away & 3, lax.shift_right_logical(away + 1, 2) & 3
    home_z, home_core = lax.shift_right_logical(home, 1) & 3, home & 1
    kz = (lax.shift_right_logical(py, 1) - home_z) & 3
    kc = (py - home_core) & 1
    return (((kc * 4 + kz) * 4 + far) * 4 + near) * coarse_count + row, home


def along(values, axis, step):
    count = lax.axis_size(axis)
    return lax.ppermute(values, axis, [(i, (i + step) % count) for i in range(count)])


def selection(neighbours):
    rows, columns, degree = neighbours.shape

    def body(codes_ref, picks_ref):
        codes = codes_ref[...]
        q = codes + (codes >= 4).astype(jnp.int32)
        down = (q >= 3).astype(jnp.int32) + (q >= 6).astype(jnp.int32)
        step = q - 3 * down
        from_row = lax.broadcasted_iota(jnp.int32, codes.shape, 1) + down - 1
        column = lax.broadcasted_iota(jnp.int32, codes.shape, 2)
        from_column = column + step - 1
        near = ((column & (BAND - 1)) + step) * rows + from_row
        outer = jnp.where(from_column < 0, columns, jnp.where(from_column >= columns, columns + 1, from_column))
        sender = jnp.where(from_row < 0, ABOVE + outer, jnp.where(from_row >= rows, BELOW + outer, near))
        lanes = lax.broadcasted_iota(jnp.int32, (rows, 256), 1)
        row = lax.broadcasted_iota(jnp.int32, (rows, 256), 0)
        for c in range(columns):
            receiver = lanes == (BAND + 2 + c % BAND) * rows + row
            for k in range(degree):
                picks = (lanes == sender[k, :, c : c + 1]) | receiver
                picks_ref[(c * degree + k) * rows : (c * degree + k + 1) * rows, :] = picks.astype(jnp.bfloat16)

    held = pl.BlockSpec(memory_space=pltpu.VMEM)
    return pl.pallas_call(
        body,
        name="selection",
        out_shape=jax.ShapeDtypeStruct((rows * columns * degree, 256), jnp.bfloat16),
        in_specs=[held],
        out_specs=held,
        compiler_params=pltpu.CompilerParams(vmem_limit_bytes=4 * MIB),
    )(neighbours.transpose(2, 0, 1))


def dot(a, b):
    return jnp.dot(a, b, preferred_element_type=jnp.float32)


def finish(before, inner_sum, outer, gains):
    hidden = jax.nn.silu(inner_sum).astype(jnp.bfloat16)
    output = dot(hidden, outer)
    center = output - jnp.mean(output, axis=-1, keepdims=True)
    spread_of = jnp.mean(center * center, axis=-1, keepdims=True)
    scaled = center * lax.rsqrt(spread_of + EPSILON) * gains
    return (before.astype(jnp.float32) + scaled).astype(jnp.bfloat16)


def fine_layer(layer, fine, picks, latents, left, right, sides, inner, outer, gain, rows, columns):
    edges, features = fine.shape
    nodes = latents.shape[0]
    hidden = inner.shape[2]
    near = (BAND + 2) * rows
    own = BAND * rows
    steps = nodes // own
    block = edges // steps
    degree = edges // nodes

    def body(fine_ref, picks_ref, latents_ref, left_ref, right_ref, sides_ref, inner_ref, outer_ref, gain_ref,
             next_ref, sum_ref, send_ref, recv_ref, table_ref):
        step = pl.program_id(0)

        @pl.when(step == 0)
        def _():
            send = inner_ref[layer, features : 2 * features, :]
            project = lambda ref: dot(ref[...], send).astype(jnp.bfloat16)
            table_ref[ABOVE : ABOVE + sides.shape[0], :] = project(sides_ref)
            table_ref[ABOVE + sides.shape[0] :, :] = jnp.zeros((256 - ABOVE - sides.shape[0], hidden), jnp.bfloat16)
            send_ref[rows : rows + nodes, :] = project(latents_ref)
            recv_ref[...] = dot(latents_ref[...], inner_ref[layer, 2 * features :, :]).astype(jnp.bfloat16)
            side = project(left_ref)
            send_ref[:rows, :] = side[:rows]
            table_ref[ABOVE + columns : ABOVE + columns + 1, :] = side[rows : rows + 1]
            table_ref[BELOW + columns : BELOW + columns + 1, :] = side[rows + 1 : rows + 2]
            side = project(right_ref)
            send_ref[rows + nodes :, :] = side[:rows]
            table_ref[ABOVE + columns + 1 : ABOVE + columns + 2, :] = side[rows : rows + 1]
            table_ref[BELOW + columns + 1 : BELOW + columns + 2, :] = side[rows + 1 : rows + 2]

        start = pl.multiple_of(step * own, own)
        table_ref[:near, :] = send_ref[pl.ds(start, near), :]
        table_ref[near : near + own, :] = recv_ref[pl.ds(start, own), :]
        before = fine_ref[...]
        total = dot(before, inner_ref[layer, :features, :]) + dot(picks_ref[...], table_ref[...])
        after = finish(before, total, outer_ref[layer], gain_ref[layer : layer + 1, :])
        next_ref[...] = after
        split = after.astype(jnp.float32).reshape(BAND, degree, rows, features)
        sum_ref[...] = jnp.sum(split, axis=1).reshape(own, features)

    held = pl.BlockSpec(memory_space=pltpu.VMEM)
    return pl.pallas_call(
        body,
        name=f"fine{layer}",
        out_shape=(
            jax.ShapeDtypeStruct(fine.shape, jnp.bfloat16),
            jax.ShapeDtypeStruct((nodes, features), jnp.float32),
        ),
        grid=(steps,),
        in_specs=[
            pl.BlockSpec((block, features), lambda i: (i, 0)),
            pl.BlockSpec((block, 256), lambda i: (i, 0)),
        ]
        + [held] * 7,
        out_specs=(
            pl.BlockSpec((block, features), lambda i: (i, 0)),
            pl.BlockSpec((own, features), lambda i: (i, 0)),
        ),
        scratch_shapes=[
            pltpu.VMEM((nodes + 2 * rows, hidden), jnp.bfloat16),
            pltpu.VMEM((nodes, hidden), jnp.bfloat16),
            pltpu.VMEM((256, hidden), jnp.bfloat16),
        ],
        compiler_params=pltpu.CompilerParams(dimension_semantics=("arbitrary",), vmem_limit_bytes=14 * MIB),
    )(fine, picks, latents, left, right, sides, inner, outer, gain)


def pick(index, width):
    lanes = lax.broadcasted_iota(jnp.int32, (index.shape[0], width), 1)
    return (lanes == index).astype(jnp.bfloat16)


def rows_to_columns(left, right):
    return lax.dot_general(left, right, (((1,), (1,)), ((), ())), preferred_element_type=jnp.float32)


def decode(tags, at):
    numbers = tags.astype(jnp.int32)
    return jnp.where(numbers[:, 4:5] > 0, numbers[:, at : at + 1] * LOW + numbers[:, at + 1 : at + 2], -1)


def blocks_of(*arrays):
    return [pl.BlockSpec(a.shape, lambda i, n=len(a.shape): (0,) * n) for a in arrays]


def send_rows(both, up_ref, down_ref, own_ref):
    half, count = up_ref.shape[0], own_ref.shape[0]
    rows = both.astype(jnp.bfloat16)
    up_ref[...] = rows[:half]
    down_ref[...] = rows[half:]
    own_ref[...] = rows[:count]


def join(own, up, two, down, latents, rows):
    count, features = own.shape
    columns = up.shape[0] - count

    def body(own_ref, up_ref, two_ref, down_ref, latents_ref, joined_ref, last_ref, first_ref, sides_ref):
        for at, ref in enumerate((own_ref, up_ref, two_ref, down_ref)):
            joined_ref[at * count : (at + 1) * count, :] = ref[:count, :]
        last_ref[:rows, :] = latents_ref[-rows:, :]
        last_ref[rows : rows + 1, :] = up_ref[-1:, :]
        last_ref[rows + 1 :, :] = down_ref[-1:, :]
        first_ref[:rows, :] = latents_ref[:rows, :]
        first_ref[rows : rows + 1, :] = up_ref[count : count + 1, :]
        first_ref[rows + 1 :, :] = down_ref[count : count + 1, :]
        sides_ref[...] = jnp.zeros(sides_ref.shape, jnp.bfloat16)
        sides_ref[:columns, :] = up_ref[count:, :]
        sides_ref[BELOW - ABOVE : BELOW - ABOVE + columns, :] = down_ref[count:, :]

    held = pl.BlockSpec(memory_space=pltpu.VMEM)
    return pl.pallas_call(
        body,
        name="join",
        out_shape=tuple(jax.ShapeDtypeStruct((n, features), jnp.bfloat16) for n in (4 * count, rows + 2, rows + 2, 256 - ABOVE - 32)),
        in_specs=[held] * 5,
        out_specs=(held,) * 4,
        compiler_params=pltpu.CompilerParams(vmem_limit_bytes=2 * MIB),
    )(own, up, two, down, latents)


def coarse_start(coarse_slots, latents, rows, columns):
    count = coarse_slots.shape[1]
    nodes, features = latents.shape
    half = count + columns

    def body(slots_ref, latents_ref, up_ref, down_ref, own_ref, choose_ref):
        slot = slots_ref[...]
        row = jnp.floor((slot.astype(jnp.float32) + 0.5) * (1.0 / columns)).astype(jnp.int32)
        at = (slot - row * columns) * rows + row
        place = (lax.broadcasted_iota(jnp.int32, (nodes, count), 0) == at).astype(jnp.bfloat16)
        out = lax.broadcasted_iota(jnp.int32, (2 * half, count), 0)
        line = lax.broadcasted_iota(jnp.int32, (2 * half, count), 1)
        same = ((out == line) | (out == line + half)).astype(jnp.bfloat16)
        out = lax.broadcasted_iota(jnp.int32, (2 * half, nodes), 0)
        node = lax.broadcasted_iota(jnp.int32, (2 * half, nodes), 1)
        edge = ((out >= count) & (out < half) & (node == (out - count) * rows + rows - 1)) | (
            (out >= half + count) & (node == (out - half - count) * rows)
        )
        choose = (rows_to_columns(same, place) + edge.astype(jnp.float32)).astype(jnp.bfloat16)
        choose_ref[...] = choose
        send_rows(dot(choose, latents_ref[...]), up_ref, down_ref, own_ref)

    shapes = (
        *(jax.ShapeDtypeStruct((n, features), jnp.bfloat16) for n in (half, half, count)),
        jax.ShapeDtypeStruct((2 * half, nodes), jnp.bfloat16),
    )
    return pl.pallas_call(
        body,
        name="coarse_start",
        out_shape=shapes,
        grid=(1,),
        in_specs=blocks_of(coarse_slots, latents),
        out_specs=blocks_of(*shapes),
        compiler_params=pltpu.CompilerParams(vmem_limit_bytes=4 * MIB),
    )(coarse_slots, latents)


def pack_edges(long_edges, senders, receivers, me, coarse_count, devices):
    count, features = long_edges.shape
    blocks = features // TAGS
    slots = devices * CAP

    def body(me_ref, long_ref, send_ref, recv_ref, sent_ref, mine_ref, wide):
        send, recv = send_ref[...], recv_ref[...]
        _, owner = table_row(0, 0, recv, coarse_count)
        here = (lax.shift_right_logical(me_ref[0], 3), me_ref[0] & 7)
        there = (lax.shift_right_logical(owner, 3), owner & 7)
        field = lax.broadcasted_iota(jnp.int32, (TAGS, count), 0)

        def fields(digits):
            sender = table_row(*digits, send, coarse_count)[0]
            receiver = table_row(*digits, recv, coarse_count)[0]
            both = jnp.where(field < 2, sender, receiver)
            high = lax.shift_right_logical(both, LOW.bit_length() - 1)
            value = jnp.where(field % 2 == 0, high, both & (LOW - 1))
            value = jnp.where(field == 4, 1, jnp.where(field == 5, owner, value))
            return jnp.where(field < 6, value, 0).astype(jnp.float32).astype(jnp.bfloat16)

        down = lax.broadcasted_iota(jnp.int32, (count, count), 0)
        across = lax.broadcasted_iota(jnp.int32, (count, count), 1)
        mine = rows_to_columns((down == across).astype(jnp.bfloat16), fields(here))
        mine_ref[...] = mine.astype(jnp.bfloat16)
        same = (mine[:, 5:6].astype(jnp.int32) == owner) & (down < across)
        rank = jnp.sum(same.astype(jnp.float32), axis=0, keepdims=True).astype(jnp.int32)
        spot = rank * devices + owner
        place = (lax.broadcasted_iota(jnp.int32, (slots, count), 0) == spot).astype(jnp.bfloat16)
        edges = dot(place, long_ref[...])
        tags = rows_to_columns(place, fields(there))
        for j in range(CAP):
            part = slice(j * devices, (j + 1) * devices)
            for b in range(blocks):
                wide[pl.ds(j * blocks + b, devices, stride=16), :] = edges[part, b * TAGS : (b + 1) * TAGS]
            wide[pl.ds(CAP * blocks + j, devices, stride=16), :] = tags[part]
        wide[pl.ds(15, devices, stride=16), :] = jnp.zeros((devices, TAGS), jnp.float32)
        sent_ref[...] = wide[...].astype(jnp.bfloat16)

    shapes = (
        jax.ShapeDtypeStruct((devices * 16, TAGS), jnp.bfloat16),
        jax.ShapeDtypeStruct((count, TAGS), jnp.bfloat16),
    )
    return pl.pallas_call(
        body,
        name="pack_edges",
        out_shape=shapes,
        grid=(1,),
        in_specs=[pl.BlockSpec(memory_space=pltpu.SMEM)] + blocks_of(long_edges, senders, receivers),
        out_specs=blocks_of(*shapes),
        scratch_shapes=[pltpu.VMEM((devices * 16, TAGS), jnp.float32)],
        compiler_params=pltpu.CompilerParams(vmem_limit_bytes=8 * MIB),
    )(me, long_edges, senders, receivers)


def unpack_edges(arrived, own_tags, choose, features, table_rows, coarse_count):
    devices = arrived.shape[0] // 16
    blocks = features // TAGS
    slots = devices * CAP
    count = own_tags.shape[0]
    nodes = choose.shape[1]

    def body(arrived_ref, tags_ref, choose_ref, rows_ref, send_ref, recv_ref, adds_ref, wide):
        wide[...] = arrived_ref[...].astype(jnp.float32)
        for j in range(CAP):
            part = slice(j * devices, (j + 1) * devices)
            for b in range(blocks):
                lanes = slice(b * TAGS, (b + 1) * TAGS)
                rows_ref[part, lanes] = wide[pl.ds(j * blocks + b, devices, stride=16), :].astype(jnp.bfloat16)
            tags = wide[pl.ds(CAP * blocks + j, devices, stride=16), :]
            send_ref[part, :] = pick(decode(tags, 0), table_rows)
            recv_ref[part, :] = pick(decode(tags, 2), TAGS)
        mine = tags_ref[...].astype(jnp.float32)
        send_ref[slots : slots + count, :] = pick(decode(mine, 0), table_rows)
        send_ref[slots + count :, :] = pick(decode(mine, 2), table_rows)
        here = recv_ref[:, :coarse_count]
        place = lax.dot_general(
            choose_ref[:coarse_count, :], here, (((0,), (1,)), ((), ())), preferred_element_type=jnp.float32
        )
        adds_ref[...] = place.astype(jnp.bfloat16)

    held = pl.BlockSpec(memory_space=pltpu.VMEM)
    return pl.pallas_call(
        body,
        name="unpack_edges",
        out_shape=(
            jax.ShapeDtypeStruct((slots, features), jnp.bfloat16),
            jax.ShapeDtypeStruct((slots + 2 * count, table_rows), jnp.bfloat16),
            jax.ShapeDtypeStruct((slots, TAGS), jnp.bfloat16),
            jax.ShapeDtypeStruct((nodes, slots), jnp.bfloat16),
        ),
        in_specs=[held] * 3,
        out_specs=(held,) * 4,
        scratch_shapes=[pltpu.VMEM(arrived.shape, jnp.float32)],
        compiler_params=pltpu.CompilerParams(vmem_limit_bytes=8 * MIB),
    )(arrived, own_tags, choose)


def long_step(before, sent, got, inner_ref, outer_ref, gain_ref, layer):
    features = before.shape[1]
    total = dot(before, inner_ref[layer, :features, :])
    total += dot(sent, inner_ref[layer, features : 2 * features, :])
    total += dot(got, inner_ref[layer, 2 * features :, :])
    return finish(before, total, outer_ref[layer], gain_ref[layer : layer + 1, :])


def coarse_layer(layer, long_rows, own_rows, sends, recvs, adds, choose, pieces, latents, fine_sum,
                 edge_inner, edge_outer, edge_gain, node_inner, node_outer, node_gain, coarse_count, last):
    slots = long_rows.shape[0]
    nodes, features = latents.shape
    count = len(pieces)
    each = pieces[0].shape[0]
    table_rows = count * each
    both = slots + own_rows.shape[0]

    def body(long_ref, own_ref, sends_ref, recvs_ref, adds_ref, choose_ref, latents_ref, sum_ref,
             ei_ref, eo_ref, eg_ref, ni_ref, no_ref, ng_ref, *rest):
        piece_refs = rest[:count]
        next_ref, *outs, ni, no, sems = rest[count:]
        table = outs[1] if last else outs[4]
        weights = [
            pltpu.make_async_copy(ni_ref.at[layer], ni, sems.at[0]),
            pltpu.make_async_copy(no_ref.at[layer], no, sems.at[1]),
        ]
        for copy in weights:
            copy.start()
        for p in range(count):
            table[p * each : (p + 1) * each, :] = piece_refs[p][...]
        got = dot(recvs_ref[...], table[:TAGS, :]).astype(jnp.bfloat16)
        if last:
            picked = dot(sends_ref[...], table[...]).astype(jnp.bfloat16)
            before = jnp.concatenate([long_ref[...], own_ref[...]], axis=0)
            got = jnp.concatenate([got, picked[both:]], axis=0)
            after = long_step(before, picked[:both], got, ei_ref, eo_ref, eg_ref, layer)
            outs[0][...] = after[slots:]
            after = after[:slots]
        else:
            sent = dot(sends_ref[:slots, :], table[...]).astype(jnp.bfloat16)
            after = long_step(long_ref[...], sent, got, ei_ref, eo_ref, eg_ref, layer)
            outs[0][...] = after
        incoming = (sum_ref[...] + dot(adds_ref[...], after)).astype(jnp.bfloat16)
        old = latents_ref[...]
        for copy in weights:
            copy.wait()
        total = dot(old, ni[:features, :]) + dot(incoming, ni[features:, :])
        new = finish(old, total, no[...], ng_ref[layer : layer + 1, :])
        next_ref[...] = new
        if not last:
            send_rows(dot(choose_ref[...], new), *outs[1:4])

    held = pl.BlockSpec(memory_space=pltpu.VMEM)
    away = pl.BlockSpec(memory_space=pl.ANY)
    table_shape = (table_rows, features)
    half = choose.shape[0] // 2
    kept = (both - slots,) if last else (slots, half, half, coarse_count, table_rows)
    shapes = [jax.ShapeDtypeStruct((n, features), jnp.bfloat16) for n in (nodes, *kept)]

    return pl.pallas_call(
        body,
        name=f"coarse{layer}",
        out_shape=tuple(shapes),
        in_specs=[held] * 11 + [away] * 2 + [held] * (1 + count),
        out_specs=(held,) * len(shapes),
        scratch_shapes=([pltpu.VMEM(table_shape, jnp.bfloat16)] if last else [])
        + [
            pltpu.VMEM(node_inner.shape[1:], jnp.bfloat16),
            pltpu.VMEM(node_outer.shape[1:], jnp.bfloat16),
            pltpu.SemaphoreType.DMA((2,)),
        ],
        compiler_params=pltpu.CompilerParams(vmem_limit_bytes=(18 if last else 14) * MIB),
    )(long_rows, own_rows, sends, recvs, adds, choose, latents, fine_sum,
      edge_inner, edge_outer, edge_gain, node_inner, node_outer, node_gain, *pieces)


def own_layer(layer, long_rows, sends, table, edge_inner, edge_outer, edge_gain):
    count = long_rows.shape[0]

    def body(long_ref, sends_ref, table_ref, ei_ref, eo_ref, eg_ref, next_ref):
        picked = dot(sends_ref[-2 * count :, :], table_ref[...]).astype(jnp.bfloat16)
        next_ref[...] = long_step(long_ref[...], picked[:count], picked[count:], ei_ref, eo_ref, eg_ref, layer)

    held = pl.BlockSpec(memory_space=pltpu.VMEM)
    return pl.pallas_call(
        body,
        name=f"own{layer}",
        out_shape=jax.ShapeDtypeStruct(long_rows.shape, jnp.bfloat16),
        in_specs=[held] * 6,
        out_specs=held,
        compiler_params=pltpu.CompilerParams(vmem_limit_bytes=8 * MIB),
    )(long_rows, sends, table, edge_inner, edge_outer, edge_gain)


def shards(
    node_latents,
    fine_edges,
    long_edges,
    neighbours,
    coarse_slots,
    long_senders,
    long_receivers,
    edge_inner,
    edge_outer,
    edge_gain,
    node_inner,
    node_outer,
    node_gain,
):
    rows, columns, features = node_latents.shape
    degree = fine_edges.shape[2]
    nodes = rows * columns
    coarse_count = coarse_slots.shape[0]
    layers = edge_inner.shape[0]
    devices = lax.axis_size("px") * lax.axis_size("py")

    latents = node_latents.transpose(1, 0, 2).reshape(nodes, features)
    fine = fine_edges.transpose(1, 2, 0, 3).reshape(nodes * degree, features)
    up, down, own, choose = coarse_start(coarse_slots[None, :], latents, rows, columns)
    long_edges, own = tie(long_edges, own)
    own_rows = long_edges
    me = lax.axis_index(AXES).reshape(1)
    payload, own_tags = pack_edges(long_edges, long_senders[None, :], long_receivers[None, :], me, coarse_count, devices)
    for layer in range(layers):
        last = layer == layers - 1
        up = along(up, "px", 1)
        down = along(down, "px", -1)
        two = along(own, "px", 2)
        if layer == 0:
            two, payload = tie(two, payload)
            packed = payload.reshape(devices, 16, TAGS)
            arrived = lax.all_to_all(packed, AXES, split_axis=0, concat_axis=0, tiled=True).reshape(payload.shape)
        joined, to_right, to_left, sides = join(own, up, two, down, latents, rows)
        joined = jnp.concatenate([joined] + [along(joined, "px", 4 * s) for s in (1, 2, 3)], axis=0)
        joined, to_right, to_left, own_rows = tie(joined, to_right, to_left, own_rows)
        pieces = [joined] + [shift(joined, Z, s) for s in (1, 2, 3)]
        left = along(to_right, "py", 1)
        right = along(to_left, "py", -1)
        if layer == 0:
            table_rows = 2 * len(pieces) * joined.shape[0]
            long_rows, sends, recvs, adds = unpack_edges(arrived, own_tags, choose, features, table_rows, coarse_count)
            left, long_rows, neighbours = tie(left, long_rows, neighbours)
            picks = selection(neighbours)
        else:
            own_rows = own_layer(layer - 1, own_rows, sends, table, edge_inner, edge_outer, edge_gain)
        fine, fine_sum = fine_layer(
            layer, fine, picks, latents, left, right, sides, edge_inner, edge_outer, edge_gain, rows, columns
        )
        first, *others, fine_sum, own_rows, long_rows = tie(*pieces, fine_sum, own_rows, long_rows)
        pieces = [first] + others
        pieces = pieces + [shift(piece, CORE, 1) for piece in pieces]
        latents, *rest = coarse_layer(
            layer, long_rows, own_rows, sends, recvs, adds, choose, pieces, latents, fine_sum,
            edge_inner, edge_outer, edge_gain, node_inner, node_outer, node_gain, coarse_count, last,
        )
        if last:
            own_rows = rest[0]
        else:
            long_rows, up, down, own, table = rest
    return (
        latents.reshape(columns, rows, features).transpose(1, 0, 2),
        fine.reshape(columns, degree, rows, features).transpose(2, 0, 1, 3),
        own_rows,
    )


def solution(mesh):
    in_specs = (
        P("px", "py", None),
        P("px", "py", None, None),
        P(AXES, None),
        P("px", "py", None),
        P(AXES),
        P(AXES),
        P(AXES),
        P(),
        P(),
        P(),
        P(),
        P(),
        P(),
    )
    out_specs = (P("px", "py", None), P("px", "py", None, None), P(AXES, None))
    return jax.shard_map(shards, mesh=mesh, in_specs=in_specs, out_specs=out_specs, check_vma=False)
```

time: 129 us -> 130 us (level)
  waiting for transfers between devices: 18 us -> 36.4 us
  local copies, waits for them, and re-layouts: 17.8 us -> 11.3 us
  starting transfers between devices: 51.7 us -> 46.5 us
  other arithmetic: 6.63 us -> 1.78 us
    ppermute x8 -> x16, waiting for transfers between devices: 4.61 us -> 27.4 us  [along(): lax.ppermute(values, axis, [(i, (i + step) % count) for i in range(count)])]
    ppermute x26 -> x14, starting transfers between devices: 26.4 us -> 12.3 us  [shift(): return lax.ppermute(values, 'py', pairs)]
    ppermute x26 -> x14, waiting for transfers between devices: 13.4 us -> 4.34 us  [shift(): return lax.ppermute(values, 'py', pairs)]
    ppermute x8 -> x16, starting transfers between devices: 15.8 us -> 22.4 us  [along(): lax.ppermute(values, axis, [(i, (i + step) % count) for i in range(count)])]
    all_to_all x1, waiting for transfers between devices: 0.01 us -> 4.65 us  [shards(): lax.all_to_all(packed, AXES, split_axis=0, concat_axis=0, tiled=True)]
    add x2 -> x0, local copies, waits for them, and re-layouts: 3.12 us -> none  [selection(): receiver = 96 + column % BAND * rows + row]
    pallas_call x2 -> x1, Pallas kernels: 4.39 us -> 1.71 us  [own_layer(): pl.pallas_call(body, name=f'own{layer}', out_shape=jax.ShapeDtypeStruct(l...]
    convert_element_type x1 -> x0, other arithmetic: 2.47 us -> none  [selection(): return picks.astype(jnp.bfloat16).reshape(-1, 256)]
  transfers between devices with their start and end apart: 35 -> 31, of which waited for: 16 -> 18; matrix products, arithmetic and copies ran while one was open for 12% -> 1% of each run, Pallas kernels for 15% -> 15%
where the time goes in v4:
time: 130 us
  starting transfers between devices  46.5 us (36%)
  waiting for transfers between devices  36.4 us (28%)
  Pallas kernels  32.7 us (25%)
  local copies, waits for them, and re-layouts  11.3 us (9%)
  other arithmetic  1.78 us (1%)
    ppermute x16, waiting for transfers between devices, along(): lax.ppermute(values, axis, [(i, (i + step) % count) for i in range(count)])  27.4 us
    ppermute x16, starting transfers between devices, along(): lax.ppermute(values, axis, [(i, (i + step) % count) for i in range(count)])  22.4 us
    pallas_call x2, Pallas kernels, fine_layer(): pl.pallas_call(body, name=f'fine{layer}', out_shape=(jax.ShapeDtypeStruct...  13.5 us
    ppermute x14, starting transfers between devices, shift(): return lax.ppermute(values, 'py', pairs)  12.3 us
    all_to_all x1, starting transfers between devices, shards(): lax.all_to_all(packed, AXES, split_axis=0, concat_axis=0, tiled=True)  11.7 us
    unnamed x48, local copies, waits for them, and re-layouts  11.3 us
    pallas_call x2, Pallas kernels, coarse_layer(): pl.pallas_call(body, name=f'coarse{layer}', out_shape=tuple(shapes), in_s...  10.9 us
    all_to_all x1, waiting for transfers between devices, shards(): lax.all_to_all(packed, AXES, split_axis=0, concat_axis=0, tiled=True)  4.65 us
  transfers between devices with their start and end apart: 31, of which 18 were waited for; matrix products, arithmetic and copies ran while one was open for 1% of the time, Pallas kernels for 15%

profile of v4, /device:TPU:1, one launch (start us, length us, event | category | flops | bytes accessed | tf_op | source)
XLA Modules:
  0.0 129.7 jit_solution(9993780888239454382)
XLA Ops:
  0.6 1.0 copy-done.4
  1.6 0.7 copy-done.21
  2.3 1.0 coarse_start.1
  3.2 2.0 %collective-permute-start = (bf16[40,512]{1,0:T(8,128)(2,1)}, bf16[40,512]{1,0:T(8,128)(2,1)}, u32[]{:S(2)}, u32[]{:S(2)}) collective-permute-start(bf16[40,512]{1,0:T(8,128)(2,1)} %get-tuple-element.64), channel_id=1, source_target_pairs={{0,8},{8,16},{16,24},{24,32},{32,40},{40,48},{48,56},{56,64},{64,7... | collective-permute-start | bytes 122888 | tf_op jit(solution)/shard_map/ppermute | solution.py:46
  5.3 3.7 %collective-permute-start.2 = (bf16[40,512]{1,0:T(8,128)(2,1)}, bf16[40,512]{1,0:T(8,128)(2,1)}, u32[]{:S(2)}, u32[]{:S(2)}) collective-permute-start(bf16[40,512]{1,0:T(8,128)(2,1)} %get-tuple-element.68), channel_id=1, source_target_pairs={{0,120},{8,0},{16,8},{24,16},{32,24},{40,32},{48,40},{56,48},{64,5... | collective-permute-start | bytes 122888 | tf_op jit(solution)/shard_map/ppermute | solution.py:46
  9.0 0.9 copy-done.9
  9.9 0.7 copy-done.19
  10.6 0.7 copy-done.20
  11.3 0.8 pack_edges.1
  12.1 3.5 %collective-permute-done.1.two_ref = bf16[20,512]{1,0:T(8,128)(2,1)} collective-permute-done((bf16[20,512]{1,0:T(8,128)(2,1)}, bf16[20,512]{1,0:T(8,128)(2,1)}, u32[]{:S(2)}, u32[]{:S(2)}) %collective-permute-start.1) | collective-permute-done | bytes 20512 | tf_op jit(solution)/shard_map/ppermute | solution.py:46
  15.6 1.0 copy-done.5
  16.6 1.5 %join.2 = (bf16[80,512]{1,0:T(8,128)(2,1)}, bf16[18,512]{1,0:T(8,128)(2,1)S(1)}, bf16[18,512]{1,0:T(8,128)(2,1)S(1)}, bf16[64,512]{1,0:T(8,128)(2,1)S(1)}) custom-call(bf16[20,512]{1,0:T(8,128)(2,1)} %get-tuple-element.63.own_ref, bf16[40,512]{1,0:T(8,128)(2,1)} %collective-permute-done.up_ref, bf16[20,512]{1,0:T(8,128)(2,1)} %collective-permute-done.1.two_ref, ...), custom_call_target="tpu_custom_call" | custom-call | tf_op jit(solution)/shard_map/join/pallas_call | solution.py:207
  18.1 0.6 copy-done.13
  18.7 0.6 copy-done.22
  19.8 1.0 collective-permute-start.3
  20.8 11.7 %all-to-all-start = ((bf16[128,16,128]{2,1,0:T(8,128)(2,1)}), bf16[128,16,128]{2,1,0:T(8,128)(2,1)}, u32[]{:S(2)}, u32[]{:S(2)}) async-start(bf16[128,16,128]{2,1,0:T(8,128)(2,1)} %bitcast.24), calls=%async_computation | async-start | bytes 1048576 | tf_op jit(solution)/shard_map/all_to_all | solution.py:483
  32.6 1.8 %pad_maximum_fusion.rest_0_ = bf16[320,512]{1,0:T(8,128)(2,1)} fusion(bf16[80,512]{1,0:T(8,128)(2,1)} %collective-permute-done.5, bf16[80,512]{1,0:T(8,128)(2,1)} %collective-permute-done.4, bf16[80,512]{1,0:T(8,128)(2,1)} %collective-permute-done.3, bf16[80,512]{1,0:T(8,128)(2,1)} %get-tuple-element.69), kind=kLoop, calls=%fused_computation | loop fusion | flops 1310720 | bytes 655360 | tf_op jit(solution)/shard_map/concatenate | solution.py:485
  34.3 3.3 %collective-permute-start.8 = (bf16[320,512]{1,0:T(8,128)(2,1)}, bf16[320,512]{1,0:T(8,128)(2,1)}, u32[]{:S(2)}, u32[]{:S(2)}) collective-permute-start(bf16[320,512]{1,0:T(8,128)(2,1)} %pad_maximum_fusion.rest_0_), channel_id=1, source_target_pairs={{0,6},{1,7},{2,0},{3,1},{4,2},{5,3},{6,4},{7,5},{8,14},{9,15},{10,... | collective-permute-start | bytes 983048 | tf_op jit(solution)/shard_map/ppermute | solution.py:26
  37.6 0.8 collective-permute-start.6
  38.5 2.9 %collective-permute-start.9 = (bf16[18,512]{1,0:T(8,128)(2,1)}, bf16[18,512]{1,0:T(8,128)(2,1)}, u32[]{:S(2)}, u32[]{:S(2)}) collective-permute-start(bf16[18,512]{1,0:T(8,128)(2,1)} %copy-done.23), channel_id=1, source_target_pairs={{0,1},{1,2},{2,3},{3,4},{4,5},{5,6},{6,7},{7,0},{8,9},{9,10},{10,1... | collective-permute-start | bytes 55304 | tf_op jit(solution)/shard_map/ppermute | solution.py:46
  41.3 4.7 %all-to-all-done = bf16[128,16,128]{2,1,0:T(8,128)(2,1)} async-done(((bf16[128,16,128]{2,1,0:T(8,128)(2,1)}), bf16[128,16,128]{2,1,0:T(8,128)(2,1)}, u32[]{:S(2)}, u32[]{:S(2)}) %all-to-all-start) | async-done | bytes 524320 | tf_op jit(solution)/shard_map/all_to_all | solution.py:483
  46.0 0.8 copy-done.17
  46.7 2.9 %unpack_edges.1 = (bf16[384,512]{1,0:T(8,128)(2,1)S(1)}, bf16[704,2560]{1,0:T(8,128)(2,1)S(1)}, bf16[384,128]{1,0:T(8,128)(2,1)S(1)}, bf16[320,384]{1,0:T(8,128)(2,1)S(1)}) custom-call(bf16[2048,128]{1,0:T(8,128)(2,1)} %bitcast.9.arrived_ref, bf16[160,128]{1,0:T(8,128)(2,1)S(1)} %copy-done.17, bf16[80,320]{1,0:T(8,128)(2,1)S(1)} %get-tuple-element.76.choose_ref), custom_call_target="tpu_custom_call" | custom-call | tf_op jit(solution)/shard_map/unpack_edges/pallas_call | solution.py:336
  49.6 5.0 %collective-permute-done.9.left_ref = bf16[18,512]{1,0:T(8,128)(2,1)} collective-permute-done((bf16[18,512]{1,0:T(8,128)(2,1)}, bf16[18,512]{1,0:T(8,128)(2,1)}, u32[]{:S(2)}, u32[]{:S(2)}) %collective-permute-start.9) | collective-permute-done | bytes 18464 | tf_op jit(solution)/shard_map/ppermute | solution.py:46
  54.6 0.8 copy-done.15
  56.1 1.2 copy-done.1
  57.3 1.5 %copy-done.8 = bf16[16,20,6,512]{3,0,2,1:T(8,128)(2,1)S(1)} copy-done((bf16[16,20,6,512]{3,0,2,1:T(8,128)(2,1)S(1)}, bf16[16,20,6,512]{3,0,2,1:T(8,128)(2,1)}, u32[]{:S(2)}) %copy-start.8) | copy-done | bytes 1966104
  58.9 0.8 copy-done.14
  59.7 6.8 %fine0.1 = (bf16[1920,512]{1,0:T(8,128)(2,1)S(1)}, f32[320,512]{1,0:T(8,128)S(1)}) custom-call(bf16[1920,512]{1,0:T(8,128)(2,1)S(1)} %bitcast.23, bf16[1920,256]{1,0:T(8,128)(2,1)S(1)} %selection.1.picks_ref, bf16[320,512]{1,0:T(8,128)(2,1)S(1)} %bitcast.21, bf16[18,512]{1,0:T(8,128)(2,1)} %collective-permute-done.9.left_ref, ...), custom_call_target="tpu_custom_call" | custom-call | tf_op jit(solution)/shard_map/fine0/pallas_call | solution.py:137
  66.6 4.0 %collective-permute-start.11 = (bf16[320,512]{1,0:T(8,128)(2,1)}, bf16[320,512]{1,0:T(8,128)(2,1)S(1)}, u32[]{:S(2)}, u32[]{:S(2)}) collective-permute-start(bf16[320,512]{1,0:T(8,128)(2,1)} %pad_maximum_fusion.rest_0_), channel_id=1, source_target_pairs={{0,1},{1,0},{2,3},{3,2},{4,5},{5,4},{6,7},{7,6},{8,9},{9,8},{10,11... | collective-permute-start | bytes 983048 | tf_op jit(solution)/shard_map/ppermute | solution.py:26
  71.2 0.9 collective-permute-done.11.rest_4_
  73.5 5.4 %coarse0.1 = (bf16[320,512]{1,0:T(8,128)(2,1)S(1)}, bf16[384,512]{1,0:T(8,128)(2,1)S(1)}, bf16[40,512]{1,0:T(8,128)(2,1)S(1)}, bf16[40,512]{1,0:T(8,128)(2,1)S(1...) custom-call(bf16[384,512]{1,0:T(8,128)(2,1)S(1)} %get-tuple-element.85.long_ref, ...), custom_call_target="tpu_custom_call" | custom-call | tf_op jit(solution)/shard_map/coarse0/pallas_call | solution.py:411
  78.8 0.7 collective-permute-start.15
  79.6 4.3 %collective-permute-start.17 = (bf16[40,512]{1,0:T(8,128)(2,1)S(1)}, bf16[40,512]{1,0:T(8,128)(2,1)S(1)}, u32[]{:S(2)}, u32[]{:S(2)}) collective-permute-start(bf16[40,512]{1,0:T(8,128)(2,1)S(1)} %get-tuple-element.97), channel_id=1, source_target_pairs={{0,120},{8,0},{16,8},{24,16},{32,24},{40,32},{48,40},{56,48},{64,5... | collective-permute-start | bytes 122888 | tf_op jit(solution)/shard_map/ppermute | solution.py:46
  83.9 6.3 %collective-permute-done.16.two_ref = bf16[20,512]{1,0:T(8,128)(2,1)S(1)} collective-permute-done((bf16[20,512]{1,0:T(8,128)(2,1)S(1)}, bf16[20,512]{1,0:T(8,128)(2,1)S(1)}, u32[]{:S(2)}, u32[]{:S(2)}) %collective-permute-start.16) | collective-permute-done | bytes 20512 | tf_op jit(solution)/shard_map/ppermute | solution.py:46
  90.4 1.4 %collective-permute-start.18 = (bf16[80,512]{1,0:T(8,128)(2,1)S(1)}, bf16[80,512]{1,0:T(8,128)(2,1)S(1)}, u32[]{:S(2)}, u32[]{:S(2)}) collective-permute-start(bf16[80,512]{1,0:T(8,128)(2,1)S(1)} %get-tuple-element.99), channel_id=1, source_target_pairs={{0,32},{8,40},{16,48},{24,56},{32,64},{40,72},{48,80},{56,88},{64,... | collective-permute-start | bytes 245768 | tf_op jit(solution)/shard_map/ppermute | solution.py:46
  91.7 1.8 %collective-permute-done.20 = bf16[80,512]{1,0:T(8,128)(2,1)S(1)} collective-permute-done((bf16[80,512]{1,0:T(8,128)(2,1)S(1)}, bf16[80,512]{1,0:T(8,128)(2,1)S(1)}, u32[]{:S(2)}, u32[]{:S(2)}) %collective-permute-start.20) | collective-permute-done | bytes 81952 | tf_op jit(solution)/shard_map/ppermute | solution.py:46
  93.5 1.6 %collective-permute-done.19 = bf16[80,512]{1,0:T(8,128)(2,1)S(1)} collective-permute-done((bf16[80,512]{1,0:T(8,128)(2,1)S(1)}, bf16[80,512]{1,0:T(8,128)(2,1)S(1)}, u32[]{:S(2)}, u32[]{:S(2)}) %collective-permute-start.19) | collective-permute-done | bytes 81952 | tf_op jit(solution)/shard_map/ppermute | solution.py:46
  95.2 0.9 collective-permute-done.18
  96.5 1.1 collective-permute-start.21
  97.6 5.8 %collective-permute-start.24 = (bf16[18,512]{1,0:T(8,128)(2,1)S(1)}, bf16[18,512]{1,0:T(8,128)(2,1)S(1)}, u32[]{:S(2)}, u32[]{:S(2)}) collective-permute-start(bf16[18,512]{1,0:T(8,128)(2,1)S(1)} %get-tuple-element.104), channel_id=1, source_target_pairs={{0,1},{1,2},{2,3},{3,4},{4,5},{5,6},{6,7},{7,0},{8,9},{9,10},{10,1... | collective-permute-start | bytes 55304 | tf_op jit(solution)/shard_map/ppermute | solution.py:46
  103.4 1.7 %own0.1.own_ref = bf16[160,512]{1,0:T(8,128)(2,1)S(1)} custom-call(bf16[160,512]{1,0:T(8,128)(2,1)S(1)} %copy-done.10, bf16[704,2560]{1,0:T(8,128)(2,1)S(1)} %get-tuple-element.87.sends_ref, bf16[2560,512]{1,0:T(8,128)(2,1)S(1)} %get-tuple-element.109.table_ref, bf16[2,1536,512]{2,1,0:T(8,128)(2,1)S(1)} %copy-done, bf16[2,512,512]{2,1,0:T(8,128)(2,1)S(1)} %copy-done.2, ...), custom_call_target="tpu_custom_call" | custom-call | tf_op jit(solution)/shard_map/own0/pallas_call | solution.py:436
  105.1 2.3 %collective-permute-done.24.left_ref = bf16[18,512]{1,0:T(8,128)(2,1)S(1)} collective-permute-done((bf16[18,512]{1,0:T(8,128)(2,1)S(1)}, bf16[18,512]{1,0:T(8,128)(2,1)S(1)}, u32[]{:S(2)}, u32[]{:S(2)}) %collective-permute-start.24) | collective-permute-done | bytes 18464 | tf_op jit(solution)/shard_map/ppermute | solution.py:46
  107.4 5.8 %collective-permute-done.25.right_ref = bf16[18,512]{1,0:T(8,128)(2,1)S(1)} collective-permute-done((bf16[18,512]{1,0:T(8,128)(2,1)S(1)}, bf16[18,512]{1,0:T(8,128)(2,1)S(1)}, u32[]{:S(2)}, u32[]{:S(2)}) %collective-permute-start.25) | collective-permute-done | bytes 18464 | tf_op jit(solution)/shard_map/ppermute | solution.py:46
  113.1 6.7 %fine1.1 = (bf16[1920,512]{1,0:T(8,128)(2,1)}, f32[320,512]{1,0:T(8,128)S(1)}) custom-call(bf16[1920,512]{1,0:T(8,128)(2,1)S(1)} %get-tuple-element.103.fine_ref, bf16[1920,256]{1,0:T(8,128)(2,1)S(1)} %selection.1.picks_ref, bf16[320,512]{1,0:T(8,128)(2,1)S(1)} %get-tuple-element.98.latents_ref, bf16[18,512]{1,0:T(8,128)(2,1)S(1)} %collective-permute-done.24.left_ref, ...), custom_call_target="tpu_custom_call" | custom-call | tf_op jit(solution)/shard_map/fine1/pallas_call | solution.py:137
  119.8 1.4 %collective-permute-start.26 = (bf16[320,512]{1,0:T(8,128)(2,1)S(1)}, bf16[320,512]{1,0:T(8,128)(2,1)S(1)}, u32[]{:S(2)}, u32[]{:S(2)}) collective-permute-start(bf16[320,512]{1,0:T(8,128)(2,1)S(1)} %pad_maximum_fusion.1.rest_0_), channel_id=1, source_target_pairs={{0,1},{1,0},{2,3},{3,2},{4,5},{5,4},{6,7},{7,6},{8,9},{9,8},{10,11... | collective-permute-start | bytes 983048 | tf_op jit(solution)/shard_map/ppermute | solution.py:26
  121.9 0.7 collective-permute-done.26.rest_4_
  123.9 5.6 %coarse1.1 = (bf16[320,512]{1,0:T(8,128)(2,1)}, bf16[160,512]{1,0:T(8,128)(2,1)}) custom-call(bf16[384,512]{1,0:T(8,128)(2,1)S(1)} %get-tuple-element.111.long_ref, bf16[160,512]{1,0:T(8,128)(2,1)S(1)} %own0.1.own_ref, bf16[704,2560]{1,0:T(8,128)(2,1)S(1)} %get-tuple-element.87.sends_ref, bf16[384,128]{1,0:T(8,128)(2,1)S(1)} %get-tuple-element.88.recvs_ref, ...), custom_call_target="tpu_custom_call" | custom-call | tf_op jit(solution)/shard_map/coarse1/pallas_call | solution.py:411
  (75 shorter events, 6.0 us)
Async XLA Ops:
  0.6 1.0 copy-start.4
  2.3 53.8 %copy-start.6 = (bf16[16,20,512]{2,0,1:T(8,128)(2,1)S(1)}, bf16[16,20,512]{2,0,1:T(8,128)(2,1)}, u32[]{:S(2)}) copy-start(bf16[16,20,512]{2,0,1:T(8,128)(2,1)} %param.13) | copy-start | bytes 983044
  3.2 52.9 %copy-start = (bf16[2,1536,512]{2,1,0:T(8,128)(2,1)S(1)}, bf16[2,1536,512]{2,1,0:T(8,128)(2,1)}, u32[]{:S(2)}) copy-start(bf16[2,1536,512]{2,1,0:T(8,128)(2,1)} %ei_ref.5) | copy-start | bytes 9437188
  3.2 12.4 %collective-permute-start = (bf16[40,512]{1,0:T(8,128)(2,1)}, bf16[40,512]{1,0:T(8,128)(2,1)}, u32[]{:S(2)}, u32[]{:S(2)}) collective-permute-start(bf16[40,512]{1,0:T(8,128)(2,1)} %get-tuple-element.64), channel_id=1, source_target_pairs={{0,8},{8,16},{16,24},{24,32},{32,40},{40,48},{48,56},{56,64},{64,7... | collective-permute-start | bytes 122888 | tf_op jit(solution)/shard_map/ppermute | solution.py:46
  5.3 10.3 %collective-permute-start.2 = (bf16[40,512]{1,0:T(8,128)(2,1)}, bf16[40,512]{1,0:T(8,128)(2,1)}, u32[]{:S(2)}, u32[]{:S(2)}) collective-permute-start(bf16[40,512]{1,0:T(8,128)(2,1)} %get-tuple-element.68), channel_id=1, source_target_pairs={{0,120},{8,0},{16,8},{24,16},{32,24},{40,32},{48,40},{56,48},{64,5... | collective-permute-start | bytes 122888 | tf_op jit(solution)/shard_map/ppermute | solution.py:46
  9.0 6.6 %collective-permute-start.1 = (bf16[20,512]{1,0:T(8,128)(2,1)}, bf16[20,512]{1,0:T(8,128)(2,1)}, u32[]{:S(2)}, u32[]{:S(2)}) collective-permute-start(bf16[20,512]{1,0:T(8,128)(2,1)} %get-tuple-element.63.own_ref), channel_id=1, source_target_pairs={{0,16},{8,24},{16,32},{24,40},{32,48},{40,56},{48,64},{56,72},{64,... | collective-permute-start | bytes 61448 | tf_op jit(solution)/shard_map/ppermute | solution.py:46
  9.0 0.9 copy-start.9
  12.1 6.0 %copy-start.16 = (bf16[160,128]{1,0:T(8,128)(2,1)}, bf16[160,128]{1,0:T(8,128)(2,1)S(1)}, u32[]{:S(2)}) copy-start(bf16[160,128]{1,0:T(8,128)(2,1)S(1)} %get-tuple-element.75.tags_ref) | copy-start | bytes 122884
  12.1 8.7 %copy-start.11 = (bf16[2048,128]{1,0:T(8,128)(2,1)}, bf16[2048,128]{1,0:T(8,128)(2,1)S(1)}, u32[]{:S(2)}) copy-start(bf16[2048,128]{1,0:T(8,128)(2,1)S(1)} %get-tuple-element.74) | copy-start | bytes 1572868
  15.6 1.0 copy-start.5
  16.6 39.5 %copy-start.12 = (f32[2,512]{1,0:T(2,128)S(1)}, f32[2,512]{1,0:T(2,128)}, u32[]{:S(2)}) copy-start(f32[2,512]{1,0:T(2,128)} %eg_ref.5) | copy-start | bytes 12292
  19.3 13.2 %collective-permute-start.5 = (bf16[80,512]{1,0:T(8,128)(2,1)}, bf16[80,512]{1,0:T(8,128)(2,1)}, u32[]{:S(2)}, u32[]{:S(2)}) collective-permute-start(bf16[80,512]{1,0:T(8,128)(2,1)} %get-tuple-element.69), channel_id=1, source_target_pairs={{0,96},{8,104},{16,112},{24,120},{32,0},{40,8},{48,16},{56,24},{64... | collective-permute-start | bytes 245768 | tf_op jit(solution)/shard_map/ppermute | solution.py:46
  19.5 13.1 %collective-permute-start.4 = (bf16[80,512]{1,0:T(8,128)(2,1)}, bf16[80,512]{1,0:T(8,128)(2,1)}, u32[]{:S(2)}, u32[]{:S(2)}) collective-permute-start(bf16[80,512]{1,0:T(8,128)(2,1)} %get-tuple-element.69), channel_id=1, source_target_pairs={{0,64},{8,72},{16,80},{24,88},{32,96},{40,104},{48,112},{56,120},{... | collective-permute-start | bytes 245768 | tf_op jit(solution)/shard_map/ppermute | solution.py:46
  19.8 12.7 %collective-permute-start.3 = (bf16[80,512]{1,0:T(8,128)(2,1)}, bf16[80,512]{1,0:T(8,128)(2,1)}, u32[]{:S(2)}, u32[]{:S(2)}) collective-permute-start(bf16[80,512]{1,0:T(8,128)(2,1)} %get-tuple-element.69), channel_id=1, source_target_pairs={{0,32},{8,40},{16,48},{24,56},{32,64},{40,72},{48,80},{56,88},{64,... | collective-permute-start | bytes 245768 | tf_op jit(solution)/shard_map/ppermute | solution.py:46
  20.8 25.2 %all-to-all-start = ((bf16[128,16,128]{2,1,0:T(8,128)(2,1)}), bf16[128,16,128]{2,1,0:T(8,128)(2,1)}, u32[]{:S(2)}, u32[]{:S(2)}) async-start(bf16[128,16,128]{2,1,0:T(8,128)(2,1)} %bitcast.24), calls=%async_computation | async-start | bytes 1048576 | tf_op jit(solution)/shard_map/all_to_all | solution.py:483
  34.3 32.2 %collective-permute-start.8 = (bf16[320,512]{1,0:T(8,128)(2,1)}, bf16[320,512]{1,0:T(8,128)(2,1)}, u32[]{:S(2)}, u32[]{:S(2)}) collective-permute-start(bf16[320,512]{1,0:T(8,128)(2,1)} %pad_maximum_fusion.rest_0_), channel_id=1, source_target_pairs={{0,6},{1,7},{2,0},{3,1},{4,2},{5,3},{6,4},{7,5},{8,14},{9,15},{10,... | collective-permute-start | bytes 983048 | tf_op jit(solution)/shard_map/ppermute | solution.py:26
  37.6 29.0 %collective-permute-start.7 = (bf16[320,512]{1,0:T(8,128)(2,1)}, bf16[320,512]{1,0:T(8,128)(2,1)}, u32[]{:S(2)}, u32[]{:S(2)}) collective-permute-start(bf16[320,512]{1,0:T(8,128)(2,1)} %pad_maximum_fusion.rest_0_), channel_id=1, source_target_pairs={{0,4},{1,5},{2,6},{3,7},{4,0},{5,1},{6,2},{7,3},{8,12},{9,13},{10,... | collective-permute-start | bytes 983048 | tf_op jit(solution)/shard_map/ppermute | solution.py:26
  37.6 28.9 %collective-permute-start.6 = (bf16[320,512]{1,0:T(8,128)(2,1)}, bf16[320,512]{1,0:T(8,128)(2,1)}, u32[]{:S(2)}, u32[]{:S(2)}) collective-permute-start(bf16[320,512]{1,0:T(8,128)(2,1)} %pad_maximum_fusion.rest_0_), channel_id=1, source_target_pairs={{0,2},{1,3},{2,4},{3,5},{4,6},{5,7},{6,0},{7,1},{8,10},{9,11},{10,... | collective-permute-start | bytes 983048 | tf_op jit(solution)/shard_map/ppermute | solution.py:26
  38.5 16.2 %collective-permute-start.9 = (bf16[18,512]{1,0:T(8,128)(2,1)}, bf16[18,512]{1,0:T(8,128)(2,1)}, u32[]{:S(2)}, u32[]{:S(2)}) collective-permute-start(bf16[18,512]{1,0:T(8,128)(2,1)} %copy-done.23), channel_id=1, source_target_pairs={{0,1},{1,2},{2,3},{3,4},{4,5},{5,6},{6,7},{7,0},{8,9},{9,10},{10,1... | collective-permute-start | bytes 55304 | tf_op jit(solution)/shard_map/ppermute | solution.py:46
  41.3 14.8 %collective-permute-start.10 = (bf16[18,512]{1,0:T(8,128)(2,1)}, bf16[18,512]{1,0:T(8,128)(2,1)}, u32[]{:S(2)}, u32[]{:S(2)}) collective-permute-start(bf16[18,512]{1,0:T(8,128)(2,1)} %copy-done.22), channel_id=1, source_target_pairs={{0,7},{1,0},{2,1},{3,2},{4,3},{5,4},{6,5},{7,6},{8,15},{9,8},{10,9... | collective-permute-start | bytes 55304 | tf_op jit(solution)/shard_map/ppermute | solution.py:46
  54.6 0.8 copy-start.15
  56.1 1.2 copy-start.1
  57.3 1.5 %copy-start.8 = (bf16[16,20,6,512]{3,0,2,1:T(8,128)(2,1)S(1)}, bf16[16,20,6,512]{3,0,2,1:T(8,128)(2,1)}, u32[]{:S(2)}) copy-start(bf16[16,20,6,512]{3,0,2,1:T(8,128)(2,1)} %param.14) | copy-start | bytes 5898244
  58.9 0.8 copy-start.14
  59.7 13.7 %copy-start.3 = (bf16[2,1024,512]{2,1,0:T(8,128)(2,1)S(1)}, bf16[2,1024,512]{2,1,0:T(8,128)(2,1)}, u32[]{:S(2)}) copy-start(bf16[2,1024,512]{2,1,0:T(8,128)(2,1)} %ni_ref.3) | copy-start | bytes 6291460
  59.7 13.7 %copy-start.7 = (bf16[2,512,512]{2,1,0:T(8,128)(2,1)S(1)}, bf16[2,512,512]{2,1,0:T(8,128)(2,1)}, u32[]{:S(2)}) copy-start(bf16[2,512,512]{2,1,0:T(8,128)(2,1)} %no_ref.3) | copy-start | bytes 3145732
  59.7 13.7 %copy-start.10 = (bf16[160,512]{1,0:T(8,128)(2,1)S(1)}, bf16[160,512]{1,0:T(8,128)(2,1)}, u32[]{:S(2)}) copy-start(bf16[160,512]{1,0:T(8,128)(2,1)} %long_ref.1) | copy-start | bytes 491524
  59.7 13.7 %copy-start.18 = (f32[2,512]{1,0:T(2,128)S(1)}, f32[2,512]{1,0:T(2,128)}, u32[]{:S(2)}) copy-start(f32[2,512]{1,0:T(2,128)} %ng_ref.3) | copy-start | bytes 12292
  66.6 5.5 %collective-permute-start.11 = (bf16[320,512]{1,0:T(8,128)(2,1)}, bf16[320,512]{1,0:T(8,128)(2,1)S(1)}, u32[]{:S(2)}, u32[]{:S(2)}) collective-permute-start(bf16[320,512]{1,0:T(8,128)(2,1)} %pad_maximum_fusion.rest_0_), channel_id=1, source_target_pairs={{0,1},{1,0},{2,3},{3,2},{4,5},{5,4},{6,7},{7,6},{8,9},{9,8},{10,11... | collective-permute-start | bytes 983048 | tf_op jit(solution)/shard_map/ppermute | solution.py:26
  70.6 1.9 %collective-permute-start.12 = (bf16[320,512]{1,0:T(8,128)(2,1)}, bf16[320,512]{1,0:T(8,128)(2,1)S(1)}, u32[]{:S(2)}, u32[]{:S(2)}) collective-permute-start(bf16[320,512]{1,0:T(8,128)(2,1)} %collective-permute-done.6.rest_1_), channel_id=1, source_target_pairs={{0,1},{1,0},{2,3},{3,2},{4,5},{5,4},{6,7},{7,6},{8,9},{9,8},{10,11... | collective-permute-start | bytes 983048 | tf_op jit(solution)/shard_map/ppermute | solution.py:26
  70.7 2.3 %collective-permute-start.13 = (bf16[320,512]{1,0:T(8,128)(2,1)}, bf16[320,512]{1,0:T(8,128)(2,1)S(1)}, u32[]{:S(2)}, u32[]{:S(2)}) collective-permute-start(bf16[320,512]{1,0:T(8,128)(2,1)} %collective-permute-done.7.rest_2_), channel_id=1, source_target_pairs={{0,1},{1,0},{2,3},{3,2},{4,5},{5,4},{6,7},{7,6},{8,9},{9,8},{10,11... | collective-permute-start | bytes 983048 | tf_op jit(solution)/shard_map/ppermute | solution.py:26
  71.1 2.4 %collective-permute-start.14 = (bf16[320,512]{1,0:T(8,128)(2,1)}, bf16[320,512]{1,0:T(8,128)(2,1)S(1)}, u32[]{:S(2)}, u32[]{:S(2)}) collective-permute-start(bf16[320,512]{1,0:T(8,128)(2,1)} %collective-permute-done.8.rest_3_), channel_id=1, source_target_pairs={{0,1},{1,0},{2,3},{3,2},{4,5},{5,4},{6,7},{7,6},{8,9},{9,8},{10,11... | collective-permute-start | bytes 983048 | tf_op jit(solution)/shard_map/ppermute | solution.py:26
  73.5 29.9 %copy-start.2 = (bf16[2,512,512]{2,1,0:T(8,128)(2,1)S(1)}, bf16[2,512,512]{2,1,0:T(8,128)(2,1)}, u32[]{:S(2)}) copy-start(bf16[2,512,512]{2,1,0:T(8,128)(2,1)} %eo_ref.5) | copy-start | bytes 3145732
  78.8 11.3 %collective-permute-start.15 = (bf16[40,512]{1,0:T(8,128)(2,1)S(1)}, bf16[40,512]{1,0:T(8,128)(2,1)S(1)}, u32[]{:S(2)}, u32[]{:S(2)}) collective-permute-start(bf16[40,512]{1,0:T(8,128)(2,1)S(1)} %get-tuple-element.96), channel_id=1, source_target_pairs={{0,8},{8,16},{16,24},{24,32},{32,40},{40,48},{48,56},{56,64},{64,7... | collective-permute-start | bytes 122888 | tf_op jit(solution)/shard_map/ppermute | solution.py:46
  79.6 10.6 %collective-permute-start.17 = (bf16[40,512]{1,0:T(8,128)(2,1)S(1)}, bf16[40,512]{1,0:T(8,128)(2,1)S(1)}, u32[]{:S(2)}, u32[]{:S(2)}) collective-permute-start(bf16[40,512]{1,0:T(8,128)(2,1)S(1)} %get-tuple-element.97), channel_id=1, source_target_pairs={{0,120},{8,0},{16,8},{24,16},{32,24},{40,32},{48,40},{56,48},{64,5... | collective-permute-start | bytes 122888 | tf_op jit(solution)/shard_map/ppermute | solution.py:46
  83.9 6.3 %collective-permute-start.16 = (bf16[20,512]{1,0:T(8,128)(2,1)S(1)}, bf16[20,512]{1,0:T(8,128)(2,1)S(1)}, u32[]{:S(2)}, u32[]{:S(2)}) collective-permute-start(bf16[20,512]{1,0:T(8,128)(2,1)S(1)} %get-tuple-element.95.own_ref), channel_id=1, source_target_pairs={{0,16},{8,24},{16,32},{24,40},{32,48},{40,56},{48,64},{56,72},{64,... | collective-permute-start | bytes 61448 | tf_op jit(solution)/shard_map/ppermute | solution.py:46
  90.2 3.4 %collective-permute-start.20 = (bf16[80,512]{1,0:T(8,128)(2,1)S(1)}, bf16[80,512]{1,0:T(8,128)(2,1)S(1)}, u32[]{:S(2)}, u32[]{:S(2)}) collective-permute-start(bf16[80,512]{1,0:T(8,128)(2,1)S(1)} %get-tuple-element.99), channel_id=1, source_target_pairs={{0,96},{8,104},{16,112},{24,120},{32,0},{40,8},{48,16},{56,24},{64... | collective-permute-start | bytes 245768 | tf_op jit(solution)/shard_map/ppermute | solution.py:46
  90.3 4.9 %collective-permute-start.19 = (bf16[80,512]{1,0:T(8,128)(2,1)S(1)}, bf16[80,512]{1,0:T(8,128)(2,1)S(1)}, u32[]{:S(2)}, u32[]{:S(2)}) collective-permute-start(bf16[80,512]{1,0:T(8,128)(2,1)S(1)} %get-tuple-element.99), channel_id=1, source_target_pairs={{0,64},{8,72},{16,80},{24,88},{32,96},{40,104},{48,112},{56,120},{... | collective-permute-start | bytes 245768 | tf_op jit(solution)/shard_map/ppermute | solution.py:46
  90.4 5.7 %collective-permute-start.18 = (bf16[80,512]{1,0:T(8,128)(2,1)S(1)}, bf16[80,512]{1,0:T(8,128)(2,1)S(1)}, u32[]{:S(2)}, u32[]{:S(2)}) collective-permute-start(bf16[80,512]{1,0:T(8,128)(2,1)S(1)} %get-tuple-element.99), channel_id=1, source_target_pairs={{0,32},{8,40},{16,48},{24,56},{32,64},{40,72},{48,80},{56,88},{64,... | collective-permute-start | bytes 245768 | tf_op jit(solution)/shard_map/ppermute | solution.py:46
  96.0 23.8 %collective-permute-start.23 = (bf16[320,512]{1,0:T(8,128)(2,1)S(1)}, bf16[320,512]{1,0:T(8,128)(2,1)S(1)}, u32[]{:S(2)}, u32[]{:S(2)}) collective-permute-start(bf16[320,512]{1,0:T(8,128)(2,1)S(1)} %pad_maximum_fusion.1.rest_0_), channel_id=1, source_target_pairs={{0,6},{1,7},{2,0},{3,1},{4,2},{5,3},{6,4},{7,5},{8,14},{9,15},{10,... | collective-permute-start | bytes 983048 | tf_op jit(solution)/shard_map/ppermute | solution.py:26
  96.5 23.4 %collective-permute-start.22 = (bf16[320,512]{1,0:T(8,128)(2,1)S(1)}, bf16[320,512]{1,0:T(8,128)(2,1)S(1)}, u32[]{:S(2)}, u32[]{:S(2)}) collective-permute-start(bf16[320,512]{1,0:T(8,128)(2,1)S(1)} %pad_maximum_fusion.1.rest_0_), channel_id=1, source_target_pairs={{0,4},{1,5},{2,6},{3,7},{4,0},{5,1},{6,2},{7,3},{8,12},{9,13},{10,... | collective-permute-start | bytes 983048 | tf_op jit(solution)/shard_map/ppermute | solution.py:26
  96.5 23.4 %collective-permute-start.21 = (bf16[320,512]{1,0:T(8,128)(2,1)S(1)}, bf16[320,512]{1,0:T(8,128)(2,1)S(1)}, u32[]{:S(2)}, u32[]{:S(2)}) collective-permute-start(bf16[320,512]{1,0:T(8,128)(2,1)S(1)} %pad_maximum_fusion.1.rest_0_), channel_id=1, source_target_pairs={{0,2},{1,3},{2,4},{3,5},{4,6},{5,7},{6,0},{7,1},{8,10},{9,11},{10,... | collective-permute-start | bytes 983048 | tf_op jit(solution)/shard_map/ppermute | solution.py:26
  97.6 9.8 %collective-permute-start.24 = (bf16[18,512]{1,0:T(8,128)(2,1)S(1)}, bf16[18,512]{1,0:T(8,128)(2,1)S(1)}, u32[]{:S(2)}, u32[]{:S(2)}) collective-permute-start(bf16[18,512]{1,0:T(8,128)(2,1)S(1)} %get-tuple-element.104), channel_id=1, source_target_pairs={{0,1},{1,2},{2,3},{3,4},{4,5},{5,6},{6,7},{7,0},{8,9},{9,10},{10,1... | collective-permute-start | bytes 55304 | tf_op jit(solution)/shard_map/ppermute | solution.py:46
  103.4 9.8 %collective-permute-start.25 = (bf16[18,512]{1,0:T(8,128)(2,1)S(1)}, bf16[18,512]{1,0:T(8,128)(2,1)S(1)}, u32[]{:S(2)}, u32[]{:S(2)}) collective-permute-start(bf16[18,512]{1,0:T(8,128)(2,1)S(1)} %get-tuple-element.105), channel_id=1, source_target_pairs={{0,7},{1,0},{2,1},{3,2},{4,3},{5,4},{6,5},{7,6},{8,15},{9,8},{10,9... | collective-permute-start | bytes 55304 | tf_op jit(solution)/shard_map/ppermute | solution.py:46
  119.8 2.7 %collective-permute-start.26 = (bf16[320,512]{1,0:T(8,128)(2,1)S(1)}, bf16[320,512]{1,0:T(8,128)(2,1)S(1)}, u32[]{:S(2)}, u32[]{:S(2)}) collective-permute-start(bf16[320,512]{1,0:T(8,128)(2,1)S(1)} %pad_maximum_fusion.1.rest_0_), channel_id=1, source_target_pairs={{0,1},{1,0},{2,3},{3,2},{4,5},{5,4},{6,7},{7,6},{8,9},{9,8},{10,11... | collective-permute-start | bytes 983048 | tf_op jit(solution)/shard_map/ppermute | solution.py:26
  121.3 1.7 %collective-permute-start.27 = (bf16[320,512]{1,0:T(8,128)(2,1)S(1)}, bf16[320,512]{1,0:T(8,128)(2,1)S(1)}, u32[]{:S(2)}, u32[]{:S(2)}) collective-permute-start(bf16[320,512]{1,0:T(8,128)(2,1)S(1)} %collective-permute-done.21.rest_1_), channel_id=1, source_target_pairs={{0,1},{1,0},{2,3},{3,2},{4,5},{5,4},{6,7},{7,6},{8,9},{9,8},{10,11... | collective-permute-start | bytes 983048 | tf_op jit(solution)/shard_map/ppermute | solution.py:26
  121.3 2.1 %collective-permute-start.28 = (bf16[320,512]{1,0:T(8,128)(2,1)S(1)}, bf16[320,512]{1,0:T(8,128)(2,1)S(1)}, u32[]{:S(2)}, u32[]{:S(2)}) collective-permute-start(bf16[320,512]{1,0:T(8,128)(2,1)S(1)} %collective-permute-done.22.rest_2_), channel_id=1, source_target_pairs={{0,1},{1,0},{2,3},{3,2},{4,5},{5,4},{6,7},{7,6},{8,9},{9,8},{10,11... | collective-permute-start | bytes 983048 | tf_op jit(solution)/shard_map/ppermute | solution.py:26
  121.8 2.2 %collective-permute-start.29 = (bf16[320,512]{1,0:T(8,128)(2,1)S(1)}, bf16[320,512]{1,0:T(8,128)(2,1)S(1)}, u32[]{:S(2)}, u32[]{:S(2)}) collective-permute-start(bf16[320,512]{1,0:T(8,128)(2,1)S(1)} %collective-permute-done.23.rest_3_), channel_id=1, source_target_pairs={{0,1},{1,0},{2,3},{3,2},{4,5},{5,4},{6,7},{7,6},{8,9},{9,8},{10,11... | collective-permute-start | bytes 983048 | tf_op jit(solution)/shard_map/ppermute | solution.py:26
  (7 other events, 4.8 us)

commit v5 on v4

--- a/solution.py
+++ b/solution.py
@@ -38,7 +38,7 @@
     home_z, home_core = lax.shift_right_logical(home, 1) & 3, home & 1
     kz = (lax.shift_right_logical(py, 1) - home_z) & 3
     kc = (py - home_core) & 1
-    return (((kc * 4 + kz) * 4 + far) * 4 + near) * coarse_count + row, home
+    return (((kc * 4 + kz) * 4 + near) * 4 + far) * coarse_count + row, home
 
 
 def along(values, axis, step):
@@ -56,10 +56,8 @@
         step = q - 3 * down
         from_row = lax.broadcasted_iota(jnp.int32, codes.shape, 1) + down - 1
         column = lax.broadcasted_iota(jnp.int32, codes.shape, 2)
-        from_column = column + step - 1
         near = ((column & (BAND - 1)) + step) * rows + from_row
-        outer = jnp.where(from_column < 0, columns, jnp.where(from_column >= columns, columns + 1, from_column))
-        sender = jnp.where(from_row < 0, ABOVE + outer, jnp.where(from_row >= rows, BELOW + outer, near))
+        sender = jnp.where(from_row < 0, ABOVE + column + step, jnp.where(from_row >= rows, BELOW + column + step, near))
         lanes = lax.broadcasted_iota(jnp.int32, (rows, 256), 1)
         row = lax.broadcasted_iota(jnp.int32, (rows, 256), 0)
         for c in range(columns):
@@ -92,7 +90,7 @@
     return (before.astype(jnp.float32) + scaled).astype(jnp.bfloat16)
 
 
-def fine_layer(layer, fine, picks, latents, left, right, sides, inner, outer, gain, rows, columns):
+def fine_layer(layer, fine, picks, latents, left, right, sides, inner, outer, gain, rows):
     edges, features = fine.shape
     nodes = latents.shape[0]
     hidden = inner.shape[2]
@@ -114,14 +112,8 @@
             table_ref[ABOVE + sides.shape[0] :, :] = jnp.zeros((256 - ABOVE - sides.shape[0], hidden), jnp.bfloat16)
             send_ref[rows : rows + nodes, :] = project(latents_ref)
             recv_ref[...] = dot(latents_ref[...], inner_ref[layer, 2 * features :, :]).astype(jnp.bfloat16)
-            side = project(left_ref)
-            send_ref[:rows, :] = side[:rows]
-            table_ref[ABOVE + columns : ABOVE + columns + 1, :] = side[rows : rows + 1]
-            table_ref[BELOW + columns : BELOW + columns + 1, :] = side[rows + 1 : rows + 2]
-            side = project(right_ref)
-            send_ref[rows + nodes :, :] = side[:rows]
-            table_ref[ABOVE + columns + 1 : ABOVE + columns + 2, :] = side[rows : rows + 1]
-            table_ref[BELOW + columns + 1 : BELOW + columns + 2, :] = side[rows + 1 : rows + 2]
+            send_ref[:rows, :] = project(left_ref)
+            send_ref[rows + nodes :, :] = project(right_ref)
 
         start = pl.multiple_of(step * own, own)
         table_ref[:near, :] = send_ref[pl.ds(start, near), :]
@@ -178,67 +170,86 @@
     return [pl.BlockSpec(a.shape, lambda i, n=len(a.shape): (0,) * n) for a in arrays]
 
 
-def send_rows(both, up_ref, down_ref, own_ref):
-    half, count = up_ref.shape[0], own_ref.shape[0]
+def send_rows(both, own_ref, last_ref, first_ref):
     rows = both.astype(jnp.bfloat16)
-    up_ref[...] = rows[:half]
-    down_ref[...] = rows[half:]
+    count, columns = own_ref.shape[0], last_ref.shape[0]
     own_ref[...] = rows[:count]
-
-
-def join(own, up, two, down, latents, rows):
+    last_ref[...] = rows[count : count + columns]
+    first_ref[...] = rows[count + columns :]
+
+
+def join_far(own, fars, left, right, last, first):
     count, features = own.shape
-    columns = up.shape[0] - count
-
-    def body(own_ref, up_ref, two_ref, down_ref, latents_ref, joined_ref, last_ref, first_ref, sides_ref):
+    rows = left.shape[0]
+    four = 4 * count
+    columns = last.shape[0]
+
+    def body(own_ref, far1_ref, far2_ref, far3_ref, left_ref, right_ref, last_ref, first_ref, two_ref, up_ref, down_ref):
+        for at, ref in enumerate((own_ref, far1_ref, far2_ref, far3_ref)):
+            two_ref[at * count : (at + 1) * count, :] = ref[...]
+        for out_ref, line_ref, row in ((up_ref, last_ref, rows - 1), (down_ref, first_ref, 0)):
+            out_ref[:four, :] = two_ref[...]
+            out_ref[four:, :] = jnp.zeros((out_ref.shape[0] - four, features), jnp.bfloat16)
+            out_ref[four : four + 1, :] = left_ref[row : row + 1, :]
+            out_ref[four + 1 : four + 1 + columns, :] = line_ref[...]
+            out_ref[four + 1 + columns : four + 2 + columns, :] = right_ref[row : row + 1, :]
+
+    held = pl.BlockSpec(memory_space=pltpu.VMEM)
+    return pl.pallas_call(
+        body,
+        name="join_far",
+        out_shape=tuple(jax.ShapeDtypeStruct((n, features), jnp.bfloat16) for n in (four, four + 32, four + 32)),
+        in_specs=[held] * 8,
+        out_specs=(held,) * 3,
+        compiler_params=pltpu.CompilerParams(vmem_limit_bytes=2 * MIB),
+    )(own, *fars, left, right, last, first)
+
+
+def join_near(own, up, two, down):
+    each, features = own.shape
+
+    def body(own_ref, up_ref, two_ref, down_ref, joined_ref, sides_ref):
         for at, ref in enumerate((own_ref, up_ref, two_ref, down_ref)):
-            joined_ref[at * count : (at + 1) * count, :] = ref[:count, :]
-        last_ref[:rows, :] = latents_ref[-rows:, :]
-        last_ref[rows : rows + 1, :] = up_ref[-1:, :]
-        last_ref[rows + 1 :, :] = down_ref[-1:, :]
-        first_ref[:rows, :] = latents_ref[:rows, :]
-        first_ref[rows : rows + 1, :] = up_ref[count : count + 1, :]
-        first_ref[rows + 1 :, :] = down_ref[count : count + 1, :]
-        sides_ref[...] = jnp.zeros(sides_ref.shape, jnp.bfloat16)
-        sides_ref[:columns, :] = up_ref[count:, :]
-        sides_ref[BELOW - ABOVE : BELOW - ABOVE + columns, :] = down_ref[count:, :]
-
-    held = pl.BlockSpec(memory_space=pltpu.VMEM)
-    return pl.pallas_call(
-        body,
-        name="join",
-        out_shape=tuple(jax.ShapeDtypeStruct((n, features), jnp.bfloat16) for n in (4 * count, rows + 2, rows + 2, 256 - ABOVE - 32)),
-        in_specs=[held] * 5,
-        out_specs=(held,) * 4,
+            joined_ref[at * each : (at + 1) * each, :] = ref[:each, :]
+        sides_ref[: BELOW - ABOVE, :] = up_ref[each:, :]
+        sides_ref[BELOW - ABOVE :, :] = down_ref[each:, :]
+
+    held = pl.BlockSpec(memory_space=pltpu.VMEM)
+    return pl.pallas_call(
+        body,
+        name="join_near",
+        cost_estimate=pl.CostEstimate(flops=3_000_000_000, bytes_accessed=0, transcendentals=0),
+        out_shape=tuple(jax.ShapeDtypeStruct((n, features), jnp.bfloat16) for n in (4 * each, 2 * (BELOW - ABOVE))),
+        in_specs=[held] * 4,
+        out_specs=(held,) * 2,
         compiler_params=pltpu.CompilerParams(vmem_limit_bytes=2 * MIB),
-    )(own, up, two, down, latents)
+    )(own, up, two, down)
 
 
 def coarse_start(coarse_slots, latents, rows, columns):
     count = coarse_slots.shape[1]
     nodes, features = latents.shape
-    half = count + columns
-
-    def body(slots_ref, latents_ref, up_ref, down_ref, own_ref, choose_ref):
+    size = count + 2 * columns
+
+    def body(slots_ref, latents_ref, own_ref, last_ref, first_ref, choose_ref):
         slot = slots_ref[...]
         row = jnp.floor((slot.astype(jnp.float32) + 0.5) * (1.0 / columns)).astype(jnp.int32)
         at = (slot - row * columns) * rows + row
         place = (lax.broadcasted_iota(jnp.int32, (nodes, count), 0) == at).astype(jnp.bfloat16)
-        out = lax.broadcasted_iota(jnp.int32, (2 * half, count), 0)
-        line = lax.broadcasted_iota(jnp.int32, (2 * half, count), 1)
-        same = ((out == line) | (out == line + half)).astype(jnp.bfloat16)
-        out = lax.broadcasted_iota(jnp.int32, (2 * half, nodes), 0)
-        node = lax.broadcasted_iota(jnp.int32, (2 * half, nodes), 1)
-        edge = ((out >= count) & (out < half) & (node == (out - count) * rows + rows - 1)) | (
-            (out >= half + count) & (node == (out - half - count) * rows)
+        out = lax.broadcasted_iota(jnp.int32, (size, count), 0)
+        same = (out == lax.broadcasted_iota(jnp.int32, (size, count), 1)).astype(jnp.bfloat16)
+        out = lax.broadcasted_iota(jnp.int32, (size, nodes), 0)
+        node = lax.broadcasted_iota(jnp.int32, (size, nodes), 1)
+        edge = ((out >= count) & (out < count + columns) & (node == (out - count) * rows + rows - 1)) | (
+            (out >= count + columns) & (node == (out - count - columns) * rows)
         )
         choose = (rows_to_columns(same, place) + edge.astype(jnp.float32)).astype(jnp.bfloat16)
         choose_ref[...] = choose
-        send_rows(dot(choose, latents_ref[...]), up_ref, down_ref, own_ref)
+        send_rows(dot(choose, latents_ref[...]), own_ref, last_ref, first_ref)
 
     shapes = (
-        *(jax.ShapeDtypeStruct((n, features), jnp.bfloat16) for n in (half, half, count)),
-        jax.ShapeDtypeStruct((2 * half, nodes), jnp.bfloat16),
+        *(jax.ShapeDtypeStruct((n, features), jnp.bfloat16) for n in (count, columns, columns)),
+        jax.ShapeDtypeStruct((size, nodes), jnp.bfloat16),
     )
     return pl.pallas_call(
         body,
@@ -299,6 +310,7 @@
         name="pack_edges",
         out_shape=shapes,
         grid=(1,),
+        cost_estimate=pl.CostEstimate(flops=12_000_000_000, bytes_accessed=0, transcendentals=0),
         in_specs=[pl.BlockSpec(memory_space=pltpu.SMEM)] + blocks_of(long_edges, senders, receivers),
         out_specs=blocks_of(*shapes),
         scratch_shapes=[pltpu.VMEM((devices * 16, TAGS), jnp.float32)],
@@ -404,8 +416,8 @@
     held = pl.BlockSpec(memory_space=pltpu.VMEM)
     away = pl.BlockSpec(memory_space=pl.ANY)
     table_shape = (table_rows, features)
-    half = choose.shape[0] // 2
-    kept = (both - slots,) if last else (slots, half, half, coarse_count, table_rows)
+    side = (choose.shape[0] - coarse_count) // 2
+    kept = (both - slots,) if last else (slots, coarse_count, side, side, table_rows)
     shapes = [jax.ShapeDtypeStruct((n, features), jnp.bfloat16) for n in (nodes, *kept)]
 
     return pl.pallas_call(
@@ -467,26 +479,28 @@
 
     latents = node_latents.transpose(1, 0, 2).reshape(nodes, features)
     fine = fine_edges.transpose(1, 2, 0, 3).reshape(nodes * degree, features)
-    up, down, own, choose = coarse_start(coarse_slots[None, :], latents, rows, columns)
+    own, last_row, first_row, choose = coarse_start(coarse_slots[None, :], latents, rows, columns)
     long_edges, own = tie(long_edges, own)
     own_rows = long_edges
     me = lax.axis_index(AXES).reshape(1)
     payload, own_tags = pack_edges(long_edges, long_senders[None, :], long_receivers[None, :], me, coarse_count, devices)
     for layer in range(layers):
         last = layer == layers - 1
+        fars = [along(own, "px", 4 * s) for s in (1, 2, 3)]
+        left = along(latents[-rows:], "py", 1)
+        right = along(latents[:rows], "py", -1)
+        if layer == 0:
+            *fars, left, right, payload = tie(*fars, left, right, payload)
+        joined, up, down = join_far(own, fars, left, right, last_row, first_row)
+        if layer == 0:
+            packed = payload.reshape(devices, 16, TAGS)
+            arrived = lax.all_to_all(packed, AXES, split_axis=0, concat_axis=0, tiled=True).reshape(payload.shape)
         up = along(up, "px", 1)
         down = along(down, "px", -1)
-        two = along(own, "px", 2)
-        if layer == 0:
-            two, payload = tie(two, payload)
-            packed = payload.reshape(devices, 16, TAGS)
-            arrived = lax.all_to_all(packed, AXES, split_axis=0, concat_axis=0, tiled=True).reshape(payload.shape)
-        joined, to_right, to_left, sides = join(own, up, two, down, latents, rows)
-        joined = jnp.concatenate([joined] + [along(joined, "px", 4 * s) for s in (1, 2, 3)], axis=0)
-        joined, to_right, to_left, own_rows = tie(joined, to_right, to_left, own_rows)
+        two = along(joined, "px", 2)
+        joined, sides = join_near(joined, up, two, down)
+        joined, sides, own_rows = tie(joined, sides, own_rows)
         pieces = [joined] + [shift(joined, Z, s) for s in (1, 2, 3)]
-        left = along(to_right, "py", 1)
-        right = along(to_left, "py", -1)
         if layer == 0:
             table_rows = 2 * len(pieces) * joined.shape[0]
             long_rows, sends, recvs, adds = unpack_edges(arrived, own_tags, choose, features, table_rows, coarse_count)
@@ -495,7 +509,7 @@
         else:
             own_rows = own_layer(layer - 1, own_rows, sends, table, edge_inner, edge_outer, edge_gain)
         fine, fine_sum = fine_layer(
-            layer, fine, picks, latents, left, right, sides, edge_inner, edge_outer, edge_gain, rows, columns
+            layer, fine, picks, latents, left, right, sides, edge_inner, edge_outer, edge_gain, rows
         )
         first, *others, fine_sum, own_rows, long_rows = tie(*pieces, fine_sum, own_rows, long_rows)
         pieces = [first] + others
@@ -507,7 +521,7 @@
         if last:
             own_rows = rest[0]
         else:
-            long_rows, up, down, own, table = rest
+            long_rows, own, last_row, first_row, table = rest
     return (
         latents.reshape(columns, rows, features).transpose(1, 0, 2),
         fine.reshape(columns, degree, rows, features).transpose(2, 0, 1, 3),

time: 130 us -> 116 us (0.89)
  waiting for transfers between devices: 36.4 us -> 24.5 us
  local copies, waits for them, and re-layouts: 11.3 us -> 15.5 us
  starting transfers between devices: 46.5 us -> 43 us
  other arithmetic: 1.78 us -> 0 us
  Pallas kernels: 32.7 us -> 31.1 us
    ppermute x16, waiting for transfers between devices: 27.4 us -> 8.54 us  [along(): lax.ppermute(values, axis, [(i, (i + step) % count) for i in range(count)])]
    ppermute x14, waiting for transfers between devices: 4.34 us -> 13.8 us  [shift(): return lax.ppermute(values, 'py', pairs)]
    unnamed x48 -> x58, local copies, waits for them, and re-layouts: 11.3 us -> 14.8 us
    ppermute x14, starting transfers between devices: 12.3 us -> 9.73 us  [shift(): return lax.ppermute(values, 'py', pairs)]
    all_to_all x1, waiting for transfers between devices: 4.65 us -> 2.14 us  [shards(): lax.all_to_all(packed, AXES, split_axis=0, concat_axis=0, tiled=True)]
    concatenate x2 -> x0, other arithmetic: 1.78 us -> none  [shards(): jnp.concatenate([joined] + [along(joined, 'px', 4 * s) for s in (1, 2, 3)...]
    all_to_all x1, starting transfers between devices: 11.7 us -> 10.2 us  [shards(): lax.all_to_all(packed, AXES, split_axis=0, concat_axis=0, tiled=True)]
  transfers between devices with their start and end apart: 31 -> 31, of which waited for: 18 -> 14; matrix products, arithmetic and copies ran while one was open for 1% -> 1% of each run, Pallas kernels for 15% -> 17%
where the time goes in v5:
time: 116 us; the launch traced here: 115 us
  starting transfers between devices  43 us (37%)
  Pallas kernels  31.1 us (27%)
  waiting for transfers between devices  24.5 us (21%)
  local copies, waits for them, and re-layouts  15.5 us (13%)
    ppermute x16, starting transfers between devices, along(): lax.ppermute(values, axis, [(i, (i + step) % count) for i in range(count)])  23.1 us
    unnamed x58, local copies, waits for them, and re-layouts  14.8 us
    ppermute x14, waiting for transfers between devices, shift(): return lax.ppermute(values, 'py', pairs)  13.8 us
    pallas_call x2, Pallas kernels, fine_layer(): pl.pallas_call(body, name=f'fine{layer}', out_shape=(jax.ShapeDtypeStruct...  12.6 us
    pallas_call x2, Pallas kernels, coarse_layer(): pl.pallas_call(body, name=f'coarse{layer}', out_shape=tuple(shapes), in_s...  10.8 us
    all_to_all x1, starting transfers between devices, shards(): lax.all_to_all(packed, AXES, split_axis=0, concat_axis=0, tiled=True)  10.2 us
    ppermute x14, starting transfers between devices, shift(): return lax.ppermute(values, 'py', pairs)  9.73 us
    ppermute x16, waiting for transfers between devices, along(): lax.ppermute(values, axis, [(i, (i + step) % count) for i in range(count)])  8.54 us
  transfers between devices with their start and end apart: 31, of which 14 were waited for; matrix products, arithmetic and copies ran while one was open for 1% of the time, Pallas kernels for 17%

profile of v5, /device:TPU:1, one launch (start us, length us, event | category | flops | bytes accessed | tf_op | source)
XLA Modules:
  0.0 115.3 jit_solution(11860548784751323852)
XLA Ops:
  0.6 1.0 copy-done.4
  1.6 0.7 copy-done.18
  2.6 3.6 %collective-permute-start.2 = (bf16[20,512]{1,0:T(8,128)(2,1)S(1)}, bf16[20,512]{1,0:T(8,128)(2,1)S(1)}, u32[]{:S(2)}, u32[]{:S(2)}) collective-permute-start(bf16[20,512]{1,0:T(8,128)(2,1)S(1)} %get-tuple-element.67.own_ref), channel_id=1, source_target_pairs={{0,96},{8,104},{16,112},{24,120},{32,0},{40,8},{48,16},{56,24},{64... | collective-permute-start | bytes 61448 | tf_op jit(solution)/shard_map/ppermute | solution.py:46
  6.6 0.7 collective-permute-start
  7.3 0.7 slice_bitcast_fusion
  8.0 1.5 %collective-permute-start.4 = (bf16[16,512]{1,0:T(8,128)(2,1)S(1)}, bf16[16,512]{1,0:T(8,128)(2,1)S(1)}, u32[]{:S(2)}, u32[]{:S(2)}) collective-permute-start(bf16[16,512]{1,0:T(8,128)(2,1)S(1)} %get-tuple-element.131), channel_id=1, source_target_pairs={{0,7},{1,0},{2,1},{3,2},{4,3},{5,4},{6,5},{7,6},{8,15},{9,8},{10,9... | collective-permute-start | bytes 49160 | tf_op jit(solution)/shard_map/ppermute | solution.py:46
  9.5 1.5 %collective-permute-start.3 = (bf16[16,512]{1,0:T(8,128)(2,1)S(1)}, bf16[16,512]{1,0:T(8,128)(2,1)S(1)}, u32[]{:S(2)}, u32[]{:S(2)}) collective-permute-start(bf16[16,512]{1,0:T(8,128)(2,1)S(1)} %get-tuple-element.132), channel_id=1, source_target_pairs={{0,1},{1,2},{2,3},{3,4},{4,5},{5,6},{6,7},{7,0},{8,9},{9,10},{10,1... | collective-permute-start | bytes 49160 | tf_op jit(solution)/shard_map/ppermute | solution.py:46
  11.1 0.9 copy-done.7
  12.0 0.7 copy-done.27
  12.6 0.7 copy-done.28
  13.3 1.6 %pack_edges.1 = (bf16[2048,128]{1,0:T(8,128)(2,1)}, bf16[160,128]{1,0:T(8,128)(2,1)S(1)}) custom-call(s32[1]{0:T(128)} %bitcast.5.me_ref, bf16[160,512]{1,0:T(8,128)(2,1)S(1)} %copy-done.7, s32[1,160]{1,0:T(1,128)S(1)} %bitcast.30, s32[1,160]{1,0:T(1,128)S(1)} %bitcast.31), custom_call_target="tpu_custom_call" | custom-call | flops 12000000000 | tf_op jit(solution)/shard_map/pack_edges/pallas_call | solution.py:308
  15.0 1.3 %collective-permute-start.5 = (bf16[112,512]{1,0:T(8,128)(2,1)S(1)}, bf16[112,512]{1,0:T(8,128)(2,1)S(1)}, u32[]{:S(2)}, u32[]{:S(2)}) collective-permute-start(bf16[112,512]{1,0:T(8,128)(2,1)S(1)} %get-tuple-element.78), channel_id=1, source_target_pairs={{0,8},{8,16},{16,24},{24,32},{32,40},{40,48},{48,56},{56,64},{64,7... | collective-permute-start | bytes 344072 | tf_op jit(solution)/shard_map/ppermute | solution.py:46
  16.3 3.6 %collective-permute-start.7 = (bf16[112,512]{1,0:T(8,128)(2,1)S(1)}, bf16[112,512]{1,0:T(8,128)(2,1)S(1)}, u32[]{:S(2)}, u32[]{:S(2)}) collective-permute-start(bf16[112,512]{1,0:T(8,128)(2,1)S(1)} %get-tuple-element.79), channel_id=1, source_target_pairs={{0,120},{8,0},{16,8},{24,16},{32,24},{40,32},{48,40},{56,48},{64,5... | collective-permute-start | bytes 344072 | tf_op jit(solution)/shard_map/ppermute | solution.py:46
  19.9 10.2 %all-to-all-start = ((bf16[128,16,128]{2,1,0:T(8,128)(2,1)}), bf16[128,16,128]{2,1,0:T(8,128)(2,1)}, u32[]{:S(2)}, u32[]{:S(2)}) async-start(bf16[128,16,128]{2,1,0:T(8,128)(2,1)} %bitcast.10), calls=%async_computation | async-start | bytes 1048576 | tf_op jit(solution)/shard_map/all_to_all | solution.py:497
  31.4 0.6 copy-done.21
  32.1 0.9 copy-done.20
  33.0 0.9 copy-done.22
  33.9 0.9 copy-done.24
  34.8 0.9 copy-done.26
  35.6 0.7 join_near.2
  37.0 3.3 %collective-permute-start.10 = (bf16[320,512]{1,0:T(8,128)(2,1)}, bf16[320,512]{1,0:T(8,128)(2,1)}, u32[]{:S(2)}, u32[]{:S(2)}) collective-permute-start(bf16[320,512]{1,0:T(8,128)(2,1)} %get-tuple-element.99.rest_0_), channel_id=1, source_target_pairs={{0,6},{1,7},{2,0},{3,1},{4,2},{5,3},{6,4},{7,5},{8,14},{9,15},{10,... | collective-permute-start | bytes 983048 | tf_op jit(solution)/shard_map/ppermute | solution.py:26
  40.3 0.8 collective-permute-start.8
  41.2 2.1 %all-to-all-done = bf16[128,16,128]{2,1,0:T(8,128)(2,1)} async-done(((bf16[128,16,128]{2,1,0:T(8,128)(2,1)}), bf16[128,16,128]{2,1,0:T(8,128)(2,1)}, u32[]{:S(2)}, u32[]{:S(2)}) %all-to-all-start) | async-done | bytes 524320 | tf_op jit(solution)/shard_map/all_to_all | solution.py:497
  43.3 0.9 copy-done.16
  44.2 2.9 %unpack_edges.1 = (bf16[384,512]{1,0:T(8,128)(2,1)S(1)}, bf16[704,2560]{1,0:T(8,128)(2,1)S(1)}, bf16[384,128]{1,0:T(8,128)(2,1)S(1)}, bf16[320,384]{1,0:T(8,128)(2,1)S(1)}) custom-call(bf16[2048,128]{1,0:T(8,128)(2,1)} %bitcast.11.arrived_ref, bf16[160,128]{1,0:T(8,128)(2,1)S(1)} %copy-done.16, bf16[60,320]{1,0:T(8,128)(2,1)S(1)} %get-tuple-element.85.choose_ref), custom_call_target="tpu_custom_call" | custom-call | tf_op jit(solution)/shard_map/unpack_edges/pallas_call | solution.py:348
  47.1 0.8 copy-done.14
  48.3 1.5 %copy-done.6 = bf16[16,20,6,512]{3,0,2,1:T(8,128)(2,1)S(1)} copy-done((bf16[16,20,6,512]{3,0,2,1:T(8,128)(2,1)S(1)}, bf16[16,20,6,512]{3,0,2,1:T(8,128)(2,1)}, u32[]{:S(2)}) %copy-start.6) | copy-done | bytes 1966104
  49.8 0.8 copy-done.11
  50.7 0.7 copy-done.13
  51.4 5.9 %fine0.1 = (bf16[1920,512]{1,0:T(8,128)(2,1)S(1)}, f32[320,512]{1,0:T(8,128)S(1)}) custom-call(bf16[1920,512]{1,0:T(8,128)(2,1)S(1)} %bitcast.27, bf16[1920,256]{1,0:T(8,128)(2,1)S(1)} %selection.1.picks_ref, bf16[320,512]{1,0:T(8,128)(2,1)S(1)} %bitcast.25, bf16[16,512]{1,0:T(8,128)(2,1)S(1)} %copy-done.13, ...), custom_call_target="tpu_custom_call" | custom-call | tf_op jit(solution)/shard_map/fine0/pallas_call | solution.py:129
  57.3 0.9 collective-permute-done.8.rest_1_
  58.2 0.8 collective-permute-start.11
  59.5 1.0 collective-permute-done.11.rest_4_
  61.9 5.2 %coarse0.1 = (bf16[320,512]{1,0:T(8,128)(2,1)S(1)}, bf16[384,512]{1,0:T(8,128)(2,1)S(1)}, bf16[20,512]{1,0:T(8,128)(2,1)S(1)}, bf16[20,512]{1,0:T(8,128)(2,1)S(1...) custom-call(bf16[384,512]{1,0:T(8,128)(2,1)S(1)} %get-tuple-element.93.long_ref, ...), custom_call_target="tpu_custom_call" | custom-call | tf_op jit(solution)/shard_map/coarse0/pallas_call | solution.py:423
  67.1 2.8 %collective-permute-start.17 = (bf16[20,512]{1,0:T(8,128)(2,1)S(1)}, bf16[20,512]{1,0:T(8,128)(2,1)S(1)}, u32[]{:S(2)}, u32[]{:S(2)}) collective-permute-start(bf16[20,512]{1,0:T(8,128)(2,1)S(1)} %get-tuple-element.103.own_ref), channel_id=1, source_target_pairs={{0,96},{8,104},{16,112},{24,120},{32,0},{40,8},{48,16},{56,24},{64... | collective-permute-start | bytes 61448 | tf_op jit(solution)/shard_map/ppermute | solution.py:46
  71.1 1.2 %collective-permute-start.19 = (bf16[16,512]{1,0:T(8,128)(2,1)S(1)}, bf16[16,512]{1,0:T(8,128)(2,1)S(1)}, u32[]{:S(2)}, u32[]{:S(2)}) collective-permute-start(bf16[16,512]{1,0:T(8,128)(2,1)S(1)} %get-tuple-element.129), channel_id=1, source_target_pairs={{0,7},{1,0},{2,1},{3,2},{4,3},{5,4},{6,5},{7,6},{8,15},{9,8},{10,9... | collective-permute-start | bytes 49160 | tf_op jit(solution)/shard_map/ppermute | solution.py:46
  72.8 1.4 %collective-permute-done.19.right_ref = bf16[16,512]{1,0:T(8,128)(2,1)S(1)} collective-permute-done((bf16[16,512]{1,0:T(8,128)(2,1)S(1)}, bf16[16,512]{1,0:T(8,128)(2,1)S(1)}, u32[]{:S(2)}, u32[]{:S(2)}) %collective-permute-start.19) | collective-permute-done | bytes 16416 | tf_op jit(solution)/shard_map/ppermute | solution.py:46
  74.5 1.4 %collective-permute-start.20 = (bf16[112,512]{1,0:T(8,128)(2,1)S(1)}, bf16[112,512]{1,0:T(8,128)(2,1)S(1)}, u32[]{:S(2)}, u32[]{:S(2)}) collective-permute-start(bf16[112,512]{1,0:T(8,128)(2,1)S(1)} %get-tuple-element.108), channel_id=1, source_target_pairs={{0,8},{8,16},{16,24},{24,32},{32,40},{40,48},{48,56},{56,64},{64,7... | collective-permute-start | bytes 344072 | tf_op jit(solution)/shard_map/ppermute | solution.py:46
  75.9 3.5 %collective-permute-start.22 = (bf16[112,512]{1,0:T(8,128)(2,1)S(1)}, bf16[112,512]{1,0:T(8,128)(2,1)S(1)}, u32[]{:S(2)}, u32[]{:S(2)}) collective-permute-start(bf16[112,512]{1,0:T(8,128)(2,1)S(1)} %get-tuple-element.109), channel_id=1, source_target_pairs={{0,120},{8,0},{16,8},{24,16},{32,24},{40,32},{48,40},{56,48},{64,5... | collective-permute-start | bytes 344072 | tf_op jit(solution)/shard_map/ppermute | solution.py:46
  79.3 6.9 %collective-permute-done.21.two_ref = bf16[80,512]{1,0:T(8,128)(2,1)S(1)} collective-permute-done((bf16[80,512]{1,0:T(8,128)(2,1)S(1)}, bf16[80,512]{1,0:T(8,128)(2,1)S(1)}, u32[]{:S(2)}, u32[]{:S(2)}) %collective-permute-start.21) | collective-permute-done | bytes 81952 | tf_op jit(solution)/shard_map/ppermute | solution.py:46
  86.3 2.2 %collective-permute-start.25 = (bf16[320,512]{1,0:T(8,128)(2,1)S(1)}, bf16[320,512]{1,0:T(8,128)(2,1)S(1)}, u32[]{:S(2)}, u32[]{:S(2)}) collective-permute-start(bf16[320,512]{1,0:T(8,128)(2,1)S(1)} %get-tuple-element.122.rest_0_), channel_id=1, source_target_pairs={{0,6},{1,7},{2,0},{3,1},{4,2},{5,3},{6,4},{7,5},{8,14},{9,15},{10,... | collective-permute-start | bytes 983048 | tf_op jit(solution)/shard_map/ppermute | solution.py:26
  88.5 0.7 collective-permute-start.23
  89.2 1.7 %own0.1.own_ref = bf16[160,512]{1,0:T(8,128)(2,1)S(1)} custom-call(bf16[160,512]{1,0:T(8,128)(2,1)S(1)} %copy-done.8, bf16[704,2560]{1,0:T(8,128)(2,1)S(1)} %get-tuple-element.95.sends_ref, bf16[2560,512]{1,0:T(8,128)(2,1)S(1)} %get-tuple-element.117.table_ref, bf16[2,1536,512]{2,1,0:T(8,128)(2,1)S(1)} %copy-done, bf16[2,512,512]{2,1,0:T(8,128)(2,1)S(1)} %copy-done.1, ...), custom_call_target="tpu_custom_call" | custom-call | tf_op jit(solution)/shard_map/own0/pallas_call | solution.py:448
  90.9 6.7 %fine1.1 = (bf16[1920,512]{1,0:T(8,128)(2,1)}, f32[320,512]{1,0:T(8,128)S(1)}) custom-call(bf16[1920,512]{1,0:T(8,128)(2,1)S(1)} %get-tuple-element.113.fine_ref, bf16[1920,256]{1,0:T(8,128)(2,1)S(1)} %selection.1.picks_ref, bf16[320,512]{1,0:T(8,128)(2,1)S(1)} %get-tuple-element.104.latents_ref, bf16[16,512]{1,0:T(8,128)(2,1)S(1)} %collective-permute-done.18.left_ref, ...), custom_call_target="tpu_custom_call" | custom-call | tf_op jit(solution)/shard_map/fine1/pallas_call | solution.py:129
  97.6 8.4 %collective-permute-done.23.rest_1_ = bf16[320,512]{1,0:T(8,128)(2,1)S(1)} collective-permute-done((bf16[320,512]{1,0:T(8,128)(2,1)S(1)}, bf16[320,512]{1,0:T(8,128)(2,1)S(1)}, u32[]{:S(2)}, u32[]{:S(2)}) %collective-permute-start.23) | collective-permute-done | bytes 327712 | tf_op jit(solution)/shard_map/ppermute | solution.py:26
  106.0 0.9 collective-permute-start.26
  107.4 0.7 collective-permute-done.26.rest_4_
  109.5 5.6 %coarse1.1 = (bf16[320,512]{1,0:T(8,128)(2,1)}, bf16[160,512]{1,0:T(8,128)(2,1)}) custom-call(bf16[384,512]{1,0:T(8,128)(2,1)S(1)} %get-tuple-element.119.long_ref, bf16[160,512]{1,0:T(8,128)(2,1)S(1)} %own0.1.own_ref, bf16[704,2560]{1,0:T(8,128)(2,1)S(1)} %get-tuple-element.95.sends_ref, bf16[384,128]{1,0:T(8,128)(2,1)S(1)} %get-tuple-element.96.recvs_ref, ...), custom_call_target="tpu_custom_call" | custom-call | tf_op jit(solution)/shard_map/coarse1/pallas_call | solution.py:423
  (87 shorter events, 8.8 us)
Async XLA Ops:
  0.6 1.0 copy-start.4
  2.6 12.4 %collective-permute-start.2 = (bf16[20,512]{1,0:T(8,128)(2,1)S(1)}, bf16[20,512]{1,0:T(8,128)(2,1)S(1)}, u32[]{:S(2)}, u32[]{:S(2)}) collective-permute-start(bf16[20,512]{1,0:T(8,128)(2,1)S(1)} %get-tuple-element.67.own_ref), channel_id=1, source_target_pairs={{0,96},{8,104},{16,112},{24,120},{32,0},{40,8},{48,16},{56,24},{64... | collective-permute-start | bytes 61448 | tf_op jit(solution)/shard_map/ppermute | solution.py:46
  6.2 8.7 %collective-permute-start.1 = (bf16[20,512]{1,0:T(8,128)(2,1)S(1)}, bf16[20,512]{1,0:T(8,128)(2,1)S(1)}, u32[]{:S(2)}, u32[]{:S(2)}) collective-permute-start(bf16[20,512]{1,0:T(8,128)(2,1)S(1)} %get-tuple-element.67.own_ref), channel_id=1, source_target_pairs={{0,64},{8,72},{16,80},{24,88},{32,96},{40,104},{48,112},{56,120},{... | collective-permute-start | bytes 61448 | tf_op jit(solution)/shard_map/ppermute | solution.py:46
  6.6 8.4 %collective-permute-start = (bf16[20,512]{1,0:T(8,128)(2,1)S(1)}, bf16[20,512]{1,0:T(8,128)(2,1)S(1)}, u32[]{:S(2)}, u32[]{:S(2)}) collective-permute-start(bf16[20,512]{1,0:T(8,128)(2,1)S(1)} %get-tuple-element.67.own_ref), channel_id=1, source_target_pairs={{0,32},{8,40},{16,48},{24,56},{32,64},{40,72},{48,80},{56,88},{64,... | collective-permute-start | bytes 61448 | tf_op jit(solution)/shard_map/ppermute | solution.py:46
  8.0 6.9 %collective-permute-start.4 = (bf16[16,512]{1,0:T(8,128)(2,1)S(1)}, bf16[16,512]{1,0:T(8,128)(2,1)S(1)}, u32[]{:S(2)}, u32[]{:S(2)}) collective-permute-start(bf16[16,512]{1,0:T(8,128)(2,1)S(1)} %get-tuple-element.131), channel_id=1, source_target_pairs={{0,7},{1,0},{2,1},{3,2},{4,3},{5,4},{6,5},{7,6},{8,15},{9,8},{10,9... | collective-permute-start | bytes 49160 | tf_op jit(solution)/shard_map/ppermute | solution.py:46
  9.5 5.4 %collective-permute-start.3 = (bf16[16,512]{1,0:T(8,128)(2,1)S(1)}, bf16[16,512]{1,0:T(8,128)(2,1)S(1)}, u32[]{:S(2)}, u32[]{:S(2)}) collective-permute-start(bf16[16,512]{1,0:T(8,128)(2,1)S(1)} %get-tuple-element.132), channel_id=1, source_target_pairs={{0,1},{1,2},{2,3},{3,4},{4,5},{5,6},{6,7},{7,0},{8,9},{9,10},{10,1... | collective-permute-start | bytes 49160 | tf_op jit(solution)/shard_map/ppermute | solution.py:46
  11.0 0.9 copy-start.7
  14.9 15.8 %copy-start.15 = (bf16[160,128]{1,0:T(8,128)(2,1)}, bf16[160,128]{1,0:T(8,128)(2,1)S(1)}, u32[]{:S(2)}) copy-start(bf16[160,128]{1,0:T(8,128)(2,1)S(1)} %get-tuple-element.84.tags_ref) | copy-start | bytes 122884
  14.9 15.8 %copy-start.12 = (bf16[16,512]{1,0:T(8,128)(2,1)}, bf16[16,512]{1,0:T(8,128)(2,1)S(1)}, u32[]{:S(2)}) copy-start(bf16[16,512]{1,0:T(8,128)(2,1)S(1)} %collective-permute-done.3.left_ref) | copy-start | bytes 49156
  15.0 15.7 %copy-start.23 = (bf16[80,512]{1,0:T(8,128)(2,1)}, bf16[80,512]{1,0:T(8,128)(2,1)S(1)}, u32[]{:S(2)}) copy-start(bf16[80,512]{1,0:T(8,128)(2,1)S(1)} %get-tuple-element.77.own_ref) | copy-start | bytes 245764
  15.0 15.7 %collective-permute-start.5 = (bf16[112,512]{1,0:T(8,128)(2,1)S(1)}, bf16[112,512]{1,0:T(8,128)(2,1)S(1)}, u32[]{:S(2)}, u32[]{:S(2)}) collective-permute-start(bf16[112,512]{1,0:T(8,128)(2,1)S(1)} %get-tuple-element.78), channel_id=1, source_target_pairs={{0,8},{8,16},{16,24},{24,32},{32,40},{40,48},{48,56},{56,64},{64,7... | collective-permute-start | bytes 344072 | tf_op jit(solution)/shard_map/ppermute | solution.py:46
  16.3 15.1 %collective-permute-start.7 = (bf16[112,512]{1,0:T(8,128)(2,1)S(1)}, bf16[112,512]{1,0:T(8,128)(2,1)S(1)}, u32[]{:S(2)}, u32[]{:S(2)}) collective-permute-start(bf16[112,512]{1,0:T(8,128)(2,1)S(1)} %get-tuple-element.79), channel_id=1, source_target_pairs={{0,120},{8,0},{16,8},{24,16},{32,24},{40,32},{48,40},{56,48},{64,5... | collective-permute-start | bytes 344072 | tf_op jit(solution)/shard_map/ppermute | solution.py:46
  19.9 10.2 %collective-permute-start.6 = (bf16[80,512]{1,0:T(8,128)(2,1)S(1)}, bf16[80,512]{1,0:T(8,128)(2,1)S(1)}, u32[]{:S(2)}, u32[]{:S(2)}) collective-permute-start(bf16[80,512]{1,0:T(8,128)(2,1)S(1)} %get-tuple-element.77.own_ref), channel_id=1, source_target_pairs={{0,16},{8,24},{16,32},{24,40},{32,48},{40,56},{48,64},{56,72},{64,... | collective-permute-start | bytes 245768 | tf_op jit(solution)/shard_map/ppermute | solution.py:46
  19.9 23.4 %all-to-all-start = ((bf16[128,16,128]{2,1,0:T(8,128)(2,1)}), bf16[128,16,128]{2,1,0:T(8,128)(2,1)}, u32[]{:S(2)}, u32[]{:S(2)}) async-start(bf16[128,16,128]{2,1,0:T(8,128)(2,1)} %bitcast.10), calls=%async_computation | async-start | bytes 1048576 | tf_op jit(solution)/shard_map/all_to_all | solution.py:497
  30.1 18.1 %copy-start.5 = (bf16[16,20,512]{2,0,1:T(8,128)(2,1)S(1)}, bf16[16,20,512]{2,0,1:T(8,128)(2,1)}, u32[]{:S(2)}) copy-start(bf16[16,20,512]{2,0,1:T(8,128)(2,1)} %param.13) | copy-start | bytes 983044
  30.1 18.1 %copy-start.9 = (f32[2,512]{1,0:T(2,128)S(1)}, f32[2,512]{1,0:T(2,128)}, u32[]{:S(2)}) copy-start(f32[2,512]{1,0:T(2,128)} %eg_ref.5) | copy-start | bytes 12292
  32.1 0.9 copy-start.20
  33.0 0.9 copy-start.22
  33.9 0.9 copy-start.24
  35.6 12.6 %copy-start = (bf16[2,1536,512]{2,1,0:T(8,128)(2,1)S(1)}, bf16[2,1536,512]{2,1,0:T(8,128)(2,1)}, u32[]{:S(2)}) copy-start(bf16[2,1536,512]{2,1,0:T(8,128)(2,1)} %ei_ref.5) | copy-start | bytes 9437188
  37.0 20.2 %collective-permute-start.10 = (bf16[320,512]{1,0:T(8,128)(2,1)}, bf16[320,512]{1,0:T(8,128)(2,1)}, u32[]{:S(2)}, u32[]{:S(2)}) collective-permute-start(bf16[320,512]{1,0:T(8,128)(2,1)} %get-tuple-element.99.rest_0_), channel_id=1, source_target_pairs={{0,6},{1,7},{2,0},{3,1},{4,2},{5,3},{6,4},{7,5},{8,14},{9,15},{10,... | collective-permute-start | bytes 983048 | tf_op jit(solution)/shard_map/ppermute | solution.py:26
  40.3 17.0 %collective-permute-start.9 = (bf16[320,512]{1,0:T(8,128)(2,1)}, bf16[320,512]{1,0:T(8,128)(2,1)}, u32[]{:S(2)}, u32[]{:S(2)}) collective-permute-start(bf16[320,512]{1,0:T(8,128)(2,1)} %get-tuple-element.99.rest_0_), channel_id=1, source_target_pairs={{0,4},{1,5},{2,6},{3,7},{4,0},{5,1},{6,2},{7,3},{8,12},{9,13},{10,... | collective-permute-start | bytes 983048 | tf_op jit(solution)/shard_map/ppermute | solution.py:26
  40.3 17.9 %collective-permute-start.8 = (bf16[320,512]{1,0:T(8,128)(2,1)}, bf16[320,512]{1,0:T(8,128)(2,1)}, u32[]{:S(2)}, u32[]{:S(2)}) collective-permute-start(bf16[320,512]{1,0:T(8,128)(2,1)} %get-tuple-element.99.rest_0_), channel_id=1, source_target_pairs={{0,2},{1,3},{2,4},{3,5},{4,6},{5,7},{6,0},{7,1},{8,10},{9,11},{10,... | collective-permute-start | bytes 983048 | tf_op jit(solution)/shard_map/ppermute | solution.py:26
  43.3 5.0 %copy-start.1 = (bf16[2,512,512]{2,1,0:T(8,128)(2,1)S(1)}, bf16[2,512,512]{2,1,0:T(8,128)(2,1)}, u32[]{:S(2)}) copy-start(bf16[2,512,512]{2,1,0:T(8,128)(2,1)} %eo_ref.5) | copy-start | bytes 3145732
  48.3 1.5 %copy-start.6 = (bf16[16,20,6,512]{3,0,2,1:T(8,128)(2,1)S(1)}, bf16[16,20,6,512]{3,0,2,1:T(8,128)(2,1)}, u32[]{:S(2)}) copy-start(bf16[16,20,6,512]{3,0,2,1:T(8,128)(2,1)} %param.14) | copy-start | bytes 5898244
  51.4 10.5 %copy-start.2 = (bf16[2,1024,512]{2,1,0:T(8,128)(2,1)S(1)}, bf16[2,1024,512]{2,1,0:T(8,128)(2,1)}, u32[]{:S(2)}) copy-start(bf16[2,1024,512]{2,1,0:T(8,128)(2,1)} %ni_ref.3) | copy-start | bytes 6291460
  51.4 10.5 %copy-start.3 = (bf16[2,512,512]{2,1,0:T(8,128)(2,1)S(1)}, bf16[2,512,512]{2,1,0:T(8,128)(2,1)}, u32[]{:S(2)}) copy-start(bf16[2,512,512]{2,1,0:T(8,128)(2,1)} %no_ref.3) | copy-start | bytes 3145732
  51.4 10.5 %copy-start.8 = (bf16[160,512]{1,0:T(8,128)(2,1)S(1)}, bf16[160,512]{1,0:T(8,128)(2,1)}, u32[]{:S(2)}) copy-start(bf16[160,512]{1,0:T(8,128)(2,1)} %long_ref.1) | copy-start | bytes 491524
  51.4 10.5 %copy-start.17 = (f32[2,512]{1,0:T(2,128)S(1)}, f32[2,512]{1,0:T(2,128)}, u32[]{:S(2)}) copy-start(f32[2,512]{1,0:T(2,128)} %ng_ref.3) | copy-start | bytes 12292
  58.2 2.3 %collective-permute-start.11 = (bf16[320,512]{1,0:T(8,128)(2,1)}, bf16[320,512]{1,0:T(8,128)(2,1)S(1)}, u32[]{:S(2)}, u32[]{:S(2)}) collective-permute-start(bf16[320,512]{1,0:T(8,128)(2,1)} %get-tuple-element.99.rest_0_), channel_id=1, source_target_pairs={{0,1},{1,0},{2,3},{3,2},{4,5},{5,4},{6,7},{7,6},{8,9},{9,8},{10,11... | collective-permute-start | bytes 983048 | tf_op jit(solution)/shard_map/ppermute | solution.py:26
  59.0 1.9 %collective-permute-start.12 = (bf16[320,512]{1,0:T(8,128)(2,1)}, bf16[320,512]{1,0:T(8,128)(2,1)S(1)}, u32[]{:S(2)}, u32[]{:S(2)}) collective-permute-start(bf16[320,512]{1,0:T(8,128)(2,1)} %collective-permute-done.8.rest_1_), channel_id=1, source_target_pairs={{0,1},{1,0},{2,3},{3,2},{4,5},{5,4},{6,7},{7,6},{8,9},{9,8},{10,11... | collective-permute-start | bytes 983048 | tf_op jit(solution)/shard_map/ppermute | solution.py:26
  59.0 2.4 %collective-permute-start.13 = (bf16[320,512]{1,0:T(8,128)(2,1)}, bf16[320,512]{1,0:T(8,128)(2,1)S(1)}, u32[]{:S(2)}, u32[]{:S(2)}) collective-permute-start(bf16[320,512]{1,0:T(8,128)(2,1)} %collective-permute-done.9.rest_2_), channel_id=1, source_target_pairs={{0,1},{1,0},{2,3},{3,2},{4,5},{5,4},{6,7},{7,6},{8,9},{9,8},{10,11... | collective-permute-start | bytes 983048 | tf_op jit(solution)/shard_map/ppermute | solution.py:26
  59.5 2.4 %collective-permute-start.14 = (bf16[320,512]{1,0:T(8,128)(2,1)}, bf16[320,512]{1,0:T(8,128)(2,1)S(1)}, u32[]{:S(2)}, u32[]{:S(2)}) collective-permute-start(bf16[320,512]{1,0:T(8,128)(2,1)} %collective-permute-done.10.rest_3_), channel_id=1, source_target_pairs={{0,1},{1,0},{2,3},{3,2},{4,5},{5,4},{6,7},{7,6},{8,9},{9,8},{10,11... | collective-permute-start | bytes 983048 | tf_op jit(solution)/shard_map/ppermute | solution.py:26
  67.1 7.1 %collective-permute-start.17 = (bf16[20,512]{1,0:T(8,128)(2,1)S(1)}, bf16[20,512]{1,0:T(8,128)(2,1)S(1)}, u32[]{:S(2)}, u32[]{:S(2)}) collective-permute-start(bf16[20,512]{1,0:T(8,128)(2,1)S(1)} %get-tuple-element.103.own_ref), channel_id=1, source_target_pairs={{0,96},{8,104},{16,112},{24,120},{32,0},{40,8},{48,16},{56,24},{64... | collective-permute-start | bytes 61448 | tf_op jit(solution)/shard_map/ppermute | solution.py:46
  70.0 4.3 %collective-permute-start.16 = (bf16[20,512]{1,0:T(8,128)(2,1)S(1)}, bf16[20,512]{1,0:T(8,128)(2,1)S(1)}, u32[]{:S(2)}, u32[]{:S(2)}) collective-permute-start(bf16[20,512]{1,0:T(8,128)(2,1)S(1)} %get-tuple-element.103.own_ref), channel_id=1, source_target_pairs={{0,64},{8,72},{16,80},{24,88},{32,96},{40,104},{48,112},{56,120},{... | collective-permute-start | bytes 61448 | tf_op jit(solution)/shard_map/ppermute | solution.py:46
  70.4 4.0 %collective-permute-start.15 = (bf16[20,512]{1,0:T(8,128)(2,1)S(1)}, bf16[20,512]{1,0:T(8,128)(2,1)S(1)}, u32[]{:S(2)}, u32[]{:S(2)}) collective-permute-start(bf16[20,512]{1,0:T(8,128)(2,1)S(1)} %get-tuple-element.103.own_ref), channel_id=1, source_target_pairs={{0,32},{8,40},{16,48},{24,56},{32,64},{40,72},{48,80},{56,88},{64,... | collective-permute-start | bytes 61448 | tf_op jit(solution)/shard_map/ppermute | solution.py:46
  71.1 3.2 %collective-permute-start.19 = (bf16[16,512]{1,0:T(8,128)(2,1)S(1)}, bf16[16,512]{1,0:T(8,128)(2,1)S(1)}, u32[]{:S(2)}, u32[]{:S(2)}) collective-permute-start(bf16[16,512]{1,0:T(8,128)(2,1)S(1)} %get-tuple-element.129), channel_id=1, source_target_pairs={{0,7},{1,0},{2,1},{3,2},{4,3},{5,4},{6,5},{7,6},{8,15},{9,8},{10,9... | collective-permute-start | bytes 49160 | tf_op jit(solution)/shard_map/ppermute | solution.py:46
  72.3 1.9 %collective-permute-start.18 = (bf16[16,512]{1,0:T(8,128)(2,1)S(1)}, bf16[16,512]{1,0:T(8,128)(2,1)S(1)}, u32[]{:S(2)}, u32[]{:S(2)}) collective-permute-start(bf16[16,512]{1,0:T(8,128)(2,1)S(1)} %get-tuple-element.130), channel_id=1, source_target_pairs={{0,1},{1,2},{2,3},{3,4},{4,5},{5,6},{6,7},{7,0},{8,9},{9,10},{10,1... | collective-permute-start | bytes 49160 | tf_op jit(solution)/shard_map/ppermute | solution.py:46
  74.5 11.8 %collective-permute-start.20 = (bf16[112,512]{1,0:T(8,128)(2,1)S(1)}, bf16[112,512]{1,0:T(8,128)(2,1)S(1)}, u32[]{:S(2)}, u32[]{:S(2)}) collective-permute-start(bf16[112,512]{1,0:T(8,128)(2,1)S(1)} %get-tuple-element.108), channel_id=1, source_target_pairs={{0,8},{8,16},{16,24},{24,32},{32,40},{40,48},{48,56},{56,64},{64,7... | collective-permute-start | bytes 344072 | tf_op jit(solution)/shard_map/ppermute | solution.py:46
  75.9 10.4 %collective-permute-start.22 = (bf16[112,512]{1,0:T(8,128)(2,1)S(1)}, bf16[112,512]{1,0:T(8,128)(2,1)S(1)}, u32[]{:S(2)}, u32[]{:S(2)}) collective-permute-start(bf16[112,512]{1,0:T(8,128)(2,1)S(1)} %get-tuple-element.109), channel_id=1, source_target_pairs={{0,120},{8,0},{16,8},{24,16},{32,24},{40,32},{48,40},{56,48},{64,5... | collective-permute-start | bytes 344072 | tf_op jit(solution)/shard_map/ppermute | solution.py:46
  79.3 6.9 %collective-permute-start.21 = (bf16[80,512]{1,0:T(8,128)(2,1)S(1)}, bf16[80,512]{1,0:T(8,128)(2,1)S(1)}, u32[]{:S(2)}, u32[]{:S(2)}) collective-permute-start(bf16[80,512]{1,0:T(8,128)(2,1)S(1)} %get-tuple-element.107.own_ref), channel_id=1, source_target_pairs={{0,16},{8,24},{16,32},{24,40},{32,48},{40,56},{48,64},{56,72},{64,... | collective-permute-start | bytes 245768 | tf_op jit(solution)/shard_map/ppermute | solution.py:46
  86.3 11.3 %collective-permute-start.25 = (bf16[320,512]{1,0:T(8,128)(2,1)S(1)}, bf16[320,512]{1,0:T(8,128)(2,1)S(1)}, u32[]{:S(2)}, u32[]{:S(2)}) collective-permute-start(bf16[320,512]{1,0:T(8,128)(2,1)S(1)} %get-tuple-element.122.rest_0_), channel_id=1, source_target_pairs={{0,6},{1,7},{2,0},{3,1},{4,2},{5,3},{6,4},{7,5},{8,14},{9,15},{10,... | collective-permute-start | bytes 983048 | tf_op jit(solution)/shard_map/ppermute | solution.py:26
  88.5 9.1 %collective-permute-start.24 = (bf16[320,512]{1,0:T(8,128)(2,1)S(1)}, bf16[320,512]{1,0:T(8,128)(2,1)S(1)}, u32[]{:S(2)}, u32[]{:S(2)}) collective-permute-start(bf16[320,512]{1,0:T(8,128)(2,1)S(1)} %get-tuple-element.122.rest_0_), channel_id=1, source_target_pairs={{0,4},{1,5},{2,6},{3,7},{4,0},{5,1},{6,2},{7,3},{8,12},{9,13},{10,... | collective-permute-start | bytes 983048 | tf_op jit(solution)/shard_map/ppermute | solution.py:26
  88.5 17.5 %collective-permute-start.23 = (bf16[320,512]{1,0:T(8,128)(2,1)S(1)}, bf16[320,512]{1,0:T(8,128)(2,1)S(1)}, u32[]{:S(2)}, u32[]{:S(2)}) collective-permute-start(bf16[320,512]{1,0:T(8,128)(2,1)S(1)} %get-tuple-element.122.rest_0_), channel_id=1, source_target_pairs={{0,2},{1,3},{2,4},{3,5},{4,6},{5,7},{6,0},{7,1},{8,10},{9,11},{10,... | collective-permute-start | bytes 983048 | tf_op jit(solution)/shard_map/ppermute | solution.py:26
  106.0 2.1 %collective-permute-start.26 = (bf16[320,512]{1,0:T(8,128)(2,1)S(1)}, bf16[320,512]{1,0:T(8,128)(2,1)S(1)}, u32[]{:S(2)}, u32[]{:S(2)}) collective-permute-start(bf16[320,512]{1,0:T(8,128)(2,1)S(1)} %get-tuple-element.122.rest_0_), channel_id=1, source_target_pairs={{0,1},{1,0},{2,3},{3,2},{4,5},{5,4},{6,7},{7,6},{8,9},{9,8},{10,11... | collective-permute-start | bytes 983048 | tf_op jit(solution)/shard_map/ppermute | solution.py:26
  106.9 1.7 %collective-permute-start.27 = (bf16[320,512]{1,0:T(8,128)(2,1)S(1)}, bf16[320,512]{1,0:T(8,128)(2,1)S(1)}, u32[]{:S(2)}, u32[]{:S(2)}) collective-permute-start(bf16[320,512]{1,0:T(8,128)(2,1)S(1)} %collective-permute-done.23.rest_1_), channel_id=1, source_target_pairs={{0,1},{1,0},{2,3},{3,2},{4,5},{5,4},{6,7},{7,6},{8,9},{9,8},{10,11... | collective-permute-start | bytes 983048 | tf_op jit(solution)/shard_map/ppermute | solution.py:26
  106.9 2.2 %collective-permute-start.28 = (bf16[320,512]{1,0:T(8,128)(2,1)S(1)}, bf16[320,512]{1,0:T(8,128)(2,1)S(1)}, u32[]{:S(2)}, u32[]{:S(2)}) collective-permute-start(bf16[320,512]{1,0:T(8,128)(2,1)S(1)} %collective-permute-done.24.rest_2_), channel_id=1, source_target_pairs={{0,1},{1,0},{2,3},{3,2},{4,5},{5,4},{6,7},{7,6},{8,9},{9,8},{10,11... | collective-permute-start | bytes 983048 | tf_op jit(solution)/shard_map/ppermute | solution.py:26
  107.4 2.2 %collective-permute-start.29 = (bf16[320,512]{1,0:T(8,128)(2,1)S(1)}, bf16[320,512]{1,0:T(8,128)(2,1)S(1)}, u32[]{:S(2)}, u32[]{:S(2)}) collective-permute-start(bf16[320,512]{1,0:T(8,128)(2,1)S(1)} %collective-permute-done.25.rest_3_), channel_id=1, source_target_pairs={{0,1},{1,0},{2,3},{3,2},{4,5},{5,4},{6,7},{7,6},{8,9},{9,8},{10,11... | collective-permute-start | bytes 983048 | tf_op jit(solution)/shard_map/ppermute | solution.py:26
  (12 other events, 8.7 us)

commit v6 on v5

--- a/solution.py
+++ b/solution.py
@@ -130,7 +130,7 @@
         body,
         name=f"fine{layer}",
         out_shape=(
-            jax.ShapeDtypeStruct(fine.shape, jnp.bfloat16),
+            pltpu.HBM(fine.shape, jnp.bfloat16),
             jax.ShapeDtypeStruct((nodes, features), jnp.float32),
         ),
         grid=(steps,),
@@ -149,7 +149,7 @@
             pltpu.VMEM((256, hidden), jnp.bfloat16),
         ],
         compiler_params=pltpu.CompilerParams(dimension_semantics=("arbitrary",), vmem_limit_bytes=14 * MIB),
-    )(fine, picks, latents, left, right, sides, inner, outer, gain)
+    )(in_hbm(fine), picks, latents, left, right, sides, inner, outer, gain)
 
 
 def pick(index, width):
@@ -164,10 +164,6 @@
 def decode(tags, at):
     numbers = tags.astype(jnp.int32)
     return jnp.where(numbers[:, 4:5] > 0, numbers[:, at : at + 1] * LOW + numbers[:, at + 1 : at + 2], -1)
-
-
-def blocks_of(*arrays):
-    return [pl.BlockSpec(a.shape, lambda i, n=len(a.shape): (0,) * n) for a in arrays]
 
 
 def send_rows(both, own_ref, last_ref, first_ref):
@@ -205,25 +201,47 @@
     )(own, *fars, left, right, last, first)
 
 
-def join_near(own, up, two, down):
+def in_hbm(values):
+    return pltpu.with_memory_space_constraint(values, pltpu.HBM)
+
+
+def fetch(pairs, sems):
+    copies = [pltpu.make_async_copy(here, there, sems.at[i]) for i, (here, there) in enumerate(pairs)]
+    for copy in copies:
+        copy.start()
+    for copy in copies:
+        copy.wait()
+
+
+def join_near(layer, own, up, two, down):
     each, features = own.shape
-
-    def body(own_ref, up_ref, two_ref, down_ref, joined_ref, sides_ref):
-        for at, ref in enumerate((own_ref, up_ref, two_ref, down_ref)):
-            joined_ref[at * each : (at + 1) * each, :] = ref[:each, :]
-        sides_ref[: BELOW - ABOVE, :] = up_ref[each:, :]
-        sides_ref[BELOW - ABOVE :, :] = down_ref[each:, :]
-
-    held = pl.BlockSpec(memory_space=pltpu.VMEM)
+    side = BELOW - ABOVE
+
+    def body(own_ref, up_ref, two_ref, down_ref, joined_ref, sides_ref, sems):
+        part = lambda at: joined_ref.at[pl.ds(at * each, each), :]
+        fetch(
+            [
+                (own_ref, part(0)),
+                (up_ref.at[pl.ds(0, each), :], part(1)),
+                (two_ref, part(2)),
+                (down_ref.at[pl.ds(0, each), :], part(3)),
+                (up_ref.at[pl.ds(each, side), :], sides_ref.at[pl.ds(0, side), :]),
+                (down_ref.at[pl.ds(each, side), :], sides_ref.at[pl.ds(side, side), :]),
+            ],
+            sems,
+        )
+
+    away = pl.BlockSpec(memory_space=pltpu.HBM)
     return pl.pallas_call(
         body,
         name="join_near",
         cost_estimate=pl.CostEstimate(flops=3_000_000_000, bytes_accessed=0, transcendentals=0),
-        out_shape=tuple(jax.ShapeDtypeStruct((n, features), jnp.bfloat16) for n in (4 * each, 2 * (BELOW - ABOVE))),
-        in_specs=[held] * 4,
-        out_specs=(held,) * 2,
+        out_shape=tuple(jax.ShapeDtypeStruct((n, features), jnp.bfloat16) for n in (4 * each, 2 * side)),
+        in_specs=[away] * 4,
+        out_specs=(away,) * 2,
+        scratch_shapes=[pltpu.SemaphoreType.DMA((6,))],
         compiler_params=pltpu.CompilerParams(vmem_limit_bytes=2 * MIB),
-    )(own, up, two, down)
+    )(*(map(in_hbm, (own, up, two, down)) if layer == 0 else (own, up, two, down)))
 
 
 def coarse_start(coarse_slots, latents, rows, columns):
@@ -231,7 +249,8 @@
     nodes, features = latents.shape
     size = count + 2 * columns
 
-    def body(slots_ref, latents_ref, own_ref, last_ref, first_ref, choose_ref):
+    def body(slots_away, latents_away, own_ref, last_ref, first_ref, left_ref, right_ref, choose_ref, slots_ref, latents_ref, sems):
+        fetch([(slots_away, slots_ref), (latents_away, latents_ref)], sems)
         slot = slots_ref[...]
         row = jnp.floor((slot.astype(jnp.float32) + 0.5) * (1.0 / columns)).astype(jnp.int32)
         at = (slot - row * columns) * rows + row
@@ -246,20 +265,28 @@
         choose = (rows_to_columns(same, place) + edge.astype(jnp.float32)).astype(jnp.bfloat16)
         choose_ref[...] = choose
         send_rows(dot(choose, latents_ref[...]), own_ref, last_ref, first_ref)
+        left_ref[...] = latents_ref[:rows, :]
+        right_ref[...] = latents_ref[-rows:, :]
 
     shapes = (
-        *(jax.ShapeDtypeStruct((n, features), jnp.bfloat16) for n in (count, columns, columns)),
+        *(jax.ShapeDtypeStruct((n, features), jnp.bfloat16) for n in (count, columns, columns, rows, rows)),
         jax.ShapeDtypeStruct((size, nodes), jnp.bfloat16),
     )
+    away = pl.BlockSpec(memory_space=pltpu.HBM)
+    held = pl.BlockSpec(memory_space=pltpu.VMEM)
     return pl.pallas_call(
         body,
         name="coarse_start",
         out_shape=shapes,
-        grid=(1,),
-        in_specs=blocks_of(coarse_slots, latents),
-        out_specs=blocks_of(*shapes),
+        in_specs=[away] * 2,
+        out_specs=(held,) * len(shapes),
+        scratch_shapes=[
+            pltpu.VMEM(coarse_slots.shape, jnp.int32),
+            pltpu.VMEM(latents.shape, jnp.bfloat16),
+            pltpu.SemaphoreType.DMA((2,)),
+        ],
         compiler_params=pltpu.CompilerParams(vmem_limit_bytes=4 * MIB),
-    )(coarse_slots, latents)
+    )(*map(in_hbm, (coarse_slots, latents)))
 
 
 def pack_edges(long_edges, senders, receivers, me, coarse_count, devices):
@@ -267,7 +294,8 @@
     blocks = features // TAGS
     slots = devices * CAP
 
-    def body(me_ref, long_ref, send_ref, recv_ref, sent_ref, mine_ref, wide):
+    def body(me_ref, long_away, send_away, recv_away, sent_ref, mine_ref, wide, long_ref, send_ref, recv_ref, sems):
+        fetch([(long_away, long_ref), (send_away, send_ref), (recv_away, recv_ref)], sems)
         send, recv = send_ref[...], recv_ref[...]
         _, owner = table_row(0, 0, recv, coarse_count)
         here = (lax.shift_right_logical(me_ref[0], 3), me_ref[0] & 7)
@@ -309,23 +337,27 @@
         body,
         name="pack_edges",
         out_shape=shapes,
-        grid=(1,),
         cost_estimate=pl.CostEstimate(flops=12_000_000_000, bytes_accessed=0, transcendentals=0),
-        in_specs=[pl.BlockSpec(memory_space=pltpu.SMEM)] + blocks_of(long_edges, senders, receivers),
-        out_specs=blocks_of(*shapes),
-        scratch_shapes=[pltpu.VMEM((devices * 16, TAGS), jnp.float32)],
+        in_specs=[pl.BlockSpec(memory_space=pltpu.SMEM)] + [pl.BlockSpec(memory_space=pltpu.HBM)] * 3,
+        out_specs=(pl.BlockSpec(memory_space=pltpu.VMEM),) * 2,
+        scratch_shapes=[
+            pltpu.VMEM((devices * 16, TAGS), jnp.float32),
+            pltpu.VMEM(long_edges.shape, jnp.bfloat16),
+            pltpu.VMEM(senders.shape, jnp.int32),
+            pltpu.VMEM(receivers.shape, jnp.int32),
+            pltpu.SemaphoreType.DMA((3,)),
+        ],
         compiler_params=pltpu.CompilerParams(vmem_limit_bytes=8 * MIB),
-    )(me, long_edges, senders, receivers)
-
-
-def unpack_edges(arrived, own_tags, choose, features, table_rows, coarse_count):
+    )(me, *map(in_hbm, (long_edges, senders, receivers)))
+
+
+def unpack_edges(arrived, choose, features, table_rows, coarse_count):
     devices = arrived.shape[0] // 16
     blocks = features // TAGS
     slots = devices * CAP
-    count = own_tags.shape[0]
     nodes = choose.shape[1]
 
-    def body(arrived_ref, tags_ref, choose_ref, rows_ref, send_ref, recv_ref, adds_ref, wide):
+    def body(arrived_ref, choose_ref, rows_ref, send_ref, recv_ref, adds_ref, wide):
         wide[...] = arrived_ref[...].astype(jnp.float32)
         for j in range(CAP):
             part = slice(j * devices, (j + 1) * devices)
@@ -335,9 +367,6 @@
             tags = wide[pl.ds(CAP * blocks + j, devices, stride=16), :]
             send_ref[part, :] = pick(decode(tags, 0), table_rows)
             recv_ref[part, :] = pick(decode(tags, 2), TAGS)
-        mine = tags_ref[...].astype(jnp.float32)
-        send_ref[slots : slots + count, :] = pick(decode(mine, 0), table_rows)
-        send_ref[slots + count :, :] = pick(decode(mine, 2), table_rows)
         here = recv_ref[:, :coarse_count]
         place = lax.dot_general(
             choose_ref[:coarse_count, :], here, (((0,), (1,)), ((), ())), preferred_element_type=jnp.float32
@@ -350,15 +379,15 @@
         name="unpack_edges",
         out_shape=(
             jax.ShapeDtypeStruct((slots, features), jnp.bfloat16),
-            jax.ShapeDtypeStruct((slots + 2 * count, table_rows), jnp.bfloat16),
+            jax.ShapeDtypeStruct((slots, table_rows), jnp.bfloat16),
             jax.ShapeDtypeStruct((slots, TAGS), jnp.bfloat16),
             jax.ShapeDtypeStruct((nodes, slots), jnp.bfloat16),
         ),
-        in_specs=[held] * 3,
+        in_specs=[held] * 2,
         out_specs=(held,) * 4,
         scratch_shapes=[pltpu.VMEM(arrived.shape, jnp.float32)],
         compiler_params=pltpu.CompilerParams(vmem_limit_bytes=8 * MIB),
-    )(arrived, own_tags, choose)
+    )(arrived, choose)
 
 
 def long_step(before, sent, got, inner_ref, outer_ref, gain_ref, layer):
@@ -400,7 +429,7 @@
             outs[0][...] = after[slots:]
             after = after[:slots]
         else:
-            sent = dot(sends_ref[:slots, :], table[...]).astype(jnp.bfloat16)
+            sent = dot(sends_ref[...], table[...]).astype(jnp.bfloat16)
             after = long_step(long_ref[...], sent, got, ei_ref, eo_ref, eg_ref, layer)
             outs[0][...] = after
         incoming = (sum_ref[...] + dot(adds_ref[...], after)).astype(jnp.bfloat16)
@@ -412,12 +441,15 @@
         next_ref[...] = new
         if not last:
             send_rows(dot(choose_ref[...], new), *outs[1:4])
-
-    held = pl.BlockSpec(memory_space=pltpu.VMEM)
-    away = pl.BlockSpec(memory_space=pl.ANY)
+            outs[5][...] = new[:rows]
+            outs[6][...] = new[-rows:]
+
+    held = pl.BlockSpec(memory_space=pltpu.VMEM)
+    away = pl.BlockSpec(memory_space=pltpu.HBM)
     table_shape = (table_rows, features)
     side = (choose.shape[0] - coarse_count) // 2
-    kept = (both - slots,) if last else (slots, coarse_count, side, side, table_rows)
+    rows = nodes // side
+    kept = (both - slots,) if last else (slots, coarse_count, side, side, table_rows, rows, rows)
     shapes = [jax.ShapeDtypeStruct((n, features), jnp.bfloat16) for n in (nodes, *kept)]
 
     return pl.pallas_call(
@@ -437,22 +469,30 @@
       edge_inner, edge_outer, edge_gain, node_inner, node_outer, node_gain, *pieces)
 
 
-def own_layer(layer, long_rows, sends, table, edge_inner, edge_outer, edge_gain):
+def own_layer(layer, long_rows, tags, sends, table, edge_inner, edge_outer, edge_gain):
     count = long_rows.shape[0]
-
-    def body(long_ref, sends_ref, table_ref, ei_ref, eo_ref, eg_ref, next_ref):
-        picked = dot(sends_ref[-2 * count :, :], table_ref[...]).astype(jnp.bfloat16)
+    slots, rows = sends.shape
+
+    def body(long_ref, tags_ref, sends_ref, table_ref, ei_ref, eo_ref, eg_ref, next_ref, all_ref):
+        mine = tags_ref[...].astype(jnp.float32)
+        all_ref[:slots, :] = sends_ref[...]
+        all_ref[slots : slots + count, :] = pick(decode(mine, 0), rows)
+        all_ref[slots + count :, :] = pick(decode(mine, 2), rows)
+        picked = dot(all_ref[slots:, :], table_ref[...]).astype(jnp.bfloat16)
         next_ref[...] = long_step(long_ref[...], picked[:count], picked[count:], ei_ref, eo_ref, eg_ref, layer)
 
     held = pl.BlockSpec(memory_space=pltpu.VMEM)
     return pl.pallas_call(
         body,
         name=f"own{layer}",
-        out_shape=jax.ShapeDtypeStruct(long_rows.shape, jnp.bfloat16),
-        in_specs=[held] * 6,
-        out_specs=held,
+        out_shape=(
+            jax.ShapeDtypeStruct(long_rows.shape, jnp.bfloat16),
+            jax.ShapeDtypeStruct((slots + 2 * count, rows), jnp.bfloat16),
+        ),
+        in_specs=[held] * 7,
+        out_specs=(held, held),
         compiler_params=pltpu.CompilerParams(vmem_limit_bytes=8 * MIB),
-    )(long_rows, sends, table, edge_inner, edge_outer, edge_gain)
+    )(long_rows, tags, sends, table, edge_inner, edge_outer, edge_gain)
 
 
 def shards(
@@ -479,7 +519,7 @@
 
     latents = node_latents.transpose(1, 0, 2).reshape(nodes, features)
     fine = fine_edges.transpose(1, 2, 0, 3).reshape(nodes * degree, features)
-    own, last_row, first_row, choose = coarse_start(coarse_slots[None, :], latents, rows, columns)
+    own, last_row, first_row, to_left, to_right, choose = coarse_start(coarse_slots[None, :], latents, rows, columns)
     long_edges, own = tie(long_edges, own)
     own_rows = long_edges
     me = lax.axis_index(AXES).reshape(1)
@@ -487,33 +527,33 @@
     for layer in range(layers):
         last = layer == layers - 1
         fars = [along(own, "px", 4 * s) for s in (1, 2, 3)]
-        left = along(latents[-rows:], "py", 1)
-        right = along(latents[:rows], "py", -1)
+        left = along(to_right, "py", 1)
+        right = along(to_left, "py", -1)
         if layer == 0:
             *fars, left, right, payload = tie(*fars, left, right, payload)
         joined, up, down = join_far(own, fars, left, right, last_row, first_row)
         if layer == 0:
             packed = payload.reshape(devices, 16, TAGS)
             arrived = lax.all_to_all(packed, AXES, split_axis=0, concat_axis=0, tiled=True).reshape(payload.shape)
+        two = along(joined, "px", 2)
         up = along(up, "px", 1)
         down = along(down, "px", -1)
-        two = along(joined, "px", 2)
-        joined, sides = join_near(joined, up, two, down)
+        joined, sides = join_near(layer, joined, up, two, down)
         joined, sides, own_rows = tie(joined, sides, own_rows)
         pieces = [joined] + [shift(joined, Z, s) for s in (1, 2, 3)]
         if layer == 0:
             table_rows = 2 * len(pieces) * joined.shape[0]
-            long_rows, sends, recvs, adds = unpack_edges(arrived, own_tags, choose, features, table_rows, coarse_count)
+            long_rows, sends, recvs, adds = unpack_edges(arrived, choose, features, table_rows, coarse_count)
             left, long_rows, neighbours = tie(left, long_rows, neighbours)
             picks = selection(neighbours)
         else:
-            own_rows = own_layer(layer - 1, own_rows, sends, table, edge_inner, edge_outer, edge_gain)
+            own_rows, sends = own_layer(layer - 1, own_rows, own_tags, sends, table, edge_inner, edge_outer, edge_gain)
         fine, fine_sum = fine_layer(
             layer, fine, picks, latents, left, right, sides, edge_inner, edge_outer, edge_gain, rows
         )
-        first, *others, fine_sum, own_rows, long_rows = tie(*pieces, fine_sum, own_rows, long_rows)
-        pieces = [first] + others
-        pieces = pieces + [shift(piece, CORE, 1) for piece in pieces]
+        swapped = shift(joined, CORE, 1)
+        *others, fine_sum, own_rows, long_rows = tie(*pieces[1:], fine_sum, own_rows, long_rows)
+        pieces = [joined] + others + [swapped] + [shift(piece, CORE, 1) for piece in others]
         latents, *rest = coarse_layer(
             layer, long_rows, own_rows, sends, recvs, adds, choose, pieces, latents, fine_sum,
             edge_inner, edge_outer, edge_gain, node_inner, node_outer, node_gain, coarse_count, last,
@@ -521,7 +561,7 @@
         if last:
             own_rows = rest[0]
         else:
-            long_rows, own, last_row, first_row, table = rest
+            long_rows, own, last_row, first_row, table, to_left, to_right = rest
     return (
         latents.reshape(columns, rows, features).transpose(1, 0, 2),
         fine.reshape(columns, degree, rows, features).transpose(2, 0, 1, 3),

time: 116 us -> 123 us (1.060)
  Pallas kernels: 31.1 us -> 47.4 us
  local copies, waits for them, and re-layouts: 15.5 us -> 4.25 us
  starting transfers between devices: 43 us -> 47 us
  waiting for transfers between devices: 24.5 us -> 22.3 us
    pallas_call x2, Pallas kernels: 0.78 us -> 11.6 us  [join_near(): pl.pallas_call(body, name='join_near', cost_estimate=pl.CostEstimate(flop...]
    unnamed x58 -> x36, local copies, waits for them, and re-layouts: 14.8 us -> 4.25 us
    pallas_call x5, Pallas kernels: 16.2 us -> 21.9 us  [the longest x2 15.8 us: fine_layer(): pl.pallas_call(body, name=f'fine{layer}', out_shape=(pltpu.HBM(fine.shape...]
    ppermute x14, starting transfers between devices: 9.73 us -> 13.9 us  [shift(): return lax.ppermute(values, 'py', pairs)]
    all_to_all x1, waiting for transfers between devices: 2.14 us -> 0.01 us  [shards(): lax.all_to_all(packed, AXES, split_axis=0, concat_axis=0, tiled=True)]
    ppermute x14, waiting for transfers between devices: 13.8 us -> 12.6 us  [shift(): return lax.ppermute(values, 'py', pairs)]
  transfers between devices with their start and end apart: 31 -> 31, of which waited for: 14 -> 13; matrix products, arithmetic and copies ran while one was open for 1% -> 0% of each run, Pallas kernels for 17% -> 28%
where the time goes in v6:
time: 123 us; the launch traced here: 122 us
  Pallas kernels  47.4 us (39%)
  starting transfers between devices  47 us (38%)
  waiting for transfers between devices  22.3 us (18%)
  local copies, waits for them, and re-layouts  4.25 us (3%)
    ppermute x16, starting transfers between devices, along(): lax.ppermute(values, axis, [(i, (i + step) % count) for i in range(count)])  22.4 us
    pallas_call x2, Pallas kernels, fine_layer(): pl.pallas_call(body, name=f'fine{layer}', out_shape=(pltpu.HBM(fine.shape...  15.8 us
    ppermute x14, starting transfers between devices, shift(): return lax.ppermute(values, 'py', pairs)  13.9 us
    ppermute x14, waiting for transfers between devices, shift(): return lax.ppermute(values, 'py', pairs)  12.6 us
    pallas_call x2, Pallas kernels, join_near(): pl.pallas_call(body, name='join_near', cost_estimate=pl.CostEstimate(flop...  11.6 us
    pallas_call x2, Pallas kernels, coarse_layer(): pl.pallas_call(body, name=f'coarse{layer}', out_shape=tuple(shapes), in_s...  11 us
    all_to_all x1, starting transfers between devices, shards(): lax.all_to_all(packed, AXES, split_axis=0, concat_axis=0, tiled=True)  10.7 us
    ppermute x16, waiting for transfers between devices, along(): lax.ppermute(values, axis, [(i, (i + step) % count) for i in range(count)])  9.76 us
  transfers between devices with their start and end apart: 31, of which 13 were waited for; matrix products, arithmetic and copies ran while one was open for 0% of the time, Pallas kernels for 28%

profile of v6, /device:TPU:1, one launch (start us, length us, event | category | flops | bytes accessed | tf_op | source)
XLA Modules:
  0.0 122.0 jit_solution(17319758795489355697)
XLA Ops:
  0.6 1.3 %coarse_start.1 = (bf16[20,512]{1,0:T(8,128)(2,1)S(1)}, bf16[20,512]{1,0:T(8,128)(2,1)S(1)}, bf16[20,512]{1,0:T(8,128)(2,1)S(1)}, bf16[16,512]{1,0:T(8,128)(2,1)...) custom-call(s32[1,20]{1,0:T(1,128)} %bitcast.24, bf16[320,512]{1,0:T(8,128)(2,1)} %bitcast.19), custom_call_target="tpu_custom_call" | custom-call | tf_op jit(solution)/shard_map/coarse_start/pallas_call | solution.py:277
  2.0 3.6 %collective-permute-start.2 = (bf16[20,512]{1,0:T(8,128)(2,1)S(1)}, bf16[20,512]{1,0:T(8,128)(2,1)S(1)}, u32[]{:S(2)}, u32[]{:S(2)}) collective-permute-start(bf16[20,512]{1,0:T(8,128)(2,1)S(1)} %get-tuple-element.71.own_ref), channel_id=1, source_target_pairs={{0,96},{8,104},{16,112},{24,120},{32,0},{40,8},{48,16},{56,24},{64... | collective-permute-start | bytes 61448 | tf_op jit(solution)/shard_map/ppermute | solution.py:46
  6.0 0.7 collective-permute-start
  6.7 3.0 %collective-permute-start.3 = (bf16[16,512]{1,0:T(8,128)(2,1)S(1)}, bf16[16,512]{1,0:T(8,128)(2,1)S(1)}, u32[]{:S(2)}, u32[]{:S(2)}) collective-permute-start(bf16[16,512]{1,0:T(8,128)(2,1)S(1)} %get-tuple-element.72), channel_id=1, source_target_pairs={{0,1},{1,2},{2,3},{3,4},{4,5},{5,6},{6,7},{7,0},{8,9},{9,10},{10,1... | collective-permute-start | bytes 49160 | tf_op jit(solution)/shard_map/ppermute | solution.py:46
  9.7 2.5 %pack_edges.1 = (bf16[2048,128]{1,0:T(8,128)(2,1)}, bf16[160,128]{1,0:T(8,128)(2,1)S(1)}) custom-call(s32[1]{0:T(128)} %bitcast.3.me_ref, bf16[160,512]{1,0:T(8,128)(2,1)} %long_ref, s32[1,160]{1,0:T(1,128)} %bitcast.27, s32[1,160]{1,0:T(1,128)} %bitcast.28), custom_call_target="tpu_custom_call" | custom-call | flops 12000000000 | tf_op jit(solution)/shard_map/pack_edges/pallas_call | solution.py:336
  12.3 0.6 collective-permute-done.4.right_ref
  12.9 1.3 %collective-permute-start.5 = (bf16[112,512]{1,0:T(8,128)(2,1)S(1)}, bf16[112,512]{1,0:T(8,128)(2,1)S(1)}, u32[]{:S(2)}, u32[]{:S(2)}) collective-permute-start(bf16[112,512]{1,0:T(8,128)(2,1)S(1)} %get-tuple-element.84), channel_id=1, source_target_pairs={{0,8},{8,16},{16,24},{24,32},{32,40},{40,48},{48,56},{56,64},{64,7... | collective-permute-start | bytes 344072 | tf_op jit(solution)/shard_map/ppermute | solution.py:46
  14.2 3.6 %collective-permute-start.7 = (bf16[112,512]{1,0:T(8,128)(2,1)S(1)}, bf16[112,512]{1,0:T(8,128)(2,1)}, u32[]{:S(2)}, u32[]{:S(2)}) collective-permute-start(bf16[112,512]{1,0:T(8,128)(2,1)S(1)} %get-tuple-element.85), channel_id=1, source_target_pairs={{0,120},{8,0},{16,8},{24,16},{32,24},{40,32},{48,40},{56,48},{64,5... | collective-permute-start | bytes 344072 | tf_op jit(solution)/shard_map/ppermute | solution.py:46
  17.8 10.7 %all-to-all-start = ((bf16[128,16,128]{2,1,0:T(8,128)(2,1)}), bf16[128,16,128]{2,1,0:T(8,128)(2,1)}, u32[]{:S(2)}, u32[]{:S(2)}) async-start(bf16[128,16,128]{2,1,0:T(8,128)(2,1)} %bitcast.8), calls=%async_computation | async-start | bytes 1048576 | tf_op jit(solution)/shard_map/all_to_all | solution.py:537
  28.5 0.6 copy-done.17
  29.1 0.6 copy-done.16
  29.8 11.1 %join_near.2 = (bf16[320,512]{1,0:T(8,128)(2,1)}, bf16[64,512]{1,0:T(8,128)(2,1)S(1)}) custom-call(bf16[80,512]{1,0:T(8,128)(2,1)} %copy-done.15, bf16[112,512]{1,0:T(8,128)(2,1)} %copy-done.16, bf16[80,512]{1,0:T(8,128)(2,1)} %copy-done.17, bf16[112,512]{1,0:T(8,128)(2,1)} %collective-permute-done.7.down_ref), custom_call_target="tpu_custom_call" | custom-call | flops 3000000000 | tf_op jit(solution)/shard_map/join_near/pallas_call | solution.py:235
  40.9 0.6 copy-done.7
  41.5 3.3 %collective-permute-start.10 = (bf16[320,512]{1,0:T(8,128)(2,1)}, bf16[320,512]{1,0:T(8,128)(2,1)}, u32[]{:S(2)}, u32[]{:S(2)}) collective-permute-start(bf16[320,512]{1,0:T(8,128)(2,1)} %get-tuple-element.88.rest_0_), channel_id=1, source_target_pairs={{0,6},{1,7},{2,0},{3,1},{4,2},{5,3},{6,4},{7,5},{8,14},{9,15},{10,... | collective-permute-start | bytes 983048 | tf_op jit(solution)/shard_map/ppermute | solution.py:26
  44.8 0.8 collective-permute-start.8
  45.6 1.2 collective-permute-start.11
  46.8 2.4 %unpack_edges.1 = (bf16[384,512]{1,0:T(8,128)(2,1)S(1)}, bf16[384,2560]{1,0:T(8,128)(2,1)S(1)}, bf16[384,128]{1,0:T(8,128)(2,1)S(1)}, bf16[320,384]{1,0:T(8,128)(2,1)S(1)}) custom-call(bf16[2048,128]{1,0:T(8,128)(2,1)} %bitcast.9.arrived_ref, bf16[60,320]{1,0:T(8,128)(2,1)S(1)} %get-tuple-element.90.choose_ref), custom_call_target="tpu_custom_call" | custom-call | tf_op jit(solution)/shard_map/unpack_edges/pallas_call | solution.py:377
  49.2 0.8 copy-done.11
  50.4 0.8 copy-done.8
  51.3 0.7 copy-done.10
  52.0 8.0 %fine0.1 = (bf16[1920,512]{1,0:T(8,128)(2,1)}, f32[320,512]{1,0:T(8,128)S(1)}) custom-call(bf16[1920,512]{1,0:T(8,128)(2,1)} %bitcast.23, bf16[1920,256]{1,0:T(8,128)(2,1)S(1)} %selection.1.picks_ref, bf16[320,512]{1,0:T(8,128)(2,1)S(1)} %bitcast.20, bf16[16,512]{1,0:T(8,128)(2,1)S(1)} %collective-permute-done.3.left_ref, bf16[16,512]{1,0:T(8,128)(2,1)S(1)} %copy-done.10, ...), custom_call_target="tpu_custom_call" | custom-call | tf_op jit(solution)/shard_map/fine0/pallas_call | solution.py:129
  60.0 2.7 %collective-permute-done.8.rest_1_ = bf16[320,512]{1,0:T(8,128)(2,1)} collective-permute-done((bf16[320,512]{1,0:T(8,128)(2,1)}, bf16[320,512]{1,0:T(8,128)(2,1)}, u32[]{:S(2)}, u32[]{:S(2)}) %collective-permute-start.8) | collective-permute-done | bytes 327712 | tf_op jit(solution)/shard_map/ppermute | solution.py:26
  62.7 0.8 collective-permute-start.12
  63.5 0.5 collective-permute-start.14
  64.0 1.0 collective-permute-done.12.rest_5_
  65.4 0.5 collective-permute-done.14.rest_7_
  65.9 5.4 %coarse0.1 = (bf16[320,512]{1,0:T(8,128)(2,1)S(1)}, bf16[384,512]{1,0:T(8,128)(2,1)S(1)}, bf16[20,512]{1,0:T(8,128)(2,1)S(1)}, bf16[20,512]{1,0:T(8,128)(2,1)S(1...) custom-call(bf16[384,512]{1,0:T(8,128)(2,1)S(1)} %get-tuple-element., ...), custom_call_target="tpu_custom_call" | custom-call | tf_op jit(solution)/shard_map/coarse0/pallas_call | solution.py:455
  71.3 2.7 %collective-permute-start.17 = (bf16[20,512]{1,0:T(8,128)(2,1)S(1)}, bf16[20,512]{1,0:T(8,128)(2,1)S(1)}, u32[]{:S(2)}, u32[]{:S(2)}) collective-permute-start(bf16[20,512]{1,0:T(8,128)(2,1)S(1)} %get-tuple-element.107.own_ref), channel_id=1, source_target_pairs={{0,96},{8,104},{16,112},{24,120},{32,0},{40,8},{48,16},{56,24},{64... | collective-permute-start | bytes 61448 | tf_op jit(solution)/shard_map/ppermute | solution.py:46
  73.9 0.5 collective-permute-start.16
  74.4 0.6 collective-permute-start.15
  75.0 1.2 %collective-permute-start.19 = (bf16[16,512]{1,0:T(8,128)(2,1)S(1)}, bf16[16,512]{1,0:T(8,128)(2,1)S(1)}, u32[]{:S(2)}, u32[]{:S(2)}) collective-permute-start(bf16[16,512]{1,0:T(8,128)(2,1)S(1)} %get-tuple-element.109), channel_id=1, source_target_pairs={{0,7},{1,0},{2,1},{3,2},{4,3},{5,4},{6,5},{7,6},{8,15},{9,8},{10,9... | collective-permute-start | bytes 49160 | tf_op jit(solution)/shard_map/ppermute | solution.py:46
  76.3 0.7 collective-permute-done.18.left_ref
  76.9 1.6 %collective-permute-done.19.right_ref = bf16[16,512]{1,0:T(8,128)(2,1)S(1)} collective-permute-done((bf16[16,512]{1,0:T(8,128)(2,1)S(1)}, bf16[16,512]{1,0:T(8,128)(2,1)S(1)}, u32[]{:S(2)}, u32[]{:S(2)}) %collective-permute-start.19) | collective-permute-done | bytes 16416 | tf_op jit(solution)/shard_map/ppermute | solution.py:46
  78.6 1.3 %collective-permute-start.20 = (bf16[112,512]{1,0:T(8,128)(2,1)S(1)}, bf16[112,512]{1,0:T(8,128)(2,1)S(1)}, u32[]{:S(2)}, u32[]{:S(2)}) collective-permute-start(bf16[112,512]{1,0:T(8,128)(2,1)S(1)} %get-tuple-element.113), channel_id=1, source_target_pairs={{0,8},{8,16},{16,24},{24,32},{32,40},{40,48},{48,56},{56,64},{64,7... | collective-permute-start | bytes 344072 | tf_op jit(solution)/shard_map/ppermute | solution.py:46
  79.8 3.6 %collective-permute-start.22 = (bf16[112,512]{1,0:T(8,128)(2,1)S(1)}, bf16[112,512]{1,0:T(8,128)(2,1)S(1)}, u32[]{:S(2)}, u32[]{:S(2)}) collective-permute-start(bf16[112,512]{1,0:T(8,128)(2,1)S(1)} %get-tuple-element.114), channel_id=1, source_target_pairs={{0,120},{8,0},{16,8},{24,16},{32,24},{40,32},{48,40},{56,48},{64,5... | collective-permute-start | bytes 344072 | tf_op jit(solution)/shard_map/ppermute | solution.py:46
  83.4 6.9 %collective-permute-done.21.two_ref = bf16[80,512]{1,0:T(8,128)(2,1)S(1)} collective-permute-done((bf16[80,512]{1,0:T(8,128)(2,1)S(1)}, bf16[80,512]{1,0:T(8,128)(2,1)S(1)}, u32[]{:S(2)}, u32[]{:S(2)}) %collective-permute-start.21) | collective-permute-done | bytes 81952 | tf_op jit(solution)/shard_map/ppermute | solution.py:46
  90.3 0.6 join_near.3
  90.9 4.8 %collective-permute-start.25 = (bf16[320,512]{1,0:T(8,128)(2,1)S(1)}, bf16[320,512]{1,0:T(8,128)(2,1)S(1)}, u32[]{:S(2)}, u32[]{:S(2)}) collective-permute-start(bf16[320,512]{1,0:T(8,128)(2,1)S(1)} %get-tuple-element.117.rest_0_), channel_id=1, source_target_pairs={{0,6},{1,7},{2,0},{3,1},{4,2},{5,3},{6,4},{7,5},{8,14},{9,15},{10,... | collective-permute-start | bytes 983048 | tf_op jit(solution)/shard_map/ppermute | solution.py:26
  95.7 0.7 collective-permute-start.23
  96.3 0.5 collective-permute-start.26
  96.9 2.3 %own0.1 = (bf16[160,512]{1,0:T(8,128)(2,1)S(1)}, bf16[704,2560]{1,0:T(8,128)(2,1)S(1)}) custom-call(bf16[160,512]{1,0:T(8,128)(2,1)S(1)} %copy-done.5, bf16[160,128]{1,0:T(8,128)(2,1)S(1)} %copy-done.13, bf16[384,2560]{1,0:T(8,128)(2,1)S(1)} %get-tuple-element.100.sends_ref, bf16[2560,512]{1,0:T(8,128)(2,1)S(1)} %get-tuple-element.124.table_ref, ...), custom_call_target="tpu_custom_call" | custom-call | tf_op jit(solution)/shard_map/own0/pallas_call | solution.py:485
  99.1 7.8 %fine1.1 = (bf16[1920,512]{1,0:T(8,128)(2,1)}, f32[320,512]{1,0:T(8,128)S(1)}) custom-call(bf16[1920,512]{1,0:T(8,128)(2,1)} %get-tuple-element.118.fine_ref, bf16[1920,256]{1,0:T(8,128)(2,1)S(1)} %selection.1.picks_ref, bf16[320,512]{1,0:T(8,128)(2,1)S(1)} %get-tuple-element.119.latents_ref, bf16[16,512]{1,0:T(8,128)(2,1)S(1)} %collective-permute-done.18.left_ref, ...), custom_call_target="tpu_custom_call" | custom-call | tf_op jit(solution)/shard_map/fine1/pallas_call | solution.py:129
  106.9 3.3 %collective-permute-done.25.rest_3_ = bf16[320,512]{1,0:T(8,128)(2,1)S(1)} collective-permute-done((bf16[320,512]{1,0:T(8,128)(2,1)S(1)}, bf16[320,512]{1,0:T(8,128)(2,1)S(1)}, u32[]{:S(2)}, u32[]{:S(2)}) %collective-permute-start.25) | collective-permute-done | bytes 327712 | tf_op jit(solution)/shard_map/ppermute | solution.py:26
  110.2 3.0 %collective-permute-done.23.rest_1_ = bf16[320,512]{1,0:T(8,128)(2,1)S(1)} collective-permute-done((bf16[320,512]{1,0:T(8,128)(2,1)S(1)}, bf16[320,512]{1,0:T(8,128)(2,1)S(1)}, u32[]{:S(2)}, u32[]{:S(2)}) %collective-permute-start.23) | collective-permute-done | bytes 327712 | tf_op jit(solution)/shard_map/ppermute | solution.py:26
  113.3 0.8 collective-permute-start.27
  114.0 0.5 collective-permute-start.29
  114.6 0.7 collective-permute-done.27.rest_5_
  116.2 5.6 %coarse1.1 = (bf16[320,512]{1,0:T(8,128)(2,1)}, bf16[160,512]{1,0:T(8,128)(2,1)}) custom-call(bf16[384,512]{1,0:T(8,128)(2,1)S(1)} %get-tuple-element.127.long_ref, bf16[160,512]{1,0:T(8,128)(2,1)S(1)} %get-tuple-element.128.own_ref, bf16[704,2560]{1,0:T(8,128)(2,1)S(1)} %get-tuple-element.129.sends_ref, bf16[384,128]{1,0:T(8,128)(2,1)S(1)} %get-tuple-element.101.recvs_ref, ...), custom_call_target="tpu_custom_call" | custom-call | tf_op jit(solution)/shard_map/coarse1/pallas_call | solution.py:455
  (63 shorter events, 2.4 us)
Async XLA Ops:
  2.0 10.9 %collective-permute-start.2 = (bf16[20,512]{1,0:T(8,128)(2,1)S(1)}, bf16[20,512]{1,0:T(8,128)(2,1)S(1)}, u32[]{:S(2)}, u32[]{:S(2)}) collective-permute-start(bf16[20,512]{1,0:T(8,128)(2,1)S(1)} %get-tuple-element.71.own_ref), channel_id=1, source_target_pairs={{0,96},{8,104},{16,112},{24,120},{32,0},{40,8},{48,16},{56,24},{64... | collective-permute-start | bytes 61448 | tf_op jit(solution)/shard_map/ppermute | solution.py:46
  5.6 7.3 %collective-permute-start.1 = (bf16[20,512]{1,0:T(8,128)(2,1)S(1)}, bf16[20,512]{1,0:T(8,128)(2,1)S(1)}, u32[]{:S(2)}, u32[]{:S(2)}) collective-permute-start(bf16[20,512]{1,0:T(8,128)(2,1)S(1)} %get-tuple-element.71.own_ref), channel_id=1, source_target_pairs={{0,64},{8,72},{16,80},{24,88},{32,96},{40,104},{48,112},{56,120},{... | collective-permute-start | bytes 61448 | tf_op jit(solution)/shard_map/ppermute | solution.py:46
  6.0 6.9 %collective-permute-start = (bf16[20,512]{1,0:T(8,128)(2,1)S(1)}, bf16[20,512]{1,0:T(8,128)(2,1)S(1)}, u32[]{:S(2)}, u32[]{:S(2)}) collective-permute-start(bf16[20,512]{1,0:T(8,128)(2,1)S(1)} %get-tuple-element.71.own_ref), channel_id=1, source_target_pairs={{0,32},{8,40},{16,48},{24,56},{32,64},{40,72},{48,80},{56,88},{64,... | collective-permute-start | bytes 61448 | tf_op jit(solution)/shard_map/ppermute | solution.py:46
  6.7 5.6 %collective-permute-start.3 = (bf16[16,512]{1,0:T(8,128)(2,1)S(1)}, bf16[16,512]{1,0:T(8,128)(2,1)S(1)}, u32[]{:S(2)}, u32[]{:S(2)}) collective-permute-start(bf16[16,512]{1,0:T(8,128)(2,1)S(1)} %get-tuple-element.72), channel_id=1, source_target_pairs={{0,1},{1,2},{2,3},{3,4},{4,5},{5,6},{6,7},{7,0},{8,9},{9,10},{10,1... | collective-permute-start | bytes 49160 | tf_op jit(solution)/shard_map/ppermute | solution.py:46
  9.7 3.2 %collective-permute-start.4 = (bf16[16,512]{1,0:T(8,128)(2,1)S(1)}, bf16[16,512]{1,0:T(8,128)(2,1)S(1)}, u32[]{:S(2)}, u32[]{:S(2)}) collective-permute-start(bf16[16,512]{1,0:T(8,128)(2,1)S(1)} %get-tuple-element.73), channel_id=1, source_target_pairs={{0,7},{1,0},{2,1},{3,2},{4,3},{5,4},{6,5},{7,6},{8,15},{9,8},{10,9... | collective-permute-start | bytes 49160 | tf_op jit(solution)/shard_map/ppermute | solution.py:46
  12.2 16.3 %copy-start.12 = (bf16[160,128]{1,0:T(8,128)(2,1)}, bf16[160,128]{1,0:T(8,128)(2,1)S(1)}, u32[]{:S(2)}) copy-start(bf16[160,128]{1,0:T(8,128)(2,1)S(1)} %get-tuple-element.123.tags_ref) | copy-start | bytes 122884
  12.9 15.7 %copy-start.9 = (bf16[16,512]{1,0:T(8,128)(2,1)}, bf16[16,512]{1,0:T(8,128)(2,1)S(1)}, u32[]{:S(2)}) copy-start(bf16[16,512]{1,0:T(8,128)(2,1)S(1)} %collective-permute-done.4.right_ref) | copy-start | bytes 49156
  12.9 15.6 %copy-start.15 = (bf16[80,512]{1,0:T(8,128)(2,1)}, bf16[80,512]{1,0:T(8,128)(2,1)S(1)}, u32[]{:S(2)}) copy-start(bf16[80,512]{1,0:T(8,128)(2,1)S(1)} %get-tuple-element.83.own_ref) | copy-start | bytes 245764
  12.9 15.6 %collective-permute-start.5 = (bf16[112,512]{1,0:T(8,128)(2,1)S(1)}, bf16[112,512]{1,0:T(8,128)(2,1)S(1)}, u32[]{:S(2)}, u32[]{:S(2)}) collective-permute-start(bf16[112,512]{1,0:T(8,128)(2,1)S(1)} %get-tuple-element.84), channel_id=1, source_target_pairs={{0,8},{8,16},{16,24},{24,32},{32,40},{40,48},{48,56},{56,64},{64,7... | collective-permute-start | bytes 344072 | tf_op jit(solution)/shard_map/ppermute | solution.py:46
  14.2 15.6 %collective-permute-start.7 = (bf16[112,512]{1,0:T(8,128)(2,1)S(1)}, bf16[112,512]{1,0:T(8,128)(2,1)}, u32[]{:S(2)}, u32[]{:S(2)}) collective-permute-start(bf16[112,512]{1,0:T(8,128)(2,1)S(1)} %get-tuple-element.85), channel_id=1, source_target_pairs={{0,120},{8,0},{16,8},{24,16},{32,24},{40,32},{48,40},{56,48},{64,5... | collective-permute-start | bytes 344072 | tf_op jit(solution)/shard_map/ppermute | solution.py:46
  17.8 10.7 %collective-permute-start.6 = (bf16[80,512]{1,0:T(8,128)(2,1)S(1)}, bf16[80,512]{1,0:T(8,128)(2,1)S(1)}, u32[]{:S(2)}, u32[]{:S(2)}) collective-permute-start(bf16[80,512]{1,0:T(8,128)(2,1)S(1)} %get-tuple-element.83.own_ref), channel_id=1, source_target_pairs={{0,16},{8,24},{16,32},{24,40},{32,48},{40,56},{48,64},{56,72},{64,... | collective-permute-start | bytes 245768 | tf_op jit(solution)/shard_map/ppermute | solution.py:46
  17.8 29.0 %all-to-all-start = ((bf16[128,16,128]{2,1,0:T(8,128)(2,1)}), bf16[128,16,128]{2,1,0:T(8,128)(2,1)}, u32[]{:S(2)}, u32[]{:S(2)}) async-start(bf16[128,16,128]{2,1,0:T(8,128)(2,1)} %bitcast.8), calls=%async_computation | async-start | bytes 1048576 | tf_op jit(solution)/shard_map/all_to_all | solution.py:537
  28.5 21.9 %copy-start.4 = (bf16[16,20,512]{2,0,1:T(8,128)(2,1)S(1)}, bf16[16,20,512]{2,0,1:T(8,128)(2,1)}, u32[]{:S(2)}) copy-start(bf16[16,20,512]{2,0,1:T(8,128)(2,1)} %param.13) | copy-start | bytes 983044
  28.5 21.9 %copy-start.6 = (f32[2,512]{1,0:T(2,128)S(1)}, f32[2,512]{1,0:T(2,128)}, u32[]{:S(2)}) copy-start(f32[2,512]{1,0:T(2,128)} %eg_ref.5) | copy-start | bytes 12292
  29.1 0.6 copy-start.16
  29.8 20.6 %copy-start = (bf16[2,1536,512]{2,1,0:T(8,128)(2,1)S(1)}, bf16[2,1536,512]{2,1,0:T(8,128)(2,1)}, u32[]{:S(2)}) copy-start(bf16[2,1536,512]{2,1,0:T(8,128)(2,1)} %ei_ref.5) | copy-start | bytes 9437188
  40.9 0.6 copy-start.7
  41.5 18.5 %collective-permute-start.10 = (bf16[320,512]{1,0:T(8,128)(2,1)}, bf16[320,512]{1,0:T(8,128)(2,1)}, u32[]{:S(2)}, u32[]{:S(2)}) collective-permute-start(bf16[320,512]{1,0:T(8,128)(2,1)} %get-tuple-element.88.rest_0_), channel_id=1, source_target_pairs={{0,6},{1,7},{2,0},{3,1},{4,2},{5,3},{6,4},{7,5},{8,14},{9,15},{10,... | collective-permute-start | bytes 983048 | tf_op jit(solution)/shard_map/ppermute | solution.py:26
  44.8 15.2 %collective-permute-start.9 = (bf16[320,512]{1,0:T(8,128)(2,1)}, bf16[320,512]{1,0:T(8,128)(2,1)}, u32[]{:S(2)}, u32[]{:S(2)}) collective-permute-start(bf16[320,512]{1,0:T(8,128)(2,1)} %get-tuple-element.88.rest_0_), channel_id=1, source_target_pairs={{0,4},{1,5},{2,6},{3,7},{4,0},{5,1},{6,2},{7,3},{8,12},{9,13},{10,... | collective-permute-start | bytes 983048 | tf_op jit(solution)/shard_map/ppermute | solution.py:26
  44.8 17.9 %collective-permute-start.8 = (bf16[320,512]{1,0:T(8,128)(2,1)}, bf16[320,512]{1,0:T(8,128)(2,1)}, u32[]{:S(2)}, u32[]{:S(2)}) collective-permute-start(bf16[320,512]{1,0:T(8,128)(2,1)} %get-tuple-element.88.rest_0_), channel_id=1, source_target_pairs={{0,2},{1,3},{2,4},{3,5},{4,6},{5,7},{6,0},{7,1},{8,10},{9,11},{10,... | collective-permute-start | bytes 983048 | tf_op jit(solution)/shard_map/ppermute | solution.py:26
  45.6 18.3 %collective-permute-start.11 = (bf16[320,512]{1,0:T(8,128)(2,1)}, bf16[320,512]{1,0:T(8,128)(2,1)}, u32[]{:S(2)}, u32[]{:S(2)}) collective-permute-start(bf16[320,512]{1,0:T(8,128)(2,1)} %get-tuple-element.88.rest_0_), channel_id=1, source_target_pairs={{0,1},{1,0},{2,3},{3,2},{4,5},{5,4},{6,7},{7,6},{8,9},{9,8},{10,11... | collective-permute-start | bytes 983048 | tf_op jit(solution)/shard_map/ppermute | solution.py:26
  46.8 3.6 %copy-start.1 = (bf16[2,512,512]{2,1,0:T(8,128)(2,1)S(1)}, bf16[2,512,512]{2,1,0:T(8,128)(2,1)}, u32[]{:S(2)}) copy-start(bf16[2,512,512]{2,1,0:T(8,128)(2,1)} %eo_ref.5) | copy-start | bytes 3145732
  49.2 0.8 copy-start.11
  50.4 0.8 copy-start.8
  51.3 0.7 copy-start.10
  52.0 13.9 %copy-start.2 = (bf16[2,1024,512]{2,1,0:T(8,128)(2,1)S(1)}, bf16[2,1024,512]{2,1,0:T(8,128)(2,1)}, u32[]{:S(2)}) copy-start(bf16[2,1024,512]{2,1,0:T(8,128)(2,1)} %ni_ref.3) | copy-start | bytes 6291460
  52.0 13.9 %copy-start.3 = (bf16[2,512,512]{2,1,0:T(8,128)(2,1)S(1)}, bf16[2,512,512]{2,1,0:T(8,128)(2,1)}, u32[]{:S(2)}) copy-start(bf16[2,512,512]{2,1,0:T(8,128)(2,1)} %no_ref.3) | copy-start | bytes 3145732
  52.0 13.9 %copy-start.5 = (bf16[160,512]{1,0:T(8,128)(2,1)S(1)}, bf16[160,512]{1,0:T(8,128)(2,1)}, u32[]{:S(2)}) copy-start(bf16[160,512]{1,0:T(8,128)(2,1)} %long_ref) | copy-start | bytes 491524
  52.0 13.9 %copy-start.14 = (f32[2,512]{1,0:T(2,128)S(1)}, f32[2,512]{1,0:T(2,128)}, u32[]{:S(2)}) copy-start(f32[2,512]{1,0:T(2,128)} %ng_ref.3) | copy-start | bytes 12292
  62.7 2.3 %collective-permute-start.12 = (bf16[320,512]{1,0:T(8,128)(2,1)}, bf16[320,512]{1,0:T(8,128)(2,1)S(1)}, u32[]{:S(2)}, u32[]{:S(2)}) collective-permute-start(bf16[320,512]{1,0:T(8,128)(2,1)} %collective-permute-done.8.rest_1_), channel_id=1, source_target_pairs={{0,1},{1,0},{2,3},{3,2},{4,5},{5,4},{6,7},{7,6},{8,9},{9,8},{10,11... | collective-permute-start | bytes 983048 | tf_op jit(solution)/shard_map/ppermute | solution.py:26
  63.5 1.9 %collective-permute-start.13 = (bf16[320,512]{1,0:T(8,128)(2,1)}, bf16[320,512]{1,0:T(8,128)(2,1)S(1)}, u32[]{:S(2)}, u32[]{:S(2)}) collective-permute-start(bf16[320,512]{1,0:T(8,128)(2,1)} %collective-permute-done.9.rest_2_), channel_id=1, source_target_pairs={{0,1},{1,0},{2,3},{3,2},{4,5},{5,4},{6,7},{7,6},{8,9},{9,8},{10,11... | collective-permute-start | bytes 983048 | tf_op jit(solution)/shard_map/ppermute | solution.py:26
  63.5 2.4 %collective-permute-start.14 = (bf16[320,512]{1,0:T(8,128)(2,1)}, bf16[320,512]{1,0:T(8,128)(2,1)S(1)}, u32[]{:S(2)}, u32[]{:S(2)}) collective-permute-start(bf16[320,512]{1,0:T(8,128)(2,1)} %collective-permute-done.10.rest_3_), channel_id=1, source_target_pairs={{0,1},{1,0},{2,3},{3,2},{4,5},{5,4},{6,7},{7,6},{8,9},{9,8},{10,11... | collective-permute-start | bytes 983048 | tf_op jit(solution)/shard_map/ppermute | solution.py:26
  71.3 7.2 %collective-permute-start.17 = (bf16[20,512]{1,0:T(8,128)(2,1)S(1)}, bf16[20,512]{1,0:T(8,128)(2,1)S(1)}, u32[]{:S(2)}, u32[]{:S(2)}) collective-permute-start(bf16[20,512]{1,0:T(8,128)(2,1)S(1)} %get-tuple-element.107.own_ref), channel_id=1, source_target_pairs={{0,96},{8,104},{16,112},{24,120},{32,0},{40,8},{48,16},{56,24},{64... | collective-permute-start | bytes 61448 | tf_op jit(solution)/shard_map/ppermute | solution.py:46
  73.9 4.6 %collective-permute-start.16 = (bf16[20,512]{1,0:T(8,128)(2,1)S(1)}, bf16[20,512]{1,0:T(8,128)(2,1)S(1)}, u32[]{:S(2)}, u32[]{:S(2)}) collective-permute-start(bf16[20,512]{1,0:T(8,128)(2,1)S(1)} %get-tuple-element.107.own_ref), channel_id=1, source_target_pairs={{0,64},{8,72},{16,80},{24,88},{32,96},{40,104},{48,112},{56,120},{... | collective-permute-start | bytes 61448 | tf_op jit(solution)/shard_map/ppermute | solution.py:46
  74.4 4.1 %collective-permute-start.15 = (bf16[20,512]{1,0:T(8,128)(2,1)S(1)}, bf16[20,512]{1,0:T(8,128)(2,1)S(1)}, u32[]{:S(2)}, u32[]{:S(2)}) collective-permute-start(bf16[20,512]{1,0:T(8,128)(2,1)S(1)} %get-tuple-element.107.own_ref), channel_id=1, source_target_pairs={{0,32},{8,40},{16,48},{24,56},{32,64},{40,72},{48,80},{56,88},{64,... | collective-permute-start | bytes 61448 | tf_op jit(solution)/shard_map/ppermute | solution.py:46
  75.0 1.9 %collective-permute-start.18 = (bf16[16,512]{1,0:T(8,128)(2,1)S(1)}, bf16[16,512]{1,0:T(8,128)(2,1)S(1)}, u32[]{:S(2)}, u32[]{:S(2)}) collective-permute-start(bf16[16,512]{1,0:T(8,128)(2,1)S(1)} %get-tuple-element.108), channel_id=1, source_target_pairs={{0,1},{1,2},{2,3},{3,4},{4,5},{5,6},{6,7},{7,0},{8,9},{9,10},{10,1... | collective-permute-start | bytes 49160 | tf_op jit(solution)/shard_map/ppermute | solution.py:46
  75.0 3.5 %collective-permute-start.19 = (bf16[16,512]{1,0:T(8,128)(2,1)S(1)}, bf16[16,512]{1,0:T(8,128)(2,1)S(1)}, u32[]{:S(2)}, u32[]{:S(2)}) collective-permute-start(bf16[16,512]{1,0:T(8,128)(2,1)S(1)} %get-tuple-element.109), channel_id=1, source_target_pairs={{0,7},{1,0},{2,1},{3,2},{4,3},{5,4},{6,5},{7,6},{8,15},{9,8},{10,9... | collective-permute-start | bytes 49160 | tf_op jit(solution)/shard_map/ppermute | solution.py:46
  78.6 11.8 %collective-permute-start.20 = (bf16[112,512]{1,0:T(8,128)(2,1)S(1)}, bf16[112,512]{1,0:T(8,128)(2,1)S(1)}, u32[]{:S(2)}, u32[]{:S(2)}) collective-permute-start(bf16[112,512]{1,0:T(8,128)(2,1)S(1)} %get-tuple-element.113), channel_id=1, source_target_pairs={{0,8},{8,16},{16,24},{24,32},{32,40},{40,48},{48,56},{56,64},{64,7... | collective-permute-start | bytes 344072 | tf_op jit(solution)/shard_map/ppermute | solution.py:46
  79.8 10.5 %collective-permute-start.22 = (bf16[112,512]{1,0:T(8,128)(2,1)S(1)}, bf16[112,512]{1,0:T(8,128)(2,1)S(1)}, u32[]{:S(2)}, u32[]{:S(2)}) collective-permute-start(bf16[112,512]{1,0:T(8,128)(2,1)S(1)} %get-tuple-element.114), channel_id=1, source_target_pairs={{0,120},{8,0},{16,8},{24,16},{32,24},{40,32},{48,40},{56,48},{64,5... | collective-permute-start | bytes 344072 | tf_op jit(solution)/shard_map/ppermute | solution.py:46
  83.4 13.5 %copy-start.13 = (bf16[160,128]{1,0:T(8,128)(2,1)S(1)}, bf16[160,128]{1,0:T(8,128)(2,1)}, u32[]{:S(2)}) copy-start(bf16[160,128]{1,0:T(8,128)(2,1)} %copy-done.12) | copy-start | bytes 122884
  83.4 6.9 %collective-permute-start.21 = (bf16[80,512]{1,0:T(8,128)(2,1)S(1)}, bf16[80,512]{1,0:T(8,128)(2,1)S(1)}, u32[]{:S(2)}, u32[]{:S(2)}) collective-permute-start(bf16[80,512]{1,0:T(8,128)(2,1)S(1)} %get-tuple-element.112.own_ref), channel_id=1, source_target_pairs={{0,16},{8,24},{16,32},{24,40},{32,48},{40,56},{48,64},{56,72},{64,... | collective-permute-start | bytes 245768 | tf_op jit(solution)/shard_map/ppermute | solution.py:46
  90.9 19.3 %collective-permute-start.25 = (bf16[320,512]{1,0:T(8,128)(2,1)S(1)}, bf16[320,512]{1,0:T(8,128)(2,1)S(1)}, u32[]{:S(2)}, u32[]{:S(2)}) collective-permute-start(bf16[320,512]{1,0:T(8,128)(2,1)S(1)} %get-tuple-element.117.rest_0_), channel_id=1, source_target_pairs={{0,6},{1,7},{2,0},{3,1},{4,2},{5,3},{6,4},{7,5},{8,14},{9,15},{10,... | collective-permute-start | bytes 983048 | tf_op jit(solution)/shard_map/ppermute | solution.py:26
  95.7 14.6 %collective-permute-start.24 = (bf16[320,512]{1,0:T(8,128)(2,1)S(1)}, bf16[320,512]{1,0:T(8,128)(2,1)S(1)}, u32[]{:S(2)}, u32[]{:S(2)}) collective-permute-start(bf16[320,512]{1,0:T(8,128)(2,1)S(1)} %get-tuple-element.117.rest_0_), channel_id=1, source_target_pairs={{0,4},{1,5},{2,6},{3,7},{4,0},{5,1},{6,2},{7,3},{8,12},{9,13},{10,... | collective-permute-start | bytes 983048 | tf_op jit(solution)/shard_map/ppermute | solution.py:26
  95.7 17.6 %collective-permute-start.23 = (bf16[320,512]{1,0:T(8,128)(2,1)S(1)}, bf16[320,512]{1,0:T(8,128)(2,1)S(1)}, u32[]{:S(2)}, u32[]{:S(2)}) collective-permute-start(bf16[320,512]{1,0:T(8,128)(2,1)S(1)} %get-tuple-element.117.rest_0_), channel_id=1, source_target_pairs={{0,2},{1,3},{2,4},{3,5},{4,6},{5,7},{6,0},{7,1},{8,10},{9,11},{10,... | collective-permute-start | bytes 983048 | tf_op jit(solution)/shard_map/ppermute | solution.py:26
  96.3 18.2 %collective-permute-start.26 = (bf16[320,512]{1,0:T(8,128)(2,1)S(1)}, bf16[320,512]{1,0:T(8,128)(2,1)S(1)}, u32[]{:S(2)}, u32[]{:S(2)}) collective-permute-start(bf16[320,512]{1,0:T(8,128)(2,1)S(1)} %get-tuple-element.117.rest_0_), channel_id=1, source_target_pairs={{0,1},{1,0},{2,3},{3,2},{4,5},{5,4},{6,7},{7,6},{8,9},{9,8},{10,11... | collective-permute-start | bytes 983048 | tf_op jit(solution)/shard_map/ppermute | solution.py:26
  113.3 2.0 %collective-permute-start.27 = (bf16[320,512]{1,0:T(8,128)(2,1)S(1)}, bf16[320,512]{1,0:T(8,128)(2,1)S(1)}, u32[]{:S(2)}, u32[]{:S(2)}) collective-permute-start(bf16[320,512]{1,0:T(8,128)(2,1)S(1)} %collective-permute-done.23.rest_1_), channel_id=1, source_target_pairs={{0,1},{1,0},{2,3},{3,2},{4,5},{5,4},{6,7},{7,6},{8,9},{9,8},{10,11... | collective-permute-start | bytes 983048 | tf_op jit(solution)/shard_map/ppermute | solution.py:26
  114.0 1.7 %collective-permute-start.28 = (bf16[320,512]{1,0:T(8,128)(2,1)S(1)}, bf16[320,512]{1,0:T(8,128)(2,1)S(1)}, u32[]{:S(2)}, u32[]{:S(2)}) collective-permute-start(bf16[320,512]{1,0:T(8,128)(2,1)S(1)} %collective-permute-done.24.rest_2_), channel_id=1, source_target_pairs={{0,1},{1,0},{2,3},{3,2},{4,5},{5,4},{6,7},{7,6},{8,9},{9,8},{10,11... | collective-permute-start | bytes 983048 | tf_op jit(solution)/shard_map/ppermute | solution.py:26
  114.0 2.2 %collective-permute-start.29 = (bf16[320,512]{1,0:T(8,128)(2,1)S(1)}, bf16[320,512]{1,0:T(8,128)(2,1)S(1)}, u32[]{:S(2)}, u32[]{:S(2)}) collective-permute-start(bf16[320,512]{1,0:T(8,128)(2,1)S(1)} %collective-permute-done.25.rest_3_), channel_id=1, source_target_pairs={{0,1},{1,0},{2,3},{3,2},{4,5},{5,4},{6,7},{7,6},{8,9},{9,8},{10,11... | collective-permute-start | bytes 983048 | tf_op jit(solution)/shard_map/ppermute | solution.py:26
  (1 other events, 0.6 us)

commit v7 on v6

--- a/solution.py
+++ b/solution.py
@@ -130,7 +130,7 @@
         body,
         name=f"fine{layer}",
         out_shape=(
-            pltpu.HBM(fine.shape, jnp.bfloat16),
+            jax.ShapeDtypeStruct(fine.shape, jnp.bfloat16),
             jax.ShapeDtypeStruct((nodes, features), jnp.float32),
         ),
         grid=(steps,),
@@ -149,7 +149,7 @@
             pltpu.VMEM((256, hidden), jnp.bfloat16),
         ],
         compiler_params=pltpu.CompilerParams(dimension_semantics=("arbitrary",), vmem_limit_bytes=14 * MIB),
-    )(in_hbm(fine), picks, latents, left, right, sides, inner, outer, gain)
+    )(fine, picks, latents, left, right, sides, inner, outer, gain)
 
 
 def pick(index, width):
@@ -217,31 +217,40 @@
     each, features = own.shape
     side = BELOW - ABOVE
 
-    def body(own_ref, up_ref, two_ref, down_ref, joined_ref, sides_ref, sems):
-        part = lambda at: joined_ref.at[pl.ds(at * each, each), :]
+    far = layer == 0
+
+    def body(own_ref, two_ref, up_ref, down_ref, joined_ref, sides_ref, sems, *near):
+        to, beside = near or (joined_ref, sides_ref)
+        part = lambda at: to.at[pl.ds(at * each, each), :]
         fetch(
             [
                 (own_ref, part(0)),
                 (up_ref.at[pl.ds(0, each), :], part(1)),
                 (two_ref, part(2)),
                 (down_ref.at[pl.ds(0, each), :], part(3)),
-                (up_ref.at[pl.ds(each, side), :], sides_ref.at[pl.ds(0, side), :]),
-                (down_ref.at[pl.ds(each, side), :], sides_ref.at[pl.ds(side, side), :]),
+                (up_ref.at[pl.ds(each, side), :], beside.at[pl.ds(0, side), :]),
+                (down_ref.at[pl.ds(each, side), :], beside.at[pl.ds(side, side), :]),
             ],
             sems,
         )
-
-    away = pl.BlockSpec(memory_space=pltpu.HBM)
+        if near:
+            fetch([(to, joined_ref), (beside, sides_ref)], sems)
+
+    away = pl.BlockSpec(memory_space=pl.ANY)
+    place = pltpu.HBM if far else jax.ShapeDtypeStruct
+    shapes = ((4 * each, features), (2 * side, features))
+    operands = (own, two, up, down)
     return pl.pallas_call(
         body,
         name="join_near",
         cost_estimate=pl.CostEstimate(flops=3_000_000_000, bytes_accessed=0, transcendentals=0),
-        out_shape=tuple(jax.ShapeDtypeStruct((n, features), jnp.bfloat16) for n in (4 * each, 2 * side)),
+        out_shape=tuple(place(shape, jnp.bfloat16) for shape in shapes),
         in_specs=[away] * 4,
         out_specs=(away,) * 2,
-        scratch_shapes=[pltpu.SemaphoreType.DMA((6,))],
+        scratch_shapes=[pltpu.SemaphoreType.DMA((6,))]
+        + [pltpu.VMEM(shape, jnp.bfloat16) for shape in shapes if far],
         compiler_params=pltpu.CompilerParams(vmem_limit_bytes=2 * MIB),
-    )(*(map(in_hbm, (own, up, two, down)) if layer == 0 else (own, up, two, down)))
+    )(*(map(in_hbm, operands) if far else operands))
 
 
 def coarse_start(coarse_slots, latents, rows, columns):

time: 123 us -> 113 us (0.919)
  Pallas kernels: 47.4 us -> 34.9 us
  waiting for transfers between devices: 22.3 us -> 25.8 us
  starting transfers between devices: 47 us -> 45.5 us
    pallas_call x2, Pallas kernels: 11.6 us -> 2.5 us  [join_near(): pl.pallas_call(body, name='join_near', cost_estimate=pl.CostEstimate(flop...]
    all_to_all x1, waiting for transfers between devices: 0.01 us -> 4.75 us  [shards(): lax.all_to_all(packed, AXES, split_axis=0, concat_axis=0, tiled=True)]
    pallas_call x2, Pallas kernels: 15.8 us -> 12.6 us  [fine_layer(): pl.pallas_call(body, name=f'fine{layer}', out_shape=(jax.ShapeDtypeStruct...]
    ppermute x14, waiting for transfers between devices: 12.6 us -> 10.4 us  [shift(): return lax.ppermute(values, 'py', pairs)]
    ppermute x16, starting transfers between devices: 22.4 us -> 20.7 us  [along(): lax.ppermute(values, axis, [(i, (i + step) % count) for i in range(count)])]
    unnamed x36 -> x38, local copies, waits for them, and re-layouts: 4.25 us -> 5.18 us
  transfers between devices with their start and end apart: 31 -> 31, of which waited for: 13 -> 14; matrix products, arithmetic and copies ran while one was open for 0% -> 0% of each run, Pallas kernels for 28% -> 20%
where the time goes in v7:
time: 113 us; the launch traced here: 112 us
  starting transfers between devices  45.5 us (40%)
  Pallas kernels  34.9 us (31%)
  waiting for transfers between devices  25.8 us (23%)
  local copies, waits for them, and re-layouts  5.18 us (5%)
    ppermute x16, starting transfers between devices, along(): lax.ppermute(values, axis, [(i, (i + step) % count) for i in range(count)])  20.7 us
    ppermute x14, starting transfers between devices, shift(): return lax.ppermute(values, 'py', pairs)  14.1 us
    pallas_call x2, Pallas kernels, fine_layer(): pl.pallas_call(body, name=f'fine{layer}', out_shape=(jax.ShapeDtypeStruct...  12.6 us
    pallas_call x2, Pallas kernels, coarse_layer(): pl.pallas_call(body, name=f'coarse{layer}', out_shape=tuple(shapes), in_s...  10.9 us
    all_to_all x1, starting transfers between devices, shards(): lax.all_to_all(packed, AXES, split_axis=0, concat_axis=0, tiled=True)  10.7 us
    ppermute x16, waiting for transfers between devices, along(): lax.ppermute(values, axis, [(i, (i + step) % count) for i in range(count)])  10.6 us
    ppermute x14, waiting for transfers between devices, shift(): return lax.ppermute(values, 'py', pairs)  10.4 us
    unnamed x38, local copies, waits for them, and re-layouts  5.18 us
  transfers between devices with their start and end apart: 31, of which 14 were waited for; matrix products, arithmetic and copies ran while one was open for 0% of the time, Pallas kernels for 20%

profile of v7, /device:TPU:1, one launch (start us, length us, event | category | flops | bytes accessed | tf_op | source)
XLA Modules:
  0.0 112.5 jit_solution(8367643042170250896)
XLA Ops:
  0.6 1.3 %coarse_start.1 = (bf16[20,512]{1,0:T(8,128)(2,1)S(1)}, bf16[20,512]{1,0:T(8,128)(2,1)S(1)}, bf16[20,512]{1,0:T(8,128)(2,1)S(1)}, bf16[16,512]{1,0:T(8,128)(2,1)...) custom-call(s32[1,20]{1,0:T(1,128)} %bitcast.24, bf16[320,512]{1,0:T(8,128)(2,1)} %bitcast.19), custom_call_target="tpu_custom_call" | custom-call | tf_op jit(solution)/shard_map/coarse_start/pallas_call | solution.py:286
  2.0 3.6 %collective-permute-start.2 = (bf16[20,512]{1,0:T(8,128)(2,1)S(1)}, bf16[20,512]{1,0:T(8,128)(2,1)S(1)}, u32[]{:S(2)}, u32[]{:S(2)}) collective-permute-start(bf16[20,512]{1,0:T(8,128)(2,1)S(1)} %get-tuple-element.71.own_ref), channel_id=1, source_target_pairs={{0,96},{8,104},{16,112},{24,120},{32,0},{40,8},{48,16},{56,24},{64... | collective-permute-start | bytes 61448 | tf_op jit(solution)/shard_map/ppermute | solution.py:46
  6.0 0.7 collective-permute-start
  6.7 3.0 %collective-permute-start.3 = (bf16[16,512]{1,0:T(8,128)(2,1)S(1)}, bf16[16,512]{1,0:T(8,128)(2,1)S(1)}, u32[]{:S(2)}, u32[]{:S(2)}) collective-permute-start(bf16[16,512]{1,0:T(8,128)(2,1)S(1)} %get-tuple-element.72), channel_id=1, source_target_pairs={{0,1},{1,2},{2,3},{3,4},{4,5},{5,6},{6,7},{7,0},{8,9},{9,10},{10,1... | collective-permute-start | bytes 49160 | tf_op jit(solution)/shard_map/ppermute | solution.py:46
  9.7 2.5 %pack_edges.1 = (bf16[2048,128]{1,0:T(8,128)(2,1)}, bf16[160,128]{1,0:T(8,128)(2,1)S(1)}) custom-call(s32[1]{0:T(128)} %bitcast.3.me_ref, bf16[160,512]{1,0:T(8,128)(2,1)} %long_ref, s32[1,160]{1,0:T(1,128)} %bitcast.27, s32[1,160]{1,0:T(1,128)} %bitcast.28), custom_call_target="tpu_custom_call" | custom-call | flops 12000000000 | tf_op jit(solution)/shard_map/pack_edges/pallas_call | solution.py:345
  12.3 0.6 collective-permute-done.4.right_ref
  12.9 1.3 %collective-permute-start.6 = (bf16[112,512]{1,0:T(8,128)(2,1)S(1)}, bf16[112,512]{1,0:T(8,128)(2,1)S(1)}, u32[]{:S(2)}, u32[]{:S(2)}) collective-permute-start(bf16[112,512]{1,0:T(8,128)(2,1)S(1)} %get-tuple-element.84), channel_id=1, source_target_pairs={{0,8},{8,16},{16,24},{24,32},{32,40},{40,48},{48,56},{56,64},{64,7... | collective-permute-start | bytes 344072 | tf_op jit(solution)/shard_map/ppermute | solution.py:46
  14.2 3.6 %collective-permute-start.7 = (bf16[112,512]{1,0:T(8,128)(2,1)S(1)}, bf16[112,512]{1,0:T(8,128)(2,1)}, u32[]{:S(2)}, u32[]{:S(2)}) collective-permute-start(bf16[112,512]{1,0:T(8,128)(2,1)S(1)} %get-tuple-element.85), channel_id=1, source_target_pairs={{0,120},{8,0},{16,8},{24,16},{32,24},{40,32},{48,40},{56,48},{64,5... | collective-permute-start | bytes 344072 | tf_op jit(solution)/shard_map/ppermute | solution.py:46
  17.8 10.7 %all-to-all-start = ((bf16[128,16,128]{2,1,0:T(8,128)(2,1)}), bf16[128,16,128]{2,1,0:T(8,128)(2,1)}, u32[]{:S(2)}, u32[]{:S(2)}) async-start(bf16[128,16,128]{2,1,0:T(8,128)(2,1)} %bitcast.8), calls=%async_computation | async-start | bytes 1048576 | tf_op jit(solution)/shard_map/all_to_all | solution.py:546
  28.5 0.6 copy-done.18
  29.1 0.6 copy-done.17
  29.8 1.9 %join_near.2 = (bf16[320,512]{1,0:T(8,128)(2,1)}, bf16[64,512]{1,0:T(8,128)(2,1)}) custom-call(bf16[80,512]{1,0:T(8,128)(2,1)} %copy-done.16, bf16[80,512]{1,0:T(8,128)(2,1)} %copy-done.18, bf16[112,512]{1,0:T(8,128)(2,1)} %copy-done.17, bf16[112,512]{1,0:T(8,128)(2,1)} %collective-permute-done.7.down_ref), custom_call_target="tpu_custom_call" | custom-call | flops 3000000000 | tf_op jit(solution)/shard_map/join_near/pallas_call | solution.py:243
  31.7 3.3 %collective-permute-start.10 = (bf16[320,512]{1,0:T(8,128)(2,1)}, bf16[320,512]{1,0:T(8,128)(2,1)}, u32[]{:S(2)}, u32[]{:S(2)}) collective-permute-start(bf16[320,512]{1,0:T(8,128)(2,1)} %get-tuple-element.88.rest_0_), channel_id=1, source_target_pairs={{0,6},{1,7},{2,0},{3,1},{4,2},{5,3},{6,4},{7,5},{8,14},{9,15},{10,... | collective-permute-start | bytes 983048 | tf_op jit(solution)/shard_map/ppermute | solution.py:26
  35.2 0.8 collective-permute-start.8
  35.9 1.2 %collective-permute-start.11 = (bf16[320,512]{1,0:T(8,128)(2,1)}, bf16[320,512]{1,0:T(8,128)(2,1)}, u32[]{:S(2)}, u32[]{:S(2)}) collective-permute-start(bf16[320,512]{1,0:T(8,128)(2,1)} %get-tuple-element.88.rest_0_), channel_id=1, source_target_pairs={{0,1},{1,0},{2,3},{3,2},{4,5},{5,4},{6,7},{7,6},{8,9},{9,8},{10,11... | collective-permute-start | bytes 983048 | tf_op jit(solution)/shard_map/ppermute | solution.py:26
  37.1 4.7 %all-to-all-done = bf16[128,16,128]{2,1,0:T(8,128)(2,1)} async-done(((bf16[128,16,128]{2,1,0:T(8,128)(2,1)}), bf16[128,16,128]{2,1,0:T(8,128)(2,1)}, u32[]{:S(2)}, u32[]{:S(2)}) %all-to-all-start) | async-done | bytes 524320 | tf_op jit(solution)/shard_map/all_to_all | solution.py:546
  41.9 2.4 %unpack_edges.1 = (bf16[384,512]{1,0:T(8,128)(2,1)S(1)}, bf16[384,2560]{1,0:T(8,128)(2,1)S(1)}, bf16[384,128]{1,0:T(8,128)(2,1)S(1)}, bf16[320,384]{1,0:T(8,128)(2,1)S(1)}) custom-call(bf16[2048,128]{1,0:T(8,128)(2,1)} %bitcast.9.arrived_ref, bf16[60,320]{1,0:T(8,128)(2,1)S(1)} %get-tuple-element.90.choose_ref), custom_call_target="tpu_custom_call" | custom-call | tf_op jit(solution)/shard_map/unpack_edges/pallas_call | solution.py:386
  44.3 0.8 copy-done.12
  45.5 1.5 %copy-done.5 = bf16[16,20,6,512]{3,0,2,1:T(8,128)(2,1)S(1)} copy-done((bf16[16,20,6,512]{3,0,2,1:T(8,128)(2,1)S(1)}, bf16[16,20,6,512]{3,0,2,1:T(8,128)(2,1)}, u32[]{:S(2)}) %copy-start.5) | copy-done | bytes 1966104
  47.0 0.8 copy-done.9
  47.9 0.7 copy-done.11
  48.6 5.9 %fine0.1 = (bf16[1920,512]{1,0:T(8,128)(2,1)S(1)}, f32[320,512]{1,0:T(8,128)S(1)}) custom-call(bf16[1920,512]{1,0:T(8,128)(2,1)S(1)} %bitcast.22, bf16[1920,256]{1,0:T(8,128)(2,1)S(1)} %selection.1.picks_ref, bf16[320,512]{1,0:T(8,128)(2,1)S(1)} %bitcast.20, bf16[16,512]{1,0:T(8,128)(2,1)S(1)} %collective-permute-done.3.left_ref, ...), custom_call_target="tpu_custom_call" | custom-call | tf_op jit(solution)/shard_map/fine0/pallas_call | solution.py:129
  54.5 1.2 %collective-permute-start.12 = (bf16[320,512]{1,0:T(8,128)(2,1)}, bf16[320,512]{1,0:T(8,128)(2,1)S(1)}, u32[]{:S(2)}, u32[]{:S(2)}) collective-permute-start(bf16[320,512]{1,0:T(8,128)(2,1)} %collective-permute-done.8.rest_1_), channel_id=1, source_target_pairs={{0,1},{1,0},{2,3},{3,2},{4,5},{5,4},{6,7},{7,6},{8,9},{9,8},{10,11... | collective-permute-start | bytes 983048 | tf_op jit(solution)/shard_map/ppermute | solution.py:26
  56.3 1.0 collective-permute-done.12.rest_5_
  57.7 0.5 collective-permute-done.14.rest_7_
  58.2 5.3 %coarse0.1 = (bf16[320,512]{1,0:T(8,128)(2,1)S(1)}, bf16[384,512]{1,0:T(8,128)(2,1)S(1)}, bf16[20,512]{1,0:T(8,128)(2,1)S(1)}, bf16[20,512]{1,0:T(8,128)(2,1)S(1...) custom-call(bf16[384,512]{1,0:T(8,128)(2,1)S(1)} %get-tuple-element., ...), custom_call_target="tpu_custom_call" | custom-call | tf_op jit(solution)/shard_map/coarse0/pallas_call | solution.py:464
  63.5 1.0 collective-permute-start.17
  64.4 1.2 %collective-permute-start.16 = (bf16[20,512]{1,0:T(8,128)(2,1)S(1)}, bf16[20,512]{1,0:T(8,128)(2,1)S(1)}, u32[]{:S(2)}, u32[]{:S(2)}) collective-permute-start(bf16[20,512]{1,0:T(8,128)(2,1)S(1)} %get-tuple-element.107.own_ref), channel_id=1, source_target_pairs={{0,64},{8,72},{16,80},{24,88},{32,96},{40,104},{48,112},{56,120},{... | collective-permute-start | bytes 61448 | tf_op jit(solution)/shard_map/ppermute | solution.py:46
  65.6 0.6 collective-permute-start.18
  66.2 0.5 collective-permute-start.19
  66.7 0.7 collective-permute-done.18.left_ref
  67.4 2.3 %collective-permute-done.19.right_ref = bf16[16,512]{1,0:T(8,128)(2,1)S(1)} collective-permute-done((bf16[16,512]{1,0:T(8,128)(2,1)S(1)}, bf16[16,512]{1,0:T(8,128)(2,1)S(1)}, u32[]{:S(2)}, u32[]{:S(2)}) %collective-permute-start.19) | collective-permute-done | bytes 16416 | tf_op jit(solution)/shard_map/ppermute | solution.py:46
  69.8 0.5 collective-permute-start.21
  70.3 4.4 %collective-permute-start.22 = (bf16[112,512]{1,0:T(8,128)(2,1)S(1)}, bf16[112,512]{1,0:T(8,128)(2,1)S(1)}, u32[]{:S(2)}, u32[]{:S(2)}) collective-permute-start(bf16[112,512]{1,0:T(8,128)(2,1)S(1)} %get-tuple-element.114), channel_id=1, source_target_pairs={{0,120},{8,0},{16,8},{24,16},{32,24},{40,32},{48,40},{56,48},{64,5... | collective-permute-start | bytes 344072 | tf_op jit(solution)/shard_map/ppermute | solution.py:46
  74.7 6.9 %collective-permute-done.20.two_ref = bf16[80,512]{1,0:T(8,128)(2,1)S(1)} collective-permute-done((bf16[80,512]{1,0:T(8,128)(2,1)S(1)}, bf16[80,512]{1,0:T(8,128)(2,1)S(1)}, u32[]{:S(2)}, u32[]{:S(2)}) %collective-permute-start.20) | collective-permute-done | bytes 81952 | tf_op jit(solution)/shard_map/ppermute | solution.py:46
  81.6 0.6 join_near.3
  82.2 4.0 %collective-permute-start.25 = (bf16[320,512]{1,0:T(8,128)(2,1)S(1)}, bf16[320,512]{1,0:T(8,128)(2,1)S(1)}, u32[]{:S(2)}, u32[]{:S(2)}) collective-permute-start(bf16[320,512]{1,0:T(8,128)(2,1)S(1)} %get-tuple-element.117.rest_0_), channel_id=1, source_target_pairs={{0,6},{1,7},{2,0},{3,1},{4,2},{5,3},{6,4},{7,5},{8,14},{9,15},{10,... | collective-permute-start | bytes 983048 | tf_op jit(solution)/shard_map/ppermute | solution.py:26
  86.2 0.7 collective-permute-start.23
  86.8 1.0 collective-permute-start.26
  87.8 2.3 %own0.1 = (bf16[160,512]{1,0:T(8,128)(2,1)S(1)}, bf16[704,2560]{1,0:T(8,128)(2,1)S(1)}) custom-call(bf16[160,512]{1,0:T(8,128)(2,1)S(1)} %copy-done.6, bf16[160,128]{1,0:T(8,128)(2,1)S(1)} %copy-done.14, bf16[384,2560]{1,0:T(8,128)(2,1)S(1)} %get-tuple-element.100.sends_ref, bf16[2560,512]{1,0:T(8,128)(2,1)S(1)} %get-tuple-element.124.table_ref, ...), custom_call_target="tpu_custom_call" | custom-call | tf_op jit(solution)/shard_map/own0/pallas_call | solution.py:494
  90.1 6.7 %fine1.1 = (bf16[1920,512]{1,0:T(8,128)(2,1)}, f32[320,512]{1,0:T(8,128)S(1)}) custom-call(bf16[1920,512]{1,0:T(8,128)(2,1)S(1)} %get-tuple-element.118.fine_ref, bf16[1920,256]{1,0:T(8,128)(2,1)S(1)} %selection.1.picks_ref, bf16[320,512]{1,0:T(8,128)(2,1)S(1)} %get-tuple-element.119.latents_ref, bf16[16,512]{1,0:T(8,128)(2,1)S(1)} %collective-permute-done.18.left_ref, ...), custom_call_target="tpu_custom_call" | custom-call | tf_op jit(solution)/shard_map/fine1/pallas_call | solution.py:129
  96.8 3.9 %collective-permute-done.25.rest_3_ = bf16[320,512]{1,0:T(8,128)(2,1)S(1)} collective-permute-done((bf16[320,512]{1,0:T(8,128)(2,1)S(1)}, bf16[320,512]{1,0:T(8,128)(2,1)S(1)}, u32[]{:S(2)}, u32[]{:S(2)}) %collective-permute-start.25) | collective-permute-done | bytes 327712 | tf_op jit(solution)/shard_map/ppermute | solution.py:26
  100.7 3.0 %collective-permute-done.23.rest_1_ = bf16[320,512]{1,0:T(8,128)(2,1)S(1)} collective-permute-done((bf16[320,512]{1,0:T(8,128)(2,1)S(1)}, bf16[320,512]{1,0:T(8,128)(2,1)S(1)}, u32[]{:S(2)}, u32[]{:S(2)}) %collective-permute-start.23) | collective-permute-done | bytes 327712 | tf_op jit(solution)/shard_map/ppermute | solution.py:26
  103.7 0.9 collective-permute-start.27
  104.5 0.5 collective-permute-start.29
  105.0 0.7 collective-permute-done.27.rest_5_
  106.2 0.5 collective-permute-done.29.rest_7_
  106.7 5.6 %coarse1.1 = (bf16[320,512]{1,0:T(8,128)(2,1)}, bf16[160,512]{1,0:T(8,128)(2,1)}) custom-call(bf16[384,512]{1,0:T(8,128)(2,1)S(1)} %get-tuple-element.127.long_ref, bf16[160,512]{1,0:T(8,128)(2,1)S(1)} %get-tuple-element.128.own_ref, bf16[704,2560]{1,0:T(8,128)(2,1)S(1)} %get-tuple-element.129.sends_ref, bf16[384,128]{1,0:T(8,128)(2,1)S(1)} %get-tuple-element.101.recvs_ref, ...), custom_call_target="tpu_custom_call" | custom-call | tf_op jit(solution)/shard_map/coarse1/pallas_call | solution.py:464
  (65 shorter events, 2.6 us)
Async XLA Ops:
  2.0 10.9 %collective-permute-start.2 = (bf16[20,512]{1,0:T(8,128)(2,1)S(1)}, bf16[20,512]{1,0:T(8,128)(2,1)S(1)}, u32[]{:S(2)}, u32[]{:S(2)}) collective-permute-start(bf16[20,512]{1,0:T(8,128)(2,1)S(1)} %get-tuple-element.71.own_ref), channel_id=1, source_target_pairs={{0,96},{8,104},{16,112},{24,120},{32,0},{40,8},{48,16},{56,24},{64... | collective-permute-start | bytes 61448 | tf_op jit(solution)/shard_map/ppermute | solution.py:46
  5.6 7.3 %collective-permute-start.1 = (bf16[20,512]{1,0:T(8,128)(2,1)S(1)}, bf16[20,512]{1,0:T(8,128)(2,1)S(1)}, u32[]{:S(2)}, u32[]{:S(2)}) collective-permute-start(bf16[20,512]{1,0:T(8,128)(2,1)S(1)} %get-tuple-element.71.own_ref), channel_id=1, source_target_pairs={{0,64},{8,72},{16,80},{24,88},{32,96},{40,104},{48,112},{56,120},{... | collective-permute-start | bytes 61448 | tf_op jit(solution)/shard_map/ppermute | solution.py:46
  6.0 6.9 %collective-permute-start = (bf16[20,512]{1,0:T(8,128)(2,1)S(1)}, bf16[20,512]{1,0:T(8,128)(2,1)S(1)}, u32[]{:S(2)}, u32[]{:S(2)}) collective-permute-start(bf16[20,512]{1,0:T(8,128)(2,1)S(1)} %get-tuple-element.71.own_ref), channel_id=1, source_target_pairs={{0,32},{8,40},{16,48},{24,56},{32,64},{40,72},{48,80},{56,88},{64,... | collective-permute-start | bytes 61448 | tf_op jit(solution)/shard_map/ppermute | solution.py:46
  6.7 5.6 %collective-permute-start.3 = (bf16[16,512]{1,0:T(8,128)(2,1)S(1)}, bf16[16,512]{1,0:T(8,128)(2,1)S(1)}, u32[]{:S(2)}, u32[]{:S(2)}) collective-permute-start(bf16[16,512]{1,0:T(8,128)(2,1)S(1)} %get-tuple-element.72), channel_id=1, source_target_pairs={{0,1},{1,2},{2,3},{3,4},{4,5},{5,6},{6,7},{7,0},{8,9},{9,10},{10,1... | collective-permute-start | bytes 49160 | tf_op jit(solution)/shard_map/ppermute | solution.py:46
  9.7 3.2 %collective-permute-start.4 = (bf16[16,512]{1,0:T(8,128)(2,1)S(1)}, bf16[16,512]{1,0:T(8,128)(2,1)S(1)}, u32[]{:S(2)}, u32[]{:S(2)}) collective-permute-start(bf16[16,512]{1,0:T(8,128)(2,1)S(1)} %get-tuple-element.73), channel_id=1, source_target_pairs={{0,7},{1,0},{2,1},{3,2},{4,3},{5,4},{6,5},{7,6},{8,15},{9,8},{10,9... | collective-permute-start | bytes 49160 | tf_op jit(solution)/shard_map/ppermute | solution.py:46
  12.2 16.3 %copy-start.13 = (bf16[160,128]{1,0:T(8,128)(2,1)}, bf16[160,128]{1,0:T(8,128)(2,1)S(1)}, u32[]{:S(2)}) copy-start(bf16[160,128]{1,0:T(8,128)(2,1)S(1)} %get-tuple-element.123.tags_ref) | copy-start | bytes 122884
  12.9 15.7 %copy-start.10 = (bf16[16,512]{1,0:T(8,128)(2,1)}, bf16[16,512]{1,0:T(8,128)(2,1)S(1)}, u32[]{:S(2)}) copy-start(bf16[16,512]{1,0:T(8,128)(2,1)S(1)} %collective-permute-done.4.right_ref) | copy-start | bytes 49156
  12.9 15.6 %copy-start.16 = (bf16[80,512]{1,0:T(8,128)(2,1)}, bf16[80,512]{1,0:T(8,128)(2,1)S(1)}, u32[]{:S(2)}) copy-start(bf16[80,512]{1,0:T(8,128)(2,1)S(1)} %get-tuple-element.83.own_ref) | copy-start | bytes 245764
  12.9 15.6 %collective-permute-start.6 = (bf16[112,512]{1,0:T(8,128)(2,1)S(1)}, bf16[112,512]{1,0:T(8,128)(2,1)S(1)}, u32[]{:S(2)}, u32[]{:S(2)}) collective-permute-start(bf16[112,512]{1,0:T(8,128)(2,1)S(1)} %get-tuple-element.84), channel_id=1, source_target_pairs={{0,8},{8,16},{16,24},{24,32},{32,40},{40,48},{48,56},{56,64},{64,7... | collective-permute-start | bytes 344072 | tf_op jit(solution)/shard_map/ppermute | solution.py:46
  14.2 15.6 %collective-permute-start.7 = (bf16[112,512]{1,0:T(8,128)(2,1)S(1)}, bf16[112,512]{1,0:T(8,128)(2,1)}, u32[]{:S(2)}, u32[]{:S(2)}) collective-permute-start(bf16[112,512]{1,0:T(8,128)(2,1)S(1)} %get-tuple-element.85), channel_id=1, source_target_pairs={{0,120},{8,0},{16,8},{24,16},{32,24},{40,32},{48,40},{56,48},{64,5... | collective-permute-start | bytes 344072 | tf_op jit(solution)/shard_map/ppermute | solution.py:46
  17.8 10.7 %collective-permute-start.5 = (bf16[80,512]{1,0:T(8,128)(2,1)S(1)}, bf16[80,512]{1,0:T(8,128)(2,1)S(1)}, u32[]{:S(2)}, u32[]{:S(2)}) collective-permute-start(bf16[80,512]{1,0:T(8,128)(2,1)S(1)} %get-tuple-element.83.own_ref), channel_id=1, source_target_pairs={{0,16},{8,24},{16,32},{24,40},{32,48},{40,56},{48,64},{56,72},{64,... | collective-permute-start | bytes 245768 | tf_op jit(solution)/shard_map/ppermute | solution.py:46
  17.8 24.1 %all-to-all-start = ((bf16[128,16,128]{2,1,0:T(8,128)(2,1)}), bf16[128,16,128]{2,1,0:T(8,128)(2,1)}, u32[]{:S(2)}, u32[]{:S(2)}) async-start(bf16[128,16,128]{2,1,0:T(8,128)(2,1)} %bitcast.8), calls=%async_computation | async-start | bytes 1048576 | tf_op jit(solution)/shard_map/all_to_all | solution.py:546
  28.5 17.0 %copy-start.4 = (bf16[16,20,512]{2,0,1:T(8,128)(2,1)S(1)}, bf16[16,20,512]{2,0,1:T(8,128)(2,1)}, u32[]{:S(2)}) copy-start(bf16[16,20,512]{2,0,1:T(8,128)(2,1)} %param.13) | copy-start | bytes 983044
  28.5 17.0 %copy-start.8 = (f32[2,512]{1,0:T(2,128)S(1)}, f32[2,512]{1,0:T(2,128)}, u32[]{:S(2)}) copy-start(f32[2,512]{1,0:T(2,128)} %eg_ref.5) | copy-start | bytes 12292
  29.8 15.7 %copy-start = (bf16[2,1536,512]{2,1,0:T(8,128)(2,1)S(1)}, bf16[2,1536,512]{2,1,0:T(8,128)(2,1)}, u32[]{:S(2)}) copy-start(bf16[2,1536,512]{2,1,0:T(8,128)(2,1)} %ei_ref.5) | copy-start | bytes 9437188
  31.7 22.7 %collective-permute-start.10 = (bf16[320,512]{1,0:T(8,128)(2,1)}, bf16[320,512]{1,0:T(8,128)(2,1)}, u32[]{:S(2)}, u32[]{:S(2)}) collective-permute-start(bf16[320,512]{1,0:T(8,128)(2,1)} %get-tuple-element.88.rest_0_), channel_id=1, source_target_pairs={{0,6},{1,7},{2,0},{3,1},{4,2},{5,3},{6,4},{7,5},{8,14},{9,15},{10,... | collective-permute-start | bytes 983048 | tf_op jit(solution)/shard_map/ppermute | solution.py:26
  35.0 19.4 %collective-permute-start.9 = (bf16[320,512]{1,0:T(8,128)(2,1)}, bf16[320,512]{1,0:T(8,128)(2,1)}, u32[]{:S(2)}, u32[]{:S(2)}) collective-permute-start(bf16[320,512]{1,0:T(8,128)(2,1)} %get-tuple-element.88.rest_0_), channel_id=1, source_target_pairs={{0,4},{1,5},{2,6},{3,7},{4,0},{5,1},{6,2},{7,3},{8,12},{9,13},{10,... | collective-permute-start | bytes 983048 | tf_op jit(solution)/shard_map/ppermute | solution.py:26
  35.2 19.3 %collective-permute-start.8 = (bf16[320,512]{1,0:T(8,128)(2,1)}, bf16[320,512]{1,0:T(8,128)(2,1)}, u32[]{:S(2)}, u32[]{:S(2)}) collective-permute-start(bf16[320,512]{1,0:T(8,128)(2,1)} %get-tuple-element.88.rest_0_), channel_id=1, source_target_pairs={{0,2},{1,3},{2,4},{3,5},{4,6},{5,7},{6,0},{7,1},{8,10},{9,11},{10,... | collective-permute-start | bytes 983048 | tf_op jit(solution)/shard_map/ppermute | solution.py:26
  35.9 20.3 %collective-permute-start.11 = (bf16[320,512]{1,0:T(8,128)(2,1)}, bf16[320,512]{1,0:T(8,128)(2,1)}, u32[]{:S(2)}, u32[]{:S(2)}) collective-permute-start(bf16[320,512]{1,0:T(8,128)(2,1)} %get-tuple-element.88.rest_0_), channel_id=1, source_target_pairs={{0,1},{1,0},{2,3},{3,2},{4,5},{5,4},{6,7},{7,6},{8,9},{9,8},{10,11... | collective-permute-start | bytes 983048 | tf_op jit(solution)/shard_map/ppermute | solution.py:26
  41.9 3.6 %copy-start.1 = (bf16[2,512,512]{2,1,0:T(8,128)(2,1)S(1)}, bf16[2,512,512]{2,1,0:T(8,128)(2,1)}, u32[]{:S(2)}) copy-start(bf16[2,512,512]{2,1,0:T(8,128)(2,1)} %eo_ref.5) | copy-start | bytes 3145732
  44.3 0.8 copy-start.12
  45.5 1.5 %copy-start.5 = (bf16[16,20,6,512]{3,0,2,1:T(8,128)(2,1)S(1)}, bf16[16,20,6,512]{3,0,2,1:T(8,128)(2,1)}, u32[]{:S(2)}) copy-start(bf16[16,20,6,512]{3,0,2,1:T(8,128)(2,1)} %param.14) | copy-start | bytes 5898244
  47.0 0.8 copy-start.9
  47.9 0.7 copy-start.11
  48.6 9.6 %copy-start.2 = (bf16[2,1024,512]{2,1,0:T(8,128)(2,1)S(1)}, bf16[2,1024,512]{2,1,0:T(8,128)(2,1)}, u32[]{:S(2)}) copy-start(bf16[2,1024,512]{2,1,0:T(8,128)(2,1)} %ni_ref.3) | copy-start | bytes 6291460
  48.6 9.6 %copy-start.3 = (bf16[2,512,512]{2,1,0:T(8,128)(2,1)S(1)}, bf16[2,512,512]{2,1,0:T(8,128)(2,1)}, u32[]{:S(2)}) copy-start(bf16[2,512,512]{2,1,0:T(8,128)(2,1)} %no_ref.3) | copy-start | bytes 3145732
  48.6 9.6 %copy-start.6 = (bf16[160,512]{1,0:T(8,128)(2,1)S(1)}, bf16[160,512]{1,0:T(8,128)(2,1)}, u32[]{:S(2)}) copy-start(bf16[160,512]{1,0:T(8,128)(2,1)} %long_ref) | copy-start | bytes 491524
  48.6 9.6 %copy-start.7 = (bf16[320,512]{1,0:T(8,128)(2,1)S(1)}, bf16[320,512]{1,0:T(8,128)(2,1)}, u32[]{:S(2)}) copy-start(bf16[320,512]{1,0:T(8,128)(2,1)} %get-tuple-element.88.rest_0_) | copy-start | bytes 983044
  48.6 9.6 %copy-start.15 = (f32[2,512]{1,0:T(2,128)S(1)}, f32[2,512]{1,0:T(2,128)}, u32[]{:S(2)}) copy-start(f32[2,512]{1,0:T(2,128)} %ng_ref.3) | copy-start | bytes 12292
  54.5 2.7 %collective-permute-start.12 = (bf16[320,512]{1,0:T(8,128)(2,1)}, bf16[320,512]{1,0:T(8,128)(2,1)S(1)}, u32[]{:S(2)}, u32[]{:S(2)}) collective-permute-start(bf16[320,512]{1,0:T(8,128)(2,1)} %collective-permute-done.8.rest_1_), channel_id=1, source_target_pairs={{0,1},{1,0},{2,3},{3,2},{4,5},{5,4},{6,7},{7,6},{8,9},{9,8},{10,11... | collective-permute-start | bytes 983048 | tf_op jit(solution)/shard_map/ppermute | solution.py:26
  55.8 1.9 %collective-permute-start.13 = (bf16[320,512]{1,0:T(8,128)(2,1)}, bf16[320,512]{1,0:T(8,128)(2,1)S(1)}, u32[]{:S(2)}, u32[]{:S(2)}) collective-permute-start(bf16[320,512]{1,0:T(8,128)(2,1)} %collective-permute-done.9.rest_2_), channel_id=1, source_target_pairs={{0,1},{1,0},{2,3},{3,2},{4,5},{5,4},{6,7},{7,6},{8,9},{9,8},{10,11... | collective-permute-start | bytes 983048 | tf_op jit(solution)/shard_map/ppermute | solution.py:26
  55.9 2.3 %collective-permute-start.14 = (bf16[320,512]{1,0:T(8,128)(2,1)}, bf16[320,512]{1,0:T(8,128)(2,1)S(1)}, u32[]{:S(2)}, u32[]{:S(2)}) collective-permute-start(bf16[320,512]{1,0:T(8,128)(2,1)} %collective-permute-done.10.rest_3_), channel_id=1, source_target_pairs={{0,1},{1,0},{2,3},{3,2},{4,5},{5,4},{6,7},{7,6},{8,9},{9,8},{10,11... | collective-permute-start | bytes 983048 | tf_op jit(solution)/shard_map/ppermute | solution.py:26
  63.5 6.2 %collective-permute-start.17 = (bf16[20,512]{1,0:T(8,128)(2,1)S(1)}, bf16[20,512]{1,0:T(8,128)(2,1)S(1)}, u32[]{:S(2)}, u32[]{:S(2)}) collective-permute-start(bf16[20,512]{1,0:T(8,128)(2,1)S(1)} %get-tuple-element.107.own_ref), channel_id=1, source_target_pairs={{0,96},{8,104},{16,112},{24,120},{32,0},{40,8},{48,16},{56,24},{64... | collective-permute-start | bytes 61448 | tf_op jit(solution)/shard_map/ppermute | solution.py:46
  64.4 5.3 %collective-permute-start.16 = (bf16[20,512]{1,0:T(8,128)(2,1)S(1)}, bf16[20,512]{1,0:T(8,128)(2,1)S(1)}, u32[]{:S(2)}, u32[]{:S(2)}) collective-permute-start(bf16[20,512]{1,0:T(8,128)(2,1)S(1)} %get-tuple-element.107.own_ref), channel_id=1, source_target_pairs={{0,64},{8,72},{16,80},{24,88},{32,96},{40,104},{48,112},{56,120},{... | collective-permute-start | bytes 61448 | tf_op jit(solution)/shard_map/ppermute | solution.py:46
  65.6 4.2 %collective-permute-start.15 = (bf16[20,512]{1,0:T(8,128)(2,1)S(1)}, bf16[20,512]{1,0:T(8,128)(2,1)S(1)}, u32[]{:S(2)}, u32[]{:S(2)}) collective-permute-start(bf16[20,512]{1,0:T(8,128)(2,1)S(1)} %get-tuple-element.107.own_ref), channel_id=1, source_target_pairs={{0,32},{8,40},{16,48},{24,56},{32,64},{40,72},{48,80},{56,88},{64,... | collective-permute-start | bytes 61448 | tf_op jit(solution)/shard_map/ppermute | solution.py:46
  65.6 1.8 %collective-permute-start.18 = (bf16[16,512]{1,0:T(8,128)(2,1)S(1)}, bf16[16,512]{1,0:T(8,128)(2,1)S(1)}, u32[]{:S(2)}, u32[]{:S(2)}) collective-permute-start(bf16[16,512]{1,0:T(8,128)(2,1)S(1)} %get-tuple-element.108), channel_id=1, source_target_pairs={{0,1},{1,2},{2,3},{3,4},{4,5},{5,6},{6,7},{7,0},{8,9},{9,10},{10,1... | collective-permute-start | bytes 49160 | tf_op jit(solution)/shard_map/ppermute | solution.py:46
  66.2 3.5 %collective-permute-start.19 = (bf16[16,512]{1,0:T(8,128)(2,1)S(1)}, bf16[16,512]{1,0:T(8,128)(2,1)S(1)}, u32[]{:S(2)}, u32[]{:S(2)}) collective-permute-start(bf16[16,512]{1,0:T(8,128)(2,1)S(1)} %get-tuple-element.109), channel_id=1, source_target_pairs={{0,7},{1,0},{2,1},{3,2},{4,3},{5,4},{6,5},{7,6},{8,15},{9,8},{10,9... | collective-permute-start | bytes 49160 | tf_op jit(solution)/shard_map/ppermute | solution.py:46
  69.8 11.8 %collective-permute-start.21 = (bf16[112,512]{1,0:T(8,128)(2,1)S(1)}, bf16[112,512]{1,0:T(8,128)(2,1)S(1)}, u32[]{:S(2)}, u32[]{:S(2)}) collective-permute-start(bf16[112,512]{1,0:T(8,128)(2,1)S(1)} %get-tuple-element.113), channel_id=1, source_target_pairs={{0,8},{8,16},{16,24},{24,32},{32,40},{40,48},{48,56},{56,64},{64,7... | collective-permute-start | bytes 344072 | tf_op jit(solution)/shard_map/ppermute | solution.py:46
  70.3 11.3 %collective-permute-start.22 = (bf16[112,512]{1,0:T(8,128)(2,1)S(1)}, bf16[112,512]{1,0:T(8,128)(2,1)S(1)}, u32[]{:S(2)}, u32[]{:S(2)}) collective-permute-start(bf16[112,512]{1,0:T(8,128)(2,1)S(1)} %get-tuple-element.114), channel_id=1, source_target_pairs={{0,120},{8,0},{16,8},{24,16},{32,24},{40,32},{48,40},{56,48},{64,5... | collective-permute-start | bytes 344072 | tf_op jit(solution)/shard_map/ppermute | solution.py:46
  74.7 13.1 %copy-start.14 = (bf16[160,128]{1,0:T(8,128)(2,1)S(1)}, bf16[160,128]{1,0:T(8,128)(2,1)}, u32[]{:S(2)}) copy-start(bf16[160,128]{1,0:T(8,128)(2,1)} %copy-done.13) | copy-start | bytes 122884
  74.7 6.9 %collective-permute-start.20 = (bf16[80,512]{1,0:T(8,128)(2,1)S(1)}, bf16[80,512]{1,0:T(8,128)(2,1)S(1)}, u32[]{:S(2)}, u32[]{:S(2)}) collective-permute-start(bf16[80,512]{1,0:T(8,128)(2,1)S(1)} %get-tuple-element.112.own_ref), channel_id=1, source_target_pairs={{0,16},{8,24},{16,32},{24,40},{32,48},{40,56},{48,64},{56,72},{64,... | collective-permute-start | bytes 245768 | tf_op jit(solution)/shard_map/ppermute | solution.py:46
  82.2 18.5 %collective-permute-start.25 = (bf16[320,512]{1,0:T(8,128)(2,1)S(1)}, bf16[320,512]{1,0:T(8,128)(2,1)S(1)}, u32[]{:S(2)}, u32[]{:S(2)}) collective-permute-start(bf16[320,512]{1,0:T(8,128)(2,1)S(1)} %get-tuple-element.117.rest_0_), channel_id=1, source_target_pairs={{0,6},{1,7},{2,0},{3,1},{4,2},{5,3},{6,4},{7,5},{8,14},{9,15},{10,... | collective-permute-start | bytes 983048 | tf_op jit(solution)/shard_map/ppermute | solution.py:26
  86.1 14.5 %collective-permute-start.24 = (bf16[320,512]{1,0:T(8,128)(2,1)S(1)}, bf16[320,512]{1,0:T(8,128)(2,1)S(1)}, u32[]{:S(2)}, u32[]{:S(2)}) collective-permute-start(bf16[320,512]{1,0:T(8,128)(2,1)S(1)} %get-tuple-element.117.rest_0_), channel_id=1, source_target_pairs={{0,4},{1,5},{2,6},{3,7},{4,0},{5,1},{6,2},{7,3},{8,12},{9,13},{10,... | collective-permute-start | bytes 983048 | tf_op jit(solution)/shard_map/ppermute | solution.py:26
  86.2 17.5 %collective-permute-start.23 = (bf16[320,512]{1,0:T(8,128)(2,1)S(1)}, bf16[320,512]{1,0:T(8,128)(2,1)S(1)}, u32[]{:S(2)}, u32[]{:S(2)}) collective-permute-start(bf16[320,512]{1,0:T(8,128)(2,1)S(1)} %get-tuple-element.117.rest_0_), channel_id=1, source_target_pairs={{0,2},{1,3},{2,4},{3,5},{4,6},{5,7},{6,0},{7,1},{8,10},{9,11},{10,... | collective-permute-start | bytes 983048 | tf_op jit(solution)/shard_map/ppermute | solution.py:26
  86.8 18.2 %collective-permute-start.26 = (bf16[320,512]{1,0:T(8,128)(2,1)S(1)}, bf16[320,512]{1,0:T(8,128)(2,1)S(1)}, u32[]{:S(2)}, u32[]{:S(2)}) collective-permute-start(bf16[320,512]{1,0:T(8,128)(2,1)S(1)} %get-tuple-element.117.rest_0_), channel_id=1, source_target_pairs={{0,1},{1,0},{2,3},{3,2},{4,5},{5,4},{6,7},{7,6},{8,9},{9,8},{10,11... | collective-permute-start | bytes 983048 | tf_op jit(solution)/shard_map/ppermute | solution.py:26
  103.7 2.1 %collective-permute-start.27 = (bf16[320,512]{1,0:T(8,128)(2,1)S(1)}, bf16[320,512]{1,0:T(8,128)(2,1)S(1)}, u32[]{:S(2)}, u32[]{:S(2)}) collective-permute-start(bf16[320,512]{1,0:T(8,128)(2,1)S(1)} %collective-permute-done.23.rest_1_), channel_id=1, source_target_pairs={{0,1},{1,0},{2,3},{3,2},{4,5},{5,4},{6,7},{7,6},{8,9},{9,8},{10,11... | collective-permute-start | bytes 983048 | tf_op jit(solution)/shard_map/ppermute | solution.py:26
  104.5 1.7 %collective-permute-start.28 = (bf16[320,512]{1,0:T(8,128)(2,1)S(1)}, bf16[320,512]{1,0:T(8,128)(2,1)S(1)}, u32[]{:S(2)}, u32[]{:S(2)}) collective-permute-start(bf16[320,512]{1,0:T(8,128)(2,1)S(1)} %collective-permute-done.24.rest_2_), channel_id=1, source_target_pairs={{0,1},{1,0},{2,3},{3,2},{4,5},{5,4},{6,7},{7,6},{8,9},{9,8},{10,11... | collective-permute-start | bytes 983048 | tf_op jit(solution)/shard_map/ppermute | solution.py:26
  104.5 2.2 %collective-permute-start.29 = (bf16[320,512]{1,0:T(8,128)(2,1)S(1)}, bf16[320,512]{1,0:T(8,128)(2,1)S(1)}, u32[]{:S(2)}, u32[]{:S(2)}) collective-permute-start(bf16[320,512]{1,0:T(8,128)(2,1)S(1)} %collective-permute-done.25.rest_3_), channel_id=1, source_target_pairs={{0,1},{1,0},{2,3},{3,2},{4,5},{5,4},{6,7},{7,6},{8,9},{9,8},{10,11... | collective-permute-start | bytes 983048 | tf_op jit(solution)/shard_map/ppermute | solution.py:26
  (2 other events, 1.3 us)

commit v8 on v6

--- a/solution.py
+++ b/solution.py
@@ -7,7 +7,6 @@
 
 EPSILON = 1e-05
 AXES = ("px", "py")
-RING = 16
 Z, CORE = (2, 4), (1, 2)
 BAND = 4
 TAGS = 128
@@ -33,12 +32,17 @@
 def table_row(px, py, coarse, coarse_count):
     home = jnp.floor((coarse.astype(jnp.float32) + 0.5) * (1.0 / coarse_count)).astype(jnp.int32)
     row = coarse - home * coarse_count
-    away = (px - lax.shift_right_logical(home, 3)) & (RING - 1)
-    near, far = away & 3, lax.shift_right_logical(away + 1, 2) & 3
+    home_px = lax.shift_right_logical(home, 3)
+    ky = (lax.shift_right_logical(px, 2) - lax.shift_right_logical(home_px, 2)) & 3
+    kx = (px - home_px) & 3
     home_z, home_core = lax.shift_right_logical(home, 1) & 3, home & 1
     kz = (lax.shift_right_logical(py, 1) - home_z) & 3
     kc = (py - home_core) & 1
-    return (((kc * 4 + kz) * 4 + near) * 4 + far) * coarse_count + row, home
+    return (((kc * 4 + kz) * 4 + kx) * 4 + ky) * coarse_count + row, home
+
+
+def around_x(values, step):
+    return lax.ppermute(values, "px", [(i, i // 4 * 4 + (i + step) % 4) for i in range(16)])
 
 
 def along(values, axis, step):
@@ -57,7 +61,9 @@
         from_row = lax.broadcasted_iota(jnp.int32, codes.shape, 1) + down - 1
         column = lax.broadcasted_iota(jnp.int32, codes.shape, 2)
         near = ((column & (BAND - 1)) + step) * rows + from_row
-        sender = jnp.where(from_row < 0, ABOVE + column + step, jnp.where(from_row >= rows, BELOW + column + step, near))
+        wide = column + step - 1
+        wide = jnp.where(wide < 0, columns, jnp.where(wide >= columns, columns + 1, wide))
+        sender = jnp.where(from_row < 0, ABOVE + wide, jnp.where(from_row >= rows, BELOW + wide, near))
         lanes = lax.broadcasted_iota(jnp.int32, (rows, 256), 1)
         row = lax.broadcasted_iota(jnp.int32, (rows, 256), 0)
         for c in range(columns):
@@ -90,30 +96,43 @@
     return (before.astype(jnp.float32) + scaled).astype(jnp.bfloat16)
 
 
-def fine_layer(layer, fine, picks, latents, left, right, sides, inner, outer, gain, rows):
+def fine_layer(layer, fine, picks, latents, left, right, above, below, inner, outer, gain, rows):
     edges, features = fine.shape
     nodes = latents.shape[0]
     hidden = inner.shape[2]
     near = (BAND + 2) * rows
     own = BAND * rows
+    columns = above.shape[0]
     steps = nodes // own
     block = edges // steps
     degree = edges // nodes
 
-    def body(fine_ref, picks_ref, latents_ref, left_ref, right_ref, sides_ref, inner_ref, outer_ref, gain_ref,
-             next_ref, sum_ref, send_ref, recv_ref, table_ref):
+    halo = (left, right, above, below)
+
+    def body(fine_ref, picks_ref, latents_ref, left_away, right_away, above_away, below_away, inner_ref, outer_ref, gain_ref,
+             next_ref, sum_ref, send_ref, recv_ref, table_ref, left_ref, right_ref, above_ref, below_ref, sems):
         step = pl.program_id(0)
 
         @pl.when(step == 0)
         def _():
+            fetch(
+                [(left_away, left_ref), (right_away, right_ref), (above_away, above_ref), (below_away, below_ref)], sems
+            )
             send = inner_ref[layer, features : 2 * features, :]
             project = lambda ref: dot(ref[...], send).astype(jnp.bfloat16)
-            table_ref[ABOVE : ABOVE + sides.shape[0], :] = project(sides_ref)
-            table_ref[ABOVE + sides.shape[0] :, :] = jnp.zeros((256 - ABOVE - sides.shape[0], hidden), jnp.bfloat16)
+            table_ref[ABOVE:, :] = jnp.zeros((256 - ABOVE, hidden), jnp.bfloat16)
+            table_ref[ABOVE : ABOVE + columns, :] = project(above_ref)
+            table_ref[BELOW : BELOW + columns, :] = project(below_ref)
             send_ref[rows : rows + nodes, :] = project(latents_ref)
             recv_ref[...] = dot(latents_ref[...], inner_ref[layer, 2 * features :, :]).astype(jnp.bfloat16)
-            send_ref[:rows, :] = project(left_ref)
-            send_ref[rows + nodes :, :] = project(right_ref)
+            side = project(left_ref)
+            send_ref[:rows, :] = side[:rows]
+            table_ref[ABOVE + columns : ABOVE + columns + 1, :] = side[rows : rows + 1]
+            table_ref[BELOW + columns : BELOW + columns + 1, :] = side[rows + 1 : rows + 2]
+            side = project(right_ref)
+            send_ref[rows + nodes :, :] = side[:rows]
+            table_ref[ABOVE + columns + 1 : ABOVE + columns + 2, :] = side[rows : rows + 1]
+            table_ref[BELOW + columns + 1 : BELOW + columns + 2, :] = side[rows + 1 : rows + 2]
 
         start = pl.multiple_of(step * own, own)
         table_ref[:near, :] = send_ref[pl.ds(start, near), :]
@@ -130,7 +149,7 @@
         body,
         name=f"fine{layer}",
         out_shape=(
-            pltpu.HBM(fine.shape, jnp.bfloat16),
+            jax.ShapeDtypeStruct(fine.shape, jnp.bfloat16),
             jax.ShapeDtypeStruct((nodes, features), jnp.float32),
         ),
         grid=(steps,),
@@ -138,7 +157,9 @@
             pl.BlockSpec((block, features), lambda i: (i, 0)),
             pl.BlockSpec((block, 256), lambda i: (i, 0)),
         ]
-        + [held] * 7,
+        + [held]
+        + [pl.BlockSpec(memory_space=pl.ANY)] * 4
+        + [held] * 3,
         out_specs=(
             pl.BlockSpec((block, features), lambda i: (i, 0)),
             pl.BlockSpec((own, features), lambda i: (i, 0)),
@@ -147,9 +168,11 @@
             pltpu.VMEM((nodes + 2 * rows, hidden), jnp.bfloat16),
             pltpu.VMEM((nodes, hidden), jnp.bfloat16),
             pltpu.VMEM((256, hidden), jnp.bfloat16),
+            *(pltpu.VMEM(part.shape, jnp.bfloat16) for part in halo),
+            pltpu.SemaphoreType.DMA((4,)),
         ],
         compiler_params=pltpu.CompilerParams(dimension_semantics=("arbitrary",), vmem_limit_bytes=14 * MIB),
-    )(in_hbm(fine), picks, latents, left, right, sides, inner, outer, gain)
+    )(fine, picks, latents, *(map(in_hbm, halo) if layer == 0 else halo), inner, outer, gain)
 
 
 def pick(index, width):
@@ -174,31 +197,28 @@
     first_ref[...] = rows[count + columns :]
 
 
-def join_far(own, fars, left, right, last, first):
+def join_far(own, fars, above, below, last_column, first_column):
     count, features = own.shape
-    rows = left.shape[0]
-    four = 4 * count
-    columns = last.shape[0]
-
-    def body(own_ref, far1_ref, far2_ref, far3_ref, left_ref, right_ref, last_ref, first_ref, two_ref, up_ref, down_ref):
+    rows = last_column.shape[0]
+
+    def body(own_ref, far1_ref, far2_ref, far3_ref, above_ref, below_ref, last_ref, first_ref, four_ref, right_ref, left_ref):
         for at, ref in enumerate((own_ref, far1_ref, far2_ref, far3_ref)):
-            two_ref[at * count : (at + 1) * count, :] = ref[...]
-        for out_ref, line_ref, row in ((up_ref, last_ref, rows - 1), (down_ref, first_ref, 0)):
-            out_ref[:four, :] = two_ref[...]
-            out_ref[four:, :] = jnp.zeros((out_ref.shape[0] - four, features), jnp.bfloat16)
-            out_ref[four : four + 1, :] = left_ref[row : row + 1, :]
-            out_ref[four + 1 : four + 1 + columns, :] = line_ref[...]
-            out_ref[four + 1 + columns : four + 2 + columns, :] = right_ref[row : row + 1, :]
+            four_ref[at * count : (at + 1) * count, :] = ref[...]
+        end = above_ref.shape[0] - 1
+        for out_ref, line_ref, at in ((right_ref, last_ref, end), (left_ref, first_ref, 0)):
+            out_ref[:rows, :] = line_ref[...]
+            out_ref[rows : rows + 1, :] = above_ref[at : at + 1, :]
+            out_ref[rows + 1 :, :] = below_ref[at : at + 1, :]
 
     held = pl.BlockSpec(memory_space=pltpu.VMEM)
     return pl.pallas_call(
         body,
         name="join_far",
-        out_shape=tuple(jax.ShapeDtypeStruct((n, features), jnp.bfloat16) for n in (four, four + 32, four + 32)),
+        out_shape=tuple(jax.ShapeDtypeStruct((n, features), jnp.bfloat16) for n in (4 * count, rows + 2, rows + 2)),
         in_specs=[held] * 8,
         out_specs=(held,) * 3,
         compiler_params=pltpu.CompilerParams(vmem_limit_bytes=2 * MIB),
-    )(own, *fars, left, right, last, first)
+    )(own, *fars, above, below, last_column, first_column)
 
 
 def in_hbm(values):
@@ -213,35 +233,30 @@
         copy.wait()
 
 
-def join_near(layer, own, up, two, down):
-    each, features = own.shape
-    side = BELOW - ABOVE
-
-    def body(own_ref, up_ref, two_ref, down_ref, joined_ref, sides_ref, sems):
-        part = lambda at: joined_ref.at[pl.ds(at * each, each), :]
-        fetch(
-            [
-                (own_ref, part(0)),
-                (up_ref.at[pl.ds(0, each), :], part(1)),
-                (two_ref, part(2)),
-                (down_ref.at[pl.ds(0, each), :], part(3)),
-                (up_ref.at[pl.ds(each, side), :], sides_ref.at[pl.ds(0, side), :]),
-                (down_ref.at[pl.ds(each, side), :], sides_ref.at[pl.ds(side, side), :]),
-            ],
-            sems,
-        )
-
-    away = pl.BlockSpec(memory_space=pltpu.HBM)
+def join_near(layer, *parts):
+    each, features = parts[0].shape
+    count = len(parts)
+    far = layer == 0
+    shape = (count * each, features)
+
+    def body(*refs):
+        joined_ref, sems, *near = refs[count:]
+        to = near[0] if far else joined_ref
+        fetch([(ref, to.at[pl.ds(at * each, each), :]) for at, ref in enumerate(refs[:count])], sems)
+        if far:
+            fetch([(to, joined_ref)], sems)
+
+    away = pl.BlockSpec(memory_space=pl.ANY)
     return pl.pallas_call(
         body,
         name="join_near",
         cost_estimate=pl.CostEstimate(flops=3_000_000_000, bytes_accessed=0, transcendentals=0),
-        out_shape=tuple(jax.ShapeDtypeStruct((n, features), jnp.bfloat16) for n in (4 * each, 2 * side)),
-        in_specs=[away] * 4,
-        out_specs=(away,) * 2,
-        scratch_shapes=[pltpu.SemaphoreType.DMA((6,))],
+        out_shape=pltpu.HBM(shape, jnp.bfloat16) if far else jax.ShapeDtypeStruct(shape, jnp.bfloat16),
+        in_specs=[away] * count,
+        out_specs=away,
+        scratch_shapes=[pltpu.SemaphoreType.DMA((count,))] + ([pltpu.VMEM(shape, jnp.bfloat16)] if far else []),
         compiler_params=pltpu.CompilerParams(vmem_limit_bytes=2 * MIB),
-    )(*(map(in_hbm, (own, up, two, down)) if layer == 0 else (own, up, two, down)))
+    )(*(map(in_hbm, parts) if far else parts))
 
 
 def coarse_start(coarse_slots, latents, rows, columns):
@@ -527,19 +542,18 @@
     for layer in range(layers):
         last = layer == layers - 1
         fars = [along(own, "px", 4 * s) for s in (1, 2, 3)]
+        above = along(last_row, "px", 1)
+        below = along(first_row, "px", -1)
+        if layer == 0:
+            *fars, above, below, payload = tie(*fars, above, below, payload)
+            packed = payload.reshape(devices, 16, TAGS)
+            arrived = lax.all_to_all(packed, AXES, split_axis=0, concat_axis=0, tiled=True).reshape(payload.shape)
+        four, to_right, to_left = join_far(own, fars, above, below, to_right, to_left)
         left = along(to_right, "py", 1)
         right = along(to_left, "py", -1)
-        if layer == 0:
-            *fars, left, right, payload = tie(*fars, left, right, payload)
-        joined, up, down = join_far(own, fars, left, right, last_row, first_row)
-        if layer == 0:
-            packed = payload.reshape(devices, 16, TAGS)
-            arrived = lax.all_to_all(packed, AXES, split_axis=0, concat_axis=0, tiled=True).reshape(payload.shape)
-        two = along(joined, "px", 2)
-        up = along(up, "px", 1)
-        down = along(down, "px", -1)
-        joined, sides = join_near(layer, joined, up, two, down)
-        joined, sides, own_rows = tie(joined, sides, own_rows)
+        *nears, left, right = tie(*(around_x(four, s) for s in (1, 2, 3)), left, right)
+        joined = join_near(layer, four, *nears)
+        joined, left, right, own_rows = tie(joined, left, right, own_rows)
         pieces = [joined] + [shift(joined, Z, s) for s in (1, 2, 3)]
         if layer == 0:
             table_rows = 2 * len(pieces) * joined.shape[0]
@@ -549,7 +563,7 @@
         else:
             own_rows, sends = own_layer(layer - 1, own_rows, own_tags, sends, table, edge_inner, edge_outer, edge_gain)
         fine, fine_sum = fine_layer(
-            layer, fine, picks, latents, left, right, sides, edge_inner, edge_outer, edge_gain, rows
+            layer, fine, picks, latents, left, right, above, below, edge_inner, edge_outer, edge_gain, rows
         )
         swapped = shift(joined, CORE, 1)
         *others, fine_sum, own_rows, long_rows = tie(*pieces[1:], fine_sum, own_rows, long_rows)

time: 123 us -> 113 us (0.919)
  Pallas kernels: 47.4 us -> 36 us
  starting transfers between devices: 47 us -> 48.5 us
    pallas_call x2, Pallas kernels: 11.6 us -> 2.38 us  [join_near(): pl.pallas_call(body, name='join_near', cost_estimate=pl.CostEstimate(flop...]
    all_to_all x1, waiting for transfers between devices: 0.01 us -> 4.74 us  [shards(): lax.all_to_all(packed, AXES, split_axis=0, concat_axis=0, tiled=True)]
    ppermute x0 -> x6, starting transfers between devices: none -> 3.07 us  [around_x(): lax.ppermute(values, 'px', [(i, i // 4 * 4 + (i + step) % 4) for i in ran...]
    ppermute x16 -> x14, waiting for transfers between devices: 9.76 us -> 6.91 us  [along(): lax.ppermute(values, axis, [(i, (i + step) % count) for i in range(count)])]
    pallas_call x2, Pallas kernels: 15.8 us -> 13.9 us  [fine_layer(): pl.pallas_call(body, name=f'fine{layer}', out_shape=(jax.ShapeDtypeStruct...]
    ppermute x14, starting transfers between devices: 13.9 us -> 12.1 us  [shift(): return lax.ppermute(values, 'py', pairs)]
    ppermute x16 -> x14, starting transfers between devices: 22.4 us -> 23.7 us  [along(): lax.ppermute(values, axis, [(i, (i + step) % count) for i in range(count)])]
    unnamed x36 -> x40, local copies, waits for them, and re-layouts: 4.25 us -> 4.22 us
  transfers between devices with their start and end apart: 31 -> 35, of which waited for: 13 -> 15; matrix products, arithmetic and copies ran while one was open for 0% -> 0% of each run, Pallas kernels for 28% -> 21%
where the time goes in v8:
time: 113 us
  starting transfers between devices  48.5 us (43%)
  Pallas kernels  36 us (32%)
  waiting for transfers between devices  23.2 us (21%)
  local copies, waits for them, and re-layouts  4.22 us (4%)
  between operations  1.18 us (1%)
    ppermute x14, starting transfers between devices, along(): lax.ppermute(values, axis, [(i, (i + step) % count) for i in range(count)])  23.7 us
    pallas_call x2, Pallas kernels, fine_layer(): pl.pallas_call(body, name=f'fine{layer}', out_shape=(jax.ShapeDtypeStruct...  13.9 us
    ppermute x14, starting transfers between devices, shift(): return lax.ppermute(values, 'py', pairs)  12.1 us
    ppermute x14, waiting for transfers between devices, shift(): return lax.ppermute(values, 'py', pairs)  11.5 us
    pallas_call x2, Pallas kernels, coarse_layer(): pl.pallas_call(body, name=f'coarse{layer}', out_shape=tuple(shapes), in_s...  10.8 us
    all_to_all x1, starting transfers between devices, shards(): lax.all_to_all(packed, AXES, split_axis=0, concat_axis=0, tiled=True)  9.59 us
    ppermute x14, waiting for transfers between devices, along(): lax.ppermute(values, axis, [(i, (i + step) % count) for i in range(count)])  6.91 us
    all_to_all x1, waiting for transfers between devices, shards(): lax.all_to_all(packed, AXES, split_axis=0, concat_axis=0, tiled=True)  4.74 us
  transfers between devices with their start and end apart: 35, of which 15 were waited for; matrix products, arithmetic and copies ran while one was open for 0% of the time, Pallas kernels for 21%

profile of v8, /device:TPU:1, one launch (start us, length us, event | category | flops | bytes accessed | tf_op | source)
XLA Modules:
  0.0 113.1 jit_solution(5201263448938213463)
XLA Ops:
  0.6 1.3 %coarse_start.1 = (bf16[20,512]{1,0:T(8,128)(2,1)S(1)}, bf16[20,512]{1,0:T(8,128)(2,1)S(1)}, bf16[20,512]{1,0:T(8,128)(2,1)S(1)}, bf16[16,512]{1,0:T(8,128)(2,1)...) custom-call(s32[1,20]{1,0:T(1,128)} %bitcast.24, bf16[320,512]{1,0:T(8,128)(2,1)} %bitcast.19), custom_call_target="tpu_custom_call" | custom-call | tf_op jit(solution)/shard_map/coarse_start/pallas_call | solution.py:292
  2.0 3.6 %collective-permute-start.2 = (bf16[20,512]{1,0:T(8,128)(2,1)S(1)}, bf16[20,512]{1,0:T(8,128)(2,1)S(1)}, u32[]{:S(2)}, u32[]{:S(2)}) collective-permute-start(bf16[20,512]{1,0:T(8,128)(2,1)S(1)} %get-tuple-element.79.own_ref), channel_id=1, source_target_pairs={{0,96},{8,104},{16,112},{24,120},{32,0},{40,8},{48,16},{56,24},{64... | collective-permute-start | bytes 61448 | tf_op jit(solution)/shard_map/ppermute | solution.py:50
  6.0 0.7 collective-permute-start
  6.7 1.2 %collective-permute-start.3 = (bf16[20,512]{1,0:T(8,128)(2,1)S(1)}, bf16[20,512]{1,0:T(8,128)(2,1)S(1)}, u32[]{:S(2)}, u32[]{:S(2)}) collective-permute-start(bf16[20,512]{1,0:T(8,128)(2,1)S(1)} %get-tuple-element.80), channel_id=1, source_target_pairs={{0,8},{8,16},{16,24},{24,32},{32,40},{40,48},{48,56},{56,64},{64,7... | collective-permute-start | bytes 61448 | tf_op jit(solution)/shard_map/ppermute | solution.py:50
  7.9 3.6 %collective-permute-start.4 = (bf16[20,512]{1,0:T(8,128)(2,1)S(1)}, bf16[20,512]{1,0:T(8,128)(2,1)S(1)}, u32[]{:S(2)}, u32[]{:S(2)}) collective-permute-start(bf16[20,512]{1,0:T(8,128)(2,1)S(1)} %get-tuple-element.81), channel_id=1, source_target_pairs={{0,120},{8,0},{16,8},{24,16},{32,24},{40,32},{48,40},{56,48},{64,5... | collective-permute-start | bytes 61448 | tf_op jit(solution)/shard_map/ppermute | solution.py:50
  11.4 2.5 %pack_edges.1 = (bf16[2048,128]{1,0:T(8,128)(2,1)}, bf16[160,128]{1,0:T(8,128)(2,1)S(1)}) custom-call(s32[1]{0:T(128)} %bitcast.3.me_ref, bf16[160,512]{1,0:T(8,128)(2,1)} %long_ref, s32[1,160]{1,0:T(1,128)} %bitcast.27, s32[1,160]{1,0:T(1,128)} %bitcast.28), custom_call_target="tpu_custom_call" | custom-call | flops 12000000000 | tf_op jit(solution)/shard_map/pack_edges/pallas_call | solution.py:351
  14.0 0.6 copy-done.12
  14.7 0.8 collective-permute-start.7
  15.6 0.7 collective-permute-start.5
  16.2 5.0 %collective-permute-start.8 = (bf16[18,512]{1,0:T(8,128)(2,1)S(1)}, bf16[18,512]{1,0:T(8,128)(2,1)S(1)}, u32[]{:S(2)}, u32[]{:S(2)}) collective-permute-start(bf16[18,512]{1,0:T(8,128)(2,1)S(1)} %get-tuple-element.92), channel_id=1, source_target_pairs={{0,1},{1,2},{2,3},{3,4},{4,5},{5,6},{6,7},{7,0},{8,9},{9,10},{10,1... | collective-permute-start | bytes 55304 | tf_op jit(solution)/shard_map/ppermute | solution.py:50
  21.3 9.6 %all-to-all-start = ((bf16[128,16,128]{2,1,0:T(8,128)(2,1)}), bf16[128,16,128]{2,1,0:T(8,128)(2,1)}, u32[]{:S(2)}, u32[]{:S(2)}) async-start(bf16[128,16,128]{2,1,0:T(8,128)(2,1)} %bitcast.8), calls=%async_computation | async-start | bytes 1048576 | tf_op jit(solution)/shard_map/all_to_all | solution.py:550
  31.0 0.5 copy-done.16
  31.6 0.6 copy-done.19
  32.2 1.9 %join_near.2.rest_0_ = bf16[320,512]{1,0:T(8,128)(2,1)} custom-call(bf16[80,512]{1,0:T(8,128)(2,1)} %copy-done.15, bf16[80,512]{1,0:T(8,128)(2,1)} %collective-permute-done.5.refs_1_, bf16[80,512]{1,0:T(8,128)(2,1)} %copy-done.19, bf16[80,512]{1,0:T(8,128)(2,1)} %copy-done.18), custom_call_target="tpu_custom_call" | custom-call | flops 3000000000 | tf_op jit(solution)/shard_map/join_near/pallas_call | solution.py:250
  34.1 3.3 %collective-permute-start.12 = (bf16[320,512]{1,0:T(8,128)(2,1)}, bf16[320,512]{1,0:T(8,128)(2,1)}, u32[]{:S(2)}, u32[]{:S(2)}) collective-permute-start(bf16[320,512]{1,0:T(8,128)(2,1)} %join_near.2.rest_0_), channel_id=1, source_target_pairs={{0,6},{1,7},{2,0},{3,1},{4,2},{5,3},{6,4},{7,5},{8,14},{9,15},{10,... | collective-permute-start | bytes 983048 | tf_op jit(solution)/shard_map/ppermute | solution.py:25
  37.6 0.8 collective-permute-start.10
  38.3 1.2 %collective-permute-start.13 = (bf16[320,512]{1,0:T(8,128)(2,1)}, bf16[320,512]{1,0:T(8,128)(2,1)}, u32[]{:S(2)}, u32[]{:S(2)}) collective-permute-start(bf16[320,512]{1,0:T(8,128)(2,1)} %join_near.2.rest_0_), channel_id=1, source_target_pairs={{0,1},{1,0},{2,3},{3,2},{4,5},{5,4},{6,7},{7,6},{8,9},{9,8},{10,11... | collective-permute-start | bytes 983048 | tf_op jit(solution)/shard_map/ppermute | solution.py:25
  39.5 4.7 %all-to-all-done = bf16[128,16,128]{2,1,0:T(8,128)(2,1)} async-done(((bf16[128,16,128]{2,1,0:T(8,128)(2,1)}), bf16[128,16,128]{2,1,0:T(8,128)(2,1)}, u32[]{:S(2)}, u32[]{:S(2)}) %all-to-all-start) | async-done | bytes 524320 | tf_op jit(solution)/shard_map/all_to_all | solution.py:550
  44.3 2.4 %unpack_edges.1 = (bf16[384,512]{1,0:T(8,128)(2,1)S(1)}, bf16[384,2560]{1,0:T(8,128)(2,1)S(1)}, bf16[384,128]{1,0:T(8,128)(2,1)S(1)}, bf16[320,384]{1,0:T(8,128)(2,1)S(1)}) custom-call(bf16[2048,128]{1,0:T(8,128)(2,1)} %bitcast.9.arrived_ref, bf16[60,320]{1,0:T(8,128)(2,1)S(1)} %get-tuple-element.102.choose_ref), custom_call_target="tpu_custom_call" | custom-call | tf_op jit(solution)/shard_map/unpack_edges/pallas_call | solution.py:392
  46.7 0.8 copy-done.11
  47.9 1.5 %copy-done.5 = bf16[16,20,6,512]{3,0,2,1:T(8,128)(2,1)S(1)} copy-done((bf16[16,20,6,512]{3,0,2,1:T(8,128)(2,1)S(1)}, bf16[16,20,6,512]{3,0,2,1:T(8,128)(2,1)}, u32[]{:S(2)}) %copy-start.5) | copy-done | bytes 1966104
  49.4 7.0 %fine0.1 = (bf16[1920,512]{1,0:T(8,128)(2,1)S(1)}, f32[320,512]{1,0:T(8,128)S(1)}) custom-call(bf16[1920,512]{1,0:T(8,128)(2,1)S(1)} %bitcast.22, bf16[1920,256]{1,0:T(8,128)(2,1)S(1)} %selection.1.picks_ref, bf16[320,512]{1,0:T(8,128)(2,1)S(1)} %bitcast.20, bf16[18,512]{1,0:T(8,128)(2,1)} %copy-done.16, bf16[18,512]{1,0:T(8,128)(2,1)} %copy-done.17, ...), custom_call_target="tpu_custom_call" | custom-call | tf_op jit(solution)/shard_map/fine0/pallas_call | solution.py:148
  56.4 0.5 collective-permute-done.10.rest_1_
  56.9 0.8 collective-permute-start.14
  58.2 1.0 collective-permute-done.14.rest_5_
  59.2 0.5 collective-permute-done.15.rest_6_
  59.6 0.5 collective-permute-done.16.rest_7_
  60.1 5.3 %coarse0.1 = (bf16[320,512]{1,0:T(8,128)(2,1)S(1)}, bf16[384,512]{1,0:T(8,128)(2,1)S(1)}, bf16[20,512]{1,0:T(8,128)(2,1)S(1)}, bf16[20,512]{1,0:T(8,128)(2,1)S(1...) custom-call(bf16[384,512]{1,0:T(8,128)(2,1)S(1)} %get-tuple-element., ...), custom_call_target="tpu_custom_call" | custom-call | tf_op jit(solution)/shard_map/coarse0/pallas_call | solution.py:470
  65.8 4.5 %collective-permute-start.21 = (bf16[20,512]{1,0:T(8,128)(2,1)S(1)}, bf16[20,512]{1,0:T(8,128)(2,1)S(1)}, u32[]{:S(2)}, u32[]{:S(2)}) collective-permute-start(bf16[20,512]{1,0:T(8,128)(2,1)S(1)} %get-tuple-element.121), channel_id=1, source_target_pairs={{0,120},{8,0},{16,8},{24,16},{32,24},{40,32},{48,40},{56,48},{64,5... | collective-permute-start | bytes 61448 | tf_op jit(solution)/shard_map/ppermute | solution.py:50
  70.4 0.7 collective-permute-start.18
  71.1 0.6 collective-permute-start.17
  71.7 1.2 %collective-permute-done.19.far3_ref = bf16[20,512]{1,0:T(8,128)(2,1)S(1)} collective-permute-done((bf16[20,512]{1,0:T(8,128)(2,1)S(1)}, bf16[20,512]{1,0:T(8,128)(2,1)S(1)}, u32[]{:S(2)}, u32[]{:S(2)}) %collective-permute-start.19) | collective-permute-done | bytes 20512 | tf_op jit(solution)/shard_map/ppermute | solution.py:50
  72.9 1.7 %collective-permute-done.18.far2_ref = bf16[20,512]{1,0:T(8,128)(2,1)S(1)} collective-permute-done((bf16[20,512]{1,0:T(8,128)(2,1)S(1)}, bf16[20,512]{1,0:T(8,128)(2,1)S(1)}, u32[]{:S(2)}, u32[]{:S(2)}) %collective-permute-start.18) | collective-permute-done | bytes 20512 | tf_op jit(solution)/shard_map/ppermute | solution.py:50
  74.6 0.7 collective-permute-done.17.far1_ref
  75.6 1.2 %collective-permute-start.22 = (bf16[80,512]{1,0:T(8,128)(2,1)S(1)}, bf16[80,512]{1,0:T(8,128)(2,1)S(1)}, u32[]{:S(2)}, u32[]{:S(2)}) collective-permute-start(bf16[80,512]{1,0:T(8,128)(2,1)S(1)} %get-tuple-element.124.refs_0_), channel_id=1, source_target_pairs={{0,8},{8,16},{16,24},{24,0},{32,40},{40,48},{48,56},{56,32},{64,72... | collective-permute-start | bytes 245768 | tf_op jit(solution)/shard_map/ppermute | solution.py:45
  76.9 2.7 %collective-permute-start.25 = (bf16[18,512]{1,0:T(8,128)(2,1)S(1)}, bf16[18,512]{1,0:T(8,128)(2,1)S(1)}, u32[]{:S(2)}, u32[]{:S(2)}) collective-permute-start(bf16[18,512]{1,0:T(8,128)(2,1)S(1)} %get-tuple-element.125), channel_id=1, source_target_pairs={{0,1},{1,2},{2,3},{3,4},{4,5},{5,6},{6,7},{7,0},{8,9},{9,10},{10,1... | collective-permute-start | bytes 55304 | tf_op jit(solution)/shard_map/ppermute | solution.py:50
  79.8 0.7 collective-permute-done.25.left_away
  80.5 2.6 %collective-permute-done.26.right_away = bf16[18,512]{1,0:T(8,128)(2,1)S(1)} collective-permute-done((bf16[18,512]{1,0:T(8,128)(2,1)S(1)}, bf16[18,512]{1,0:T(8,128)(2,1)S(1)}, u32[]{:S(2)}, u32[]{:S(2)}) %collective-permute-start.26) | collective-permute-done | bytes 18464 | tf_op jit(solution)/shard_map/ppermute | solution.py:50
  83.6 3.8 %collective-permute-start.29 = (bf16[320,512]{1,0:T(8,128)(2,1)S(1)}, bf16[320,512]{1,0:T(8,128)(2,1)S(1)}, u32[]{:S(2)}, u32[]{:S(2)}) collective-permute-start(bf16[320,512]{1,0:T(8,128)(2,1)S(1)} %join_near.3.rest_0_), channel_id=1, source_target_pairs={{0,6},{1,7},{2,0},{3,1},{4,2},{5,3},{6,4},{7,5},{8,14},{9,15},{10,... | collective-permute-start | bytes 983048 | tf_op jit(solution)/shard_map/ppermute | solution.py:25
  87.4 0.7 collective-permute-start.27
  88.1 2.2 %own0.1 = (bf16[160,512]{1,0:T(8,128)(2,1)S(1)}, bf16[704,2560]{1,0:T(8,128)(2,1)S(1)}) custom-call(bf16[160,512]{1,0:T(8,128)(2,1)S(1)} %copy-done.6, bf16[160,128]{1,0:T(8,128)(2,1)S(1)} %copy-done.13, bf16[384,2560]{1,0:T(8,128)(2,1)S(1)} %get-tuple-element.112.sends_ref, bf16[2560,512]{1,0:T(8,128)(2,1)S(1)} %get-tuple-element.140.table_ref, ...), custom_call_target="tpu_custom_call" | custom-call | tf_op jit(solution)/shard_map/own0/pallas_call | solution.py:500
  90.3 7.0 %fine1.1 = (bf16[1920,512]{1,0:T(8,128)(2,1)}, f32[320,512]{1,0:T(8,128)S(1)}) custom-call(bf16[1920,512]{1,0:T(8,128)(2,1)S(1)} %get-tuple-element.133.fine_ref, bf16[1920,256]{1,0:T(8,128)(2,1)S(1)} %selection.1.picks_ref, bf16[320,512]{1,0:T(8,128)(2,1)S(1)} %get-tuple-element.134.latents_ref, bf16[18,512]{1,0:T(8,128)(2,1)S(1)} %collective-permute-done.25.left_away, ...), custom_call_target="tpu_custom_call" | custom-call | tf_op jit(solution)/shard_map/fine1/pallas_call | solution.py:148
  97.3 3.5 %collective-permute-done.29.rest_3_ = bf16[320,512]{1,0:T(8,128)(2,1)S(1)} collective-permute-done((bf16[320,512]{1,0:T(8,128)(2,1)S(1)}, bf16[320,512]{1,0:T(8,128)(2,1)S(1)}, u32[]{:S(2)}, u32[]{:S(2)}) %collective-permute-start.29) | collective-permute-done | bytes 327712 | tf_op jit(solution)/shard_map/ppermute | solution.py:25
  100.8 3.9 %collective-permute-done.27.rest_1_ = bf16[320,512]{1,0:T(8,128)(2,1)S(1)} collective-permute-done((bf16[320,512]{1,0:T(8,128)(2,1)S(1)}, bf16[320,512]{1,0:T(8,128)(2,1)S(1)}, u32[]{:S(2)}, u32[]{:S(2)}) %collective-permute-start.27) | collective-permute-done | bytes 327712 | tf_op jit(solution)/shard_map/ppermute | solution.py:25
  105.7 0.7 collective-permute-done.31.rest_5_
  106.4 0.5 collective-permute-done.32.rest_6_
  106.9 0.5 collective-permute-done.33.rest_7_
  107.4 5.6 %coarse1.1 = (bf16[320,512]{1,0:T(8,128)(2,1)}, bf16[160,512]{1,0:T(8,128)(2,1)}) custom-call(bf16[384,512]{1,0:T(8,128)(2,1)S(1)} %get-tuple-element.143.long_ref, bf16[160,512]{1,0:T(8,128)(2,1)S(1)} %get-tuple-element.144.own_ref, bf16[704,2560]{1,0:T(8,128)(2,1)S(1)} %get-tuple-element.145.sends_ref, bf16[384,128]{1,0:T(8,128)(2,1)S(1)} %get-tuple-element.113.recvs_ref, ...), custom_call_target="tpu_custom_call" | custom-call | tf_op jit(solution)/shard_map/coarse1/pallas_call | solution.py:470
  (75 shorter events, 4.1 us)
Async XLA Ops:
  2.0 12.6 %collective-permute-start.2 = (bf16[20,512]{1,0:T(8,128)(2,1)S(1)}, bf16[20,512]{1,0:T(8,128)(2,1)S(1)}, u32[]{:S(2)}, u32[]{:S(2)}) collective-permute-start(bf16[20,512]{1,0:T(8,128)(2,1)S(1)} %get-tuple-element.79.own_ref), channel_id=1, source_target_pairs={{0,96},{8,104},{16,112},{24,120},{32,0},{40,8},{48,16},{56,24},{64... | collective-permute-start | bytes 61448 | tf_op jit(solution)/shard_map/ppermute | solution.py:50
  5.6 9.0 %collective-permute-start.1 = (bf16[20,512]{1,0:T(8,128)(2,1)S(1)}, bf16[20,512]{1,0:T(8,128)(2,1)S(1)}, u32[]{:S(2)}, u32[]{:S(2)}) collective-permute-start(bf16[20,512]{1,0:T(8,128)(2,1)S(1)} %get-tuple-element.79.own_ref), channel_id=1, source_target_pairs={{0,64},{8,72},{16,80},{24,88},{32,96},{40,104},{48,112},{56,120},{... | collective-permute-start | bytes 61448 | tf_op jit(solution)/shard_map/ppermute | solution.py:50
  6.0 8.7 %collective-permute-start = (bf16[20,512]{1,0:T(8,128)(2,1)S(1)}, bf16[20,512]{1,0:T(8,128)(2,1)S(1)}, u32[]{:S(2)}, u32[]{:S(2)}) collective-permute-start(bf16[20,512]{1,0:T(8,128)(2,1)S(1)} %get-tuple-element.79.own_ref), channel_id=1, source_target_pairs={{0,32},{8,40},{16,48},{24,56},{32,64},{40,72},{48,80},{56,88},{64,... | collective-permute-start | bytes 61448 | tf_op jit(solution)/shard_map/ppermute | solution.py:50
  6.7 8.0 %collective-permute-start.3 = (bf16[20,512]{1,0:T(8,128)(2,1)S(1)}, bf16[20,512]{1,0:T(8,128)(2,1)S(1)}, u32[]{:S(2)}, u32[]{:S(2)}) collective-permute-start(bf16[20,512]{1,0:T(8,128)(2,1)S(1)} %get-tuple-element.80), channel_id=1, source_target_pairs={{0,8},{8,16},{16,24},{24,32},{32,40},{40,48},{48,56},{56,64},{64,7... | collective-permute-start | bytes 61448 | tf_op jit(solution)/shard_map/ppermute | solution.py:50
  7.9 6.8 %collective-permute-start.4 = (bf16[20,512]{1,0:T(8,128)(2,1)S(1)}, bf16[20,512]{1,0:T(8,128)(2,1)S(1)}, u32[]{:S(2)}, u32[]{:S(2)}) collective-permute-start(bf16[20,512]{1,0:T(8,128)(2,1)S(1)} %get-tuple-element.81), channel_id=1, source_target_pairs={{0,120},{8,0},{16,8},{24,16},{32,24},{40,32},{48,40},{56,48},{64,5... | collective-permute-start | bytes 61448 | tf_op jit(solution)/shard_map/ppermute | solution.py:50
  14.6 19.5 %copy-start.9 = (bf16[20,512]{1,0:T(8,128)(2,1)}, bf16[20,512]{1,0:T(8,128)(2,1)S(1)}, u32[]{:S(2)}) copy-start(bf16[20,512]{1,0:T(8,128)(2,1)S(1)} %collective-permute-done.3.above_ref.above_away) | copy-start | bytes 61444
  14.7 16.3 %copy-start.10 = (bf16[20,512]{1,0:T(8,128)(2,1)}, bf16[20,512]{1,0:T(8,128)(2,1)S(1)}, u32[]{:S(2)}) copy-start(bf16[20,512]{1,0:T(8,128)(2,1)S(1)} %collective-permute-done.4.below_ref.below_away) | copy-start | bytes 61444
  14.7 16.3 %copy-start.15 = (bf16[80,512]{1,0:T(8,128)(2,1)}, bf16[80,512]{1,0:T(8,128)(2,1)S(1)}, u32[]{:S(2)}) copy-start(bf16[80,512]{1,0:T(8,128)(2,1)S(1)} %get-tuple-element.91.refs_0_) | copy-start | bytes 245764
  14.7 16.2 %collective-permute-start.7 = (bf16[80,512]{1,0:T(8,128)(2,1)S(1)}, bf16[80,512]{1,0:T(8,128)(2,1)S(1)}, u32[]{:S(2)}, u32[]{:S(2)}) collective-permute-start(bf16[80,512]{1,0:T(8,128)(2,1)S(1)} %get-tuple-element.91.refs_0_), channel_id=1, source_target_pairs={{0,24},{8,0},{16,8},{24,16},{32,56},{40,32},{48,40},{56,48},{64,88... | collective-permute-start | bytes 245768 | tf_op jit(solution)/shard_map/ppermute | solution.py:45
  15.6 15.4 %collective-permute-start.6 = (bf16[80,512]{1,0:T(8,128)(2,1)S(1)}, bf16[80,512]{1,0:T(8,128)(2,1)S(1)}, u32[]{:S(2)}, u32[]{:S(2)}) collective-permute-start(bf16[80,512]{1,0:T(8,128)(2,1)S(1)} %get-tuple-element.91.refs_0_), channel_id=1, source_target_pairs={{0,16},{8,24},{16,0},{24,8},{32,48},{40,56},{48,32},{56,40},{64,80... | collective-permute-start | bytes 245768 | tf_op jit(solution)/shard_map/ppermute | solution.py:45
  15.6 16.6 %collective-permute-start.5 = (bf16[80,512]{1,0:T(8,128)(2,1)S(1)}, bf16[80,512]{1,0:T(8,128)(2,1)}, u32[]{:S(2)}, u32[]{:S(2)}) collective-permute-start(bf16[80,512]{1,0:T(8,128)(2,1)S(1)} %get-tuple-element.91.refs_0_), channel_id=1, source_target_pairs={{0,8},{8,16},{16,24},{24,0},{32,40},{40,48},{48,56},{56,32},{64,72... | collective-permute-start | bytes 245768 | tf_op jit(solution)/shard_map/ppermute | solution.py:45
  16.2 14.6 %collective-permute-start.8 = (bf16[18,512]{1,0:T(8,128)(2,1)S(1)}, bf16[18,512]{1,0:T(8,128)(2,1)S(1)}, u32[]{:S(2)}, u32[]{:S(2)}) collective-permute-start(bf16[18,512]{1,0:T(8,128)(2,1)S(1)} %get-tuple-element.92), channel_id=1, source_target_pairs={{0,1},{1,2},{2,3},{3,4},{4,5},{5,6},{6,7},{7,0},{8,9},{9,10},{10,1... | collective-permute-start | bytes 55304 | tf_op jit(solution)/shard_map/ppermute | solution.py:50
  21.2 9.7 %collective-permute-start.9 = (bf16[18,512]{1,0:T(8,128)(2,1)S(1)}, bf16[18,512]{1,0:T(8,128)(2,1)S(1)}, u32[]{:S(2)}, u32[]{:S(2)}) collective-permute-start(bf16[18,512]{1,0:T(8,128)(2,1)S(1)} %get-tuple-element.93), channel_id=1, source_target_pairs={{0,7},{1,0},{2,1},{3,2},{4,3},{5,4},{6,5},{7,6},{8,15},{9,8},{10,9... | collective-permute-start | bytes 55304 | tf_op jit(solution)/shard_map/ppermute | solution.py:50
  21.3 23.0 %all-to-all-start = ((bf16[128,16,128]{2,1,0:T(8,128)(2,1)}), bf16[128,16,128]{2,1,0:T(8,128)(2,1)}, u32[]{:S(2)}, u32[]{:S(2)}) async-start(bf16[128,16,128]{2,1,0:T(8,128)(2,1)} %bitcast.8), calls=%async_computation | async-start | bytes 1048576 | tf_op jit(solution)/shard_map/all_to_all | solution.py:550
  30.9 17.0 %copy-start.4 = (bf16[16,20,512]{2,0,1:T(8,128)(2,1)S(1)}, bf16[16,20,512]{2,0,1:T(8,128)(2,1)}, u32[]{:S(2)}) copy-start(bf16[16,20,512]{2,0,1:T(8,128)(2,1)} %param.13) | copy-start | bytes 983044
  30.9 17.0 %copy-start.8 = (f32[2,512]{1,0:T(2,128)S(1)}, f32[2,512]{1,0:T(2,128)}, u32[]{:S(2)}) copy-start(f32[2,512]{1,0:T(2,128)} %eg_ref.5) | copy-start | bytes 12292
  32.2 15.7 %copy-start = (bf16[2,1536,512]{2,1,0:T(8,128)(2,1)S(1)}, bf16[2,1536,512]{2,1,0:T(8,128)(2,1)}, u32[]{:S(2)}) copy-start(bf16[2,1536,512]{2,1,0:T(8,128)(2,1)} %ei_ref.5) | copy-start | bytes 9437188
  34.1 22.3 %collective-permute-start.12 = (bf16[320,512]{1,0:T(8,128)(2,1)}, bf16[320,512]{1,0:T(8,128)(2,1)}, u32[]{:S(2)}, u32[]{:S(2)}) collective-permute-start(bf16[320,512]{1,0:T(8,128)(2,1)} %join_near.2.rest_0_), channel_id=1, source_target_pairs={{0,6},{1,7},{2,0},{3,1},{4,2},{5,3},{6,4},{7,5},{8,14},{9,15},{10,... | collective-permute-start | bytes 983048 | tf_op jit(solution)/shard_map/ppermute | solution.py:25
  37.5 19.0 %collective-permute-start.11 = (bf16[320,512]{1,0:T(8,128)(2,1)}, bf16[320,512]{1,0:T(8,128)(2,1)}, u32[]{:S(2)}, u32[]{:S(2)}) collective-permute-start(bf16[320,512]{1,0:T(8,128)(2,1)} %join_near.2.rest_0_), channel_id=1, source_target_pairs={{0,4},{1,5},{2,6},{3,7},{4,0},{5,1},{6,2},{7,3},{8,12},{9,13},{10,... | collective-permute-start | bytes 983048 | tf_op jit(solution)/shard_map/ppermute | solution.py:25
  37.6 19.4 %collective-permute-start.10 = (bf16[320,512]{1,0:T(8,128)(2,1)}, bf16[320,512]{1,0:T(8,128)(2,1)}, u32[]{:S(2)}, u32[]{:S(2)}) collective-permute-start(bf16[320,512]{1,0:T(8,128)(2,1)} %join_near.2.rest_0_), channel_id=1, source_target_pairs={{0,2},{1,3},{2,4},{3,5},{4,6},{5,7},{6,0},{7,1},{8,10},{9,11},{10,... | collective-permute-start | bytes 983048 | tf_op jit(solution)/shard_map/ppermute | solution.py:25
  38.3 19.9 %collective-permute-start.13 = (bf16[320,512]{1,0:T(8,128)(2,1)}, bf16[320,512]{1,0:T(8,128)(2,1)}, u32[]{:S(2)}, u32[]{:S(2)}) collective-permute-start(bf16[320,512]{1,0:T(8,128)(2,1)} %join_near.2.rest_0_), channel_id=1, source_target_pairs={{0,1},{1,0},{2,3},{3,2},{4,5},{5,4},{6,7},{7,6},{8,9},{9,8},{10,11... | collective-permute-start | bytes 983048 | tf_op jit(solution)/shard_map/ppermute | solution.py:25
  44.3 3.6 %copy-start.1 = (bf16[2,512,512]{2,1,0:T(8,128)(2,1)S(1)}, bf16[2,512,512]{2,1,0:T(8,128)(2,1)}, u32[]{:S(2)}) copy-start(bf16[2,512,512]{2,1,0:T(8,128)(2,1)} %eo_ref.5) | copy-start | bytes 3145732
  49.4 10.7 %copy-start.2 = (bf16[2,1024,512]{2,1,0:T(8,128)(2,1)S(1)}, bf16[2,1024,512]{2,1,0:T(8,128)(2,1)}, u32[]{:S(2)}) copy-start(bf16[2,1024,512]{2,1,0:T(8,128)(2,1)} %ni_ref.3) | copy-start | bytes 6291460
  49.4 10.7 %copy-start.3 = (bf16[2,512,512]{2,1,0:T(8,128)(2,1)S(1)}, bf16[2,512,512]{2,1,0:T(8,128)(2,1)}, u32[]{:S(2)}) copy-start(bf16[2,512,512]{2,1,0:T(8,128)(2,1)} %no_ref.3) | copy-start | bytes 3145732
  49.4 10.7 %copy-start.6 = (bf16[160,512]{1,0:T(8,128)(2,1)S(1)}, bf16[160,512]{1,0:T(8,128)(2,1)}, u32[]{:S(2)}) copy-start(bf16[160,512]{1,0:T(8,128)(2,1)} %long_ref) | copy-start | bytes 491524
  49.4 10.7 %copy-start.7 = (bf16[320,512]{1,0:T(8,128)(2,1)S(1)}, bf16[320,512]{1,0:T(8,128)(2,1)}, u32[]{:S(2)}) copy-start(bf16[320,512]{1,0:T(8,128)(2,1)} %join_near.2.rest_0_) | copy-start | bytes 983044
  49.4 10.7 %copy-start.14 = (f32[2,512]{1,0:T(2,128)S(1)}, f32[2,512]{1,0:T(2,128)}, u32[]{:S(2)}) copy-start(f32[2,512]{1,0:T(2,128)} %ng_ref.3) | copy-start | bytes 12292
  56.9 2.2 %collective-permute-start.14 = (bf16[320,512]{1,0:T(8,128)(2,1)}, bf16[320,512]{1,0:T(8,128)(2,1)S(1)}, u32[]{:S(2)}, u32[]{:S(2)}) collective-permute-start(bf16[320,512]{1,0:T(8,128)(2,1)} %collective-permute-done.10.rest_1_), channel_id=1, source_target_pairs={{0,1},{1,0},{2,3},{3,2},{4,5},{5,4},{6,7},{7,6},{8,9},{9,8},{10,11... | collective-permute-start | bytes 983048 | tf_op jit(solution)/shard_map/ppermute | solution.py:25
  57.7 1.9 %collective-permute-start.15 = (bf16[320,512]{1,0:T(8,128)(2,1)}, bf16[320,512]{1,0:T(8,128)(2,1)S(1)}, u32[]{:S(2)}, u32[]{:S(2)}) collective-permute-start(bf16[320,512]{1,0:T(8,128)(2,1)} %collective-permute-done.11.rest_2_), channel_id=1, source_target_pairs={{0,1},{1,0},{2,3},{3,2},{4,5},{5,4},{6,7},{7,6},{8,9},{9,8},{10,11... | collective-permute-start | bytes 983048 | tf_op jit(solution)/shard_map/ppermute | solution.py:25
  57.8 2.3 %collective-permute-start.16 = (bf16[320,512]{1,0:T(8,128)(2,1)}, bf16[320,512]{1,0:T(8,128)(2,1)S(1)}, u32[]{:S(2)}, u32[]{:S(2)}) collective-permute-start(bf16[320,512]{1,0:T(8,128)(2,1)} %collective-permute-done.12.rest_3_), channel_id=1, source_target_pairs={{0,1},{1,0},{2,3},{3,2},{4,5},{5,4},{6,7},{7,6},{8,9},{9,8},{10,11... | collective-permute-start | bytes 983048 | tf_op jit(solution)/shard_map/ppermute | solution.py:25
  65.4 6.3 %collective-permute-start.20 = (bf16[20,512]{1,0:T(8,128)(2,1)S(1)}, bf16[20,512]{1,0:T(8,128)(2,1)S(1)}, u32[]{:S(2)}, u32[]{:S(2)}) collective-permute-start(bf16[20,512]{1,0:T(8,128)(2,1)S(1)} %get-tuple-element.120), channel_id=1, source_target_pairs={{0,8},{8,16},{16,24},{24,32},{32,40},{40,48},{48,56},{56,64},{64,7... | collective-permute-start | bytes 61448 | tf_op jit(solution)/shard_map/ppermute | solution.py:50
  65.8 6.0 %collective-permute-start.21 = (bf16[20,512]{1,0:T(8,128)(2,1)S(1)}, bf16[20,512]{1,0:T(8,128)(2,1)S(1)}, u32[]{:S(2)}, u32[]{:S(2)}) collective-permute-start(bf16[20,512]{1,0:T(8,128)(2,1)S(1)} %get-tuple-element.121), channel_id=1, source_target_pairs={{0,120},{8,0},{16,8},{24,16},{32,24},{40,32},{48,40},{56,48},{64,5... | collective-permute-start | bytes 61448 | tf_op jit(solution)/shard_map/ppermute | solution.py:50
  70.2 2.7 %collective-permute-start.19 = (bf16[20,512]{1,0:T(8,128)(2,1)S(1)}, bf16[20,512]{1,0:T(8,128)(2,1)S(1)}, u32[]{:S(2)}, u32[]{:S(2)}) collective-permute-start(bf16[20,512]{1,0:T(8,128)(2,1)S(1)} %get-tuple-element.119.own_ref), channel_id=1, source_target_pairs={{0,96},{8,104},{16,112},{24,120},{32,0},{40,8},{48,16},{56,24},{64... | collective-permute-start | bytes 61448 | tf_op jit(solution)/shard_map/ppermute | solution.py:50
  70.4 4.2 %collective-permute-start.18 = (bf16[20,512]{1,0:T(8,128)(2,1)S(1)}, bf16[20,512]{1,0:T(8,128)(2,1)S(1)}, u32[]{:S(2)}, u32[]{:S(2)}) collective-permute-start(bf16[20,512]{1,0:T(8,128)(2,1)S(1)} %get-tuple-element.119.own_ref), channel_id=1, source_target_pairs={{0,64},{8,72},{16,80},{24,88},{32,96},{40,104},{48,112},{56,120},{... | collective-permute-start | bytes 61448 | tf_op jit(solution)/shard_map/ppermute | solution.py:50
  71.1 4.2 %collective-permute-start.17 = (bf16[20,512]{1,0:T(8,128)(2,1)S(1)}, bf16[20,512]{1,0:T(8,128)(2,1)S(1)}, u32[]{:S(2)}, u32[]{:S(2)}) collective-permute-start(bf16[20,512]{1,0:T(8,128)(2,1)S(1)} %get-tuple-element.119.own_ref), channel_id=1, source_target_pairs={{0,32},{8,40},{16,48},{24,56},{32,64},{40,72},{48,80},{56,88},{64,... | collective-permute-start | bytes 61448 | tf_op jit(solution)/shard_map/ppermute | solution.py:50
  75.3 7.8 %collective-permute-start.24 = (bf16[80,512]{1,0:T(8,128)(2,1)S(1)}, bf16[80,512]{1,0:T(8,128)(2,1)S(1)}, u32[]{:S(2)}, u32[]{:S(2)}) collective-permute-start(bf16[80,512]{1,0:T(8,128)(2,1)S(1)} %get-tuple-element.124.refs_0_), channel_id=1, source_target_pairs={{0,24},{8,0},{16,8},{24,16},{32,56},{40,32},{48,40},{56,48},{64,88... | collective-permute-start | bytes 245768 | tf_op jit(solution)/shard_map/ppermute | solution.py:45
  75.4 7.7 %collective-permute-start.23 = (bf16[80,512]{1,0:T(8,128)(2,1)S(1)}, bf16[80,512]{1,0:T(8,128)(2,1)S(1)}, u32[]{:S(2)}, u32[]{:S(2)}) collective-permute-start(bf16[80,512]{1,0:T(8,128)(2,1)S(1)} %get-tuple-element.124.refs_0_), channel_id=1, source_target_pairs={{0,16},{8,24},{16,0},{24,8},{32,48},{40,56},{48,32},{56,40},{64,80... | collective-permute-start | bytes 245768 | tf_op jit(solution)/shard_map/ppermute | solution.py:45
  75.6 7.5 %collective-permute-start.22 = (bf16[80,512]{1,0:T(8,128)(2,1)S(1)}, bf16[80,512]{1,0:T(8,128)(2,1)S(1)}, u32[]{:S(2)}, u32[]{:S(2)}) collective-permute-start(bf16[80,512]{1,0:T(8,128)(2,1)S(1)} %get-tuple-element.124.refs_0_), channel_id=1, source_target_pairs={{0,8},{8,16},{16,24},{24,0},{32,40},{40,48},{48,56},{56,32},{64,72... | collective-permute-start | bytes 245768 | tf_op jit(solution)/shard_map/ppermute | solution.py:45
  76.9 3.6 %collective-permute-start.25 = (bf16[18,512]{1,0:T(8,128)(2,1)S(1)}, bf16[18,512]{1,0:T(8,128)(2,1)S(1)}, u32[]{:S(2)}, u32[]{:S(2)}) collective-permute-start(bf16[18,512]{1,0:T(8,128)(2,1)S(1)} %get-tuple-element.125), channel_id=1, source_target_pairs={{0,1},{1,2},{2,3},{3,4},{4,5},{5,6},{6,7},{7,0},{8,9},{9,10},{10,1... | collective-permute-start | bytes 55304 | tf_op jit(solution)/shard_map/ppermute | solution.py:50
  79.6 8.5 %copy-start.13 = (bf16[160,128]{1,0:T(8,128)(2,1)S(1)}, bf16[160,128]{1,0:T(8,128)(2,1)}, u32[]{:S(2)}) copy-start(bf16[160,128]{1,0:T(8,128)(2,1)} %copy-done.12) | copy-start | bytes 122884
  79.6 3.5 %collective-permute-start.26 = (bf16[18,512]{1,0:T(8,128)(2,1)S(1)}, bf16[18,512]{1,0:T(8,128)(2,1)S(1)}, u32[]{:S(2)}, u32[]{:S(2)}) collective-permute-start(bf16[18,512]{1,0:T(8,128)(2,1)S(1)} %get-tuple-element.126), channel_id=1, source_target_pairs={{0,7},{1,0},{2,1},{3,2},{4,3},{5,4},{6,5},{7,6},{8,15},{9,8},{10,9... | collective-permute-start | bytes 55304 | tf_op jit(solution)/shard_map/ppermute | solution.py:50
  83.6 17.2 %collective-permute-start.29 = (bf16[320,512]{1,0:T(8,128)(2,1)S(1)}, bf16[320,512]{1,0:T(8,128)(2,1)S(1)}, u32[]{:S(2)}, u32[]{:S(2)}) collective-permute-start(bf16[320,512]{1,0:T(8,128)(2,1)S(1)} %join_near.3.rest_0_), channel_id=1, source_target_pairs={{0,6},{1,7},{2,0},{3,1},{4,2},{5,3},{6,4},{7,5},{8,14},{9,15},{10,... | collective-permute-start | bytes 983048 | tf_op jit(solution)/shard_map/ppermute | solution.py:25
  87.4 13.4 %collective-permute-start.28 = (bf16[320,512]{1,0:T(8,128)(2,1)S(1)}, bf16[320,512]{1,0:T(8,128)(2,1)S(1)}, u32[]{:S(2)}, u32[]{:S(2)}) collective-permute-start(bf16[320,512]{1,0:T(8,128)(2,1)S(1)} %join_near.3.rest_0_), channel_id=1, source_target_pairs={{0,4},{1,5},{2,6},{3,7},{4,0},{5,1},{6,2},{7,3},{8,12},{9,13},{10,... | collective-permute-start | bytes 983048 | tf_op jit(solution)/shard_map/ppermute | solution.py:25
  87.4 17.3 %collective-permute-start.27 = (bf16[320,512]{1,0:T(8,128)(2,1)S(1)}, bf16[320,512]{1,0:T(8,128)(2,1)S(1)}, u32[]{:S(2)}, u32[]{:S(2)}) collective-permute-start(bf16[320,512]{1,0:T(8,128)(2,1)S(1)} %join_near.3.rest_0_), channel_id=1, source_target_pairs={{0,2},{1,3},{2,4},{3,5},{4,6},{5,7},{6,0},{7,1},{8,10},{9,11},{10,... | collective-permute-start | bytes 983048 | tf_op jit(solution)/shard_map/ppermute | solution.py:25
  88.1 17.6 %collective-permute-start.30 = (bf16[320,512]{1,0:T(8,128)(2,1)S(1)}, bf16[320,512]{1,0:T(8,128)(2,1)S(1)}, u32[]{:S(2)}, u32[]{:S(2)}) collective-permute-start(bf16[320,512]{1,0:T(8,128)(2,1)S(1)} %join_near.3.rest_0_), channel_id=1, source_target_pairs={{0,1},{1,0},{2,3},{3,2},{4,5},{5,4},{6,7},{7,6},{8,9},{9,8},{10,11... | collective-permute-start | bytes 983048 | tf_op jit(solution)/shard_map/ppermute | solution.py:25
  104.7 1.7 %collective-permute-start.31 = (bf16[320,512]{1,0:T(8,128)(2,1)S(1)}, bf16[320,512]{1,0:T(8,128)(2,1)S(1)}, u32[]{:S(2)}, u32[]{:S(2)}) collective-permute-start(bf16[320,512]{1,0:T(8,128)(2,1)S(1)} %collective-permute-done.27.rest_1_), channel_id=1, source_target_pairs={{0,1},{1,0},{2,3},{3,2},{4,5},{5,4},{6,7},{7,6},{8,9},{9,8},{10,11... | collective-permute-start | bytes 983048 | tf_op jit(solution)/shard_map/ppermute | solution.py:25
  105.2 1.7 %collective-permute-start.32 = (bf16[320,512]{1,0:T(8,128)(2,1)S(1)}, bf16[320,512]{1,0:T(8,128)(2,1)S(1)}, u32[]{:S(2)}, u32[]{:S(2)}) collective-permute-start(bf16[320,512]{1,0:T(8,128)(2,1)S(1)} %collective-permute-done.28.rest_2_), channel_id=1, source_target_pairs={{0,1},{1,0},{2,3},{3,2},{4,5},{5,4},{6,7},{7,6},{8,9},{9,8},{10,11... | collective-permute-start | bytes 983048 | tf_op jit(solution)/shard_map/ppermute | solution.py:25
  105.2 2.1 %collective-permute-start.33 = (bf16[320,512]{1,0:T(8,128)(2,1)S(1)}, bf16[320,512]{1,0:T(8,128)(2,1)S(1)}, u32[]{:S(2)}, u32[]{:S(2)}) collective-permute-start(bf16[320,512]{1,0:T(8,128)(2,1)S(1)} %collective-permute-done.29.rest_3_), channel_id=1, source_target_pairs={{0,1},{1,0},{2,3},{3,2},{4,5},{5,4},{6,7},{7,6},{8,9},{9,8},{10,11... | collective-permute-start | bytes 983048 | tf_op jit(solution)/shard_map/ppermute | solution.py:25
  (7 other events, 5.4 us)

commit v9 on v7

--- a/solution.py
+++ b/solution.py
@@ -7,7 +7,6 @@
 
 EPSILON = 1e-05
 AXES = ("px", "py")
-RING = 16
 Z, CORE = (2, 4), (1, 2)
 BAND = 4
 TAGS = 128
@@ -33,12 +32,19 @@
 def table_row(px, py, coarse, coarse_count):
     home = jnp.floor((coarse.astype(jnp.float32) + 0.5) * (1.0 / coarse_count)).astype(jnp.int32)
     row = coarse - home * coarse_count
-    away = (px - lax.shift_right_logical(home, 3)) & (RING - 1)
-    near, far = away & 3, lax.shift_right_logical(away + 1, 2) & 3
+    home_px = lax.shift_right_logical(home, 3)
+    near = (px - home_px) & 3
+    x = px & 3
+    turn = jnp.where((near == 1) & (x == 0), -1, jnp.where((near == 3) & (x == 3), 1, 0))
+    far = (lax.shift_right_logical(px, 2) + turn - lax.shift_right_logical(home_px, 2)) & 3
     home_z, home_core = lax.shift_right_logical(home, 1) & 3, home & 1
     kz = (lax.shift_right_logical(py, 1) - home_z) & 3
     kc = (py - home_core) & 1
     return (((kc * 4 + kz) * 4 + near) * 4 + far) * coarse_count + row, home
+
+
+def around_x(values, step):
+    return lax.ppermute(values, "px", [(i, i // 4 * 4 + (i + step) % 4) for i in range(16)])
 
 
 def along(values, axis, step):
@@ -544,7 +550,7 @@
         if layer == 0:
             packed = payload.reshape(devices, 16, TAGS)
             arrived = lax.all_to_all(packed, AXES, split_axis=0, concat_axis=0, tiled=True).reshape(payload.shape)
-        two = along(joined, "px", 2)
+        two = around_x(joined, 2)
         up = along(up, "px", 1)
         down = along(down, "px", -1)
         joined, sides = join_near(layer, joined, up, two, down)

time: 113 us -> 109 us (0.965)
  waiting for transfers between devices: 25.8 us -> 23.7 us
  starting transfers between devices: 45.5 us -> 43.9 us
    ppermute x16 -> x14, waiting for transfers between devices: 10.6 us -> 3.65 us  [along(): lax.ppermute(values, axis, [(i, (i + step) % count) for i in range(count)])]
    ppermute x0 -> x2, waiting for transfers between devices: none -> 4.8 us  [around_x(): lax.ppermute(values, 'px', [(i, i // 4 * 4 + (i + step) % 4) for i in ran...]
    all_to_all x1, starting transfers between devices: 10.7 us -> 9.04 us  [shards(): lax.all_to_all(packed, AXES, split_axis=0, concat_axis=0, tiled=True)]
    ppermute x16 -> x14, starting transfers between devices: 20.7 us -> 20.7 us  [along(): lax.ppermute(values, axis, [(i, (i + step) % count) for i in range(count)])]
where the time goes in v9:
time: 109 us
  starting transfers between devices  43.9 us (40%)
  Pallas kernels  34.9 us (32%)
  waiting for transfers between devices  23.7 us (22%)
  local copies, waits for them, and re-layouts  5.18 us (5%)
  between operations  1.09 us (1%)
    ppermute x14, starting transfers between devices, along(): lax.ppermute(values, axis, [(i, (i + step) % count) for i in range(count)])  20.7 us
    ppermute x14, starting transfers between devices, shift(): return lax.ppermute(values, 'py', pairs)  14.1 us
    pallas_call x2, Pallas kernels, fine_layer(): pl.pallas_call(body, name=f'fine{layer}', out_shape=(jax.ShapeDtypeStruct...  12.6 us
    pallas_call x2, Pallas kernels, coarse_layer(): pl.pallas_call(body, name=f'coarse{layer}', out_shape=tuple(shapes), in_s...  10.8 us
    ppermute x14, waiting for transfers between devices, shift(): return lax.ppermute(values, 'py', pairs)  10.5 us
    all_to_all x1, starting transfers between devices, shards(): lax.all_to_all(packed, AXES, split_axis=0, concat_axis=0, tiled=True)  9.04 us
    unnamed x38, local copies, waits for them, and re-layouts  5.18 us
    ppermute x2, waiting for transfers between devices, around_x(): lax.ppermute(values, 'px', [(i, i // 4 * 4 + (i + step) % 4) for i in ran...  4.8 us
  transfers between devices with their start and end apart: 31, of which 14 were waited for; matrix products, arithmetic and copies ran while one was open for 0% of the time, Pallas kernels for 20%

profile of v9, /device:TPU:1, one launch (start us, length us, event | category | flops | bytes accessed | tf_op | source)
XLA Modules:
  0.0 108.7 jit_solution(6078792198552358902)
XLA Ops:
  0.6 1.3 %coarse_start.1 = (bf16[20,512]{1,0:T(8,128)(2,1)S(1)}, bf16[20,512]{1,0:T(8,128)(2,1)S(1)}, bf16[20,512]{1,0:T(8,128)(2,1)S(1)}, bf16[16,512]{1,0:T(8,128)(2,1)...) custom-call(s32[1,20]{1,0:T(1,128)} %bitcast.24, bf16[320,512]{1,0:T(8,128)(2,1)} %bitcast.19), custom_call_target="tpu_custom_call" | custom-call | tf_op jit(solution)/shard_map/coarse_start/pallas_call | solution.py:292
  2.0 3.6 %collective-permute-start.2 = (bf16[20,512]{1,0:T(8,128)(2,1)S(1)}, bf16[20,512]{1,0:T(8,128)(2,1)S(1)}, u32[]{:S(2)}, u32[]{:S(2)}) collective-permute-start(bf16[20,512]{1,0:T(8,128)(2,1)S(1)} %get-tuple-element.71.own_ref), channel_id=1, source_target_pairs={{0,96},{8,104},{16,112},{24,120},{32,0},{40,8},{48,16},{56,24},{64... | collective-permute-start | bytes 61448 | tf_op jit(solution)/shard_map/ppermute | solution.py:52
  6.0 0.7 collective-permute-start
  6.7 3.0 %collective-permute-start.3 = (bf16[16,512]{1,0:T(8,128)(2,1)S(1)}, bf16[16,512]{1,0:T(8,128)(2,1)S(1)}, u32[]{:S(2)}, u32[]{:S(2)}) collective-permute-start(bf16[16,512]{1,0:T(8,128)(2,1)S(1)} %get-tuple-element.72), channel_id=1, source_target_pairs={{0,1},{1,2},{2,3},{3,4},{4,5},{5,6},{6,7},{7,0},{8,9},{9,10},{10,1... | collective-permute-start | bytes 49160 | tf_op jit(solution)/shard_map/ppermute | solution.py:52
  9.7 2.5 %pack_edges.1 = (bf16[2048,128]{1,0:T(8,128)(2,1)}, bf16[160,128]{1,0:T(8,128)(2,1)S(1)}) custom-call(s32[1]{0:T(128)} %bitcast.3.me_ref, bf16[160,512]{1,0:T(8,128)(2,1)} %long_ref, s32[1,160]{1,0:T(1,128)} %bitcast.27, s32[1,160]{1,0:T(1,128)} %bitcast.28), custom_call_target="tpu_custom_call" | custom-call | flops 12000000000 | tf_op jit(solution)/shard_map/pack_edges/pallas_call | solution.py:351
  12.3 0.6 collective-permute-done.4.right_ref
  12.9 1.3 %collective-permute-start.6 = (bf16[112,512]{1,0:T(8,128)(2,1)S(1)}, bf16[112,512]{1,0:T(8,128)(2,1)S(1)}, u32[]{:S(2)}, u32[]{:S(2)}) collective-permute-start(bf16[112,512]{1,0:T(8,128)(2,1)S(1)} %get-tuple-element.84), channel_id=1, source_target_pairs={{0,8},{8,16},{16,24},{24,32},{32,40},{40,48},{48,56},{56,64},{64,7... | collective-permute-start | bytes 344072 | tf_op jit(solution)/shard_map/ppermute | solution.py:52
  14.2 3.6 %collective-permute-start.7 = (bf16[112,512]{1,0:T(8,128)(2,1)S(1)}, bf16[112,512]{1,0:T(8,128)(2,1)}, u32[]{:S(2)}, u32[]{:S(2)}) collective-permute-start(bf16[112,512]{1,0:T(8,128)(2,1)S(1)} %get-tuple-element.85), channel_id=1, source_target_pairs={{0,120},{8,0},{16,8},{24,16},{32,24},{40,32},{48,40},{56,48},{64,5... | collective-permute-start | bytes 344072 | tf_op jit(solution)/shard_map/ppermute | solution.py:52
  17.8 9.0 %all-to-all-start = ((bf16[128,16,128]{2,1,0:T(8,128)(2,1)}), bf16[128,16,128]{2,1,0:T(8,128)(2,1)}, u32[]{:S(2)}, u32[]{:S(2)}) async-start(bf16[128,16,128]{2,1,0:T(8,128)(2,1)} %bitcast.8), calls=%async_computation | async-start | bytes 1048576 | tf_op jit(solution)/shard_map/all_to_all | solution.py:552
  26.9 0.6 copy-done.18
  27.5 0.6 copy-done.17
  28.2 1.9 %join_near.2 = (bf16[320,512]{1,0:T(8,128)(2,1)}, bf16[64,512]{1,0:T(8,128)(2,1)}) custom-call(bf16[80,512]{1,0:T(8,128)(2,1)} %copy-done.16, bf16[80,512]{1,0:T(8,128)(2,1)} %copy-done.18, bf16[112,512]{1,0:T(8,128)(2,1)} %copy-done.17, bf16[112,512]{1,0:T(8,128)(2,1)} %collective-permute-done.7.down_ref), custom_call_target="tpu_custom_call" | custom-call | flops 3000000000 | tf_op jit(solution)/shard_map/join_near/pallas_call | solution.py:249
  30.1 3.3 %collective-permute-start.10 = (bf16[320,512]{1,0:T(8,128)(2,1)}, bf16[320,512]{1,0:T(8,128)(2,1)}, u32[]{:S(2)}, u32[]{:S(2)}) collective-permute-start(bf16[320,512]{1,0:T(8,128)(2,1)} %get-tuple-element.88.rest_0_), channel_id=1, source_target_pairs={{0,6},{1,7},{2,0},{3,1},{4,2},{5,3},{6,4},{7,5},{8,14},{9,15},{10,... | collective-permute-start | bytes 983048 | tf_op jit(solution)/shard_map/ppermute | solution.py:25
  33.6 0.8 collective-permute-start.8
  34.3 1.2 %collective-permute-start.11 = (bf16[320,512]{1,0:T(8,128)(2,1)}, bf16[320,512]{1,0:T(8,128)(2,1)}, u32[]{:S(2)}, u32[]{:S(2)}) collective-permute-start(bf16[320,512]{1,0:T(8,128)(2,1)} %get-tuple-element.88.rest_0_), channel_id=1, source_target_pairs={{0,1},{1,0},{2,3},{3,2},{4,5},{5,4},{6,7},{7,6},{8,9},{9,8},{10,11... | collective-permute-start | bytes 983048 | tf_op jit(solution)/shard_map/ppermute | solution.py:25
  35.5 4.7 %all-to-all-done = bf16[128,16,128]{2,1,0:T(8,128)(2,1)} async-done(((bf16[128,16,128]{2,1,0:T(8,128)(2,1)}), bf16[128,16,128]{2,1,0:T(8,128)(2,1)}, u32[]{:S(2)}, u32[]{:S(2)}) %all-to-all-start) | async-done | bytes 524320 | tf_op jit(solution)/shard_map/all_to_all | solution.py:552
  40.3 2.4 %unpack_edges.1 = (bf16[384,512]{1,0:T(8,128)(2,1)S(1)}, bf16[384,2560]{1,0:T(8,128)(2,1)S(1)}, bf16[384,128]{1,0:T(8,128)(2,1)S(1)}, bf16[320,384]{1,0:T(8,128)(2,1)S(1)}) custom-call(bf16[2048,128]{1,0:T(8,128)(2,1)} %bitcast.9.arrived_ref, bf16[60,320]{1,0:T(8,128)(2,1)S(1)} %get-tuple-element.90.choose_ref), custom_call_target="tpu_custom_call" | custom-call | tf_op jit(solution)/shard_map/unpack_edges/pallas_call | solution.py:392
  42.7 0.8 copy-done.12
  43.9 1.5 %copy-done.5 = bf16[16,20,6,512]{3,0,2,1:T(8,128)(2,1)S(1)} copy-done((bf16[16,20,6,512]{3,0,2,1:T(8,128)(2,1)S(1)}, bf16[16,20,6,512]{3,0,2,1:T(8,128)(2,1)}, u32[]{:S(2)}) %copy-start.5) | copy-done | bytes 1966104
  45.4 0.8 copy-done.9
  46.2 0.7 copy-done.11
  47.0 5.9 %fine0.1 = (bf16[1920,512]{1,0:T(8,128)(2,1)S(1)}, f32[320,512]{1,0:T(8,128)S(1)}) custom-call(bf16[1920,512]{1,0:T(8,128)(2,1)S(1)} %bitcast.22, bf16[1920,256]{1,0:T(8,128)(2,1)S(1)} %selection.1.picks_ref, bf16[320,512]{1,0:T(8,128)(2,1)S(1)} %bitcast.20, bf16[16,512]{1,0:T(8,128)(2,1)S(1)} %collective-permute-done.3.left_ref, ...), custom_call_target="tpu_custom_call" | custom-call | tf_op jit(solution)/shard_map/fine0/pallas_call | solution.py:135
  52.9 1.2 %collective-permute-start.12 = (bf16[320,512]{1,0:T(8,128)(2,1)}, bf16[320,512]{1,0:T(8,128)(2,1)S(1)}, u32[]{:S(2)}, u32[]{:S(2)}) collective-permute-start(bf16[320,512]{1,0:T(8,128)(2,1)} %collective-permute-done.8.rest_1_), channel_id=1, source_target_pairs={{0,1},{1,0},{2,3},{3,2},{4,5},{5,4},{6,7},{7,6},{8,9},{9,8},{10,11... | collective-permute-start | bytes 983048 | tf_op jit(solution)/shard_map/ppermute | solution.py:25
  54.7 1.0 collective-permute-done.12.rest_5_
  56.1 0.5 collective-permute-done.14.rest_7_
  56.6 5.3 %coarse0.1 = (bf16[320,512]{1,0:T(8,128)(2,1)S(1)}, bf16[384,512]{1,0:T(8,128)(2,1)S(1)}, bf16[20,512]{1,0:T(8,128)(2,1)S(1)}, bf16[20,512]{1,0:T(8,128)(2,1)S(1...) custom-call(bf16[384,512]{1,0:T(8,128)(2,1)S(1)} %get-tuple-element., ...), custom_call_target="tpu_custom_call" | custom-call | tf_op jit(solution)/shard_map/coarse0/pallas_call | solution.py:470
  61.8 1.0 collective-permute-start.17
  62.8 1.2 %collective-permute-start.16 = (bf16[20,512]{1,0:T(8,128)(2,1)S(1)}, bf16[20,512]{1,0:T(8,128)(2,1)S(1)}, u32[]{:S(2)}, u32[]{:S(2)}) collective-permute-start(bf16[20,512]{1,0:T(8,128)(2,1)S(1)} %get-tuple-element.107.own_ref), channel_id=1, source_target_pairs={{0,64},{8,72},{16,80},{24,88},{32,96},{40,104},{48,112},{56,120},{... | collective-permute-start | bytes 61448 | tf_op jit(solution)/shard_map/ppermute | solution.py:52
  64.0 0.6 collective-permute-start.18
  64.6 0.5 collective-permute-start.19
  65.1 0.7 collective-permute-done.18.left_ref
  65.8 2.3 %collective-permute-done.19.right_ref = bf16[16,512]{1,0:T(8,128)(2,1)S(1)} collective-permute-done((bf16[16,512]{1,0:T(8,128)(2,1)S(1)}, bf16[16,512]{1,0:T(8,128)(2,1)S(1)}, u32[]{:S(2)}, u32[]{:S(2)}) %collective-permute-start.19) | collective-permute-done | bytes 16416 | tf_op jit(solution)/shard_map/ppermute | solution.py:52
  68.2 0.5 collective-permute-start.21
  68.7 4.4 %collective-permute-start.22 = (bf16[112,512]{1,0:T(8,128)(2,1)S(1)}, bf16[112,512]{1,0:T(8,128)(2,1)S(1)}, u32[]{:S(2)}, u32[]{:S(2)}) collective-permute-start(bf16[112,512]{1,0:T(8,128)(2,1)S(1)} %get-tuple-element.114), channel_id=1, source_target_pairs={{0,120},{8,0},{16,8},{24,16},{32,24},{40,32},{48,40},{56,48},{64,5... | collective-permute-start | bytes 344072 | tf_op jit(solution)/shard_map/ppermute | solution.py:52
  73.1 4.8 %collective-permute-done.20.two_ref = bf16[80,512]{1,0:T(8,128)(2,1)S(1)} collective-permute-done((bf16[80,512]{1,0:T(8,128)(2,1)S(1)}, bf16[80,512]{1,0:T(8,128)(2,1)S(1)}, u32[]{:S(2)}, u32[]{:S(2)}) %collective-permute-start.20) | collective-permute-done | bytes 81952 | tf_op jit(solution)/shard_map/ppermute | solution.py:47
  77.9 0.6 join_near.3
  78.5 4.0 %collective-permute-start.25 = (bf16[320,512]{1,0:T(8,128)(2,1)S(1)}, bf16[320,512]{1,0:T(8,128)(2,1)S(1)}, u32[]{:S(2)}, u32[]{:S(2)}) collective-permute-start(bf16[320,512]{1,0:T(8,128)(2,1)S(1)} %get-tuple-element.117.rest_0_), channel_id=1, source_target_pairs={{0,6},{1,7},{2,0},{3,1},{4,2},{5,3},{6,4},{7,5},{8,14},{9,15},{10,... | collective-permute-start | bytes 983048 | tf_op jit(solution)/shard_map/ppermute | solution.py:25
  82.4 0.7 collective-permute-start.23
  83.1 0.9 collective-permute-start.26
  84.0 2.3 %own0.1 = (bf16[160,512]{1,0:T(8,128)(2,1)S(1)}, bf16[704,2560]{1,0:T(8,128)(2,1)S(1)}) custom-call(bf16[160,512]{1,0:T(8,128)(2,1)S(1)} %copy-done.6, bf16[160,128]{1,0:T(8,128)(2,1)S(1)} %copy-done.14, bf16[384,2560]{1,0:T(8,128)(2,1)S(1)} %get-tuple-element.100.sends_ref, bf16[2560,512]{1,0:T(8,128)(2,1)S(1)} %get-tuple-element.124.table_ref, ...), custom_call_target="tpu_custom_call" | custom-call | tf_op jit(solution)/shard_map/own0/pallas_call | solution.py:500
  86.3 6.7 %fine1.1 = (bf16[1920,512]{1,0:T(8,128)(2,1)}, f32[320,512]{1,0:T(8,128)S(1)}) custom-call(bf16[1920,512]{1,0:T(8,128)(2,1)S(1)} %get-tuple-element.118.fine_ref, bf16[1920,256]{1,0:T(8,128)(2,1)S(1)} %selection.1.picks_ref, bf16[320,512]{1,0:T(8,128)(2,1)S(1)} %get-tuple-element.119.latents_ref, bf16[16,512]{1,0:T(8,128)(2,1)S(1)} %collective-permute-done.18.left_ref, ...), custom_call_target="tpu_custom_call" | custom-call | tf_op jit(solution)/shard_map/fine1/pallas_call | solution.py:135
  93.1 3.9 %collective-permute-done.25.rest_3_ = bf16[320,512]{1,0:T(8,128)(2,1)S(1)} collective-permute-done((bf16[320,512]{1,0:T(8,128)(2,1)S(1)}, bf16[320,512]{1,0:T(8,128)(2,1)S(1)}, u32[]{:S(2)}, u32[]{:S(2)}) %collective-permute-start.25) | collective-permute-done | bytes 327712 | tf_op jit(solution)/shard_map/ppermute | solution.py:25
  97.0 3.0 %collective-permute-done.23.rest_1_ = bf16[320,512]{1,0:T(8,128)(2,1)S(1)} collective-permute-done((bf16[320,512]{1,0:T(8,128)(2,1)S(1)}, bf16[320,512]{1,0:T(8,128)(2,1)S(1)}, u32[]{:S(2)}, u32[]{:S(2)}) %collective-permute-start.23) | collective-permute-done | bytes 327712 | tf_op jit(solution)/shard_map/ppermute | solution.py:25
  99.9 0.9 collective-permute-start.27
  100.8 0.5 collective-permute-start.29
  101.3 0.7 collective-permute-done.27.rest_5_
  102.5 0.5 collective-permute-done.29.rest_7_
  103.0 5.6 %coarse1.1 = (bf16[320,512]{1,0:T(8,128)(2,1)}, bf16[160,512]{1,0:T(8,128)(2,1)}) custom-call(bf16[384,512]{1,0:T(8,128)(2,1)S(1)} %get-tuple-element.127.long_ref, bf16[160,512]{1,0:T(8,128)(2,1)S(1)} %get-tuple-element.128.own_ref, bf16[704,2560]{1,0:T(8,128)(2,1)S(1)} %get-tuple-element.129.sends_ref, bf16[384,128]{1,0:T(8,128)(2,1)S(1)} %get-tuple-element.101.recvs_ref, ...), custom_call_target="tpu_custom_call" | custom-call | tf_op jit(solution)/shard_map/coarse1/pallas_call | solution.py:470
  (65 shorter events, 2.6 us)
Async XLA Ops:
  2.0 10.9 %collective-permute-start.2 = (bf16[20,512]{1,0:T(8,128)(2,1)S(1)}, bf16[20,512]{1,0:T(8,128)(2,1)S(1)}, u32[]{:S(2)}, u32[]{:S(2)}) collective-permute-start(bf16[20,512]{1,0:T(8,128)(2,1)S(1)} %get-tuple-element.71.own_ref), channel_id=1, source_target_pairs={{0,96},{8,104},{16,112},{24,120},{32,0},{40,8},{48,16},{56,24},{64... | collective-permute-start | bytes 61448 | tf_op jit(solution)/shard_map/ppermute | solution.py:52
  5.6 7.3 %collective-permute-start.1 = (bf16[20,512]{1,0:T(8,128)(2,1)S(1)}, bf16[20,512]{1,0:T(8,128)(2,1)S(1)}, u32[]{:S(2)}, u32[]{:S(2)}) collective-permute-start(bf16[20,512]{1,0:T(8,128)(2,1)S(1)} %get-tuple-element.71.own_ref), channel_id=1, source_target_pairs={{0,64},{8,72},{16,80},{24,88},{32,96},{40,104},{48,112},{56,120},{... | collective-permute-start | bytes 61448 | tf_op jit(solution)/shard_map/ppermute | solution.py:52
  6.0 6.9 %collective-permute-start = (bf16[20,512]{1,0:T(8,128)(2,1)S(1)}, bf16[20,512]{1,0:T(8,128)(2,1)S(1)}, u32[]{:S(2)}, u32[]{:S(2)}) collective-permute-start(bf16[20,512]{1,0:T(8,128)(2,1)S(1)} %get-tuple-element.71.own_ref), channel_id=1, source_target_pairs={{0,32},{8,40},{16,48},{24,56},{32,64},{40,72},{48,80},{56,88},{64,... | collective-permute-start | bytes 61448 | tf_op jit(solution)/shard_map/ppermute | solution.py:52
  6.7 5.6 %collective-permute-start.3 = (bf16[16,512]{1,0:T(8,128)(2,1)S(1)}, bf16[16,512]{1,0:T(8,128)(2,1)S(1)}, u32[]{:S(2)}, u32[]{:S(2)}) collective-permute-start(bf16[16,512]{1,0:T(8,128)(2,1)S(1)} %get-tuple-element.72), channel_id=1, source_target_pairs={{0,1},{1,2},{2,3},{3,4},{4,5},{5,6},{6,7},{7,0},{8,9},{9,10},{10,1... | collective-permute-start | bytes 49160 | tf_op jit(solution)/shard_map/ppermute | solution.py:52
  9.7 3.2 %collective-permute-start.4 = (bf16[16,512]{1,0:T(8,128)(2,1)S(1)}, bf16[16,512]{1,0:T(8,128)(2,1)S(1)}, u32[]{:S(2)}, u32[]{:S(2)}) collective-permute-start(bf16[16,512]{1,0:T(8,128)(2,1)S(1)} %get-tuple-element.73), channel_id=1, source_target_pairs={{0,7},{1,0},{2,1},{3,2},{4,3},{5,4},{6,5},{7,6},{8,15},{9,8},{10,9... | collective-permute-start | bytes 49160 | tf_op jit(solution)/shard_map/ppermute | solution.py:52
  12.3 14.7 %copy-start.13 = (bf16[160,128]{1,0:T(8,128)(2,1)}, bf16[160,128]{1,0:T(8,128)(2,1)S(1)}, u32[]{:S(2)}) copy-start(bf16[160,128]{1,0:T(8,128)(2,1)S(1)} %get-tuple-element.123.tags_ref) | copy-start | bytes 122884
  12.9 14.1 %copy-start.10 = (bf16[16,512]{1,0:T(8,128)(2,1)}, bf16[16,512]{1,0:T(8,128)(2,1)S(1)}, u32[]{:S(2)}) copy-start(bf16[16,512]{1,0:T(8,128)(2,1)S(1)} %collective-permute-done.4.right_ref) | copy-start | bytes 49156
  12.9 14.0 %copy-start.16 = (bf16[80,512]{1,0:T(8,128)(2,1)}, bf16[80,512]{1,0:T(8,128)(2,1)S(1)}, u32[]{:S(2)}) copy-start(bf16[80,512]{1,0:T(8,128)(2,1)S(1)} %get-tuple-element.83.own_ref) | copy-start | bytes 245764
  12.9 14.0 %collective-permute-start.6 = (bf16[112,512]{1,0:T(8,128)(2,1)S(1)}, bf16[112,512]{1,0:T(8,128)(2,1)S(1)}, u32[]{:S(2)}, u32[]{:S(2)}) collective-permute-start(bf16[112,512]{1,0:T(8,128)(2,1)S(1)} %get-tuple-element.84), channel_id=1, source_target_pairs={{0,8},{8,16},{16,24},{24,32},{32,40},{40,48},{48,56},{56,64},{64,7... | collective-permute-start | bytes 344072 | tf_op jit(solution)/shard_map/ppermute | solution.py:52
  14.2 13.9 %collective-permute-start.7 = (bf16[112,512]{1,0:T(8,128)(2,1)S(1)}, bf16[112,512]{1,0:T(8,128)(2,1)}, u32[]{:S(2)}, u32[]{:S(2)}) collective-permute-start(bf16[112,512]{1,0:T(8,128)(2,1)S(1)} %get-tuple-element.85), channel_id=1, source_target_pairs={{0,120},{8,0},{16,8},{24,16},{32,24},{40,32},{48,40},{56,48},{64,5... | collective-permute-start | bytes 344072 | tf_op jit(solution)/shard_map/ppermute | solution.py:52
  17.8 9.1 %collective-permute-start.5 = (bf16[80,512]{1,0:T(8,128)(2,1)S(1)}, bf16[80,512]{1,0:T(8,128)(2,1)S(1)}, u32[]{:S(2)}, u32[]{:S(2)}) collective-permute-start(bf16[80,512]{1,0:T(8,128)(2,1)S(1)} %get-tuple-element.83.own_ref), channel_id=1, source_target_pairs={{0,16},{8,24},{16,0},{24,8},{32,48},{40,56},{48,32},{56,40},{64,80... | collective-permute-start | bytes 245768 | tf_op jit(solution)/shard_map/ppermute | solution.py:47
  17.8 22.5 %all-to-all-start = ((bf16[128,16,128]{2,1,0:T(8,128)(2,1)}), bf16[128,16,128]{2,1,0:T(8,128)(2,1)}, u32[]{:S(2)}, u32[]{:S(2)}) async-start(bf16[128,16,128]{2,1,0:T(8,128)(2,1)} %bitcast.8), calls=%async_computation | async-start | bytes 1048576 | tf_op jit(solution)/shard_map/all_to_all | solution.py:552
  26.8 17.0 %copy-start.4 = (bf16[16,20,512]{2,0,1:T(8,128)(2,1)S(1)}, bf16[16,20,512]{2,0,1:T(8,128)(2,1)}, u32[]{:S(2)}) copy-start(bf16[16,20,512]{2,0,1:T(8,128)(2,1)} %param.13) | copy-start | bytes 983044
  26.9 17.0 %copy-start.8 = (f32[2,512]{1,0:T(2,128)S(1)}, f32[2,512]{1,0:T(2,128)}, u32[]{:S(2)}) copy-start(f32[2,512]{1,0:T(2,128)} %eg_ref.5) | copy-start | bytes 12292
  28.2 15.7 %copy-start = (bf16[2,1536,512]{2,1,0:T(8,128)(2,1)S(1)}, bf16[2,1536,512]{2,1,0:T(8,128)(2,1)}, u32[]{:S(2)}) copy-start(bf16[2,1536,512]{2,1,0:T(8,128)(2,1)} %ei_ref.5) | copy-start | bytes 9437188
  30.1 22.7 %collective-permute-start.10 = (bf16[320,512]{1,0:T(8,128)(2,1)}, bf16[320,512]{1,0:T(8,128)(2,1)}, u32[]{:S(2)}, u32[]{:S(2)}) collective-permute-start(bf16[320,512]{1,0:T(8,128)(2,1)} %get-tuple-element.88.rest_0_), channel_id=1, source_target_pairs={{0,6},{1,7},{2,0},{3,1},{4,2},{5,3},{6,4},{7,5},{8,14},{9,15},{10,... | collective-permute-start | bytes 983048 | tf_op jit(solution)/shard_map/ppermute | solution.py:25
  33.4 19.4 %collective-permute-start.9 = (bf16[320,512]{1,0:T(8,128)(2,1)}, bf16[320,512]{1,0:T(8,128)(2,1)}, u32[]{:S(2)}, u32[]{:S(2)}) collective-permute-start(bf16[320,512]{1,0:T(8,128)(2,1)} %get-tuple-element.88.rest_0_), channel_id=1, source_target_pairs={{0,4},{1,5},{2,6},{3,7},{4,0},{5,1},{6,2},{7,3},{8,12},{9,13},{10,... | collective-permute-start | bytes 983048 | tf_op jit(solution)/shard_map/ppermute | solution.py:25
  33.6 19.3 %collective-permute-start.8 = (bf16[320,512]{1,0:T(8,128)(2,1)}, bf16[320,512]{1,0:T(8,128)(2,1)}, u32[]{:S(2)}, u32[]{:S(2)}) collective-permute-start(bf16[320,512]{1,0:T(8,128)(2,1)} %get-tuple-element.88.rest_0_), channel_id=1, source_target_pairs={{0,2},{1,3},{2,4},{3,5},{4,6},{5,7},{6,0},{7,1},{8,10},{9,11},{10,... | collective-permute-start | bytes 983048 | tf_op jit(solution)/shard_map/ppermute | solution.py:25
  34.3 20.3 %collective-permute-start.11 = (bf16[320,512]{1,0:T(8,128)(2,1)}, bf16[320,512]{1,0:T(8,128)(2,1)}, u32[]{:S(2)}, u32[]{:S(2)}) collective-permute-start(bf16[320,512]{1,0:T(8,128)(2,1)} %get-tuple-element.88.rest_0_), channel_id=1, source_target_pairs={{0,1},{1,0},{2,3},{3,2},{4,5},{5,4},{6,7},{7,6},{8,9},{9,8},{10,11... | collective-permute-start | bytes 983048 | tf_op jit(solution)/shard_map/ppermute | solution.py:25
  40.3 3.6 %copy-start.1 = (bf16[2,512,512]{2,1,0:T(8,128)(2,1)S(1)}, bf16[2,512,512]{2,1,0:T(8,128)(2,1)}, u32[]{:S(2)}) copy-start(bf16[2,512,512]{2,1,0:T(8,128)(2,1)} %eo_ref.5) | copy-start | bytes 3145732
  42.6 0.8 copy-start.12
  43.9 1.5 %copy-start.5 = (bf16[16,20,6,512]{3,0,2,1:T(8,128)(2,1)S(1)}, bf16[16,20,6,512]{3,0,2,1:T(8,128)(2,1)}, u32[]{:S(2)}) copy-start(bf16[16,20,6,512]{3,0,2,1:T(8,128)(2,1)} %param.14) | copy-start | bytes 5898244
  45.4 0.8 copy-start.9
  46.2 0.7 copy-start.11
  47.0 9.6 %copy-start.2 = (bf16[2,1024,512]{2,1,0:T(8,128)(2,1)S(1)}, bf16[2,1024,512]{2,1,0:T(8,128)(2,1)}, u32[]{:S(2)}) copy-start(bf16[2,1024,512]{2,1,0:T(8,128)(2,1)} %ni_ref.3) | copy-start | bytes 6291460
  47.0 9.6 %copy-start.3 = (bf16[2,512,512]{2,1,0:T(8,128)(2,1)S(1)}, bf16[2,512,512]{2,1,0:T(8,128)(2,1)}, u32[]{:S(2)}) copy-start(bf16[2,512,512]{2,1,0:T(8,128)(2,1)} %no_ref.3) | copy-start | bytes 3145732
  47.0 9.6 %copy-start.6 = (bf16[160,512]{1,0:T(8,128)(2,1)S(1)}, bf16[160,512]{1,0:T(8,128)(2,1)}, u32[]{:S(2)}) copy-start(bf16[160,512]{1,0:T(8,128)(2,1)} %long_ref) | copy-start | bytes 491524
  47.0 9.6 %copy-start.7 = (bf16[320,512]{1,0:T(8,128)(2,1)S(1)}, bf16[320,512]{1,0:T(8,128)(2,1)}, u32[]{:S(2)}) copy-start(bf16[320,512]{1,0:T(8,128)(2,1)} %get-tuple-element.88.rest_0_) | copy-start | bytes 983044
  47.0 9.6 %copy-start.15 = (f32[2,512]{1,0:T(2,128)S(1)}, f32[2,512]{1,0:T(2,128)}, u32[]{:S(2)}) copy-start(f32[2,512]{1,0:T(2,128)} %ng_ref.3) | copy-start | bytes 12292
  52.9 2.7 %collective-permute-start.12 = (bf16[320,512]{1,0:T(8,128)(2,1)}, bf16[320,512]{1,0:T(8,128)(2,1)S(1)}, u32[]{:S(2)}, u32[]{:S(2)}) collective-permute-start(bf16[320,512]{1,0:T(8,128)(2,1)} %collective-permute-done.8.rest_1_), channel_id=1, source_target_pairs={{0,1},{1,0},{2,3},{3,2},{4,5},{5,4},{6,7},{7,6},{8,9},{9,8},{10,11... | collective-permute-start | bytes 983048 | tf_op jit(solution)/shard_map/ppermute | solution.py:25
  54.1 1.9 %collective-permute-start.13 = (bf16[320,512]{1,0:T(8,128)(2,1)}, bf16[320,512]{1,0:T(8,128)(2,1)S(1)}, u32[]{:S(2)}, u32[]{:S(2)}) collective-permute-start(bf16[320,512]{1,0:T(8,128)(2,1)} %collective-permute-done.9.rest_2_), channel_id=1, source_target_pairs={{0,1},{1,0},{2,3},{3,2},{4,5},{5,4},{6,7},{7,6},{8,9},{9,8},{10,11... | collective-permute-start | bytes 983048 | tf_op jit(solution)/shard_map/ppermute | solution.py:25
  54.2 2.3 %collective-permute-start.14 = (bf16[320,512]{1,0:T(8,128)(2,1)}, bf16[320,512]{1,0:T(8,128)(2,1)S(1)}, u32[]{:S(2)}, u32[]{:S(2)}) collective-permute-start(bf16[320,512]{1,0:T(8,128)(2,1)} %collective-permute-done.10.rest_3_), channel_id=1, source_target_pairs={{0,1},{1,0},{2,3},{3,2},{4,5},{5,4},{6,7},{7,6},{8,9},{9,8},{10,11... | collective-permute-start | bytes 983048 | tf_op jit(solution)/shard_map/ppermute | solution.py:25
  61.8 6.2 %collective-permute-start.17 = (bf16[20,512]{1,0:T(8,128)(2,1)S(1)}, bf16[20,512]{1,0:T(8,128)(2,1)S(1)}, u32[]{:S(2)}, u32[]{:S(2)}) collective-permute-start(bf16[20,512]{1,0:T(8,128)(2,1)S(1)} %get-tuple-element.107.own_ref), channel_id=1, source_target_pairs={{0,96},{8,104},{16,112},{24,120},{32,0},{40,8},{48,16},{56,24},{64... | collective-permute-start | bytes 61448 | tf_op jit(solution)/shard_map/ppermute | solution.py:52
  62.8 5.3 %collective-permute-start.16 = (bf16[20,512]{1,0:T(8,128)(2,1)S(1)}, bf16[20,512]{1,0:T(8,128)(2,1)S(1)}, u32[]{:S(2)}, u32[]{:S(2)}) collective-permute-start(bf16[20,512]{1,0:T(8,128)(2,1)S(1)} %get-tuple-element.107.own_ref), channel_id=1, source_target_pairs={{0,64},{8,72},{16,80},{24,88},{32,96},{40,104},{48,112},{56,120},{... | collective-permute-start | bytes 61448 | tf_op jit(solution)/shard_map/ppermute | solution.py:52
  64.0 4.2 %collective-permute-start.15 = (bf16[20,512]{1,0:T(8,128)(2,1)S(1)}, bf16[20,512]{1,0:T(8,128)(2,1)S(1)}, u32[]{:S(2)}, u32[]{:S(2)}) collective-permute-start(bf16[20,512]{1,0:T(8,128)(2,1)S(1)} %get-tuple-element.107.own_ref), channel_id=1, source_target_pairs={{0,32},{8,40},{16,48},{24,56},{32,64},{40,72},{48,80},{56,88},{64,... | collective-permute-start | bytes 61448 | tf_op jit(solution)/shard_map/ppermute | solution.py:52
  64.0 1.8 %collective-permute-start.18 = (bf16[16,512]{1,0:T(8,128)(2,1)S(1)}, bf16[16,512]{1,0:T(8,128)(2,1)S(1)}, u32[]{:S(2)}, u32[]{:S(2)}) collective-permute-start(bf16[16,512]{1,0:T(8,128)(2,1)S(1)} %get-tuple-element.108), channel_id=1, source_target_pairs={{0,1},{1,2},{2,3},{3,4},{4,5},{5,6},{6,7},{7,0},{8,9},{9,10},{10,1... | collective-permute-start | bytes 49160 | tf_op jit(solution)/shard_map/ppermute | solution.py:52
  64.6 3.5 %collective-permute-start.19 = (bf16[16,512]{1,0:T(8,128)(2,1)S(1)}, bf16[16,512]{1,0:T(8,128)(2,1)S(1)}, u32[]{:S(2)}, u32[]{:S(2)}) collective-permute-start(bf16[16,512]{1,0:T(8,128)(2,1)S(1)} %get-tuple-element.109), channel_id=1, source_target_pairs={{0,7},{1,0},{2,1},{3,2},{4,3},{5,4},{6,5},{7,6},{8,15},{9,8},{10,9... | collective-permute-start | bytes 49160 | tf_op jit(solution)/shard_map/ppermute | solution.py:52
  68.2 9.7 %collective-permute-start.21 = (bf16[112,512]{1,0:T(8,128)(2,1)S(1)}, bf16[112,512]{1,0:T(8,128)(2,1)S(1)}, u32[]{:S(2)}, u32[]{:S(2)}) collective-permute-start(bf16[112,512]{1,0:T(8,128)(2,1)S(1)} %get-tuple-element.113), channel_id=1, source_target_pairs={{0,8},{8,16},{16,24},{24,32},{32,40},{40,48},{48,56},{56,64},{64,7... | collective-permute-start | bytes 344072 | tf_op jit(solution)/shard_map/ppermute | solution.py:52
  68.7 9.2 %collective-permute-start.22 = (bf16[112,512]{1,0:T(8,128)(2,1)S(1)}, bf16[112,512]{1,0:T(8,128)(2,1)S(1)}, u32[]{:S(2)}, u32[]{:S(2)}) collective-permute-start(bf16[112,512]{1,0:T(8,128)(2,1)S(1)} %get-tuple-element.114), channel_id=1, source_target_pairs={{0,120},{8,0},{16,8},{24,16},{32,24},{40,32},{48,40},{56,48},{64,5... | collective-permute-start | bytes 344072 | tf_op jit(solution)/shard_map/ppermute | solution.py:52
  73.1 11.0 %copy-start.14 = (bf16[160,128]{1,0:T(8,128)(2,1)S(1)}, bf16[160,128]{1,0:T(8,128)(2,1)}, u32[]{:S(2)}) copy-start(bf16[160,128]{1,0:T(8,128)(2,1)} %copy-done.13) | copy-start | bytes 122884
  73.1 4.8 %collective-permute-start.20 = (bf16[80,512]{1,0:T(8,128)(2,1)S(1)}, bf16[80,512]{1,0:T(8,128)(2,1)S(1)}, u32[]{:S(2)}, u32[]{:S(2)}) collective-permute-start(bf16[80,512]{1,0:T(8,128)(2,1)S(1)} %get-tuple-element.112.own_ref), channel_id=1, source_target_pairs={{0,16},{8,24},{16,0},{24,8},{32,48},{40,56},{48,32},{56,40},{64,80... | collective-permute-start | bytes 245768 | tf_op jit(solution)/shard_map/ppermute | solution.py:47
  78.5 18.5 %collective-permute-start.25 = (bf16[320,512]{1,0:T(8,128)(2,1)S(1)}, bf16[320,512]{1,0:T(8,128)(2,1)S(1)}, u32[]{:S(2)}, u32[]{:S(2)}) collective-permute-start(bf16[320,512]{1,0:T(8,128)(2,1)S(1)} %get-tuple-element.117.rest_0_), channel_id=1, source_target_pairs={{0,6},{1,7},{2,0},{3,1},{4,2},{5,3},{6,4},{7,5},{8,14},{9,15},{10,... | collective-permute-start | bytes 983048 | tf_op jit(solution)/shard_map/ppermute | solution.py:25
  82.4 14.6 %collective-permute-start.24 = (bf16[320,512]{1,0:T(8,128)(2,1)S(1)}, bf16[320,512]{1,0:T(8,128)(2,1)S(1)}, u32[]{:S(2)}, u32[]{:S(2)}) collective-permute-start(bf16[320,512]{1,0:T(8,128)(2,1)S(1)} %get-tuple-element.117.rest_0_), channel_id=1, source_target_pairs={{0,4},{1,5},{2,6},{3,7},{4,0},{5,1},{6,2},{7,3},{8,12},{9,13},{10,... | collective-permute-start | bytes 983048 | tf_op jit(solution)/shard_map/ppermute | solution.py:25
  82.4 17.5 %collective-permute-start.23 = (bf16[320,512]{1,0:T(8,128)(2,1)S(1)}, bf16[320,512]{1,0:T(8,128)(2,1)S(1)}, u32[]{:S(2)}, u32[]{:S(2)}) collective-permute-start(bf16[320,512]{1,0:T(8,128)(2,1)S(1)} %get-tuple-element.117.rest_0_), channel_id=1, source_target_pairs={{0,2},{1,3},{2,4},{3,5},{4,6},{5,7},{6,0},{7,1},{8,10},{9,11},{10,... | collective-permute-start | bytes 983048 | tf_op jit(solution)/shard_map/ppermute | solution.py:25
  83.1 18.2 %collective-permute-start.26 = (bf16[320,512]{1,0:T(8,128)(2,1)S(1)}, bf16[320,512]{1,0:T(8,128)(2,1)S(1)}, u32[]{:S(2)}, u32[]{:S(2)}) collective-permute-start(bf16[320,512]{1,0:T(8,128)(2,1)S(1)} %get-tuple-element.117.rest_0_), channel_id=1, source_target_pairs={{0,1},{1,0},{2,3},{3,2},{4,5},{5,4},{6,7},{7,6},{8,9},{9,8},{10,11... | collective-permute-start | bytes 983048 | tf_op jit(solution)/shard_map/ppermute | solution.py:25
  99.9 2.1 %collective-permute-start.27 = (bf16[320,512]{1,0:T(8,128)(2,1)S(1)}, bf16[320,512]{1,0:T(8,128)(2,1)S(1)}, u32[]{:S(2)}, u32[]{:S(2)}) collective-permute-start(bf16[320,512]{1,0:T(8,128)(2,1)S(1)} %collective-permute-done.23.rest_1_), channel_id=1, source_target_pairs={{0,1},{1,0},{2,3},{3,2},{4,5},{5,4},{6,7},{7,6},{8,9},{9,8},{10,11... | collective-permute-start | bytes 983048 | tf_op jit(solution)/shard_map/ppermute | solution.py:25
  100.8 1.7 %collective-permute-start.28 = (bf16[320,512]{1,0:T(8,128)(2,1)S(1)}, bf16[320,512]{1,0:T(8,128)(2,1)S(1)}, u32[]{:S(2)}, u32[]{:S(2)}) collective-permute-start(bf16[320,512]{1,0:T(8,128)(2,1)S(1)} %collective-permute-done.24.rest_2_), channel_id=1, source_target_pairs={{0,1},{1,0},{2,3},{3,2},{4,5},{5,4},{6,7},{7,6},{8,9},{9,8},{10,11... | collective-permute-start | bytes 983048 | tf_op jit(solution)/shard_map/ppermute | solution.py:25
  100.8 2.2 %collective-permute-start.29 = (bf16[320,512]{1,0:T(8,128)(2,1)S(1)}, bf16[320,512]{1,0:T(8,128)(2,1)S(1)}, u32[]{:S(2)}, u32[]{:S(2)}) collective-permute-start(bf16[320,512]{1,0:T(8,128)(2,1)S(1)} %collective-permute-done.25.rest_3_), channel_id=1, source_target_pairs={{0,1},{1,0},{2,3},{3,2},{4,5},{5,4},{6,7},{7,6},{8,9},{9,8},{10,11... | collective-permute-start | bytes 983048 | tf_op jit(solution)/shard_map/ppermute | solution.py:25
  (2 other events, 1.3 us)

commit v10 on v9

--- a/solution.py
+++ b/solution.py
@@ -259,13 +259,22 @@
     )(*(map(in_hbm, operands) if far else operands))
 
 
-def coarse_start(coarse_slots, latents, rows, columns):
+def coarse_start(coarse_slots, latents, staged, rows, columns):
     count = coarse_slots.shape[1]
     nodes, features = latents.shape
     size = count + 2 * columns
 
-    def body(slots_away, latents_away, own_ref, last_ref, first_ref, left_ref, right_ref, choose_ref, slots_ref, latents_ref, sems):
+    def body(slots_away, latents_away, *refs):
+        away_refs, refs = refs[: len(staged)], refs[len(staged) :]
+        own_ref, last_ref, first_ref, left_ref, right_ref, choose_ref, *refs = refs
+        here_refs, (slots_ref, latents_ref, sems, later) = refs[: len(staged)], refs[len(staged) :]
+        copies = [
+            pltpu.make_async_copy(away, here, later.at[i])
+            for i, (away, here) in enumerate(zip(away_refs, here_refs, strict=True))
+        ]
         fetch([(slots_away, slots_ref), (latents_away, latents_ref)], sems)
+        for copy in copies:
+            copy.start()
         slot = slots_ref[...]
         row = jnp.floor((slot.astype(jnp.float32) + 0.5) * (1.0 / columns)).astype(jnp.int32)
         at = (slot - row * columns) * rows + row
@@ -282,10 +291,13 @@
         send_rows(dot(choose, latents_ref[...]), own_ref, last_ref, first_ref)
         left_ref[...] = latents_ref[:rows, :]
         right_ref[...] = latents_ref[-rows:, :]
+        for copy in copies:
+            copy.wait()
 
     shapes = (
         *(jax.ShapeDtypeStruct((n, features), jnp.bfloat16) for n in (count, columns, columns, rows, rows)),
         jax.ShapeDtypeStruct((size, nodes), jnp.bfloat16),
+        *(jax.ShapeDtypeStruct(a.shape, a.dtype) for a in staged),
     )
     away = pl.BlockSpec(memory_space=pltpu.HBM)
     held = pl.BlockSpec(memory_space=pltpu.VMEM)
@@ -293,15 +305,16 @@
         body,
         name="coarse_start",
         out_shape=shapes,
-        in_specs=[away] * 2,
+        in_specs=[away] * (2 + len(staged)),
         out_specs=(held,) * len(shapes),
         scratch_shapes=[
             pltpu.VMEM(coarse_slots.shape, jnp.int32),
             pltpu.VMEM(latents.shape, jnp.bfloat16),
             pltpu.SemaphoreType.DMA((2,)),
+            pltpu.SemaphoreType.DMA((len(staged),)),
         ],
         compiler_params=pltpu.CompilerParams(vmem_limit_bytes=4 * MIB),
-    )(*map(in_hbm, (coarse_slots, latents)))
+    )(*map(in_hbm, (coarse_slots, latents, *staged)))
 
 
 def pack_edges(long_edges, senders, receivers, me, coarse_count, devices):
@@ -309,8 +322,7 @@
     blocks = features // TAGS
     slots = devices * CAP
 
-    def body(me_ref, long_away, send_away, recv_away, sent_ref, mine_ref, wide, long_ref, send_ref, recv_ref, sems):
-        fetch([(long_away, long_ref), (send_away, send_ref), (recv_away, recv_ref)], sems)
+    def body(me_ref, long_ref, send_ref, recv_ref, sent_ref, mine_ref, wide):
         send, recv = send_ref[...], recv_ref[...]
         _, owner = table_row(0, 0, recv, coarse_count)
         here = (lax.shift_right_logical(me_ref[0], 3), me_ref[0] & 7)
@@ -353,17 +365,13 @@
         name="pack_edges",
         out_shape=shapes,
         cost_estimate=pl.CostEstimate(flops=12_000_000_000, bytes_accessed=0, transcendentals=0),
-        in_specs=[pl.BlockSpec(memory_space=pltpu.SMEM)] + [pl.BlockSpec(memory_space=pltpu.HBM)] * 3,
+        in_specs=[pl.BlockSpec(memory_space=pltpu.SMEM)] + [pl.BlockSpec(memory_space=pltpu.VMEM)] * 3,
         out_specs=(pl.BlockSpec(memory_space=pltpu.VMEM),) * 2,
         scratch_shapes=[
             pltpu.VMEM((devices * 16, TAGS), jnp.float32),
-            pltpu.VMEM(long_edges.shape, jnp.bfloat16),
-            pltpu.VMEM(senders.shape, jnp.int32),
-            pltpu.VMEM(receivers.shape, jnp.int32),
-            pltpu.SemaphoreType.DMA((3,)),
         ],
         compiler_params=pltpu.CompilerParams(vmem_limit_bytes=8 * MIB),
-    )(me, *map(in_hbm, (long_edges, senders, receivers)))
+    )(me, long_edges, senders, receivers)
 
 
 def unpack_edges(arrived, choose, features, table_rows, coarse_count):
@@ -534,11 +542,13 @@
 
     latents = node_latents.transpose(1, 0, 2).reshape(nodes, features)
     fine = fine_edges.transpose(1, 2, 0, 3).reshape(nodes * degree, features)
-    own, last_row, first_row, to_left, to_right, choose = coarse_start(coarse_slots[None, :], latents, rows, columns)
-    long_edges, own = tie(long_edges, own)
+    staged = (long_edges, long_senders[None, :], long_receivers[None, :])
+    own, last_row, first_row, to_left, to_right, choose, *staged = coarse_start(
+        coarse_slots[None, :], latents, staged, rows, columns
+    )
     own_rows = long_edges
     me = lax.axis_index(AXES).reshape(1)
-    payload, own_tags = pack_edges(long_edges, long_senders[None, :], long_receivers[None, :], me, coarse_count, devices)
+    payload, own_tags = pack_edges(*staged, me, coarse_count, devices)
     for layer in range(layers):
         last = layer == layers - 1
         fars = [along(own, "px", 4 * s) for s in (1, 2, 3)]

time: 109 us -> 109 us (level)
  transfers between devices with their start and end apart: 31 -> 31, of which waited for: 14 -> 14; matrix products, arithmetic and copies ran while one was open for 0% -> 0% of each run, Pallas kernels for 20% -> 19%
where the time goes in v10:
time: 109 us
  starting transfers between devices  43.1 us (40%)
  Pallas kernels  34.6 us (32%)
  waiting for transfers between devices  24.6 us (23%)
  local copies, waits for them, and re-layouts  5.18 us (5%)
    ppermute x14, starting transfers between devices, along(): lax.ppermute(values, axis, [(i, (i + step) % count) for i in range(count)])  20.7 us
    ppermute x14, starting transfers between devices, shift(): return lax.ppermute(values, 'py', pairs)  14.1 us
    pallas_call x2, Pallas kernels, fine_layer(): pl.pallas_call(body, name=f'fine{layer}', out_shape=(jax.ShapeDtypeStruct...  12.6 us
    pallas_call x2, Pallas kernels, coarse_layer(): pl.pallas_call(body, name=f'coarse{layer}', out_shape=tuple(shapes), in_s...  10.8 us
    ppermute x14, waiting for transfers between devices, shift(): return lax.ppermute(values, 'py', pairs)  10.4 us
    all_to_all x1, starting transfers between devices, shards(): lax.all_to_all(packed, AXES, split_axis=0, concat_axis=0, tiled=True)  8.31 us
    unnamed x38, local copies, waits for them, and re-layouts  5.18 us
    ppermute x2, waiting for transfers between devices, around_x(): lax.ppermute(values, 'px', [(i, i // 4 * 4 + (i + step) % 4) for i in ran...  4.8 us
  transfers between devices with their start and end apart: 31, of which 14 were waited for; matrix products, arithmetic and copies ran while one was open for 0% of the time, Pallas kernels for 19%

profile of v10, /device:TPU:1, one launch (start us, length us, event | category | flops | bytes accessed | tf_op | source)
XLA Modules:
  0.0 108.6 jit_solution(3486641253592122504)
XLA Ops:
  0.6 2.0 %coarse_start.1 = (bf16[20,512]{1,0:T(8,128)(2,1)S(1)}, bf16[20,512]{1,0:T(8,128)(2,1)S(1)}, bf16[20,512]{1,0:T(8,128)(2,1)S(1)}, bf16[16,512]{1,0:T(8,128)(2,1)...) custom-call(s32[1,20]{1,0:T(1,128)} %bitcast.26, ...), custom_call_target="tpu_custom_call" | custom-call | tf_op jit(solution)/shard_map/coarse_start/pallas_call | solution.py:304
  2.6 3.6 %collective-permute-start.2 = (bf16[20,512]{1,0:T(8,128)(2,1)S(1)}, bf16[20,512]{1,0:T(8,128)(2,1)S(1)}, u32[]{:S(2)}, u32[]{:S(2)}) collective-permute-start(bf16[20,512]{1,0:T(8,128)(2,1)S(1)} %get-tuple-element.71.own_ref), channel_id=1, source_target_pairs={{0,96},{8,104},{16,112},{24,120},{32,0},{40,8},{48,16},{56,24},{64... | collective-permute-start | bytes 61448 | tf_op jit(solution)/shard_map/ppermute | solution.py:52
  6.6 0.7 collective-permute-start
  7.3 3.0 %collective-permute-start.3 = (bf16[16,512]{1,0:T(8,128)(2,1)S(1)}, bf16[16,512]{1,0:T(8,128)(2,1)S(1)}, u32[]{:S(2)}, u32[]{:S(2)}) collective-permute-start(bf16[16,512]{1,0:T(8,128)(2,1)S(1)} %get-tuple-element.72), channel_id=1, source_target_pairs={{0,1},{1,2},{2,3},{3,4},{4,5},{5,6},{6,7},{7,0},{8,9},{9,10},{10,1... | collective-permute-start | bytes 49160 | tf_op jit(solution)/shard_map/ppermute | solution.py:52
  10.3 1.6 %pack_edges.1 = (bf16[2048,128]{1,0:T(8,128)(2,1)}, bf16[160,128]{1,0:T(8,128)(2,1)S(1)}) custom-call(s32[1]{0:T(128)} %bitcast.5.me_ref, bf16[160,512]{1,0:T(8,128)(2,1)S(1)} %get-tuple-element.74.long_ref, s32[1,160]{1,0:T(1,128)S(1)} %get-tuple-element.75.send_ref, s32[1,160]{1,0:T(1,128)S(1)} %get-tuple-element.76.recv_ref), custom_call_target="tpu_custom_call" | custom-call | flops 12000000000 | tf_op jit(solution)/shard_map/pack_edges/pallas_call | solution.py:363
  11.9 1.6 %collective-permute-done.4.right_ref = bf16[16,512]{1,0:T(8,128)(2,1)S(1)} collective-permute-done((bf16[16,512]{1,0:T(8,128)(2,1)S(1)}, bf16[16,512]{1,0:T(8,128)(2,1)S(1)}, u32[]{:S(2)}, u32[]{:S(2)}) %collective-permute-start.4) | collective-permute-done | bytes 16416 | tf_op jit(solution)/shard_map/ppermute | solution.py:52
  13.6 1.3 %collective-permute-start.6 = (bf16[112,512]{1,0:T(8,128)(2,1)S(1)}, bf16[112,512]{1,0:T(8,128)(2,1)S(1)}, u32[]{:S(2)}, u32[]{:S(2)}) collective-permute-start(bf16[112,512]{1,0:T(8,128)(2,1)S(1)} %get-tuple-element.86), channel_id=1, source_target_pairs={{0,8},{8,16},{16,24},{24,32},{32,40},{40,48},{48,56},{56,64},{64,7... | collective-permute-start | bytes 344072 | tf_op jit(solution)/shard_map/ppermute | solution.py:52
  14.8 3.6 %collective-permute-start.7 = (bf16[112,512]{1,0:T(8,128)(2,1)S(1)}, bf16[112,512]{1,0:T(8,128)(2,1)}, u32[]{:S(2)}, u32[]{:S(2)}) collective-permute-start(bf16[112,512]{1,0:T(8,128)(2,1)S(1)} %get-tuple-element.87), channel_id=1, source_target_pairs={{0,120},{8,0},{16,8},{24,16},{32,24},{40,32},{48,40},{56,48},{64,5... | collective-permute-start | bytes 344072 | tf_op jit(solution)/shard_map/ppermute | solution.py:52
  18.4 8.3 %all-to-all-start = ((bf16[128,16,128]{2,1,0:T(8,128)(2,1)}), bf16[128,16,128]{2,1,0:T(8,128)(2,1)}, u32[]{:S(2)}, u32[]{:S(2)}) async-start(bf16[128,16,128]{2,1,0:T(8,128)(2,1)} %bitcast.8), calls=%async_computation | async-start | bytes 1048576 | tf_op jit(solution)/shard_map/all_to_all | solution.py:562
  26.8 0.6 copy-done.18
  27.4 0.6 copy-done.17
  28.0 1.9 %join_near.2 = (bf16[320,512]{1,0:T(8,128)(2,1)}, bf16[64,512]{1,0:T(8,128)(2,1)}) custom-call(bf16[80,512]{1,0:T(8,128)(2,1)} %copy-done.16, bf16[80,512]{1,0:T(8,128)(2,1)} %copy-done.18, bf16[112,512]{1,0:T(8,128)(2,1)} %copy-done.17, bf16[112,512]{1,0:T(8,128)(2,1)} %collective-permute-done.7.down_ref), custom_call_target="tpu_custom_call" | custom-call | flops 3000000000 | tf_op jit(solution)/shard_map/join_near/pallas_call | solution.py:249
  30.0 3.3 %collective-permute-start.10 = (bf16[320,512]{1,0:T(8,128)(2,1)}, bf16[320,512]{1,0:T(8,128)(2,1)}, u32[]{:S(2)}, u32[]{:S(2)}) collective-permute-start(bf16[320,512]{1,0:T(8,128)(2,1)} %get-tuple-element.90.rest_0_), channel_id=1, source_target_pairs={{0,6},{1,7},{2,0},{3,1},{4,2},{5,3},{6,4},{7,5},{8,14},{9,15},{10,... | collective-permute-start | bytes 983048 | tf_op jit(solution)/shard_map/ppermute | solution.py:25
  33.4 0.8 collective-permute-start.8
  34.2 1.2 %collective-permute-start.11 = (bf16[320,512]{1,0:T(8,128)(2,1)}, bf16[320,512]{1,0:T(8,128)(2,1)}, u32[]{:S(2)}, u32[]{:S(2)}) collective-permute-start(bf16[320,512]{1,0:T(8,128)(2,1)} %get-tuple-element.90.rest_0_), channel_id=1, source_target_pairs={{0,1},{1,0},{2,3},{3,2},{4,5},{5,4},{6,7},{7,6},{8,9},{9,8},{10,11... | collective-permute-start | bytes 983048 | tf_op jit(solution)/shard_map/ppermute | solution.py:25
  35.4 4.7 %all-to-all-done = bf16[128,16,128]{2,1,0:T(8,128)(2,1)} async-done(((bf16[128,16,128]{2,1,0:T(8,128)(2,1)}), bf16[128,16,128]{2,1,0:T(8,128)(2,1)}, u32[]{:S(2)}, u32[]{:S(2)}) %all-to-all-start) | async-done | bytes 524320 | tf_op jit(solution)/shard_map/all_to_all | solution.py:562
  40.2 2.4 %unpack_edges.1 = (bf16[384,512]{1,0:T(8,128)(2,1)S(1)}, bf16[384,2560]{1,0:T(8,128)(2,1)S(1)}, bf16[384,128]{1,0:T(8,128)(2,1)S(1)}, bf16[320,384]{1,0:T(8,128)(2,1)S(1)}) custom-call(bf16[2048,128]{1,0:T(8,128)(2,1)} %bitcast.9.arrived_ref, bf16[60,320]{1,0:T(8,128)(2,1)S(1)} %get-tuple-element.92.choose_ref), custom_call_target="tpu_custom_call" | custom-call | tf_op jit(solution)/shard_map/unpack_edges/pallas_call | solution.py:400
  42.5 0.8 copy-done.12
  43.7 1.5 %copy-done.5 = bf16[16,20,6,512]{3,0,2,1:T(8,128)(2,1)S(1)} copy-done((bf16[16,20,6,512]{3,0,2,1:T(8,128)(2,1)S(1)}, bf16[16,20,6,512]{3,0,2,1:T(8,128)(2,1)}, u32[]{:S(2)}) %copy-start.5) | copy-done | bytes 1966104
  45.3 0.8 copy-done.9
  46.1 0.7 copy-done.11
  46.9 5.9 %fine0.1 = (bf16[1920,512]{1,0:T(8,128)(2,1)S(1)}, f32[320,512]{1,0:T(8,128)S(1)}) custom-call(bf16[1920,512]{1,0:T(8,128)(2,1)S(1)} %bitcast.22, bf16[1920,256]{1,0:T(8,128)(2,1)S(1)} %selection.1.picks_ref, bf16[320,512]{1,0:T(8,128)(2,1)S(1)} %bitcast.20, bf16[16,512]{1,0:T(8,128)(2,1)S(1)} %collective-permute-done.3.left_ref, ...), custom_call_target="tpu_custom_call" | custom-call | tf_op jit(solution)/shard_map/fine0/pallas_call | solution.py:135
  52.8 1.2 %collective-permute-start.12 = (bf16[320,512]{1,0:T(8,128)(2,1)}, bf16[320,512]{1,0:T(8,128)(2,1)S(1)}, u32[]{:S(2)}, u32[]{:S(2)}) collective-permute-start(bf16[320,512]{1,0:T(8,128)(2,1)} %collective-permute-done.8.rest_1_), channel_id=1, source_target_pairs={{0,1},{1,0},{2,3},{3,2},{4,5},{5,4},{6,7},{7,6},{8,9},{9,8},{10,11... | collective-permute-start | bytes 983048 | tf_op jit(solution)/shard_map/ppermute | solution.py:25
  54.5 1.0 collective-permute-done.12.rest_5_
  56.0 0.5 collective-permute-done.14.rest_7_
  56.5 5.3 %coarse0.1 = (bf16[320,512]{1,0:T(8,128)(2,1)S(1)}, bf16[384,512]{1,0:T(8,128)(2,1)S(1)}, bf16[20,512]{1,0:T(8,128)(2,1)S(1)}, bf16[20,512]{1,0:T(8,128)(2,1)S(1...) custom-call(bf16[384,512]{1,0:T(8,128)(2,1)S(1)} %get-tuple-element., ...), custom_call_target="tpu_custom_call" | custom-call | tf_op jit(solution)/shard_map/coarse0/pallas_call | solution.py:478
  61.7 1.0 collective-permute-start.17
  62.7 1.2 %collective-permute-start.16 = (bf16[20,512]{1,0:T(8,128)(2,1)S(1)}, bf16[20,512]{1,0:T(8,128)(2,1)S(1)}, u32[]{:S(2)}, u32[]{:S(2)}) collective-permute-start(bf16[20,512]{1,0:T(8,128)(2,1)S(1)} %get-tuple-element.109.own_ref), channel_id=1, source_target_pairs={{0,64},{8,72},{16,80},{24,88},{32,96},{40,104},{48,112},{56,120},{... | collective-permute-start | bytes 61448 | tf_op jit(solution)/shard_map/ppermute | solution.py:52
  63.9 0.6 collective-permute-start.18
  64.5 0.5 collective-permute-start.19
  65.0 0.7 collective-permute-done.18.left_ref
  65.7 2.3 %collective-permute-done.19.right_ref = bf16[16,512]{1,0:T(8,128)(2,1)S(1)} collective-permute-done((bf16[16,512]{1,0:T(8,128)(2,1)S(1)}, bf16[16,512]{1,0:T(8,128)(2,1)S(1)}, u32[]{:S(2)}, u32[]{:S(2)}) %collective-permute-start.19) | collective-permute-done | bytes 16416 | tf_op jit(solution)/shard_map/ppermute | solution.py:52
  68.1 0.5 collective-permute-start.21
  68.6 4.4 %collective-permute-start.22 = (bf16[112,512]{1,0:T(8,128)(2,1)S(1)}, bf16[112,512]{1,0:T(8,128)(2,1)S(1)}, u32[]{:S(2)}, u32[]{:S(2)}) collective-permute-start(bf16[112,512]{1,0:T(8,128)(2,1)S(1)} %get-tuple-element.116), channel_id=1, source_target_pairs={{0,120},{8,0},{16,8},{24,16},{32,24},{40,32},{48,40},{56,48},{64,5... | collective-permute-start | bytes 344072 | tf_op jit(solution)/shard_map/ppermute | solution.py:52
  73.0 4.8 %collective-permute-done.20.two_ref = bf16[80,512]{1,0:T(8,128)(2,1)S(1)} collective-permute-done((bf16[80,512]{1,0:T(8,128)(2,1)S(1)}, bf16[80,512]{1,0:T(8,128)(2,1)S(1)}, u32[]{:S(2)}, u32[]{:S(2)}) %collective-permute-start.20) | collective-permute-done | bytes 81952 | tf_op jit(solution)/shard_map/ppermute | solution.py:47
  77.8 0.6 join_near.3
  78.3 4.0 %collective-permute-start.25 = (bf16[320,512]{1,0:T(8,128)(2,1)S(1)}, bf16[320,512]{1,0:T(8,128)(2,1)S(1)}, u32[]{:S(2)}, u32[]{:S(2)}) collective-permute-start(bf16[320,512]{1,0:T(8,128)(2,1)S(1)} %get-tuple-element.119.rest_0_), channel_id=1, source_target_pairs={{0,6},{1,7},{2,0},{3,1},{4,2},{5,3},{6,4},{7,5},{8,14},{9,15},{10,... | collective-permute-start | bytes 983048 | tf_op jit(solution)/shard_map/ppermute | solution.py:25
  82.3 0.7 collective-permute-start.23
  83.0 1.0 collective-permute-start.26
  83.9 2.3 %own0.1 = (bf16[160,512]{1,0:T(8,128)(2,1)S(1)}, bf16[704,2560]{1,0:T(8,128)(2,1)S(1)}) custom-call(bf16[160,512]{1,0:T(8,128)(2,1)S(1)} %copy-done.6, bf16[160,128]{1,0:T(8,128)(2,1)S(1)} %copy-done.14, bf16[384,2560]{1,0:T(8,128)(2,1)S(1)} %get-tuple-element.102.sends_ref, bf16[2560,512]{1,0:T(8,128)(2,1)S(1)} %get-tuple-element.126.table_ref, ...), custom_call_target="tpu_custom_call" | custom-call | tf_op jit(solution)/shard_map/own0/pallas_call | solution.py:508
  86.2 6.7 %fine1.1 = (bf16[1920,512]{1,0:T(8,128)(2,1)}, f32[320,512]{1,0:T(8,128)S(1)}) custom-call(bf16[1920,512]{1,0:T(8,128)(2,1)S(1)} %get-tuple-element.120.fine_ref, bf16[1920,256]{1,0:T(8,128)(2,1)S(1)} %selection.1.picks_ref, bf16[320,512]{1,0:T(8,128)(2,1)S(1)} %get-tuple-element.121.latents_ref, bf16[16,512]{1,0:T(8,128)(2,1)S(1)} %collective-permute-done.18.left_ref, ...), custom_call_target="tpu_custom_call" | custom-call | tf_op jit(solution)/shard_map/fine1/pallas_call | solution.py:135
  93.0 3.9 %collective-permute-done.25.rest_3_ = bf16[320,512]{1,0:T(8,128)(2,1)S(1)} collective-permute-done((bf16[320,512]{1,0:T(8,128)(2,1)S(1)}, bf16[320,512]{1,0:T(8,128)(2,1)S(1)}, u32[]{:S(2)}, u32[]{:S(2)}) %collective-permute-start.25) | collective-permute-done | bytes 327712 | tf_op jit(solution)/shard_map/ppermute | solution.py:25
  96.9 3.0 %collective-permute-done.23.rest_1_ = bf16[320,512]{1,0:T(8,128)(2,1)S(1)} collective-permute-done((bf16[320,512]{1,0:T(8,128)(2,1)S(1)}, bf16[320,512]{1,0:T(8,128)(2,1)S(1)}, u32[]{:S(2)}, u32[]{:S(2)}) %collective-permute-start.23) | collective-permute-done | bytes 327712 | tf_op jit(solution)/shard_map/ppermute | solution.py:25
  99.8 0.9 collective-permute-start.27
  100.7 0.5 collective-permute-start.29
  101.2 0.7 collective-permute-done.27.rest_5_
  102.4 0.5 collective-permute-done.29.rest_7_
  102.9 5.6 %coarse1.1 = (bf16[320,512]{1,0:T(8,128)(2,1)}, bf16[160,512]{1,0:T(8,128)(2,1)}) custom-call(bf16[384,512]{1,0:T(8,128)(2,1)S(1)} %get-tuple-element.129.long_ref, bf16[160,512]{1,0:T(8,128)(2,1)S(1)} %get-tuple-element.130.own_ref, bf16[704,2560]{1,0:T(8,128)(2,1)S(1)} %get-tuple-element.131.sends_ref, bf16[384,128]{1,0:T(8,128)(2,1)S(1)} %get-tuple-element.103.recvs_ref, ...), custom_call_target="tpu_custom_call" | custom-call | tf_op jit(solution)/shard_map/coarse1/pallas_call | solution.py:478
  (65 shorter events, 2.6 us)
Async XLA Ops:
  2.6 10.9 %collective-permute-start.2 = (bf16[20,512]{1,0:T(8,128)(2,1)S(1)}, bf16[20,512]{1,0:T(8,128)(2,1)S(1)}, u32[]{:S(2)}, u32[]{:S(2)}) collective-permute-start(bf16[20,512]{1,0:T(8,128)(2,1)S(1)} %get-tuple-element.71.own_ref), channel_id=1, source_target_pairs={{0,96},{8,104},{16,112},{24,120},{32,0},{40,8},{48,16},{56,24},{64... | collective-permute-start | bytes 61448 | tf_op jit(solution)/shard_map/ppermute | solution.py:52
  6.2 7.3 %collective-permute-start.1 = (bf16[20,512]{1,0:T(8,128)(2,1)S(1)}, bf16[20,512]{1,0:T(8,128)(2,1)S(1)}, u32[]{:S(2)}, u32[]{:S(2)}) collective-permute-start(bf16[20,512]{1,0:T(8,128)(2,1)S(1)} %get-tuple-element.71.own_ref), channel_id=1, source_target_pairs={{0,64},{8,72},{16,80},{24,88},{32,96},{40,104},{48,112},{56,120},{... | collective-permute-start | bytes 61448 | tf_op jit(solution)/shard_map/ppermute | solution.py:52
  6.6 6.9 %collective-permute-start = (bf16[20,512]{1,0:T(8,128)(2,1)S(1)}, bf16[20,512]{1,0:T(8,128)(2,1)S(1)}, u32[]{:S(2)}, u32[]{:S(2)}) collective-permute-start(bf16[20,512]{1,0:T(8,128)(2,1)S(1)} %get-tuple-element.71.own_ref), channel_id=1, source_target_pairs={{0,32},{8,40},{16,48},{24,56},{32,64},{40,72},{48,80},{56,88},{64,... | collective-permute-start | bytes 61448 | tf_op jit(solution)/shard_map/ppermute | solution.py:52
  7.3 4.6 %collective-permute-start.3 = (bf16[16,512]{1,0:T(8,128)(2,1)S(1)}, bf16[16,512]{1,0:T(8,128)(2,1)S(1)}, u32[]{:S(2)}, u32[]{:S(2)}) collective-permute-start(bf16[16,512]{1,0:T(8,128)(2,1)S(1)} %get-tuple-element.72), channel_id=1, source_target_pairs={{0,1},{1,2},{2,3},{3,4},{4,5},{5,6},{6,7},{7,0},{8,9},{9,10},{10,1... | collective-permute-start | bytes 49160 | tf_op jit(solution)/shard_map/ppermute | solution.py:52
  10.3 3.2 %collective-permute-start.4 = (bf16[16,512]{1,0:T(8,128)(2,1)S(1)}, bf16[16,512]{1,0:T(8,128)(2,1)S(1)}, u32[]{:S(2)}, u32[]{:S(2)}) collective-permute-start(bf16[16,512]{1,0:T(8,128)(2,1)S(1)} %get-tuple-element.73), channel_id=1, source_target_pairs={{0,7},{1,0},{2,1},{3,2},{4,3},{5,4},{6,5},{7,6},{8,15},{9,8},{10,9... | collective-permute-start | bytes 49160 | tf_op jit(solution)/shard_map/ppermute | solution.py:52
  11.9 14.9 %copy-start.13 = (bf16[160,128]{1,0:T(8,128)(2,1)}, bf16[160,128]{1,0:T(8,128)(2,1)S(1)}, u32[]{:S(2)}) copy-start(bf16[160,128]{1,0:T(8,128)(2,1)S(1)} %get-tuple-element.125.tags_ref) | copy-start | bytes 122884
  13.5 13.3 %copy-start.10 = (bf16[16,512]{1,0:T(8,128)(2,1)}, bf16[16,512]{1,0:T(8,128)(2,1)S(1)}, u32[]{:S(2)}) copy-start(bf16[16,512]{1,0:T(8,128)(2,1)S(1)} %collective-permute-done.4.right_ref) | copy-start | bytes 49156
  13.5 13.3 %copy-start.16 = (bf16[80,512]{1,0:T(8,128)(2,1)}, bf16[80,512]{1,0:T(8,128)(2,1)S(1)}, u32[]{:S(2)}) copy-start(bf16[80,512]{1,0:T(8,128)(2,1)S(1)} %get-tuple-element.85.own_ref) | copy-start | bytes 245764
  13.6 13.2 %collective-permute-start.6 = (bf16[112,512]{1,0:T(8,128)(2,1)S(1)}, bf16[112,512]{1,0:T(8,128)(2,1)S(1)}, u32[]{:S(2)}, u32[]{:S(2)}) collective-permute-start(bf16[112,512]{1,0:T(8,128)(2,1)S(1)} %get-tuple-element.86), channel_id=1, source_target_pairs={{0,8},{8,16},{16,24},{24,32},{32,40},{40,48},{48,56},{56,64},{64,7... | collective-permute-start | bytes 344072 | tf_op jit(solution)/shard_map/ppermute | solution.py:52
  14.8 13.2 %collective-permute-start.7 = (bf16[112,512]{1,0:T(8,128)(2,1)S(1)}, bf16[112,512]{1,0:T(8,128)(2,1)}, u32[]{:S(2)}, u32[]{:S(2)}) collective-permute-start(bf16[112,512]{1,0:T(8,128)(2,1)S(1)} %get-tuple-element.87), channel_id=1, source_target_pairs={{0,120},{8,0},{16,8},{24,16},{32,24},{40,32},{48,40},{56,48},{64,5... | collective-permute-start | bytes 344072 | tf_op jit(solution)/shard_map/ppermute | solution.py:52
  18.4 8.3 %collective-permute-start.5 = (bf16[80,512]{1,0:T(8,128)(2,1)S(1)}, bf16[80,512]{1,0:T(8,128)(2,1)S(1)}, u32[]{:S(2)}, u32[]{:S(2)}) collective-permute-start(bf16[80,512]{1,0:T(8,128)(2,1)S(1)} %get-tuple-element.85.own_ref), channel_id=1, source_target_pairs={{0,16},{8,24},{16,0},{24,8},{32,48},{40,56},{48,32},{56,40},{64,80... | collective-permute-start | bytes 245768 | tf_op jit(solution)/shard_map/ppermute | solution.py:47
  18.4 21.7 %all-to-all-start = ((bf16[128,16,128]{2,1,0:T(8,128)(2,1)}), bf16[128,16,128]{2,1,0:T(8,128)(2,1)}, u32[]{:S(2)}, u32[]{:S(2)}) async-start(bf16[128,16,128]{2,1,0:T(8,128)(2,1)} %bitcast.8), calls=%async_computation | async-start | bytes 1048576 | tf_op jit(solution)/shard_map/all_to_all | solution.py:562
  26.7 17.0 %copy-start.4 = (bf16[16,20,512]{2,0,1:T(8,128)(2,1)S(1)}, bf16[16,20,512]{2,0,1:T(8,128)(2,1)}, u32[]{:S(2)}) copy-start(bf16[16,20,512]{2,0,1:T(8,128)(2,1)} %param.13) | copy-start | bytes 983044
  26.7 17.0 %copy-start.8 = (f32[2,512]{1,0:T(2,128)S(1)}, f32[2,512]{1,0:T(2,128)}, u32[]{:S(2)}) copy-start(f32[2,512]{1,0:T(2,128)} %eg_ref.5) | copy-start | bytes 12292
  28.0 15.7 %copy-start = (bf16[2,1536,512]{2,1,0:T(8,128)(2,1)S(1)}, bf16[2,1536,512]{2,1,0:T(8,128)(2,1)}, u32[]{:S(2)}) copy-start(bf16[2,1536,512]{2,1,0:T(8,128)(2,1)} %ei_ref.5) | copy-start | bytes 9437188
  30.0 22.7 %collective-permute-start.10 = (bf16[320,512]{1,0:T(8,128)(2,1)}, bf16[320,512]{1,0:T(8,128)(2,1)}, u32[]{:S(2)}, u32[]{:S(2)}) collective-permute-start(bf16[320,512]{1,0:T(8,128)(2,1)} %get-tuple-element.90.rest_0_), channel_id=1, source_target_pairs={{0,6},{1,7},{2,0},{3,1},{4,2},{5,3},{6,4},{7,5},{8,14},{9,15},{10,... | collective-permute-start | bytes 983048 | tf_op jit(solution)/shard_map/ppermute | solution.py:25
  33.3 19.4 %collective-permute-start.9 = (bf16[320,512]{1,0:T(8,128)(2,1)}, bf16[320,512]{1,0:T(8,128)(2,1)}, u32[]{:S(2)}, u32[]{:S(2)}) collective-permute-start(bf16[320,512]{1,0:T(8,128)(2,1)} %get-tuple-element.90.rest_0_), channel_id=1, source_target_pairs={{0,4},{1,5},{2,6},{3,7},{4,0},{5,1},{6,2},{7,3},{8,12},{9,13},{10,... | collective-permute-start | bytes 983048 | tf_op jit(solution)/shard_map/ppermute | solution.py:25
  33.4 19.3 %collective-permute-start.8 = (bf16[320,512]{1,0:T(8,128)(2,1)}, bf16[320,512]{1,0:T(8,128)(2,1)}, u32[]{:S(2)}, u32[]{:S(2)}) collective-permute-start(bf16[320,512]{1,0:T(8,128)(2,1)} %get-tuple-element.90.rest_0_), channel_id=1, source_target_pairs={{0,2},{1,3},{2,4},{3,5},{4,6},{5,7},{6,0},{7,1},{8,10},{9,11},{10,... | collective-permute-start | bytes 983048 | tf_op jit(solution)/shard_map/ppermute | solution.py:25
  34.2 20.3 %collective-permute-start.11 = (bf16[320,512]{1,0:T(8,128)(2,1)}, bf16[320,512]{1,0:T(8,128)(2,1)}, u32[]{:S(2)}, u32[]{:S(2)}) collective-permute-start(bf16[320,512]{1,0:T(8,128)(2,1)} %get-tuple-element.90.rest_0_), channel_id=1, source_target_pairs={{0,1},{1,0},{2,3},{3,2},{4,5},{5,4},{6,7},{7,6},{8,9},{9,8},{10,11... | collective-permute-start | bytes 983048 | tf_op jit(solution)/shard_map/ppermute | solution.py:25
  40.2 3.6 %copy-start.1 = (bf16[2,512,512]{2,1,0:T(8,128)(2,1)S(1)}, bf16[2,512,512]{2,1,0:T(8,128)(2,1)}, u32[]{:S(2)}) copy-start(bf16[2,512,512]{2,1,0:T(8,128)(2,1)} %eo_ref.5) | copy-start | bytes 3145732
  42.5 0.8 copy-start.12
  43.7 1.5 %copy-start.5 = (bf16[16,20,6,512]{3,0,2,1:T(8,128)(2,1)S(1)}, bf16[16,20,6,512]{3,0,2,1:T(8,128)(2,1)}, u32[]{:S(2)}) copy-start(bf16[16,20,6,512]{3,0,2,1:T(8,128)(2,1)} %param.14) | copy-start | bytes 5898244
  45.3 0.8 copy-start.9
  46.1 0.7 copy-start.11
  46.8 9.6 %copy-start.2 = (bf16[2,1024,512]{2,1,0:T(8,128)(2,1)S(1)}, bf16[2,1024,512]{2,1,0:T(8,128)(2,1)}, u32[]{:S(2)}) copy-start(bf16[2,1024,512]{2,1,0:T(8,128)(2,1)} %ni_ref.3) | copy-start | bytes 6291460
  46.8 9.6 %copy-start.3 = (bf16[2,512,512]{2,1,0:T(8,128)(2,1)S(1)}, bf16[2,512,512]{2,1,0:T(8,128)(2,1)}, u32[]{:S(2)}) copy-start(bf16[2,512,512]{2,1,0:T(8,128)(2,1)} %no_ref.3) | copy-start | bytes 3145732
  46.8 9.6 %copy-start.6 = (bf16[160,512]{1,0:T(8,128)(2,1)S(1)}, bf16[160,512]{1,0:T(8,128)(2,1)}, u32[]{:S(2)}) copy-start(bf16[160,512]{1,0:T(8,128)(2,1)} %long_ref) | copy-start | bytes 491524
  46.8 9.6 %copy-start.7 = (bf16[320,512]{1,0:T(8,128)(2,1)S(1)}, bf16[320,512]{1,0:T(8,128)(2,1)}, u32[]{:S(2)}) copy-start(bf16[320,512]{1,0:T(8,128)(2,1)} %get-tuple-element.90.rest_0_) | copy-start | bytes 983044
  46.9 9.6 %copy-start.15 = (f32[2,512]{1,0:T(2,128)S(1)}, f32[2,512]{1,0:T(2,128)}, u32[]{:S(2)}) copy-start(f32[2,512]{1,0:T(2,128)} %ng_ref.3) | copy-start | bytes 12292
  52.8 2.7 %collective-permute-start.12 = (bf16[320,512]{1,0:T(8,128)(2,1)}, bf16[320,512]{1,0:T(8,128)(2,1)S(1)}, u32[]{:S(2)}, u32[]{:S(2)}) collective-permute-start(bf16[320,512]{1,0:T(8,128)(2,1)} %collective-permute-done.8.rest_1_), channel_id=1, source_target_pairs={{0,1},{1,0},{2,3},{3,2},{4,5},{5,4},{6,7},{7,6},{8,9},{9,8},{10,11... | collective-permute-start | bytes 983048 | tf_op jit(solution)/shard_map/ppermute | solution.py:25
  54.0 1.9 %collective-permute-start.13 = (bf16[320,512]{1,0:T(8,128)(2,1)}, bf16[320,512]{1,0:T(8,128)(2,1)S(1)}, u32[]{:S(2)}, u32[]{:S(2)}) collective-permute-start(bf16[320,512]{1,0:T(8,128)(2,1)} %collective-permute-done.9.rest_2_), channel_id=1, source_target_pairs={{0,1},{1,0},{2,3},{3,2},{4,5},{5,4},{6,7},{7,6},{8,9},{9,8},{10,11... | collective-permute-start | bytes 983048 | tf_op jit(solution)/shard_map/ppermute | solution.py:25
  54.1 2.3 %collective-permute-start.14 = (bf16[320,512]{1,0:T(8,128)(2,1)}, bf16[320,512]{1,0:T(8,128)(2,1)S(1)}, u32[]{:S(2)}, u32[]{:S(2)}) collective-permute-start(bf16[320,512]{1,0:T(8,128)(2,1)} %collective-permute-done.10.rest_3_), channel_id=1, source_target_pairs={{0,1},{1,0},{2,3},{3,2},{4,5},{5,4},{6,7},{7,6},{8,9},{9,8},{10,11... | collective-permute-start | bytes 983048 | tf_op jit(solution)/shard_map/ppermute | solution.py:25
  61.7 6.2 %collective-permute-start.17 = (bf16[20,512]{1,0:T(8,128)(2,1)S(1)}, bf16[20,512]{1,0:T(8,128)(2,1)S(1)}, u32[]{:S(2)}, u32[]{:S(2)}) collective-permute-start(bf16[20,512]{1,0:T(8,128)(2,1)S(1)} %get-tuple-element.109.own_ref), channel_id=1, source_target_pairs={{0,96},{8,104},{16,112},{24,120},{32,0},{40,8},{48,16},{56,24},{64... | collective-permute-start | bytes 61448 | tf_op jit(solution)/shard_map/ppermute | solution.py:52
  62.7 5.3 %collective-permute-start.16 = (bf16[20,512]{1,0:T(8,128)(2,1)S(1)}, bf16[20,512]{1,0:T(8,128)(2,1)S(1)}, u32[]{:S(2)}, u32[]{:S(2)}) collective-permute-start(bf16[20,512]{1,0:T(8,128)(2,1)S(1)} %get-tuple-element.109.own_ref), channel_id=1, source_target_pairs={{0,64},{8,72},{16,80},{24,88},{32,96},{40,104},{48,112},{56,120},{... | collective-permute-start | bytes 61448 | tf_op jit(solution)/shard_map/ppermute | solution.py:52
  63.9 4.2 %collective-permute-start.15 = (bf16[20,512]{1,0:T(8,128)(2,1)S(1)}, bf16[20,512]{1,0:T(8,128)(2,1)S(1)}, u32[]{:S(2)}, u32[]{:S(2)}) collective-permute-start(bf16[20,512]{1,0:T(8,128)(2,1)S(1)} %get-tuple-element.109.own_ref), channel_id=1, source_target_pairs={{0,32},{8,40},{16,48},{24,56},{32,64},{40,72},{48,80},{56,88},{64,... | collective-permute-start | bytes 61448 | tf_op jit(solution)/shard_map/ppermute | solution.py:52
  63.9 1.8 %collective-permute-start.18 = (bf16[16,512]{1,0:T(8,128)(2,1)S(1)}, bf16[16,512]{1,0:T(8,128)(2,1)S(1)}, u32[]{:S(2)}, u32[]{:S(2)}) collective-permute-start(bf16[16,512]{1,0:T(8,128)(2,1)S(1)} %get-tuple-element.110), channel_id=1, source_target_pairs={{0,1},{1,2},{2,3},{3,4},{4,5},{5,6},{6,7},{7,0},{8,9},{9,10},{10,1... | collective-permute-start | bytes 49160 | tf_op jit(solution)/shard_map/ppermute | solution.py:52
  64.5 3.5 %collective-permute-start.19 = (bf16[16,512]{1,0:T(8,128)(2,1)S(1)}, bf16[16,512]{1,0:T(8,128)(2,1)S(1)}, u32[]{:S(2)}, u32[]{:S(2)}) collective-permute-start(bf16[16,512]{1,0:T(8,128)(2,1)S(1)} %get-tuple-element.111), channel_id=1, source_target_pairs={{0,7},{1,0},{2,1},{3,2},{4,3},{5,4},{6,5},{7,6},{8,15},{9,8},{10,9... | collective-permute-start | bytes 49160 | tf_op jit(solution)/shard_map/ppermute | solution.py:52
  68.1 9.7 %collective-permute-start.21 = (bf16[112,512]{1,0:T(8,128)(2,1)S(1)}, bf16[112,512]{1,0:T(8,128)(2,1)S(1)}, u32[]{:S(2)}, u32[]{:S(2)}) collective-permute-start(bf16[112,512]{1,0:T(8,128)(2,1)S(1)} %get-tuple-element.115), channel_id=1, source_target_pairs={{0,8},{8,16},{16,24},{24,32},{32,40},{40,48},{48,56},{56,64},{64,7... | collective-permute-start | bytes 344072 | tf_op jit(solution)/shard_map/ppermute | solution.py:52
  68.6 9.2 %collective-permute-start.22 = (bf16[112,512]{1,0:T(8,128)(2,1)S(1)}, bf16[112,512]{1,0:T(8,128)(2,1)S(1)}, u32[]{:S(2)}, u32[]{:S(2)}) collective-permute-start(bf16[112,512]{1,0:T(8,128)(2,1)S(1)} %get-tuple-element.116), channel_id=1, source_target_pairs={{0,120},{8,0},{16,8},{24,16},{32,24},{40,32},{48,40},{56,48},{64,5... | collective-permute-start | bytes 344072 | tf_op jit(solution)/shard_map/ppermute | solution.py:52
  73.0 11.0 %copy-start.14 = (bf16[160,128]{1,0:T(8,128)(2,1)S(1)}, bf16[160,128]{1,0:T(8,128)(2,1)}, u32[]{:S(2)}) copy-start(bf16[160,128]{1,0:T(8,128)(2,1)} %copy-done.13) | copy-start | bytes 122884
  73.0 4.8 %collective-permute-start.20 = (bf16[80,512]{1,0:T(8,128)(2,1)S(1)}, bf16[80,512]{1,0:T(8,128)(2,1)S(1)}, u32[]{:S(2)}, u32[]{:S(2)}) collective-permute-start(bf16[80,512]{1,0:T(8,128)(2,1)S(1)} %get-tuple-element.114.own_ref), channel_id=1, source_target_pairs={{0,16},{8,24},{16,0},{24,8},{32,48},{40,56},{48,32},{56,40},{64,80... | collective-permute-start | bytes 245768 | tf_op jit(solution)/shard_map/ppermute | solution.py:47
  78.3 18.5 %collective-permute-start.25 = (bf16[320,512]{1,0:T(8,128)(2,1)S(1)}, bf16[320,512]{1,0:T(8,128)(2,1)S(1)}, u32[]{:S(2)}, u32[]{:S(2)}) collective-permute-start(bf16[320,512]{1,0:T(8,128)(2,1)S(1)} %get-tuple-element.119.rest_0_), channel_id=1, source_target_pairs={{0,6},{1,7},{2,0},{3,1},{4,2},{5,3},{6,4},{7,5},{8,14},{9,15},{10,... | collective-permute-start | bytes 983048 | tf_op jit(solution)/shard_map/ppermute | solution.py:25
  82.3 14.6 %collective-permute-start.24 = (bf16[320,512]{1,0:T(8,128)(2,1)S(1)}, bf16[320,512]{1,0:T(8,128)(2,1)S(1)}, u32[]{:S(2)}, u32[]{:S(2)}) collective-permute-start(bf16[320,512]{1,0:T(8,128)(2,1)S(1)} %get-tuple-element.119.rest_0_), channel_id=1, source_target_pairs={{0,4},{1,5},{2,6},{3,7},{4,0},{5,1},{6,2},{7,3},{8,12},{9,13},{10,... | collective-permute-start | bytes 983048 | tf_op jit(solution)/shard_map/ppermute | solution.py:25
  82.3 17.5 %collective-permute-start.23 = (bf16[320,512]{1,0:T(8,128)(2,1)S(1)}, bf16[320,512]{1,0:T(8,128)(2,1)S(1)}, u32[]{:S(2)}, u32[]{:S(2)}) collective-permute-start(bf16[320,512]{1,0:T(8,128)(2,1)S(1)} %get-tuple-element.119.rest_0_), channel_id=1, source_target_pairs={{0,2},{1,3},{2,4},{3,5},{4,6},{5,7},{6,0},{7,1},{8,10},{9,11},{10,... | collective-permute-start | bytes 983048 | tf_op jit(solution)/shard_map/ppermute | solution.py:25
  83.0 18.2 %collective-permute-start.26 = (bf16[320,512]{1,0:T(8,128)(2,1)S(1)}, bf16[320,512]{1,0:T(8,128)(2,1)S(1)}, u32[]{:S(2)}, u32[]{:S(2)}) collective-permute-start(bf16[320,512]{1,0:T(8,128)(2,1)S(1)} %get-tuple-element.119.rest_0_), channel_id=1, source_target_pairs={{0,1},{1,0},{2,3},{3,2},{4,5},{5,4},{6,7},{7,6},{8,9},{9,8},{10,11... | collective-permute-start | bytes 983048 | tf_op jit(solution)/shard_map/ppermute | solution.py:25
  99.8 2.1 %collective-permute-start.27 = (bf16[320,512]{1,0:T(8,128)(2,1)S(1)}, bf16[320,512]{1,0:T(8,128)(2,1)S(1)}, u32[]{:S(2)}, u32[]{:S(2)}) collective-permute-start(bf16[320,512]{1,0:T(8,128)(2,1)S(1)} %collective-permute-done.23.rest_1_), channel_id=1, source_target_pairs={{0,1},{1,0},{2,3},{3,2},{4,5},{5,4},{6,7},{7,6},{8,9},{9,8},{10,11... | collective-permute-start | bytes 983048 | tf_op jit(solution)/shard_map/ppermute | solution.py:25
  100.7 1.7 %collective-permute-start.28 = (bf16[320,512]{1,0:T(8,128)(2,1)S(1)}, bf16[320,512]{1,0:T(8,128)(2,1)S(1)}, u32[]{:S(2)}, u32[]{:S(2)}) collective-permute-start(bf16[320,512]{1,0:T(8,128)(2,1)S(1)} %collective-permute-done.24.rest_2_), channel_id=1, source_target_pairs={{0,1},{1,0},{2,3},{3,2},{4,5},{5,4},{6,7},{7,6},{8,9},{9,8},{10,11... | collective-permute-start | bytes 983048 | tf_op jit(solution)/shard_map/ppermute | solution.py:25
  100.7 2.2 %collective-permute-start.29 = (bf16[320,512]{1,0:T(8,128)(2,1)S(1)}, bf16[320,512]{1,0:T(8,128)(2,1)S(1)}, u32[]{:S(2)}, u32[]{:S(2)}) collective-permute-start(bf16[320,512]{1,0:T(8,128)(2,1)S(1)} %collective-permute-done.25.rest_3_), channel_id=1, source_target_pairs={{0,1},{1,0},{2,3},{3,2},{4,5},{5,4},{6,7},{7,6},{8,9},{9,8},{10,11... | collective-permute-start | bytes 983048 | tf_op jit(solution)/shard_map/ppermute | solution.py:25
  (2 other events, 1.3 us)
